TPU v7x, 128 devices: a whole 4x4x4 slice. The times are simulated.
128 devices in a mesh: dp: 64 (over x, y_hi, z, core), tensor: 2 (over y_lo).
Axes of the slice: x: 4, y: 4 (y_hi: 2, y_lo: 2; y = y_hi * 2 + y_lo), z: 4, core: 2. Of those that a mesh axis runs over, the one named last changes fastest.
Arguments:
- hidden_in: bfloat16 [16384, 2048], P(('dp', 'tensor')), may hold values from -6 to 6
- doc_ids: int32 [64, 256], P('dp'), may hold values from 0 to 2, never falling along the last dimension, each value on 1 to 192 neighbouring positions
- expert_ids: int32 [16384, 8], P(('dp', 'tensor')), may hold values from 0 to 127, all different within a row; in each aligned block of 128 rows (0 to 127, 128 to 255, ...) at most 8 rows name the same one
- attn_gain: float32 [2048], replicated, may hold values from 0.1 to 1.9
- query_weight: bfloat16 [2048, 4096], P('dp', 'tensor'), may hold values from -0.125 to 0.125
- key_weight: bfloat16 [2048, 512], P('dp', 'tensor'), may hold values from -0.125 to 0.125
- value_weight: bfloat16 [2048, 512], P('dp', 'tensor'), may hold values from -0.125 to 0.125
- output_weight: bfloat16 [4096, 2048], P('tensor', 'dp'), may hold values from -0.75 to 0.75
- query_gain: float32 [128], replicated, may hold values from 0.1 to 1.9
- key_gain: float32 [128], replicated, may hold values from 0.1 to 1.9
- moe_gain: float32 [2048], replicated, may hold values from 0.1 to 1.9
- router_weight: bfloat16 [2048, 128], replicated, may hold values from -0.0625 to 0.0625
- gate_weight: bfloat16 [128, 2048, 768], P(('dp', 'tensor')), may hold values from -0.125 to 0.125
- up_weight: bfloat16 [128, 2048, 768], P(('dp', 'tensor')), may hold values from -0.125 to 0.125
- down_weight: bfloat16 [128, 768, 2048], P(('dp', 'tensor')), may hold values from -0.625 to 0.625
- cotangent: bfloat16 [16384, 2048], P(('dp', 'tensor')), may hold values from -6 to 6
Outputs:
- layer_out: bfloat16 [16384, 2048], P(('dp', 'tensor'))
- input_grad: float32 [16384, 2048], P(('dp', 'tensor'))
- attngain_grad: float32 [2048], replicated
- qweight_grad: float32 [2048, 4096], P('dp', 'tensor')
- kweight_grad: float32 [2048, 512], P('dp', 'tensor')
- vweight_grad: float32 [2048, 512], P('dp', 'tensor')
- oweight_grad: float32 [4096, 2048], P('tensor', 'dp')
- qgain_grad: float32 [128], replicated
- kgain_grad: float32 [128], replicated
- moegain_grad: float32 [2048], replicated
- router_grad: float32 [2048, 128], replicated
- gate_grad: float32 [128, 2048, 768], P(('dp', 'tensor'))
- up_grad: float32 [128, 2048, 768], P(('dp', 'tensor'))
- down_grad: float32 [128, 768, 2048], P(('dp', 'tensor'))
Inputs may be any that keep to these rules, and one draw needn't show every extreme that they name: `doc_ids`: each row is one group of 256 tokens: 3 sequences, ids never falling, each 1 to 192 tokens long, one exactly 192. `expert_ids`: each row names 8 different experts; in the 128 rows of one device every expert is named exactly 8 times.
All inputs are finite; a program needn't handle non-finite values.
Results may differ from a plain program's by a relative error of at most 0.023.
Values may be sent and summed in bfloat16 or wider, within the bound.
A program may use at most 192 MiB of HBM per device.

v0:
```python
import math

import jax
import jax.numpy as jnp
from jax import lax
from jax.sharding import PartitionSpec as P

BLOCK = 128


EPSILON = 1e-06
ROPE_BASE = 1000000.0
MASKED = -1e30


def dot_inner(first_op, second_op):
    return lax.dot_general(
        first_op, second_op, (((1,), (1,)), ((), ())), preferred_element_type=jnp.float32
    )


def dot_outer(first_op, second_op):
    return lax.dot_general(
        first_op, second_op, (((0,), (0,)), ((), ())), preferred_element_type=jnp.float32
    )


def plain_dot(first_op, second_op):
    return jnp.dot(first_op, second_op, preferred_element_type=jnp.float32)


def rms_scale(values, norm_gain):
    return (
        values * lax.rsqrt(jnp.mean(values * values, axis=-1, keepdims=True) + EPSILON) * norm_gain
    )


def rms_back(values, norm_gain, upstream):
    reciprocal = lax.rsqrt(jnp.mean(values * values, axis=-1, keepdims=True) + EPSILON)
    scaled = upstream * norm_gain
    inner_mean = jnp.mean(scaled * values, axis=-1, keepdims=True)
    grad_values = reciprocal * scaled - values * reciprocal * reciprocal * reciprocal * inner_mean
    grad_gain = jnp.sum(upstream * values * reciprocal, axis=0)
    return (grad_values, grad_gain)


def rotate(values, cosine, sine_table):
    half_size = values.shape[-1] // 2
    leading = values[..., :half_size]
    trailing = values[..., half_size:]
    return jnp.concatenate(
        [leading * cosine - trailing * sine_table, trailing * cosine + leading * sine_table],
        axis=-1,
    )


def layout(doc_row):
    length = doc_row.shape[0]
    indices = jnp.arange(length, dtype=jnp.int32)
    same_doc = doc_row[:, None] == doc_row[None, :]
    earlier = indices[None, :] < indices[:, None]
    position = jnp.sum(jnp.where(same_doc & earlier, 1, 0), axis=1).astype(jnp.int32)
    blocks = position // BLOCK
    allowed = same_doc & (blocks[None, :] <= blocks[:, None])
    return (position, allowed)


def rotary(position, head_size):
    half_size = head_size // 2
    frequency = jnp.exp(
        -jnp.log(ROPE_BASE) * jnp.arange(half_size, dtype=jnp.float32) * 2.0 / head_size
    )
    angles = position.astype(jnp.float32)[:, None] * frequency[None, :]
    return (jnp.cos(angles)[:, None, :], jnp.sin(angles)[:, None, :])


def block_scores(query_block, key_rows, allowed_block, score_scale):
    products = (
        jnp.einsum("qkgd,tkd->kgqt", query_block, key_rows, preferred_element_type=jnp.float32)
        * score_scale
    )
    return jnp.where(allowed_block[None, None], products, MASKED)


def on_device(
    hidden_in,
    doc_ids,
    expert_ids,
    attn_gain,
    query_weight,
    key_weight,
    value_weight,
    output_weight,
    query_gain,
    key_gain,
    moe_gain,
    router_weight,
    gate_weight,
    up_weight,
    down_weight,
    cotangent,
):
    tok_dev, model_width = hidden_in.shape
    head_size = query_gain.shape[0]
    kv_local = key_weight.shape[1] // head_size
    heads_local = query_weight.shape[1] // head_size
    group_size = heads_local // kv_local
    expert_count = router_weight.shape[1]
    route_count = expert_ids.shape[1]
    capacity = tok_dev * route_count // expert_count
    assign_count = tok_dev * route_count
    score_scale = 1.0 / math.sqrt(head_size)
    doc_row = doc_ids[0]
    group_tokens = doc_row.shape[0]
    block_rows = min(512, group_tokens)
    block_count = group_tokens // block_rows
    hidden = hidden_in.astype(jnp.float32)
    normed_local = rms_scale(hidden, attn_gain).astype(jnp.bfloat16)
    normed = lax.all_gather(normed_local, "tensor", axis=0, tiled=True)
    query_full, key_full, value_full, output_full = (
        lax.all_gather(query_weight, "dp", axis=0, tiled=True),
        lax.all_gather(key_weight, "dp", axis=0, tiled=True),
        lax.all_gather(value_weight, "dp", axis=0, tiled=True),
        lax.all_gather(output_weight, "dp", axis=1, tiled=True),
    )
    position, allowed = layout(doc_row)
    cosine, sine_table = rotary(position, head_size)

    def shape_heads(projected, norm_gain):
        return rotate(
            rms_scale(projected.reshape(group_tokens, -1, head_size), norm_gain), cosine, sine_table
        )

    query_rot, query_pull = jax.vjp(shape_heads, plain_dot(normed, query_full), query_gain)
    key_rot, key_pull = jax.vjp(shape_heads, plain_dot(normed, key_full), key_gain)
    value_rows = (
        plain_dot(normed, value_full)
        .astype(jnp.bfloat16)
        .reshape(group_tokens, kv_local, head_size)
    )
    query_low = query_rot.astype(jnp.bfloat16).reshape(
        block_count, block_rows, kv_local, group_size, head_size
    )
    key_low = key_rot.astype(jnp.bfloat16)
    allowed_blocks = allowed.reshape(block_count, block_rows, group_tokens)

    def forward_block(pieces):
        query_block, allowed_block = pieces
        scores = block_scores(query_block, key_low, allowed_block, score_scale)
        row_peak = jnp.max(scores, axis=-1, keepdims=True)
        totals = jnp.sum(jnp.exp(scores - row_peak), axis=-1, keepdims=True)
        logsum = row_peak + jnp.log(totals)
        attention_low = jnp.exp(scores - logsum).astype(jnp.bfloat16)
        mixed_block = jnp.einsum(
            "kgqt,tkd->qkgd", attention_low, value_rows, preferred_element_type=jnp.float32
        )
        return (mixed_block.astype(jnp.bfloat16), logsum)

    mixed_blocks, logsum_blocks = lax.map(forward_block, (query_low, allowed_blocks))
    mixed_heads = mixed_blocks.reshape(group_tokens, heads_local * head_size)
    attn_out = lax.psum_scatter(
        plain_dot(mixed_heads, output_full).astype(jnp.bfloat16),
        "tensor",
        scatter_dimension=0,
        tiled=True,
    ).astype(jnp.float32)
    residual = hidden + attn_out
    moe_input = rms_scale(residual, moe_gain).astype(jnp.bfloat16)
    logits = plain_dot(moe_input, router_weight)
    chosen_mask = expert_ids[:, :, None] == lax.broadcasted_iota(jnp.int32, (1, 1, expert_count), 2)
    chosen = jnp.sum(jnp.where(chosen_mask, logits[:, None, :], 0.0), axis=-1)
    gate_probs = jax.nn.softmax(chosen, axis=-1)
    flat_ids = expert_ids.reshape(-1)
    onehot = (flat_ids[:, None] == lax.broadcasted_iota(jnp.int32, (1, expert_count), 1)).astype(
        jnp.int32
    )
    ranking = jnp.sum((jnp.cumsum(onehot, axis=0) - 1) * onehot, axis=1)
    slot_index = flat_ids * capacity + ranking
    owner_row = (
        jnp.zeros((assign_count,), jnp.int32).at[slot_index].set(lax.iota(jnp.int32, assign_count))
    )
    outgoing = moe_input[owner_row // route_count].reshape(expert_count, capacity, model_width)
    arrived = lax.all_to_all(outgoing, ("dp", "tensor"), split_axis=0, concat_axis=0, tiled=True)
    expert_rows = arrived.reshape(assign_count, model_width)
    gate_mat = gate_weight[0]
    up_mat = up_weight[0]
    down_mat = down_weight[0]
    gate_pre = plain_dot(expert_rows, gate_mat)
    up_pre = plain_dot(expert_rows, up_mat)
    inner_act = (jax.nn.silu(gate_pre) * up_pre).astype(jnp.bfloat16)
    expert_out = (
        plain_dot(inner_act, down_mat)
        .astype(jnp.bfloat16)
        .reshape(expert_count, capacity, model_width)
    )
    returned = lax.all_to_all(expert_out, ("dp", "tensor"), split_axis=0, concat_axis=0, tiled=True)
    picked = (
        returned.reshape(assign_count, model_width)[slot_index]
        .astype(jnp.float32)
        .reshape(tok_dev, route_count, model_width)
    )
    moe_out = jnp.sum(gate_probs[:, :, None] * picked, axis=1)
    layer_out = (residual + moe_out).astype(jnp.bfloat16)
    upstream = cotangent.astype(jnp.float32)
    gate_upstream = jnp.sum(upstream[:, None, :] * picked, axis=-1)
    grad_chosen = gate_probs * (
        gate_upstream - jnp.sum(gate_probs * gate_upstream, axis=-1, keepdims=True)
    )
    grad_logits = jnp.sum(jnp.where(chosen_mask, grad_chosen[:, :, None], 0.0), axis=1).astype(
        jnp.bfloat16
    )
    grad_picked = (
        (gate_probs[:, :, None] * upstream[:, None, :])
        .astype(jnp.bfloat16)
        .reshape(assign_count, model_width)
    )
    grad_outgoing = grad_picked[owner_row].reshape(expert_count, capacity, model_width)
    grad_arrived = lax.all_to_all(
        grad_outgoing, ("dp", "tensor"), split_axis=0, concat_axis=0, tiled=True
    ).reshape(assign_count, model_width)
    grad_inner = dot_inner(grad_arrived, down_mat)
    down_grad = dot_outer(inner_act, grad_arrived)
    gate_sigmoid = jax.nn.sigmoid(gate_pre)
    gate_silu = gate_pre * gate_sigmoid
    grad_gate_pre = (
        grad_inner * up_pre * gate_sigmoid * (1.0 + gate_pre * (1.0 - gate_sigmoid))
    ).astype(jnp.bfloat16)
    grad_up_pre = (grad_inner * gate_silu).astype(jnp.bfloat16)
    gate_grad = dot_outer(expert_rows, grad_gate_pre)
    up_grad = dot_outer(expert_rows, grad_up_pre)
    grad_rows = (dot_inner(grad_gate_pre, gate_mat) + dot_inner(grad_up_pre, up_mat)).astype(
        jnp.bfloat16
    )
    grad_home = lax.all_to_all(
        grad_rows.reshape(expert_count, capacity, model_width),
        ("dp", "tensor"),
        split_axis=0,
        concat_axis=0,
        tiled=True,
    )
    grad_assign = (
        grad_home.reshape(assign_count, model_width)[slot_index]
        .astype(jnp.float32)
        .reshape(tok_dev, route_count, model_width)
    )
    grad_moe_input = jnp.sum(grad_assign, axis=1) + dot_inner(grad_logits, router_weight)
    router_part = dot_outer(moe_input, grad_logits)
    grad_resid_norm, moegain_part = rms_back(residual, moe_gain, grad_moe_input)
    grad_residual = upstream + grad_resid_norm
    grad_attn = lax.all_gather(grad_residual.astype(jnp.bfloat16), "tensor", axis=0, tiled=True)
    query_again, key_again, value_again, output_again = (
        lax.all_gather(query_weight, "dp", axis=0, tiled=True),
        lax.all_gather(key_weight, "dp", axis=0, tiled=True),
        lax.all_gather(value_weight, "dp", axis=0, tiled=True),
        lax.all_gather(output_weight, "dp", axis=1, tiled=True),
    )
    oweight_part = dot_outer(mixed_heads, grad_attn)
    grad_mixed = (
        dot_inner(grad_attn, output_again)
        .astype(jnp.bfloat16)
        .reshape(block_count, block_rows, kv_local, group_size, head_size)
    )

    def backward_block(running, pieces):
        grad_key_sum, grad_value_sum = running
        query_block, allowed_block, logsum, grad_block = pieces
        scores = block_scores(query_block, key_low, allowed_block, score_scale)
        attention = jnp.exp(scores - logsum)
        attention_low = attention.astype(jnp.bfloat16)
        grad_value_sum = grad_value_sum + jnp.einsum(
            "kgqt,qkgd->tkd", attention_low, grad_block, preferred_element_type=jnp.float32
        )
        grad_soft = jnp.einsum(
            "qkgd,tkd->kgqt", grad_block, value_rows, preferred_element_type=jnp.float32
        )
        row_delta = jnp.sum(attention * grad_soft, axis=-1, keepdims=True)
        grad_scores = (attention * (grad_soft - row_delta)).astype(jnp.bfloat16)
        grad_query_block = (
            jnp.einsum("kgqt,tkd->qkgd", grad_scores, key_low, preferred_element_type=jnp.float32)
            * score_scale
        )
        grad_key_sum = (
            grad_key_sum
            + jnp.einsum(
                "kgqt,qkgd->tkd", grad_scores, query_block, preferred_element_type=jnp.float32
            )
            * score_scale
        )
        return ((grad_key_sum, grad_value_sum), grad_query_block)

    empty_rows = jnp.zeros((group_tokens, kv_local, head_size), jnp.float32)
    (grad_keys, grad_values), grad_query_blocks = lax.scan(
        backward_block,
        (empty_rows, empty_rows),
        (query_low, allowed_blocks, logsum_blocks, grad_mixed),
    )
    grad_query_raw, qgain_part = query_pull(
        grad_query_blocks.reshape(group_tokens, heads_local, head_size)
    )
    grad_key_raw, kgain_part = key_pull(grad_keys)
    grad_query_low = grad_query_raw.astype(jnp.bfloat16)
    grad_key_low = grad_key_raw.astype(jnp.bfloat16)
    grad_value_low = grad_values.astype(jnp.bfloat16).reshape(group_tokens, kv_local * head_size)
    qweight_part = dot_outer(normed, grad_query_low)
    kweight_part = dot_outer(normed, grad_key_low)
    vweight_part = dot_outer(normed, grad_value_low)
    total = dot_inner(grad_query_low, query_again)
    total = total + dot_inner(grad_key_low, key_again)
    grad_normed = lax.psum_scatter(
        (total + dot_inner(grad_value_low, value_again)).astype(jnp.bfloat16),
        "tensor",
        scatter_dimension=0,
        tiled=True,
    ).astype(jnp.float32)
    grad_hidden_norm, attngain_part = rms_back(hidden, attn_gain, grad_normed)
    input_grad = grad_residual + grad_hidden_norm
    qweight_grad, kweight_grad, vweight_grad, oweight_grad = (
        lax.psum_scatter(qweight_part, "dp", scatter_dimension=0, tiled=True),
        lax.psum_scatter(kweight_part, "dp", scatter_dimension=0, tiled=True),
        lax.psum_scatter(vweight_part, "dp", scatter_dimension=0, tiled=True),
        lax.psum_scatter(oweight_part, "dp", scatter_dimension=1, tiled=True),
    )
    router_grad, attngain_grad, moegain_grad, qgain_grad, kgain_grad = lax.psum(
        (router_part, attngain_part, moegain_part, qgain_part, kgain_part), ("dp", "tensor")
    )
    return (
        layer_out,
        input_grad,
        attngain_grad,
        qweight_grad,
        kweight_grad,
        vweight_grad,
        oweight_grad,
        qgain_grad,
        kgain_grad,
        moegain_grad,
        router_grad,
        gate_grad[None],
        up_grad[None],
        down_grad[None],
    )


def solution(mesh):
    in_specs = (
        P(("dp", "tensor"), None),
        P("dp", None),
        P(("dp", "tensor"), None),
        P(),
        P("dp", "tensor"),
        P("dp", "tensor"),
        P("dp", "tensor"),
        P("tensor", "dp"),
        P(),
        P(),
        P(),
        P(),
        P(("dp", "tensor"), None, None),
        P(("dp", "tensor"), None, None),
        P(("dp", "tensor"), None, None),
        P(("dp", "tensor"), None),
    )
    out_specs = (
        P(("dp", "tensor"), None),
        P(("dp", "tensor"), None),
        P(),
        P("dp", "tensor"),
        P("dp", "tensor"),
        P("dp", "tensor"),
        P("tensor", "dp"),
        P(),
        P(),
        P(),
        P(),
        P(("dp", "tensor"), None, None),
        P(("dp", "tensor"), None, None),
        P(("dp", "tensor"), None, None),
    )
    return jax.shard_map(
        on_device, mesh=mesh, in_specs=in_specs, out_specs=out_specs, check_vma=False
    )
```

profile of v0, /device:TPU:1, one launch (start us, length us, event | category | flops | bytes accessed | tf_op | source)
XLA Modules:
  0.0 2284.3 jit_solution(5101487308311068792)
XLA Ops:
  9.2 2.0 fusion.47
  17.0 21.5 all-gather.7.cloned.1.call-done
  38.4 70.4 %all-gather.11.cloned.1.call-done = bf16[2048,256]{1,0:T(8,128)(2,1)} async-done(((bf16[32,256]{1,0:T(8,128)(2,1)}), bf16[2048,256]{1,0:T(8,128)(2,1)}) %all-gather.11.cloned.1.call-update) | async-done | bytes 1048592 | tf_op jit(solution)/shard_map/all_gather | solution.py:122
  108.8 2.8 multiply_reduce_fusion.8
  113.5 1.8 subtract_convert_fusion.1
  115.3 59.3 %all-gather.9.cloned.1.call-done = bf16[2048,256]{1,0:T(8,128)(2,1)} async-done(((bf16[32,256]{1,0:T(8,128)(2,1)}), bf16[2048,256]{1,0:T(8,128)(2,1)}) %all-gather.9.cloned.1.call-update) | async-done | bytes 1048592 | tf_op jit(solution)/shard_map/all_gather | solution.py:123
  174.6 2.7 convolution_convert_fusion.3
  177.3 79.0 %all-gather.13.cloned.1.call-done = bf16[2048,2048]{1,0:T(8,128)(2,1)} async-done(((bf16[32,2048]{1,0:T(8,128)(2,1)}), bf16[2048,2048]{1,0:T(8,128)(2,1)}) %all-gather.13.cloned.1.call-update) | async-done | bytes 8388624 | tf_op jit(solution)/shard_map/all_gather | solution.py:121
  256.3 6.0 convolution_bitcast_fusion
  267.2 2.2 multiply_multiply_fusion
  277.4 61.5 %all-gather.15.cloned.1.call-done = bf16[2048,2048]{0,1:T(8,128)(2,1)} async-done(((bf16[2048,32]{0,1:T(8,128)(2,1)}), bf16[2048,2048]{0,1:T(8,128)(2,1)}) %all-gather.15.cloned.1.call-update) | async-done | bytes 8388624 | tf_op jit(solution)/shard_map/all_gather | solution.py:124
  338.9 7.1 convolution_convert_fusion.1
  358.7 1.5 mul.534
  363.5 5.0 scatter_custom_fusion
  371.8 2.2 multiply_convert_fusion.3
  374.0 10.0 gather_fusion
  384.1 6.8 all-to-all-start
  390.9 2.1 convert_element_type.142
  399.1 1.5 div.109
  400.6 3.5 fusion.2
  404.0 11.7 gather_fusion.2
  415.7 29.2 %all-to-all-done = bf16[128,8,2048]{2,1,0:T(8,128)(2,1)} async-done(((bf16[128,8,2048]{2,1,0:T(8,128)(2,1)}), bf16[128,8,2048]{2,1,0:T(8,128)(2,1)}, u32[]{:S(2)}, u32[]{:S(2)}) %all-to-all-start) | async-done | bytes 4194336 | tf_op jit(solution)/shard_map/all_to_all | solution.py:183
  444.9 5.5 all-to-all-start.2
  450.5 8.4 fusion.15
  458.9 7.3 fusion.17
  466.2 38.8 %all-to-all-done.2 = bf16[128,8,2048]{2,1,0:T(8,128)(2,1)} async-done(((bf16[128,8,2048]{2,1,0:T(8,128)(2,1)}), bf16[128,8,2048]{2,1,0:T(8,128)(2,1)}, u32[]{:S(2)}, u32[]{:S(2)}) %all-to-all-start.2) | async-done | bytes 4194336 | tf_op jit(solution)/shard_map/all_to_all | solution.py:218
  504.9 10.1 multiply_convert_fusion
  516.2 4.9 convert_bitcast_fusion
  521.1 6.1 all-to-all-start.1
  527.2 5.0 fusion.33
  532.3 5.0 fusion.3
  537.3 44.1 %all-to-all-done.1 = bf16[128,8,2048]{2,1,0:T(8,128)(2,1)} async-done(((bf16[128,8,2048]{2,1,0:T(8,128)(2,1)}), bf16[128,8,2048]{2,1,0:T(8,128)(2,1)}, u32[]{:S(2)}, u32[]{:S(2)}) %all-to-all-start.1) | async-done | bytes 4194336 | tf_op jit(solution)/shard_map/all_to_all | solution.py:196
  581.4 5.5 all-to-all-start.3
  587.0 11.6 gather_fusion.1
  598.7 5.8 fusion.1
  605.2 36.2 %all-to-all-done.3 = bf16[128,8,2048]{2,1,0:T(8,128)(2,1)} async-done(((bf16[128,8,2048]{2,1,0:T(8,128)(2,1)}), bf16[128,8,2048]{2,1,0:T(8,128)(2,1)}, u32[]{:S(2)}, u32[]{:S(2)}) %all-to-all-start.3) | async-done | bytes 4194336 | tf_op jit(solution)/shard_map/all_to_all | solution.py:234
  641.4 11.5 gather_fusion.3
  653.0 5.2 convert_reduce_fusion
  661.2 3.3 copy.146
  664.5 17.0 all-gather.17.cloned.1.call-done
  681.5 6.2 fusion.40
  692.3 1.6 fusion.45
  694.0 2.5 copy.161
  696.5 2.5 copy.162
  699.0 2.8 multiply_add_fusion.1
  701.9 2.2 multiply_reduce_fusion
  704.4 5.3 fusion.39
  710.9 2.1 fusion.46
  713.1 5.8 fusion.58
  723.1 1.8 fusion.89
  725.1 1.8 fusion.90
  727.0 9.5 fusion.56
  738.0 8.1 fusion.91
  747.6 7.8 fusion.25
  755.4 8.5 fusion.19
  763.9 8.4 fusion.22
  773.8 66.5 %all-reduce.4 = (f32[2048]{0:T(1024)}, f32[128]{0:T(128)}, f32[128]{0:T(128)}, f32[2048]{0:T(1024)}) all-reduce(f32[2048]{0:T(1024)S(1)} %get-tuple-element.71, f32[128]{0:T(128)S(1)} %get-tuple-element.55, f32[128]{0:T(128)S(1)} %get-tuple-element.73, ...), channel_id=1, replica_groups=mesh['dp'=64,'tensor'=2] {'dp','tensor'}, use_global_device_ids=true, to_apply=%region_27.28 | all-reduce | flops 4352 | bytes 34816 | tf_op jit(solution)/shard_map/psum | solution.py:323
  840.3 4.4 fusion.51
  844.6 54.2 %all-reduce.7.cloned.1.call-done = f32[2048,128]{1,0:T(8,128)} async-done(((f32[2048,128]{1,0:T(8,128)}), f32[2048,128]{1,0:T(8,128)}) %all-reduce.7.cloned.1.call-update) | async-done | bytes 1048592 | tf_op jit(solution)/shard_map/psum | solution.py:323
  898.8 329.3 %reduce-scatter.13.cloned.1.call-done = f32[32,256]{1,0:T(8,128)} async-done(((f32[2048,256]{1,0:T(8,128)}), f32[32,256]{1,0:T(8,128)}) %reduce-scatter.13.cloned.1.call-update) | async-done | bytes 32784 | tf_op jit(solution)/shard_map/reduce_scatter | solution.py:319
  1228.1 332.2 %reduce-scatter.15.cloned.1.call-done = f32[32,256]{1,0:T(8,128)} async-done(((f32[2048,256]{1,0:T(8,128)}), f32[32,256]{1,0:T(8,128)}) %reduce-scatter.15.cloned.1.call-update) | async-done | bytes 32784 | tf_op jit(solution)/shard_map/reduce_scatter | solution.py:320
  1560.3 357.3 %reduce-scatter.11.cloned.1.call-done = f32[32,2048]{1,0:T(8,128)} async-done(((f32[2048,2048]{1,0:T(8,128)}), f32[32,2048]{1,0:T(8,128)}) %reduce-scatter.11.cloned.1.call-update) | async-done | bytes 262160 | tf_op jit(solution)/shard_map/reduce_scatter | solution.py:318
  1917.6 357.7 %reduce-scatter.17.cloned.1.call-done = f32[2048,32]{0,1:T(8,128)} async-done(((f32[2048,2048]{0,1:T(8,128)}), f32[2048,32]{0,1:T(8,128)}) %reduce-scatter.17.cloned.1.call-update) | async-done | bytes 262160 | tf_op jit(solution)/shard_map/reduce_scatter | solution.py:321
  2275.3 2.3 copy.179
  (251 shorter events, 66.9 us)
Async XLA Ops:
  7.2 497.8 %copy-start = (bf16[1,768,2048]{2,1,0:T(8,128)(2,1)S(1)}, bf16[1,768,2048]{2,1,0:T(8,128)(2,1)}, u32[]{:S(2)}) copy-start(bf16[1,768,2048]{2,1,0:T(8,128)(2,1)} %param.30) | copy-start | bytes 9437188
  7.2 106.1 %copy-start.64 = (f32[128]{0:T(128)S(1)}, f32[128]{0:T(128)}, u32[]{:S(2)}) copy-start(f32[128]{0:T(128)} %param.25) | copy-start | bytes 1540
  7.2 31.2 %all-gather.7.cloned.1.call-start = ((), (), s32[]{:S(2)}) async-start(), calls=%async_computation.10 | async-start | bytes 1572864 | tf_op jit(solution)/shard_map/all_gather | solution.py:119
  11.2 97.6 %all-gather.11.cloned.1.call-start = ((), (), s32[]{:S(2)}) async-start(), calls=%async_computation.12 | async-start | bytes 1064960 | tf_op jit(solution)/shard_map/all_gather | solution.py:122
  12.0 162.6 %all-gather.9.cloned.1.call-start = ((), (), s32[]{:S(2)}) async-start(), calls=%async_computation.11 | async-start | bytes 1064960 | tf_op jit(solution)/shard_map/all_gather | solution.py:123
  12.7 243.6 %all-gather.13.cloned.1.call-start = ((), (), s32[]{:S(2)}) async-start(), calls=%async_computation.13 | async-start | bytes 8519680 | tf_op jit(solution)/shard_map/all_gather | solution.py:121
  13.3 325.6 %all-gather.15.cloned.1.call-start = ((), (), s32[]{:S(2)}) async-start(), calls=%async_computation.14 | async-start | bytes 8519680 | tf_op jit(solution)/shard_map/all_gather | solution.py:124
  13.9 356.0 %reduce-scatter.7.cloned.1.call-start = ((), (), s32[]{:S(2)}) async-start(), calls=%async_computation.15 | async-start | bytes 1572864 | tf_op jit(solution)/shard_map/reduce_scatter | solution.py:161
  111.6 150.8 %copy-start.53 = (f32[256,2]{0,1:T(2,128)}, f32[256,2]{0,1:T(2,128)S(1)}, u32[]{:S(2)}) copy-start(f32[256,2]{0,1:T(2,128)S(1)} %get-tuple-element.100) | copy-start | bytes 6148
  112.7 149.7 %copy-start.24 = (f32[256,2,128]{2,0,1:T(8,128)}, f32[256,2,128]{2,0,1:T(8,128)S(1)}, u32[]{:S(2)}) copy-start(f32[256,2,128]{2,0,1:T(8,128)S(1)} %copy.120) | copy-start | bytes 786436
  262.4 4.8 copy-start.62
  264.2 5.2 copy-start.29
  264.2 5.2 copy-start.30
  266.4 3.8 copy-start.47
  273.5 2.5 copy-start.39
  346.8 37.2 %copy-start.35 = (s32[128,8]{1,0:T(8,128)}, s32[128,8]{1,0:T(8,128)S(1)}, u32[]{:S(2)}) copy-start(s32[128,8]{1,0:T(8,128)S(1)} %copy.126) | copy-start | bytes 12292
  384.1 60.9 %all-to-all-start = ((bf16[128,8,2048]{2,1,0:T(8,128)(2,1)}), bf16[128,8,2048]{2,1,0:T(8,128)(2,1)}, u32[]{:S(2)}, u32[]{:S(2)}) async-start(bf16[128,8,2048]{2,1,0:T(8,128)(2,1)} %bitcast.200), calls=%async_computation.1 | async-start | bytes 8388608 | tf_op jit(solution)/shard_map/all_to_all | solution.py:183
  444.9 60.0 %all-to-all-start.2 = ((bf16[128,8,2048]{2,1,0:T(8,128)(2,1)}), bf16[128,8,2048]{2,1,0:T(8,128)(2,1)}, u32[]{:S(2)}, u32[]{:S(2)}) async-start(bf16[128,8,2048]{2,1,0:T(8,128)(2,1)} %bitcast.201), calls=%async_computation.3 | async-start | bytes 8388608 | tf_op jit(solution)/shard_map/all_to_all | solution.py:218
  450.5 8.4 copy-start.70
  521.1 6.1 copy-start.71
  521.1 60.3 %all-to-all-start.1 = ((bf16[128,8,2048]{2,1,0:T(8,128)(2,1)}), bf16[128,8,2048]{2,1,0:T(8,128)(2,1)}, u32[]{:S(2)}, u32[]{:S(2)}) async-start(bf16[128,8,2048]{2,1,0:T(8,128)(2,1)} %convert_bitcast_fusion), calls=%async_computation.2 | async-start | bytes 8388608 | tf_op jit(solution)/shard_map/all_to_all | solution.py:196
  527.2 5.0 copy-start.72
  527.2 5.0 copy-start.74
  537.3 49.7 %copy-start.55 = (s32[1024,1]{0,1:T(1,128)S(1)}, s32[1024,1]{0,1:T(1,128)}, u32[]{:S(2)}) copy-start(s32[1024,1]{0,1:T(1,128)} %compare_select_fusion) | copy-start | bytes 12292
  581.4 60.0 %all-to-all-start.3 = ((bf16[128,8,2048]{2,1,0:T(8,128)(2,1)}), bf16[128,8,2048]{2,1,0:T(8,128)(2,1)}, u32[]{:S(2)}, u32[]{:S(2)}) async-start(bf16[128,8,2048]{2,1,0:T(8,128)(2,1)} %fusion.3), calls=%async_computation.4 | async-start | bytes 8388608 | tf_op jit(solution)/shard_map/all_to_all | solution.py:234
  586.9 94.6 %all-gather.17.cloned.1.call-start = ((), (), s32[]{:S(2)}) async-start(), calls=%async_computation.16 | async-start | bytes 1572864 | tf_op jit(solution)/shard_map/all_gather | solution.py:250
  587.0 11.7 copy-start.20
  587.0 11.6 copy-start.46
  598.7 5.9 copy-start.56
  598.7 5.9 copy-start.58
  598.7 6.2 copy-start.36
  652.9 5.2 copy-start.7
  652.9 5.2 copy-start.13
  652.9 5.2 copy-start.34
  652.9 5.2 copy-start.49
  652.9 5.2 copy-start.60
  658.2 3.0 copy-start.10
  658.8 5.7 copy-start.68
  661.1 111.2 %reduce-scatter.9.cloned.1.call-start = ((), (), s32[]{:S(2)}) async-start(), calls=%async_computation.17 | async-start | bytes 1572864 | tf_op jit(solution)/shard_map/reduce_scatter | solution.py:309
  664.5 23.5 %copy-start.40 = (bf16[256,256]{0,1:T(8,128)(2,1)S(1)}, bf16[256,256]{0,1:T(8,128)(2,1)}, u32[]{:S(2)}) copy-start(bf16[256,256]{0,1:T(8,128)(2,1)} %convolution_convert_fusion.3) | copy-start | bytes 393220
  681.5 6.5 copy-start.4
  699.0 2.9 copy-start.6
  699.0 2.9 copy-start.33
  699.0 2.9 copy-start.63
  704.3 5.3 copy-start.31
  704.3 5.5 copy-start.25
  704.4 5.5 copy-start.52
  704.4 5.5 copy-start.65
  704.4 5.8 copy-start.54
  709.7 3.4 copy-start.26
  713.1 5.9 copy-start.28
  720.1 3.0 copy-start.8
  721.6 177.2 %all-reduce.7.cloned.1.call-start = ((), (), s32[]{:S(2)}) async-start(), calls=%async_computation.22 | async-start | bytes 2097152 | tf_op jit(solution)/shard_map/psum | solution.py:323
  723.1 505.0 %reduce-scatter.13.cloned.1.call-start = ((), (), s32[]{:S(2)}) async-start(), calls=%async_computation.19 | async-start | bytes 2129920 | tf_op jit(solution)/shard_map/reduce_scatter | solution.py:319
  725.0 835.3 %reduce-scatter.15.cloned.1.call-start = ((), (), s32[]{:S(2)}) async-start(), calls=%async_computation.20 | async-start | bytes 2129920 | tf_op jit(solution)/shard_map/reduce_scatter | solution.py:320
  726.9 1190.7 %reduce-scatter.11.cloned.1.call-start = ((), (), s32[]{:S(2)}) async-start(), calls=%async_computation.18 | async-start | bytes 17039360 | tf_op jit(solution)/shard_map/reduce_scatter | solution.py:318
  736.5 1538.8 %reduce-scatter.17.cloned.1.call-start = ((), (), s32[]{:S(2)}) async-start(), calls=%async_computation.21 | async-start | bytes 17039360 | tf_op jit(solution)/shard_map/reduce_scatter | solution.py:321
  747.6 7.8 copy-start.73
  755.4 8.5 copy-start.75
  763.9 8.4 copy-start.50
  763.9 8.4 copy-start.67
  763.9 76.3 %copy-start.61 = (f32[128]{0:T(128)S(1)}, f32[128]{0:T(128)}, u32[]{:S(2)}) copy-start(f32[128]{0:T(128)} %copy-done.59) | copy-start | bytes 1540
  763.9 76.3 %copy-start.69 = (f32[128]{0:T(128)S(1)}, f32[128]{0:T(128)}, u32[]{:S(2)}) copy-start(f32[128]{0:T(128)} %copy-done.68) | copy-start | bytes 1540
  840.3 1437.3 %copy-start.1 = (bf16[1,768,2048]{2,1,0:T(8,128)(2,1)S(1)}, bf16[1,768,2048]{2,1,0:T(8,128)(2,1)}, u32[]{:S(2)}) copy-start(bf16[1,768,2048]{2,1,0:T(8,128)(2,1)} %param.30) | copy-start | bytes 9437188
  (29 other events, 39.9 us)
Sparse Core Ops, SparseCore 0:
  11.3 27.0 all-gather.6
  41.7 67.0 all-gather.10
  112.1 62.4 all-gather.8
  177.7 78.5 all-gather.12
  259.4 79.4 all-gather.14
  346.1 20.0 reduce-scatter.6
  661.2 20.1 all-gather.16
  721.8 23.8 reduce-scatter.8
  750.4 148.3 all-reduce.6
  901.7 326.3 reduce-scatter.12
  1231.0 329.2 reduce-scatter.14
  1563.2 354.3 reduce-scatter.10
  1920.7 354.5 reduce-scatter.16
where the time goes:
time: 2300 us; the launch traced here: 2280 us
  waiting for transfers between devices  1890 us (82%)
  matrix products  131 us (6%)
  local copies, waits for them, and re-layouts  89 us (4%)
  other arithmetic  67.5 us (3%)
  blocking collectives  66.5 us (3%)
  starting transfers between devices  24.5 us (1%)
    reduce_scatter x1, waiting for transfers between devices, on_device(): lax.psum_scatter(oweight_part, 'dp', scatter_dimension=1, tiled=True)  358 us
    reduce_scatter x1, waiting for transfers between devices, on_device(): lax.psum_scatter(qweight_part, 'dp', scatter_dimension=0, tiled=True)  357 us
    reduce_scatter x1, waiting for transfers between devices, on_device(): lax.psum_scatter(vweight_part, 'dp', scatter_dimension=0, tiled=True)  332 us
    reduce_scatter x1, waiting for transfers between devices, on_device(): lax.psum_scatter(kweight_part, 'dp', scatter_dimension=0, tiled=True)  329 us
    all_gather x1, waiting for transfers between devices, on_device(): lax.all_gather(query_weight, 'dp', axis=0, tiled=True)  79 us
    all_gather x1, waiting for transfers between devices, on_device(): lax.all_gather(key_weight, 'dp', axis=0, tiled=True)  70.4 us
    psum x1, blocking collectives, on_device(): lax.psum((router_part, attngain_part, moegain_part, qgain_part, kgain_par...  66.5 us
    all_gather x1, waiting for transfers between devices, on_device(): lax.all_gather(output_weight, 'dp', axis=1, tiled=True)  61.5 us
  transfers between devices with their start and end apart: 17, of which 15 were waited for; matrix products, arithmetic and copies ran while one was open for 8% of the time, Pallas kernels for 0%

commit v1 on v0

v1 whole, which is shorter than its diff:
```python
import math

import jax
import jax.numpy as jnp
from jax import lax
from jax.sharding import PartitionSpec as P

BLOCK = 128
EPSILON = 1e-06
ROPE_BASE = 1000000.0
MASKED = -1e30
F32 = jnp.float32
BF16 = jnp.bfloat16


def dot_nt(a, b):
    return lax.dot_general(a, b, (((1,), (1,)), ((), ())), preferred_element_type=F32)


def dot_tn(a, b):
    return lax.dot_general(a, b, (((0,), (0,)), ((), ())), preferred_element_type=F32)


def dot_nn(a, b):
    return lax.dot_general(a, b, (((1,), (0,)), ((), ())), preferred_element_type=F32)


def rms_recip(values):
    return lax.rsqrt(jnp.mean(values * values, axis=-1, keepdims=True) + EPSILON)


def rms_scale(values, gain):
    return values * rms_recip(values) * gain


def rms_back(values, gain, upstream):
    r = rms_recip(values)
    scaled = upstream * gain
    inner = jnp.mean(scaled * values, axis=-1, keepdims=True)
    grad_values = r * scaled - values * (r * r * r) * inner
    return grad_values, upstream * values * r


def rotate(values, cosine, sine):
    half = values.shape[-1] // 2
    a = values[..., :half]
    b = values[..., half:]
    return jnp.concatenate([a * cosine - b * sine, b * cosine + a * sine], axis=-1)


def layout(doc_row):
    length = doc_row.shape[0]
    indices = jnp.arange(length, dtype=jnp.int32)
    same_doc = doc_row[:, None] == doc_row[None, :]
    earlier = indices[None, :] < indices[:, None]
    position = jnp.sum(jnp.where(same_doc & earlier, 1, 0), axis=1).astype(jnp.int32)
    blocks = position // BLOCK
    allowed = same_doc & (blocks[None, :] <= blocks[:, None])
    return position, allowed


def rotary(position, head_size):
    half = head_size // 2
    frequency = jnp.exp(-jnp.log(ROPE_BASE) * jnp.arange(half, dtype=F32) * 2.0 / head_size)
    angles = position.astype(F32)[:, None] * frequency[None, :]
    return jnp.cos(angles)[:, None, :], jnp.sin(angles)[:, None, :]


def on_device(
    hidden_in,
    doc_ids,
    expert_ids,
    attn_gain,
    query_weight,
    key_weight,
    value_weight,
    output_weight,
    query_gain,
    key_gain,
    moe_gain,
    router_weight,
    gate_weight,
    up_weight,
    down_weight,
    cotangent,
):
    both = ("dp", "tensor")
    tok, width = hidden_in.shape
    hd = query_gain.shape[0]
    nkv = key_weight.shape[1] // hd
    nq = query_weight.shape[1] // hd
    group = nq // nkv
    experts = router_weight.shape[1]
    routes = expert_ids.shape[1]
    cap = tok * routes // experts
    slots = experts * cap
    scale = 1.0 / math.sqrt(hd)
    tokens = doc_ids.shape[1]
    me = lax.axis_index(both)

    lane = lax.broadcasted_iota(jnp.int32, (1, 1, experts), 2)
    chosen = jnp.sum((expert_ids[:, :, None] == lane).astype(F32), axis=1)
    below = (
        lax.broadcasted_iota(jnp.int32, (tok, tok), 1)
        < lax.broadcasted_iota(jnp.int32, (tok, tok), 0)
    ).astype(BF16)
    rank = dot_nn(below, chosen.astype(BF16))
    place = jnp.where(chosen > 0, rank, -1.0).T
    spread = (
        place[:, None, :] == lax.broadcasted_iota(jnp.int32, (1, cap, 1), 1).astype(F32)
    ).astype(BF16).reshape(slots, tok)

    cot_out = dot_nn(spread, jnp.concatenate([cotangent, chosen.astype(BF16)], axis=1)).astype(BF16)
    cot_in = lax.all_to_all(
        cot_out.reshape(experts, cap, width + experts), both, split_axis=0, concat_axis=0, tiled=True
    ).reshape(slots, width + experts)

    hidden = hidden_in.astype(F32)
    normed_local = rms_scale(hidden, attn_gain).astype(BF16)
    normed = lax.all_gather(normed_local, "tensor", axis=0, tiled=True)
    shard = jnp.concatenate([query_weight, key_weight, value_weight, output_weight.T], axis=1)
    weights = lax.all_gather(shard, "dp", axis=0, tiled=True)
    nqkv = (nq + 2 * nkv) * hd
    in_weights = weights[:, :nqkv]
    out_weights = weights[:, nqkv:]

    position, allowed = layout(doc_ids[0])
    cosine, sine = rotary(position, hd)
    raw = dot_nn(normed, in_weights)
    query_raw = raw[:, : nq * hd].reshape(tokens, nq, hd)
    key_raw = raw[:, nq * hd : (nq + nkv) * hd].reshape(tokens, nkv, hd)
    values = raw[:, (nq + nkv) * hd :].astype(BF16).reshape(tokens, nkv, hd)
    query = rotate(rms_scale(query_raw, query_gain), cosine, sine).astype(BF16)
    query = query.reshape(tokens, nkv, group, hd)
    key = rotate(rms_scale(key_raw, key_gain), cosine, sine).astype(BF16)
    scores = jnp.einsum("qkgd,tkd->kgqt", query, key, preferred_element_type=F32) * scale
    scores = jnp.where(allowed[None, None], scores, MASKED)
    weight = jnp.exp(scores - jnp.max(scores, axis=-1, keepdims=True))
    attention = weight / jnp.sum(weight, axis=-1, keepdims=True)
    attention_low = attention.astype(BF16)
    mixed = jnp.einsum("kgqt,tkd->qkgd", attention_low, values, preferred_element_type=F32)
    mixed = mixed.astype(BF16).reshape(tokens, nq * hd)
    attn_out = lax.psum_scatter(
        dot_nt(mixed, out_weights).astype(BF16), "tensor", scatter_dimension=0, tiled=True
    ).astype(F32)

    residual = hidden + attn_out
    moe_input = rms_scale(residual, moe_gain).astype(BF16)
    sent = dot_nn(spread, moe_input).astype(BF16)
    rows = lax.all_to_all(
        sent.reshape(experts, cap, width), both, split_axis=0, concat_axis=0, tiled=True
    ).reshape(slots, width)
    logits = dot_nn(moe_input, router_weight)
    masked = jnp.where(chosen > 0, logits, MASKED)
    probs = jnp.exp(masked - jnp.max(masked, axis=-1, keepdims=True))
    probs = probs / jnp.sum(probs, axis=-1, keepdims=True)

    gate_mat, up_mat, down_mat = gate_weight[0], up_weight[0], down_weight[0]
    cot_rows = cot_in[:, :width]
    inner_up = dot_nt(cot_rows, down_mat)
    row_logits = jnp.where(cot_in[:, width:] > 0, dot_nn(rows, router_weight), MASKED)
    row_probs = jnp.exp(row_logits - jnp.max(row_logits, axis=-1, keepdims=True))
    mine = lax.broadcasted_iota(jnp.int32, (1, experts), 1) == me
    prob = jnp.sum(jnp.where(mine, row_probs, 0.0), axis=-1, keepdims=True) / jnp.sum(
        row_probs, axis=-1, keepdims=True
    )
    gate_pre = dot_nn(rows, gate_mat)
    up_pre = dot_nn(rows, up_mat)
    sigmoid = jax.nn.sigmoid(gate_pre)
    silu = gate_pre * sigmoid
    inner = silu * up_pre
    gate_up = jnp.sum(inner * inner_up, axis=-1, keepdims=True)
    inner_low = (prob * inner).astype(BF16)
    grad_inner = prob * inner_up
    grad_gate = (grad_inner * up_pre * sigmoid * (1.0 + gate_pre * (1.0 - sigmoid))).astype(BF16)
    grad_up = (grad_inner * silu).astype(BF16)
    grad_rows = (dot_nt(grad_gate, gate_mat) + dot_nt(grad_up, up_mat)).astype(BF16)
    gate_up_high = gate_up.astype(BF16)
    gate_up_rest = (gate_up - gate_up_high.astype(F32)).astype(BF16)
    none = jnp.zeros((), BF16)
    home_out = jnp.concatenate(
        [grad_rows, jnp.where(mine, gate_up_high, none), jnp.where(mine, gate_up_rest, none)], axis=1
    )
    home = lax.all_to_all(
        home_out.reshape(experts, cap, width + 2 * experts), both, split_axis=0, concat_axis=0, tiled=True
    ).reshape(slots, width + 2 * experts)
    expert_out = dot_nn(inner_low, down_mat).astype(BF16)
    returned = lax.all_to_all(
        expert_out.reshape(experts, cap, width), both, split_axis=0, concat_axis=0, tiled=True
    ).reshape(slots, width)
    down_grad = dot_tn(inner_low, cot_rows)
    gate_grad = dot_tn(rows, grad_gate)
    up_grad = dot_tn(rows, grad_up)

    upstream = cotangent.astype(F32)
    summed = dot_tn(spread, home)
    gate_upstream = summed[:, width : width + experts] + summed[:, width + experts :]
    grad_chosen = probs * (gate_upstream - jnp.sum(probs * gate_upstream, axis=-1, keepdims=True))
    grad_logits = grad_chosen.astype(BF16)
    grad_moe_input = summed[:, :width] + dot_nt(grad_logits, router_weight)
    router_part = dot_tn(moe_input, grad_logits)
    grad_norm, moegain_rows = rms_back(residual, moe_gain, grad_moe_input)
    moegain_part = jnp.sum(moegain_rows, axis=0)
    grad_residual = upstream + grad_norm
    grad_attn = lax.all_gather(grad_residual.astype(BF16), "tensor", axis=0, tiled=True)
    layer_out = (residual + dot_tn(spread, returned)).astype(BF16)

    grad_mixed = dot_nn(grad_attn, out_weights).astype(BF16).reshape(tokens, nkv, group, hd)
    grad_values = jnp.einsum("kgqt,qkgd->tkd", attention_low, grad_mixed, preferred_element_type=F32)
    grad_soft = jnp.einsum("qkgd,tkd->kgqt", grad_mixed, values, preferred_element_type=F32)
    row_delta = jnp.sum(attention * grad_soft, axis=-1, keepdims=True)
    grad_scores = (attention * (grad_soft - row_delta)).astype(BF16)
    grad_query = jnp.einsum("kgqt,tkd->qkgd", grad_scores, key, preferred_element_type=F32) * scale
    grad_key = jnp.einsum("kgqt,qkgd->tkd", grad_scores, query, preferred_element_type=F32) * scale
    grad_query_raw, qgain_rows = rms_back(
        query_raw, query_gain, rotate(grad_query.reshape(tokens, nq, hd), cosine, -sine)
    )
    grad_key_raw, kgain_rows = rms_back(key_raw, key_gain, rotate(grad_key, cosine, -sine))
    grad_raw = jnp.concatenate(
        [
            grad_query_raw.astype(BF16).reshape(tokens, nq * hd),
            grad_key_raw.astype(BF16).reshape(tokens, nkv * hd),
            grad_values.astype(BF16).reshape(tokens, nkv * hd),
        ],
        axis=1,
    )
    grad_normed = lax.psum_scatter(
        dot_nt(grad_raw, in_weights).astype(BF16), "tensor", scatter_dimension=0, tiled=True
    ).astype(F32)
    weight_part = jnp.concatenate([dot_tn(normed, grad_raw), dot_tn(grad_attn, mixed)], axis=1)
    weight_grad = lax.psum_scatter(weight_part, "dp", scatter_dimension=0, tiled=True)
    grad_hidden, attngain_rows = rms_back(hidden, attn_gain, grad_normed)
    input_grad = grad_residual + grad_hidden
    router_grad, attngain_grad, moegain_grad, qgain_grad, kgain_grad = lax.psum(
        (
            router_part,
            jnp.sum(attngain_rows, axis=0),
            moegain_part,
            jnp.sum(qgain_rows, axis=(0, 1)),
            jnp.sum(kgain_rows, axis=(0, 1)),
        ),
        both,
    )
    return (
        layer_out,
        input_grad,
        attngain_grad,
        weight_grad[:, : nq * hd],
        weight_grad[:, nq * hd : (nq + nkv) * hd],
        weight_grad[:, (nq + nkv) * hd : nqkv],
        weight_grad[:, nqkv:].T,
        qgain_grad,
        kgain_grad,
        moegain_grad,
        router_grad,
        gate_grad[None],
        up_grad[None],
        down_grad[None],
    )


def solution(mesh):
    both = ("dp", "tensor")
    in_specs = (
        P(both, None),
        P("dp", None),
        P(both, None),
        P(),
        P("dp", "tensor"),
        P("dp", "tensor"),
        P("dp", "tensor"),
        P("tensor", "dp"),
        P(),
        P(),
        P(),
        P(),
        P(both, None, None),
        P(both, None, None),
        P(both, None, None),
        P(both, None),
    )
    out_specs = (
        P(both, None),
        P(both, None),
        P(),
        P("dp", "tensor"),
        P("dp", "tensor"),
        P("dp", "tensor"),
        P("tensor", "dp"),
        P(),
        P(),
        P(),
        P(),
        P(both, None, None),
        P(both, None, None),
        P(both, None, None),
    )
    return jax.shard_map(
        on_device, mesh=mesh, in_specs=in_specs, out_specs=out_specs, check_vma=False
    )
```

time: 2300 us -> 1020 us (0.44)
  waiting for transfers between devices: 1890 us -> 613 us
  local copies, waits for them, and re-layouts: 89 us -> 58.5 us
    reduce_scatter x6 -> x3, waiting for transfers between devices: 1380 us -> 170 us  [the longest x1 150 us: on_device(): lax.psum_scatter(weight_part, 'dp', scatter_dimension=0, tiled=True)]
    all_gather x5 -> x2, waiting for transfers between devices: 287 us -> 144 us  [the longest x1 130 us: on_device(): weights = lax.all_gather(shard, 'dp', axis=0, tiled=True)]
    psum x1, waiting for transfers between devices: 54.2 us -> 147 us  [on_device(): lax.psum((router_part, jnp.sum(attngain_rows, axis=0), moegain_part, jnp....]
    gather x4 -> x0, local copies, waits for them, and re-layouts: 44.9 us -> none  [the longest x1 11.7 us: on_device(): grad_picked[owner_row].reshape(expert_count, capacity, model_width)]
    concatenate x0 -> x2, other arithmetic: none -> 26.5 us  [the longest x1 24.7 us: on_device(): jnp.concatenate([dot_tn(normed, grad_raw), dot_tn(grad_attn, mixed)], axi...]
    dot_general x30 -> x29, matrix products: 131 us -> 144 us  [the longest x8 54.5 us: dot_tn(): lax.dot_general(a, b, (((0,), (0,)), ((), ())), preferred_element_type=F32)]
  transfers between devices with their start and end apart: 17 -> 11, of which waited for: 15 -> 9; matrix products, arithmetic and copies ran while one was open for 8% -> 17% of each run, Pallas kernels for 0% -> 0%
where the time goes in v1:
time: 1020 us; the launch traced here: 1010 us
  waiting for transfers between devices  613 us (60%)
  matrix products  150 us (15%)
  other arithmetic  71.6 us (7%)
  blocking collectives  69.1 us (7%)
  local copies, waits for them, and re-layouts  58.5 us (6%)
  starting transfers between devices  37.4 us (4%)
  between operations  15.5 us (2%)
    reduce_scatter x1, waiting for transfers between devices, on_device(): lax.psum_scatter(weight_part, 'dp', scatter_dimension=0, tiled=True)  150 us
    psum x1, waiting for transfers between devices, on_device(): lax.psum((router_part, jnp.sum(attngain_rows, axis=0), moegain_part, jnp....  147 us
    all_gather x1, waiting for transfers between devices, on_device(): weights = lax.all_gather(shard, 'dp', axis=0, tiled=True)  130 us
    psum x1, blocking collectives, on_device(): lax.psum((router_part, jnp.sum(attngain_rows, axis=0), moegain_part, jnp....  69.1 us
    all_to_all x1, waiting for transfers between devices, on_device(): lax.all_to_all(home_out.reshape(experts, cap, width + 2 * experts), both,...  59.9 us
    dot_general x8, matrix products, dot_tn(): lax.dot_general(a, b, (((0,), (0,)), ((), ())), preferred_element_type=F32)  54.5 us
    dot_general x10, matrix products, dot_nn(): lax.dot_general(a, b, (((1,), (0,)), ((), ())), preferred_element_type=F32)  47.3 us
    all_to_all x1, waiting for transfers between devices, on_device(): lax.all_to_all(sent.reshape(experts, cap, width), both, split_axis=0, con...  42.1 us
  transfers between devices with their start and end apart: 11, of which 9 were waited for; matrix products, arithmetic and copies ran while one was open for 17% of the time, Pallas kernels for 0%

profile of v1, /device:TPU:1, one launch (start us, length us, event | category | flops | bytes accessed | tf_op | source)
XLA Modules:
  0.0 1014.7 jit_solution(16936073172691260147)
XLA Ops:
  9.6 2.0 fusion.74
  11.7 1.7 pad_maximum_fusion.6
  16.1 4.5 fusion.9
  20.6 11.9 %all-to-all-start = ((bf16[128,8,2176]{2,1,0:T(8,128)(2,1)}), bf16[128,8,2176]{2,1,0:T(8,128)(2,1)}, u32[]{:S(2)}, u32[]{:S(2)}) async-start(bf16[128,8,2176]{2,1,0:T(8,128)(2,1)} %fusion.9), calls=%async_computation.1 | async-start | bytes 8912896 | tf_op jit(solution)/shard_map/all_to_all | solution.py:114
  34.7 22.5 %all-gather.4.cloned.1.call-done = bf16[256,2048]{1,0:T(8,128)(2,1)} async-done(((bf16[128,2048]{1,0:T(8,128)(2,1)}), bf16[256,2048]{1,0:T(8,128)(2,1)}) %all-gather.4.cloned.1.call-update) | async-done | bytes 1048592 | tf_op jit(solution)/shard_map/all_gather | solution.py:120
  57.2 130.1 %all-gather.6.cloned.1.call-done = bf16[2048,4608]{1,0:T(8,128)(2,1)} async-done(((bf16[32,4608]{1,0:T(8,128)(2,1)}), bf16[2048,4608]{1,0:T(8,128)(2,1)}) %all-gather.6.cloned.1.call-update) | async-done | bytes 18874384 | tf_op jit(solution)/shard_map/all_gather | solution.py:122
  187.3 6.1 fusion.3
  196.4 1.8 reshape.380
  198.2 2.0 multiply_reduce_fusion.6
  200.2 1.6 copy.185
  203.0 2.0 copy.243
  211.5 6.2 fusion.121
  217.7 4.0 fusion.115
  221.7 1.6 slice.152
  223.3 1.6 reshape.379
  224.9 2.2 convolution_convert_fusion.1
  228.0 6.7 fusion.44
  234.8 20.2 %reduce-scatter.4.cloned.1.call-done = bf16[128,2048]{1,0:T(8,128)(2,1)} async-done(((bf16[256,2048]{1,0:T(8,128)(2,1)}), bf16[128,2048]{1,0:T(8,128)(2,1)}) %reduce-scatter.4.cloned.1.call-update) | async-done | bytes 524304 | tf_op jit(solution)/shard_map/reduce_scatter | solution.py:143
  259.9 4.2 convert_bitcast_fusion.1
  264.0 9.7 all-to-all-start.1
  274.3 1.7 slice.98
  276.0 1.8 copy.233
  277.7 8.3 fusion.30
  286.0 42.1 %all-to-all-done.1 = bf16[128,8,2048]{2,1,0:T(8,128)(2,1)} async-done(((bf16[128,8,2048]{2,1,0:T(8,128)(2,1)}), bf16[128,8,2048]{2,1,0:T(8,128)(2,1)}, u32[]{:S(2)}, u32[]{:S(2)}) %all-to-all-start.1) | async-done | bytes 4194336 | tf_op jit(solution)/shard_map/all_to_all | solution.py:150
  328.1 4.0 fusion.122
  332.3 5.5 fusion.17
  337.8 9.4 multiply_convert_fusion.1
  348.2 1.8 copy.195
  350.0 1.8 copy.194
  351.7 5.0 fusion.37
  356.8 3.7 add_convert_fusion
  360.6 2.4 maximum_bitcast_fusion
  363.0 5.6 all-to-all-start.3
  369.1 59.9 %all-to-all-done.3 = bf16[128,8,2304]{2,1,0:T(8,128)(2,1)} async-done(((bf16[128,8,2304]{2,1,0:T(8,128)(2,1)}), bf16[128,8,2304]{2,1,0:T(8,128)(2,1)}, u32[]{:S(2)}, u32[]{:S(2)}) %all-to-all-start.3) | async-done | bytes 4718624 | tf_op jit(solution)/shard_map/all_to_all | solution.py:184
  429.0 3.2 convolution_bitcast_fusion.1
  433.9 2.1 multiply_reduce_fusion.3
  437.0 2.3 fusion.114
  441.9 3.1 copy.212
  447.9 13.9 %all-gather.8.cloned.1.call-done = bf16[256,2048]{1,0:T(8,128)(2,1)} async-done(((bf16[128,2048]{1,0:T(8,128)(2,1)}), bf16[256,2048]{1,0:T(8,128)(2,1)}) %all-gather.8.cloned.1.call-update) | async-done | bytes 1048592 | tf_op jit(solution)/shard_map/all_gather | solution.py:205
  461.7 6.2 fusion.60
  470.9 1.6 fusion.68
  472.5 1.9 convolution_multiply_fusion
  475.6 1.7 copy.232
  481.7 3.8 copy.237
  485.5 2.5 copy.236
  488.0 2.8 multiply_subtract_fusion
  495.3 4.6 fusion.56
  500.9 8.0 fusion.41
  509.0 9.5 fusion.124
  518.5 8.9 fusion.86
  527.5 24.7 %pad_maximum_fusion = f32[2048,4608]{1,0:T(8,128)} fusion(f32[2048,2048]{1,0:T(8,128)} %fusion.124, f32[2048,2560]{1,0:T(8,128)} %fusion.86), kind=kLoop, calls=%fused_computation.1 | loop fusion | flops 9437184 | bytes 75497472 | tf_op jit(solution)/shard_map/concatenate | solution.py:230
  553.6 6.9 convert_bitcast_fusion
  560.5 9.7 all-to-all-start.2
  570.5 9.5 convolution_bitcast_fusion
  580.1 8.9 fusion.23
  589.0 8.9 fusion.26
  597.9 26.7 %all-to-all-done.2 = bf16[128,8,2048]{2,1,0:T(8,128)(2,1)} async-done(((bf16[128,8,2048]{2,1,0:T(8,128)(2,1)}), bf16[128,8,2048]{2,1,0:T(8,128)(2,1)}, u32[]{:S(2)}, u32[]{:S(2)}) %all-to-all-start.2) | async-done | bytes 4194336 | tf_op jit(solution)/shard_map/all_to_all | solution.py:188
  624.6 4.1 fusion.51
  631.6 69.1 %all-reduce = (f32[2048]{0:T(1024)}, f32[128]{0:T(128)}, f32[128]{0:T(128)}, f32[2048]{0:T(1024)}) all-reduce(f32[2048]{0:T(1024)S(1)} %get-tuple-element.16, f32[128]{0:T(128)S(1)} %bitcast_reduce_fusion, f32[128]{0:T(128)S(1)} %bitcast_reduce_fusion.1, ...), channel_id=1, replica_groups=mesh['dp'=64,'tensor'=2] {'dp','tensor'}, use_global_device_ids=true, to_apply=%region_23.24 | all-reduce | flops 4352 | bytes 34816 | tf_op jit(solution)/shard_map/psum | solution.py:234
  700.7 4.0 fusion.71
  704.7 150.2 %reduce-scatter.8.cloned.1.call-done = f32[32,4608]{1,0:T(8,128)} async-done(((f32[2048,4608]{1,0:T(8,128)}), f32[32,4608]{1,0:T(8,128)}) %reduce-scatter.8.cloned.1.call-update) | async-done | bytes 589840 | tf_op jit(solution)/shard_map/reduce_scatter | solution.py:231
  856.3 1.9 slice_bitcast_fusion.1
  858.2 147.0 %all-reduce.3.cloned.1.call-done = f32[2048,128]{1,0:T(8,128)} async-done(((f32[2048,128]{1,0:T(8,128)}), f32[2048,128]{1,0:T(8,128)}) %all-reduce.3.cloned.1.call-update) | async-done | bytes 1048592 | tf_op jit(solution)/shard_map/psum | solution.py:234
  1005.2 2.3 copy.280
  (239 shorter events, 53.8 us)
Async XLA Ops:
  7.2 330.6 %copy-start = (bf16[1,2048,768]{2,1,0:T(8,128)(2,1)S(1)}, bf16[1,2048,768]{2,1,0:T(8,128)(2,1)}, u32[]{:S(2)}) copy-start(bf16[1,2048,768]{2,1,0:T(8,128)(2,1)} %param.28) | copy-start | bytes 9437188
  7.2 50.0 %all-gather.4.cloned.1.call-start = ((), (), s32[]{:S(2)}) async-start(), calls=%async_computation.7 | async-start | bytes 1572864 | tf_op jit(solution)/shard_map/all_gather | solution.py:120
  11.7 175.6 %all-gather.6.cloned.1.call-start = ((), (), s32[]{:S(2)}) async-start(), calls=%async_computation.8 | async-start | bytes 19169280 | tf_op jit(solution)/shard_map/all_gather | solution.py:122
  15.3 5.4 copy-start.45
  20.6 12.0 %copy-start.52 = (s32[1,256]{1,0:T(1,128)S(1)}, s32[1,256]{1,0:T(1,128)}, u32[]{:S(2)}) copy-start(s32[1,256]{1,0:T(1,128)} %param.17) | copy-start | bytes 3076
  20.6 243.4 %all-to-all-start = ((bf16[128,8,2176]{2,1,0:T(8,128)(2,1)}), bf16[128,8,2176]{2,1,0:T(8,128)(2,1)}, u32[]{:S(2)}, u32[]{:S(2)}) async-start(bf16[128,8,2176]{2,1,0:T(8,128)(2,1)} %fusion.9), calls=%async_computation.1 | async-start | bytes 8912896 | tf_op jit(solution)/shard_map/all_to_all | solution.py:114
  32.5 222.5 %reduce-scatter.4.cloned.1.call-start = ((), (), s32[]{:S(2)}) async-start(), calls=%async_computation.9 | async-start | bytes 1572864 | tf_op jit(solution)/shard_map/reduce_scatter | solution.py:143
  203.0 4.2 copy-start.51
  203.0 3.3 copy-start.60
  205.0 2.2 copy-start.3
  205.0 2.2 copy-start.62
  264.0 64.0 %all-to-all-start.1 = ((bf16[128,8,2048]{2,1,0:T(8,128)(2,1)}), bf16[128,8,2048]{2,1,0:T(8,128)(2,1)}, u32[]{:S(2)}, u32[]{:S(2)}) async-start(bf16[128,8,2048]{2,1,0:T(8,128)(2,1)} %convert_bitcast_fusion.1), calls=%async_computation.2 | async-start | bytes 8388608 | tf_op jit(solution)/shard_map/all_to_all | solution.py:150
  328.1 4.1 copy-start.66
  328.1 4.2 copy-start.69
  332.3 5.5 copy-start.72
  351.7 5.0 copy-start.70
  351.7 5.0 copy-start.74
  356.8 3.8 copy-start.33
  356.8 3.8 copy-start.34
  363.0 5.6 copy-start.14
  363.0 5.6 copy-start.16
  363.0 66.0 %copy-start.26 = (f32[128,128]{1,0:T(8,128)S(1)}, f32[128,128]{1,0:T(8,128)}, u32[]{:S(2)}) copy-start(f32[128,128]{1,0:T(8,128)} %copy-done.25) | copy-start | bytes 196612
  363.0 66.0 %copy-start.58 = (f32[8]{0:T(128)S(1)}, f32[8]{0:T(128)}, u32[]{:S(2)}) copy-start(f32[8]{0:T(128)} %copy-done.57) | copy-start | bytes 100
  363.0 65.9 %all-to-all-start.3 = ((bf16[128,8,2304]{2,1,0:T(8,128)(2,1)}), bf16[128,8,2304]{2,1,0:T(8,128)(2,1)}, u32[]{:S(2)}, u32[]{:S(2)}) async-start(bf16[128,8,2304]{2,1,0:T(8,128)(2,1)} %maximum_bitcast_fusion), calls=%async_computation.4 | async-start | bytes 9437184 | tf_op jit(solution)/shard_map/all_to_all | solution.py:184
  368.6 93.1 %all-gather.8.cloned.1.call-start = ((), (), s32[]{:S(2)}) async-start(), calls=%async_computation.10 | async-start | bytes 1572864 | tf_op jit(solution)/shard_map/all_gather | solution.py:205
  369.0 64.8 %copy-start.2 = (bf16[128,2048]{1,0:T(8,128)(2,1)S(1)}, bf16[128,2048]{1,0:T(8,128)(2,1)}, u32[]{:S(2)}) copy-start(bf16[128,2048]{1,0:T(8,128)(2,1)} %param.16) | copy-start | bytes 1572868
  369.1 64.8 %copy-start.6 = (bf16[128,2048]{1,0:T(8,128)(2,1)S(1)}, bf16[128,2048]{1,0:T(8,128)(2,1)}, u32[]{:S(2)}) copy-start(bf16[128,2048]{1,0:T(8,128)(2,1)} %reduce-scatter.4.cloned.1.call-done) | copy-start | bytes 1572868
  369.1 64.8 %copy-start.46 = (f32[2048]{0:T(1024)S(1)}, f32[2048]{0:T(1024)}, u32[]{:S(2)}) copy-start(f32[2048]{0:T(1024)} %param.26) | copy-start | bytes 24580
  433.9 8.0 copy-start.5
  439.3 190.8 %reduce-scatter.6.cloned.1.call-start = ((), (), s32[]{:S(2)}) async-start(), calls=%async_computation.11 | async-start | bytes 1572864 | tf_op jit(solution)/shard_map/reduce_scatter | solution.py:227
  447.8 20.3 %copy-start.38 = (bf16[256,2,128]{2,1,0:T(2,128)(2,1)S(1)}, bf16[256,2,128]{2,1,0:T(2,128)(2,1)}, u32[]{:S(2)}) copy-start(bf16[256,2,128]{2,1,0:T(2,128)(2,1)} %reshape.379) | copy-start | bytes 393220
  447.9 20.3 %copy-start.48 = (f32[2,8,256]{2,1,0:T(8,128)S(1)}, f32[2,8,256]{2,1,0:T(8,128)}, u32[]{:S(2)}) copy-start(f32[2,8,256]{2,1,0:T(8,128)} %get-tuple-element.73) | copy-start | bytes 49156
  461.7 6.4 copy-start.7
  472.5 1.9 copy-start.11
  474.4 5.8 copy-start.12
  481.7 3.8 copy-start.22
  481.7 6.3 copy-start.29
  488.0 2.9 copy-start.4
  488.0 2.9 copy-start.61
  490.8 2.0 copy-start.39
  490.8 2.4 copy-start.10
  490.8 2.4 copy-start.35
  490.9 2.4 copy-start.67
  490.9 2.5 copy-start.31
  495.2 5.6 copy-start.36
  500.9 8.1 copy-start.19
  508.9 9.6 copy-start.24
  508.9 346.0 %reduce-scatter.8.cloned.1.call-start = ((), (), s32[]{:S(2)}) async-start(), calls=%async_computation.12 | async-start | bytes 38338560 | tf_op jit(solution)/shard_map/reduce_scatter | solution.py:231
  509.0 9.6 copy-start.28
  560.5 64.0 %all-to-all-start.2 = ((bf16[128,8,2048]{2,1,0:T(8,128)(2,1)}), bf16[128,8,2048]{2,1,0:T(8,128)(2,1)}, u32[]{:S(2)}, u32[]{:S(2)}) async-start(bf16[128,8,2048]{2,1,0:T(8,128)(2,1)} %convert_bitcast_fusion), calls=%async_computation.3 | async-start | bytes 8388608 | tf_op jit(solution)/shard_map/all_to_all | solution.py:188
  570.2 9.9 copy-start.71
  570.2 434.9 %all-reduce.3.cloned.1.call-start = ((), (), s32[]{:S(2)}) async-start(), calls=%async_computation.13 | async-start | bytes 2097152 | tf_op jit(solution)/shard_map/psum | solution.py:234
  580.1 8.9 copy-start.75
  589.0 35.6 %copy-start.27 = (f32[128,128]{1,0:T(8,128)S(1)}, f32[128,128]{1,0:T(8,128)}, u32[]{:S(2)}) copy-start(f32[128,128]{1,0:T(8,128)} %copy-done.25) | copy-start | bytes 196612
  589.0 35.6 %copy-start.59 = (f32[8]{0:T(128)S(1)}, f32[8]{0:T(128)}, u32[]{:S(2)}) copy-start(f32[8]{0:T(128)} %copy-done.57) | copy-start | bytes 100
  597.9 30.8 %copy-start.15 = (bf16[128,2048]{1,0:T(8,128)(2,1)S(1)}, bf16[128,2048]{1,0:T(8,128)(2,1)}, u32[]{:S(2)}) copy-start(bf16[128,2048]{1,0:T(8,128)(2,1)} %copy-done.13) | copy-start | bytes 1572868
  597.9 30.8 %copy-start.44 = (bf16[128,128]{0,1:T(8,128)(2,1)S(1)}, bf16[128,128]{0,1:T(8,128)(2,1)}, u32[]{:S(2)}) copy-start(bf16[128,128]{0,1:T(8,128)(2,1)} %copy-done.43) | copy-start | bytes 98308
  597.9 32.2 %copy-start.47 = (f32[2048]{0:T(1024)S(1)}, f32[2048]{0:T(1024)}, u32[]{:S(2)}) copy-start(f32[2048]{0:T(1024)} %param.19) | copy-start | bytes 24580
  597.9 32.2 %copy-start.56 = (f32[128]{0:T(128)S(1)}, f32[128]{0:T(128)}, u32[]{:S(2)}) copy-start(f32[128]{0:T(128)} %copy-done.55) | copy-start | bytes 1540
  628.7 72.0 %copy-start.54 = (f32[128]{0:T(128)S(1)}, f32[128]{0:T(128)}, u32[]{:S(2)}) copy-start(f32[128]{0:T(128)} %copy-done.53) | copy-start | bytes 1540
  628.7 72.0 %copy-start.63 = (f32[128]{0:T(128)S(1)}, f32[128]{0:T(128)}, u32[]{:S(2)}) copy-start(f32[128]{0:T(128)} %get-tuple-element.69) | copy-start | bytes 1540
  628.7 72.0 %copy-start.65 = (f32[128]{0:T(128)S(1)}, f32[128]{0:T(128)}, u32[]{:S(2)}) copy-start(f32[128]{0:T(128)} %copy-done.64) | copy-start | bytes 1540
  628.7 72.0 %copy-start.68 = (f32[128]{0:T(128)S(1)}, f32[128]{0:T(128)}, u32[]{:S(2)}) copy-start(f32[128]{0:T(128)} %get-tuple-element.67) | copy-start | bytes 1540
  700.7 306.7 %copy-start.1 = (bf16[1,2048,768]{2,1,0:T(8,128)(2,1)S(1)}, bf16[1,2048,768]{2,1,0:T(8,128)(2,1)}, u32[]{:S(2)}) copy-start(bf16[1,2048,768]{2,1,0:T(8,128)(2,1)} %param.28) | copy-start | bytes 9437188
  (23 other events, 26.4 us)
Sparse Core Ops, SparseCore 0:
  11.8 45.3 all-gather.3
  61.1 126.1 all-gather.5
  234.9 20.0 reduce-scatter.3
  439.4 22.2 all-gather.7
  509.0 23.8 reduce-scatter.5
  552.3 302.5 reduce-scatter.7
  859.7 145.4 all-reduce.2

commit v2 on v1

--- a/solution.py
+++ b/solution.py
@@ -3,6 +3,8 @@
 import jax
 import jax.numpy as jnp
 from jax import lax
+from jax.experimental import pallas as pl
+from jax.experimental.pallas import tpu as pltpu
 from jax.sharding import PartitionSpec as P
 
 BLOCK = 128
@@ -64,6 +66,450 @@
     frequency = jnp.exp(-jnp.log(ROPE_BASE) * jnp.arange(half, dtype=F32) * 2.0 / head_size)
     angles = position.astype(F32)[:, None] * frequency[None, :]
     return jnp.cos(angles)[:, None, :], jnp.sin(angles)[:, None, :]
+
+
+MESH = pl.DeviceIdType.MESH
+ANY = pl.BlockSpec(memory_space=pl.ANY)
+VMEM = pl.BlockSpec(memory_space=pltpu.VMEM)
+NX, NYH, NZ, NC = 4, 2, 4, 2
+RING = 4
+
+
+class Place:
+    def __init__(self):
+        dp = lax.axis_index("dp")
+        self.t = lax.axis_index("tensor")
+        self.c = lax.rem(dp, NC)
+        self.z = lax.rem(dp // NC, NZ)
+        self.yh = lax.rem(dp // (NC * NZ), NYH)
+        self.x = dp // (NC * NZ * NYH)
+
+    def device(self, x=None, yh=None, z=None, c=None, t=None):
+        pick = lambda given, own: own if given is None else given
+        x, yh, z, c = pick(x, self.x), pick(yh, self.yh), pick(z, self.z), pick(c, self.c)
+        return (((x * NYH + yh) * NZ + z) * NC + c, pick(t, self.t))
+
+
+def after(i):
+    return lax.rem(i + 1, RING)
+
+
+def before(i):
+    return lax.rem(i + RING - 1, RING)
+
+
+def across(i):
+    return lax.rem(i + 2, RING)
+
+
+def greet(peers):
+    barrier = pltpu.get_barrier_semaphore()
+    for peer in peers:
+        pl.semaphore_signal(barrier, inc=1, device_id=peer, device_id_type=MESH)
+    pl.semaphore_wait(barrier, len(peers))
+
+
+class Copies:
+    def __init__(self, send, recv, local):
+        self.send, self.recv, self.local = send, recv, local
+        self.n = self.m = 0
+        self.sent = []
+
+    def put(self, src, dst, peer):
+        copy = pltpu.make_async_remote_copy(
+            src_ref=src,
+            dst_ref=dst,
+            send_sem=self.send.at[self.n],
+            recv_sem=self.recv.at[self.n],
+            device_id=peer,
+            device_id_type=MESH,
+        )
+        self.n += 1
+        copy.start()
+        self.sent.append(copy)
+        return copy
+
+    def keep(self, src, dst):
+        copy = pltpu.make_async_copy(src, dst, self.local.at[self.m])
+        self.m += 1
+        copy.start()
+        return copy
+
+    def finish(self):
+        for copy in self.sent:
+            copy.wait_send()
+
+
+def gather_kernel(sa, sb, tok, doc, wa, wb, toks, docs, send, recv, local):
+    me = Place()
+    x, yh, z, c, t = me.x, me.yh, me.z, me.c, me.t
+    sibling = me.device(c=1 - c)
+    pair = me.device(yh=1 - yh)
+    partner = me.device(t=1 - t)
+    ring_x = (me.device(x=after(x)), me.device(x=before(x)))
+    ring_z = (me.device(z=after(z)), me.device(z=before(z)))
+    greet([sibling, pair, partner, *ring_x, *ring_z])
+    go = Copies(send, recv, local)
+
+    shards = ((sa, wa), (sb, wb))
+    cores = [go.put(s.at[1 - c], w.at[x, yh, z, c], sibling) for s, w in shards]
+    kept = [go.keep(s.at[c], w.at[x, yh, z, c]) for s, w in shards]
+    to_partner = go.put(tok, toks.at[c, t], partner)
+    rest = [go.keep(tok, toks.at[c, t]), go.keep(doc, docs.at[c])]
+    tail = [go.put(tok, toks.at[c, t], sibling), go.put(doc, docs.at[c], sibling)]
+    for copy in kept:
+        copy.wait()
+    for copy in cores:
+        copy.wait_recv()
+    pairs = [go.put(w.at[x, yh, z], w.at[x, yh, z], pair) for _, w in shards]
+
+    ways = (
+        (wa, x, z, ring_x, ring_z, lambda w, i, j, y: w.at[i, y, j], lambda w, j, y: w.at[:, y, j]),
+        (wb, z, x, ring_z, ring_x, lambda w, i, j, y: w.at[j, y, i], lambda w, j, y: w.at[j, y]),
+    )
+
+    def first(y):
+        out = []
+        for w, i, j, one, two, unit, slab in ways:
+            own = unit(w, i, j, y)
+            out.append((go.put(own, own, one[0]), go.put(own, own, one[1])))
+        return out
+
+    def second(y, firsts):
+        out = []
+        for (w, i, j, one, two, unit, slab), (up, down) in zip(ways, firsts):
+            up.wait_recv()
+            low = unit(w, before(i), j, y).at[0]
+            a = go.put(low, low, one[0])
+            down.wait_recv()
+            high = unit(w, after(i), j, y).at[1]
+            out.append((a, go.put(high, high, one[1])))
+        return out
+
+    def third(y, seconds):
+        out = []
+        for (w, i, j, one, two, unit, slab), (up, down) in zip(ways, seconds):
+            up.wait_recv()
+            down.wait_recv()
+            own = slab(w, j, y)
+            out.append((go.put(own, own, two[0]), go.put(own, own, two[1])))
+        return out
+
+    def fourth(y, thirds):
+        out = []
+        for (w, i, j, one, two, unit, slab), (up, down) in zip(ways, thirds):
+            up.wait_recv()
+            low = slab(w, before(j), y).at[:, 0]
+            a = go.put(low, low, two[0])
+            down.wait_recv()
+            high = slab(w, after(j), y).at[:, 1]
+            out.append((a, go.put(high, high, two[1])))
+        return out
+
+    near = first(yh)
+    near = second(yh, near)
+    for copy in pairs:
+        copy.wait_recv()
+    far = first(1 - yh)
+    near = third(yh, near)
+    far = second(1 - yh, far)
+    to_partner.wait_recv()
+    other = toks.at[c, 1 - t]
+    tail.append(go.put(other, other, sibling))
+    far = third(1 - yh, far)
+    near = fourth(yh, near)
+    far = fourth(1 - yh, far)
+    for up, down in near + far:
+        up.wait_recv()
+        down.wait_recv()
+    for copy in tail:
+        copy.wait_recv()
+    for copy in rest:
+        copy.wait()
+    go.finish()
+
+
+def gather(shard_a, shard_b, tokens, docs):
+    width_a, width_b = shard_a.shape[-1], shard_b.shape[-1]
+    rows = shard_a.shape[1]
+    lead = (NX, NYH, NZ, NC, rows)
+    wa, wb, toks, docs = pl.pallas_call(
+        gather_kernel,
+        name="gather_weights",
+        out_shape=(
+            jax.ShapeDtypeStruct((*lead, width_a), BF16),
+            jax.ShapeDtypeStruct((*lead, width_b), BF16),
+            jax.ShapeDtypeStruct((NC, 2, *tokens.shape), BF16),
+            jax.ShapeDtypeStruct((NC, *docs.shape), docs.dtype),
+        ),
+        in_specs=[ANY] * 4,
+        out_specs=(ANY,) * 4,
+        scratch_shapes=[
+            pltpu.SemaphoreType.DMA((40,)),
+            pltpu.SemaphoreType.DMA((40,)),
+            pltpu.SemaphoreType.DMA((4,)),
+        ],
+        compiler_params=pltpu.CompilerParams(collective_id=1, has_side_effects=True),
+    )(shard_a, shard_b, tokens, docs)
+    depth = NX * NYH * NZ * NC * rows
+    return (
+        wa.reshape(depth, width_a),
+        wb.reshape(depth, width_b),
+        toks.reshape(NC * 2 * tokens.shape[0], tokens.shape[1]),
+        docs,
+    )
+
+
+def share_kernel(tok, toks, send, recv, local):
+    me = Place()
+    c, t = me.c, me.t
+    sibling, partner = me.device(c=1 - c), me.device(t=1 - t)
+    greet([sibling, partner])
+    go = Copies(send, recv, local)
+    half = tok.shape[0] // 2
+    parts = [pl.ds(i * half, half) for i in range(2)]
+    over = [go.put(tok.at[p], toks.at[c, t, p], partner) for p in parts]
+    near = [go.put(tok, toks.at[c, t], sibling)]
+    kept = go.keep(tok, toks.at[c, t])
+    for copy, p in zip(over, parts):
+        copy.wait_recv()
+        other = toks.at[c, 1 - t, p]
+        near.append(go.put(other, other, sibling))
+    for copy in near:
+        copy.wait_recv()
+    kept.wait()
+    go.finish()
+
+
+def share(tokens, ident):
+    toks = pl.pallas_call(
+        share_kernel,
+        name=f"share_rows_{ident}",
+        out_shape=jax.ShapeDtypeStruct((NC, 2, *tokens.shape), tokens.dtype),
+        in_specs=[ANY],
+        out_specs=ANY,
+        scratch_shapes=[
+            pltpu.SemaphoreType.DMA((5,)),
+            pltpu.SemaphoreType.DMA((5,)),
+            pltpu.SemaphoreType.DMA((1,)),
+        ],
+        compiler_params=pltpu.CompilerParams(collective_id=ident, has_side_effects=True),
+    )(tokens)
+    return toks.reshape(NC * 2 * tokens.shape[0], tokens.shape[1])
+
+
+def reduce_kernel(part, out, near, own, sums, far, send, recv, local):
+    me = Place()
+    c, t = me.c, me.t
+    sibling, partner = me.device(c=1 - c), me.device(t=1 - t)
+    greet([sibling, partner])
+    go = Copies(send, recv, local)
+    half = out.shape[0] // 2
+    parts = [pl.ds(i * half, half) for i in range(2)]
+    away = [go.put(part.at[1 - c, 1 - t, p], near.at[0, p], sibling) for p in parts]
+    home = go.put(part.at[1 - c, t], near.at[1], sibling)
+    kept = [go.keep(part.at[c, 1 - t], own.at[0]), go.keep(part.at[c, t], own.at[1])]
+    kept[0].wait()
+    over = []
+    for copy, p in zip(away, parts):
+        copy.wait_recv()
+        sums[p] = (own[0, p].astype(F32) + near[0, p].astype(F32)).astype(BF16)
+        over.append(go.put(sums.at[p], far.at[p], partner))
+    kept[1].wait()
+    home.wait_recv()
+    out[...] = own[1].astype(F32) + near[1].astype(F32)
+    for copy, p in zip(over, parts):
+        copy.wait_recv()
+        out[p] += far[p].astype(F32)
+    go.finish()
+
+
+def reduce(part, ident):
+    rows, width = part.shape[0] // (NC * 2), part.shape[1]
+    return pl.pallas_call(
+        reduce_kernel,
+        name=f"reduce_rows_{ident}",
+        out_shape=jax.ShapeDtypeStruct((rows, width), F32),
+        in_specs=[ANY],
+        out_specs=VMEM,
+        scratch_shapes=[
+            pltpu.VMEM((2, rows, width), BF16),
+            pltpu.VMEM((2, rows, width), BF16),
+            pltpu.VMEM((rows, width), BF16),
+            pltpu.VMEM((rows, width), BF16),
+            pltpu.SemaphoreType.DMA((5,)),
+            pltpu.SemaphoreType.DMA((5,)),
+            pltpu.SemaphoreType.DMA((2,)),
+        ],
+        compiler_params=pltpu.CompilerParams(
+            collective_id=ident, has_side_effects=True, vmem_limit_bytes=24 << 20
+        ),
+    )(part.reshape(NC, 2, rows, width))
+
+
+def scatter_kernel(
+    ga, gb, oa, ob, ka, kb, ra, rb, qa, qb, sa, sb, ya, yb, ma, mb, ta, tb, ca, cb, send, recv, local
+):
+    me = Place()
+    x, yh, z, c = me.x, me.yh, me.z, me.c
+    sibling = me.device(c=1 - c)
+    pair = me.device(yh=1 - yh)
+    ring_x = (me.device(x=after(x)), me.device(x=before(x)))
+    ring_z = (me.device(z=after(z)), me.device(z=before(z)))
+    greet([sibling, pair, *ring_x, *ring_z])
+    go = Copies(send, recv, local)
+
+    def slab_a(i, r):
+        return ga.at[i, :, :, r]
+
+    def slab_b(i, r):
+        return gb.at[:, :, i, r]
+
+    ways = ((slab_a, x, ring_x, ka, ra), (slab_b, z, ring_z, kb, rb))
+    cross, straight, kept = [], [], []
+    for slab, i, ring, k, r in ways:
+        cross.append((go.put(slab(across(i), 0), r.at[0], ring[0]), go.put(slab(across(i), 1), r.at[1], ring[1])))
+    for slab, i, ring, k, r in ways:
+        kept.append(
+            [
+                go.keep(slab(after(i), 0), k.at[0]),
+                go.keep(slab(before(i), 1), k.at[1]),
+                go.keep(slab(i, 0), k.at[2]),
+                go.keep(slab(i, 1), k.at[3]),
+            ]
+        )
+        straight.append((go.put(slab(after(i), 1), r.at[2], ring[0]), go.put(slab(before(i), 0), r.at[3], ring[1])))
+    summed = []
+    for (slab, i, ring, k, r), copies, own in zip(ways, cross, kept):
+        both = []
+        for side in range(2):
+            own[side].wait()
+            copies[side].wait_recv()
+
+            def add(n, _, k=k, r=r, side=side):
+                at = (side, n // k.shape[2], lax.rem(n, k.shape[2]))
+                k[at] = (k[at].astype(F32) + r[at].astype(F32)).astype(BF16)
+                return 0
+
+            lax.fori_loop(0, k.shape[1] * k.shape[2], add, 0)
+            both.append(go.put(k.at[side], r.at[4 + side], ring[side]))
+        summed.append(both)
+    for (slab, i, ring, k, r), one, two, own in zip(ways, straight, summed, kept):
+        own[2].wait()
+        own[3].wait()
+        one[0].wait_recv()
+        one[1].wait_recv()
+        two[0].wait_recv()
+        two[1].wait_recv()
+
+        def close(n, _, k=k, r=r):
+            at = (n // k.shape[2], lax.rem(n, k.shape[2]))
+            for own, summed_side, straight_side in ((2, 4, 3), (3, 5, 2)):
+                k[(own, *at)] = (
+                    k[(own, *at)].astype(F32)
+                    + r[(summed_side, *at)].astype(F32)
+                    + r[(straight_side, *at)].astype(F32)
+                ).astype(BF16)
+            return 0
+
+        lax.fori_loop(0, k.shape[1] * k.shape[2], close, 0)
+
+    def part_a(r, j, y):
+        return ka.at[r, y, j]
+
+    def part_b(r, j, y):
+        return kb.at[r, j, y]
+
+    ways = ((part_a, z, ring_z, qa, sa), (part_b, x, ring_x, qb, sb))
+    cross, straight, summed = [], [], []
+    for part, j, ring, q, s in ways:
+        cross.append(
+            [
+                [go.put(part(2 + side, across(j), y), q.at[side, y], ring[side]) for y in range(NYH)]
+                for side in range(2)
+            ]
+        )
+    for part, j, ring, q, s in ways:
+        straight.append(
+            [
+                [go.put(part(3 - side, (after, before)[side](j), y), q.at[2 + side, y], ring[side]) for y in range(NYH)]
+                for side in range(2)
+            ]
+        )
+    for (part, j, ring, q, s), copies in zip(ways, cross):
+        both = []
+        for side in range(2):
+            sent = []
+            for y in range(NYH):
+                copies[side][y].wait_recv()
+                mine = part(2 + side, (after, before)[side](j), y)
+                s[side, y] = (mine[...].astype(F32) + q[side, y].astype(F32)).astype(BF16)
+                sent.append(go.put(s.at[side, y], q.at[4 + side, y], ring[side]))
+            both.append(sent)
+        summed.append(both)
+    for (part, j, ring, q, s), one, two in zip(ways, straight, summed):
+        for copies in (*one, *two):
+            for copy in copies:
+                copy.wait_recv()
+
+    def total(part, j, q, side, y):
+        return part(2 + side, j, y)[...].astype(F32) + q[4 + side, y].astype(F32) + q[3 - side, y].astype(F32)
+
+    ways = ((part_a, z, qa, ya, ma, ta, ca, oa), (part_b, x, qb, yb, mb, tb, cb, ob))
+    crossed = []
+    for part, j, q, yy, m, tt, cc, o in ways:
+        for side in range(2):
+            yy[side] = total(part, j, q, side, 1 - yh).astype(BF16)
+        crossed.append(go.put(yy, m, pair))
+    last = []
+    for (part, j, q, yy, m, tt, cc, o), copy in zip(ways, crossed):
+        for side in range(2):
+            tt[side] = total(part, j, q, side, yh)
+        copy.wait_recv()
+        tt[...] += m[...].astype(F32)
+        last.append(go.put(tt.at[1 - c], cc, sibling))
+        o[c] = tt[c]
+    for (part, j, q, yy, m, tt, cc, o), copy in zip(ways, last):
+        copy.wait_recv()
+        o[1 - c] = cc[...]
+    go.finish()
+
+
+def scatter(grad_a, grad_b):
+    rows = grad_a.shape[0] // (NX * NYH * NZ * NC)
+    lead = (NX, NYH, NZ, NC, rows)
+    widths = (grad_a.shape[1], grad_b.shape[1])
+
+    def each(shape, dtype):
+        return [pltpu.VMEM((*shape, rows, w), dtype) for w in widths]
+
+    def held(count):
+        dims = ((NYH, NZ), (NX, NYH))
+        return [pltpu.VMEM((count, *d, rows, w), BF16) for d, w in zip(dims, widths)]
+
+    return pl.pallas_call(
+        scatter_kernel,
+        name="scatter_weights",
+        out_shape=tuple(jax.ShapeDtypeStruct((NC, rows, w), F32) for w in widths),
+        in_specs=[ANY, ANY],
+        out_specs=(VMEM, VMEM),
+        scratch_shapes=[
+            *held(4),
+            *held(6),
+            *each((6, NYH), BF16),
+            *each((2, NYH), BF16),
+            *each((2,), BF16),
+            *each((2,), BF16),
+            *each((2,), F32),
+            *each((), F32),
+            pltpu.SemaphoreType.DMA((40,)),
+            pltpu.SemaphoreType.DMA((40,)),
+            pltpu.SemaphoreType.DMA((8,)),
+        ],
+        compiler_params=pltpu.CompilerParams(
+            collective_id=5, has_side_effects=True, vmem_limit_bytes=40 << 20
+        ),
+    )(grad_a.reshape(*lead, widths[0]), grad_b.reshape(*lead, widths[1]))
 
 
 def on_device(
@@ -117,32 +563,35 @@
 
     hidden = hidden_in.astype(F32)
     normed_local = rms_scale(hidden, attn_gain).astype(BF16)
-    normed = lax.all_gather(normed_local, "tensor", axis=0, tiled=True)
-    shard = jnp.concatenate([query_weight, key_weight, value_weight, output_weight.T], axis=1)
-    weights = lax.all_gather(shard, "dp", axis=0, tiled=True)
-    nqkv = (nq + 2 * nkv) * hd
-    in_weights = weights[:, :nqkv]
-    out_weights = weights[:, nqkv:]
-
-    position, allowed = layout(doc_ids[0])
-    cosine, sine = rotary(position, hd)
+
+    def core_parts(shards):
+        split = [s.reshape(s.shape[0], NC, s.shape[1] // NC) for s in shards]
+        return jnp.concatenate(split, axis=2).transpose(1, 0, 2)
+
+    in_weights, out_weights, normed, docs = gather(
+        core_parts([query_weight, key_weight, value_weight]),
+        core_parts([output_weight.T]),
+        normed_local,
+        jnp.broadcast_to(doc_ids, (8, tokens)).astype(F32),
+    )
+
+    position, allowed = jax.vmap(layout)(docs[:, 0])
+    cosine, sine = jax.vmap(lambda p: rotary(p, hd))(position)
     raw = dot_nn(normed, in_weights)
-    query_raw = raw[:, : nq * hd].reshape(tokens, nq, hd)
-    key_raw = raw[:, nq * hd : (nq + nkv) * hd].reshape(tokens, nkv, hd)
-    values = raw[:, (nq + nkv) * hd :].astype(BF16).reshape(tokens, nkv, hd)
+    heads = group * hd
+    query_raw = raw[:, :heads].reshape(NC, tokens, group, hd)
+    key_raw = raw[:, heads : heads + hd].reshape(NC, tokens, 1, hd)
+    values = raw[:, heads + hd :].astype(BF16).reshape(NC, tokens, hd)
     query = rotate(rms_scale(query_raw, query_gain), cosine, sine).astype(BF16)
-    query = query.reshape(tokens, nkv, group, hd)
-    key = rotate(rms_scale(key_raw, key_gain), cosine, sine).astype(BF16)
-    scores = jnp.einsum("qkgd,tkd->kgqt", query, key, preferred_element_type=F32) * scale
-    scores = jnp.where(allowed[None, None], scores, MASKED)
+    key = rotate(rms_scale(key_raw, key_gain), cosine, sine).astype(BF16)[:, :, 0]
+    scores = jnp.einsum("bqgd,btd->bgqt", query, key, preferred_element_type=F32) * scale
+    scores = jnp.where(allowed[:, None], scores, MASKED)
     weight = jnp.exp(scores - jnp.max(scores, axis=-1, keepdims=True))
     attention = weight / jnp.sum(weight, axis=-1, keepdims=True)
     attention_low = attention.astype(BF16)
-    mixed = jnp.einsum("kgqt,tkd->qkgd", attention_low, values, preferred_element_type=F32)
-    mixed = mixed.astype(BF16).reshape(tokens, nq * hd)
-    attn_out = lax.psum_scatter(
-        dot_nt(mixed, out_weights).astype(BF16), "tensor", scatter_dimension=0, tiled=True
-    ).astype(F32)
+    mixed = jnp.einsum("bgqt,btd->bqgd", attention_low, values, preferred_element_type=F32)
+    mixed = mixed.astype(BF16).reshape(NC * tokens, heads)
+    attn_out = reduce(dot_nt(mixed, out_weights).astype(BF16), 2)
 
     residual = hidden + attn_out
     moe_input = rms_scale(residual, moe_gain).astype(BF16)
@@ -202,53 +651,72 @@
     grad_norm, moegain_rows = rms_back(residual, moe_gain, grad_moe_input)
     moegain_part = jnp.sum(moegain_rows, axis=0)
     grad_residual = upstream + grad_norm
-    grad_attn = lax.all_gather(grad_residual.astype(BF16), "tensor", axis=0, tiled=True)
+    grad_attn = share(grad_residual.astype(BF16), 3)
     layer_out = (residual + dot_tn(spread, returned)).astype(BF16)
 
-    grad_mixed = dot_nn(grad_attn, out_weights).astype(BF16).reshape(tokens, nkv, group, hd)
-    grad_values = jnp.einsum("kgqt,qkgd->tkd", attention_low, grad_mixed, preferred_element_type=F32)
-    grad_soft = jnp.einsum("qkgd,tkd->kgqt", grad_mixed, values, preferred_element_type=F32)
+    grad_mixed = dot_nn(grad_attn, out_weights).astype(BF16).reshape(NC, tokens, group, hd)
+    grad_values = jnp.einsum("bgqt,bqgd->btd", attention_low, grad_mixed, preferred_element_type=F32)
+    grad_soft = jnp.einsum("bqgd,btd->bgqt", grad_mixed, values, preferred_element_type=F32)
     row_delta = jnp.sum(attention * grad_soft, axis=-1, keepdims=True)
     grad_scores = (attention * (grad_soft - row_delta)).astype(BF16)
-    grad_query = jnp.einsum("kgqt,tkd->qkgd", grad_scores, key, preferred_element_type=F32) * scale
-    grad_key = jnp.einsum("kgqt,qkgd->tkd", grad_scores, query, preferred_element_type=F32) * scale
-    grad_query_raw, qgain_rows = rms_back(
-        query_raw, query_gain, rotate(grad_query.reshape(tokens, nq, hd), cosine, -sine)
-    )
-    grad_key_raw, kgain_rows = rms_back(key_raw, key_gain, rotate(grad_key, cosine, -sine))
+    grad_query = jnp.einsum("bgqt,btd->bqgd", grad_scores, key, preferred_element_type=F32) * scale
+    grad_key = jnp.einsum("bgqt,bqgd->btd", grad_scores, query, preferred_element_type=F32) * scale
+    grad_query_raw, qgain_rows = rms_back(query_raw, query_gain, rotate(grad_query, cosine, -sine))
+    grad_key_raw, kgain_rows = rms_back(
+        key_raw, key_gain, rotate(grad_key[:, :, None], cosine, -sine)
+    )
     grad_raw = jnp.concatenate(
         [
-            grad_query_raw.astype(BF16).reshape(tokens, nq * hd),
-            grad_key_raw.astype(BF16).reshape(tokens, nkv * hd),
-            grad_values.astype(BF16).reshape(tokens, nkv * hd),
+            grad_query_raw.astype(BF16).reshape(NC * tokens, heads),
+            grad_key_raw.astype(BF16).reshape(NC * tokens, hd),
+            grad_values.astype(BF16).reshape(NC * tokens, hd),
         ],
         axis=1,
     )
-    grad_normed = lax.psum_scatter(
-        dot_nt(grad_raw, in_weights).astype(BF16), "tensor", scatter_dimension=0, tiled=True
-    ).astype(F32)
-    weight_part = jnp.concatenate([dot_tn(normed, grad_raw), dot_tn(grad_attn, mixed)], axis=1)
-    weight_grad = lax.psum_scatter(weight_part, "dp", scatter_dimension=0, tiled=True)
+    grad_normed = reduce(dot_nt(grad_raw, in_weights).astype(BF16), 4)
+    in_grad, out_grad = scatter(
+        dot_tn(normed, grad_raw).astype(BF16), dot_tn(grad_attn, mixed).astype(BF16)
+    )
     grad_hidden, attngain_rows = rms_back(hidden, attn_gain, grad_normed)
     input_grad = grad_residual + grad_hidden
-    router_grad, attngain_grad, moegain_grad, qgain_grad, kgain_grad = lax.psum(
-        (
-            router_part,
-            jnp.sum(attngain_rows, axis=0),
-            moegain_part,
-            jnp.sum(qgain_rows, axis=(0, 1)),
-            jnp.sum(kgain_rows, axis=(0, 1)),
-        ),
-        both,
-    )
+
+    def all_sum(flat):
+        copies = jnp.broadcast_to(flat[None], (experts, *flat.shape))
+        return jnp.sum(lax.all_to_all(copies, both, 0, 0, tiled=True), axis=0)
+
+    def all_sum_long(rows):
+        pieces = rows.reshape(experts, rows.shape[0] // experts, rows.shape[1])
+        piece = jnp.sum(lax.all_to_all(pieces, both, 0, 0, tiled=True), axis=0)
+        copies = jnp.broadcast_to(piece[None], pieces.shape)
+        return lax.all_to_all(copies, both, 0, 0, tiled=True).reshape(rows.shape)
+
+    router_grad = all_sum_long(router_part)
+    gains = all_sum(
+        jnp.concatenate(
+            [
+                jnp.sum(attngain_rows, axis=0),
+                moegain_part,
+                jnp.sum(qgain_rows, axis=(0, 1, 2)),
+                jnp.sum(kgain_rows, axis=(0, 1, 2)),
+            ]
+        ).reshape(-1, hd)
+    ).reshape(-1)
+    attngain_grad = gains[:width]
+    moegain_grad = gains[width : 2 * width]
+    qgain_grad = gains[2 * width : 2 * width + hd]
+    kgain_grad = gains[2 * width + hd :]
+
+    def join(parts):
+        return jnp.concatenate([parts[i] for i in range(NC)], axis=1)
+
     return (
         layer_out,
         input_grad,
         attngain_grad,
-        weight_grad[:, : nq * hd],
-        weight_grad[:, nq * hd : (nq + nkv) * hd],
-        weight_grad[:, (nq + nkv) * hd : nqkv],
-        weight_grad[:, nqkv:].T,
+        join(in_grad[:, :, :heads]),
+        join(in_grad[:, :, heads : heads + hd]),
+        join(in_grad[:, :, heads + hd :]),
+        join(out_grad).T,
         qgain_grad,
         kgain_grad,
         moegain_grad,

time: 1020 us -> 680 us (0.67)
  waiting for transfers between devices: 613 us -> 176 us
  Pallas kernels: 0 us -> 226 us
  blocking collectives: 69.1 us -> 0 us
  other arithmetic: 71.6 us -> 45.6 us
  matrix products: 150 us -> 129 us
  local copies, waits for them, and re-layouts: 58.5 us -> 44.6 us
  between operations: 15.5 us -> 1.93 us
    pallas_call x0 -> x5, Pallas kernels: none -> 226 us  [the longest x1 96.3 us: scatter(): pl.pallas_call(scatter_kernel, name='scatter_weights', out_shape=tuple((j...]
    reduce_scatter x3 -> x0, waiting for transfers between devices: 170 us -> none  [the longest x1 150 us: on_device(): lax.psum_scatter(weight_part, 'dp', scatter_dimension=0, tiled=True)]
    all_gather x3 -> x0, waiting for transfers between devices: 166 us -> none  [the longest x1 130 us: on_device(): weights = lax.all_gather(shard, 'dp', axis=0, tiled=True)]
    psum x1 -> x0, waiting for transfers between devices: 147 us -> none  [on_device(): lax.psum((router_part, jnp.sum(attngain_rows, axis=0), moegain_part, jnp....]
    psum x1 -> x0, blocking collectives: 69.1 us -> none  [on_device(): lax.psum((router_part, jnp.sum(attngain_rows, axis=0), moegain_part, jnp....]
    all_to_all x1, waiting for transfers between devices: 0.01 us -> 49 us  [on_device(): lax.all_to_all(cot_out.reshape(experts, cap, width + experts), both, spli...]
    all_to_all x1, waiting for transfers between devices: 59.9 us -> 27.1 us  [on_device(): lax.all_to_all(home_out.reshape(experts, cap, width + 2 * experts), both,...]
    concatenate x2 -> x4, other arithmetic: 26.5 us -> 3.81 us  [the longest x3 1.96 us: join(): return jnp.concatenate([parts[i] for i in range(NC)], axis=1)]
  transfers between devices with their start and end apart: 11 -> 7, of which waited for: 9 -> 5; matrix products, arithmetic and copies ran while one was open for 17% -> 13% of each run, Pallas kernels for 0% -> 17%
where the time goes in v2:
time: 680 us; the launch traced here: 668 us
  Pallas kernels  226 us (33%)
  waiting for transfers between devices  176 us (26%)
  matrix products  129 us (19%)
  other arithmetic  45.6 us (7%)
  starting transfers between devices  45.3 us (7%)
  local copies, waits for them, and re-layouts  44.6 us (7%)
    pallas_call x1, Pallas kernels, scatter(): pl.pallas_call(scatter_kernel, name='scatter_weights', out_shape=tuple((j...  96.3 us
    pallas_call x1, Pallas kernels, gather(): pl.pallas_call(gather_kernel, name='gather_weights', out_shape=(jax.Shape...  75.2 us
    all_to_all x1, waiting for transfers between devices, on_device(): lax.all_to_all(sent.reshape(experts, cap, width), both, split_axis=0, con...  49.8 us
    all_to_all x1, waiting for transfers between devices, on_device(): lax.all_to_all(cot_out.reshape(experts, cap, width + experts), both, spli...  49 us
    dot_general x10, matrix products, dot_nn(): lax.dot_general(a, b, (((1,), (0,)), ((), ())), preferred_element_type=F32)  45.8 us
    dot_general x8, matrix products, dot_tn(): lax.dot_general(a, b, (((0,), (0,)), ((), ())), preferred_element_type=F32)  42.9 us
    all_to_all x1, waiting for transfers between devices, on_device(): lax.all_to_all(expert_out.reshape(experts, cap, width), both, split_axis=...  38.5 us
    pallas_call x2, Pallas kernels, reduce(): pl.pallas_call(reduce_kernel, name=f'reduce_rows_{ident}', out_shape=jax....  35.9 us
  transfers between devices with their start and end apart: 7, of which 5 were waited for; matrix products, arithmetic and copies ran while one was open for 13% of the time, Pallas kernels for 17%

profile of v2, /device:TPU:1, one launch (start us, length us, event | category | flops | bytes accessed | tf_op | source)
XLA Modules:
  0.0 667.8 jit_solution(11847674435533786140)
XLA Ops:
  0.7 1.4 fusion.51
  3.5 1.6 copy.299
  5.8 2.0 fusion.53.tok
  9.8 75.2 %gather_weights.1 = (bf16[4,2,4,2,32,1280]{5,4,3,2,1,0:T(8,128)(2,1)}, bf16[4,2,4,2,32,1024]{5,4,3,2,1,0:T(8,128)(2,1)}, bf16[2,2,128,2048]{3,2,1,0:T(8,128)(2,1)}, f32[2,8,256]{2,1,0:T(8,128)}) custom-call(bf16[2,32,1280]{2,1,0:T(8,128)(2,1)} %maximum_bitcast_fusion.2.sa, bf16[2,32,1024]{2,1,0:T(8,128)(2,1)} %bitcast.310, bf16[128,2048]{1,0:T(8,128)(2,1)} %fusion.53.tok, ...), custom_call_target="tpu_custom_call" | custom-call | tf_op jit(solution)/shard_map/gather_weights/pallas_call | solution.py:236
  85.1 6.0 fusion.116
  91.1 1.8 slice_bitcast_fusion
  96.5 2.1 copy.265
  102.8 1.9 fusion.102
  106.0 1.9 fusion.101
  110.0 2.1 subtract_convert_fusion
  112.1 5.5 fusion.113
  117.6 3.8 fusion.44
  121.4 2.4 copy.211
  123.8 4.9 convolution_convert_fusion.3
  128.8 16.5 %reduce_rows_2.1 = f32[128,2048]{1,0:T(8,128)S(1)} custom-call(bf16[2,2,128,2048]{3,2,1,0:T(8,128)(2,1)S(1)} %bitcast.289), custom_call_target="tpu_custom_call" | custom-call | tf_op jit(solution)/shard_map/reduce_rows_2/pallas_call | solution.py:329
  147.2 1.4 multiply_convert_fusion.3
  149.4 3.3 convert_bitcast_fusion.1
  152.7 6.7 %all-to-all-start.1 = ((bf16[128,8,2048]{2,1,0:T(8,128)(2,1)}), bf16[128,8,2048]{2,1,0:T(8,128)(2,1)}, u32[]{:S(2)}, u32[]{:S(2)}) async-start(bf16[128,8,2048]{2,1,0:T(8,128)(2,1)} %convert_bitcast_fusion.1), calls=%async_computation.1 | async-start | bytes 8388608 | tf_op jit(solution)/shard_map/all_to_all | solution.py:599
  159.4 4.5 fusion.1
  164.0 49.8 %all-to-all-done.1 = bf16[128,8,2048]{2,1,0:T(8,128)(2,1)} async-done(((bf16[128,8,2048]{2,1,0:T(8,128)(2,1)}), bf16[128,8,2048]{2,1,0:T(8,128)(2,1)}, u32[]{:S(2)}, u32[]{:S(2)}) %all-to-all-start.1) | async-done | bytes 4194336 | tf_op jit(solution)/shard_map/all_to_all | solution.py:599
  213.8 5.8 all-to-all-start
  219.6 8.3 %fusion.9 = f32[1024,768]{0,1:T(8,128)} fusion(bf16[128,8,2048]{2,1,0:T(8,128)(2,1)} %all-to-all-done.1, bf16[1,2048,768]{2,1,0:T(8,128)(2,1)} %param.29), kind=kOutput, calls=%fused_computation.15 | convolution fusion | flops 3221225472 | bytes 10485760 | tf_op jit(solution)/shard_map/dot_general | solution.py:27
  227.9 49.0 %all-to-all-done = bf16[128,8,2176]{2,1,0:T(8,128)(2,1)} async-done(((bf16[128,8,2176]{2,1,0:T(8,128)(2,1)}), bf16[128,8,2176]{2,1,0:T(8,128)(2,1)}, u32[]{:S(2)}, u32[]{:S(2)}) %all-to-all-start) | async-done | bytes 4456480 | tf_op jit(solution)/shard_map/all_to_all | solution.py:560
  276.8 1.7 slice.149
  278.5 1.8 copy.251
  280.3 6.3 fusion.22
  286.6 3.9 fusion.114
  290.7 8.9 %multiply_convert_fusion.1 = (bf16[1024,768]{0,1:T(8,128)(2,1)}, f32[1024]{0:T(1024)S(1)}, bf16[1024,768]{0,1:T(8,128)(2,1)}, bf16[1024,768]{0,1:T(8,128)(2,1)S(1)}) fusion(f32[1024,768]{0,1:T(8,128)S(1)} %copy-done.70, f32[1024,768]{0,1:T(8,128)S(1)} %fusion.22, f32[1024]{0:T(1024)S(1)} %div.87, bf16[1,2048,768]{2,1,0:T(8,128)(2,1)S(1)} %copy-done, ...), kind=kOutput, calls=%fused_computation.43 | convolution fusion | flops 3236166656 | bytes 18358272 | tf_op jit(solution)/shard_map/dot_general | solution.py:27
  300.7 5.0 convert_bitcast_fusion
  305.8 5.7 all-to-all-start.2
  312.4 1.8 copy.215
  314.2 1.8 copy.216
  316.0 5.0 fusion.29
  321.1 3.8 add_convert_fusion
  324.8 2.4 maximum_bitcast_fusion
  327.3 38.5 %all-to-all-done.2 = bf16[128,8,2048]{2,1,0:T(8,128)(2,1)} async-done(((bf16[128,8,2048]{2,1,0:T(8,128)(2,1)}), bf16[128,8,2048]{2,1,0:T(8,128)(2,1)}, u32[]{:S(2)}, u32[]{:S(2)}) %all-to-all-start.2) | async-done | bytes 4194336 | tf_op jit(solution)/shard_map/all_to_all | solution.py:637
  365.8 5.6 all-to-all-start.3
  374.6 8.9 %convolution_bitcast_fusion = f32[1,768,2048]{2,1,0:T(8,128)} fusion(bf16[1024,768]{0,1:T(8,128)(2,1)} %copy-done.71, bf16[1024,2176]{1,0:T(8,128)(2,1)} %bitcast.20), kind=kOutput, calls=%fused_computation.27 | convolution fusion | flops 3221225472 | bytes 12058624 | tf_op jit(solution)/shard_map/dot_general | solution.py:23
  383.5 8.6 %fusion.15 = f32[1,2048,768]{2,1,0:T(8,128)} fusion(bf16[1024,768]{0,1:T(8,128)(2,1)S(1)} %copy-done.69, bf16[128,8,2048]{2,1,0:T(8,128)(2,1)} %all-to-all-done.1), kind=kOutput, calls=%fused_computation.25 | convolution fusion | flops 3221225472 | bytes 12058624 | tf_op jit(solution)/shard_map/dot_general | solution.py:23
  392.1 8.6 %fusion.18 = f32[1,2048,768]{2,1,0:T(8,128)} fusion(bf16[1024,768]{0,1:T(8,128)(2,1)S(1)} %copy-done.73, bf16[128,8,2048]{2,1,0:T(8,128)(2,1)} %all-to-all-done.1), kind=kOutput, calls=%fused_computation.26 | convolution fusion | flops 3221225472 | bytes 12058624 | tf_op jit(solution)/shard_map/dot_general | solution.py:23
  400.7 3.8 fusion.34
  404.5 27.1 %all-to-all-done.3 = bf16[128,8,2304]{2,1,0:T(8,128)(2,1)} async-done(((bf16[128,8,2304]{2,1,0:T(8,128)(2,1)}), bf16[128,8,2304]{2,1,0:T(8,128)(2,1)}, u32[]{:S(2)}, u32[]{:S(2)}) %all-to-all-start.3) | async-done | bytes 4718624 | tf_op jit(solution)/shard_map/all_to_all | solution.py:633
  431.6 3.2 convolution_bitcast_fusion.1
  436.4 1.6 copy.253
  439.6 2.0 multiply_reduce_fusion.3
  441.6 2.2 fusion.110
  443.9 18.1 %share_rows_3.1 = bf16[2,2,128,2048]{3,2,1,0:T(8,128)(2,1)} custom-call(bf16[128,2048]{1,0:T(8,128)(2,1)} %get-tuple-element.36.tok), custom_call_target="tpu_custom_call" | custom-call | tf_op jit(solution)/shard_map/share_rows_3/pallas_call | solution.py:285
  462.0 5.3 fusion.43
  477.1 2.6 copy.224
  480.9 8.2 %all-to-all-start.5 = ((f32[128,16,128]{2,1,0:T(8,128)}), f32[128,16,128]{2,1,0:T(8,128)}, u32[]{:S(2)}, u32[]{:S(2)}) async-start(f32[128,16,128]{2,1,0:T(8,128)} %bitcast.298), calls=%async_computation.5 | async-start | bytes 2097152 | tf_op jit(solution)/shard_map/all_to_all | solution.py:689
  489.5 1.6 mul.652
  492.6 3.2 fusion.39
  496.9 11.5 %all-to-all-done.5 = f32[128,16,128]{2,1,0:T(8,128)} async-done(((f32[128,16,128]{2,1,0:T(8,128)}), f32[128,16,128]{2,1,0:T(8,128)}, u32[]{:S(2)}, u32[]{:S(2)}) %all-to-all-start.5) | async-done | bytes 1048608 | tf_op jit(solution)/shard_map/all_to_all | solution.py:689
  510.8 3.6 all-to-all-start.6
  514.4 5.6 convolution_convert_fusion.4
  520.1 19.4 %reduce_rows_4.1 = f32[128,2048]{1,0:T(8,128)S(1)} custom-call(bf16[2,2,128,2048]{3,2,1,0:T(8,128)(2,1)S(1)} %bitcast.288), custom_call_target="tpu_custom_call" | custom-call | tf_op jit(solution)/shard_map/reduce_rows_4/pallas_call | solution.py:329
  540.8 4.7 convolution_convert_fusion
  546.5 1.7 broadcast_in_dim.154
  548.2 9.7 %all-to-all-start.4 = ((f32[128,34,128]{2,1,0:T(8,128)}), f32[128,34,128]{2,1,0:T(8,128)}, u32[]{:S(2)}, u32[]{:S(2)}) async-start(f32[128,34,128]{2,1,0:T(8,128)} %broadcast_in_dim.154), calls=%async_computation.4 | async-start | bytes 5242880 | tf_op jit(solution)/shard_map/all_to_all | solution.py:685
  557.9 3.8 convolution_convert_fusion.2
  561.8 96.3 %scatter_weights.1 = (f32[2,32,1280]{2,1,0:T(8,128)S(1)}, f32[2,32,1024]{2,1,0:T(8,128)S(1)}) custom-call(bf16[4,2,4,2,32,1280]{5,4,3,2,1,0:T(8,128)(2,1)S(1)} %bitcast.286, bf16[4,2,4,2,32,1024]{5,4,3,2,1,0:T(8,128)(2,1)S(1)} %bitcast.287), custom_call_target="tpu_custom_call" | custom-call | tf_op jit(solution)/shard_map/scatter_weights/pallas_call | solution.py:490
  660.9 1.4 fusion.56
  662.3 2.0 reduce_sum.253
  665.4 2.3 copy.306
  (235 shorter events, 49.1 us)
Async XLA Ops:
  0.6 290.0 %copy-start = (bf16[1,2048,768]{2,1,0:T(8,128)(2,1)S(1)}, bf16[1,2048,768]{2,1,0:T(8,128)(2,1)}, u32[]{:S(2)}) copy-start(bf16[1,2048,768]{2,1,0:T(8,128)(2,1)} %param.28) | copy-start | bytes 9437188
  0.7 102.1 %copy-start.62 = (f32[64]{0:T(128)}, f32[64]{0:T(128)S(1)}, u32[]{:S(2)}) copy-start(f32[64]{0:T(128)S(1)} %multiply_exponential_fusion) | copy-start | bytes 772
  2.6 3.2 copy-start.56
  91.1 3.3 copy-start.64
  98.6 6.2 copy-start.54
  102.8 5.9 copy-start.5
  104.8 5.2 copy-start.24
  107.8 4.3 copy-start.37
  117.6 3.8 copy-start.49
  128.7 16.5 %copy-start.8 = (bf16[128,2048]{1,0:T(8,128)(2,1)S(1)}, bf16[128,2048]{1,0:T(8,128)(2,1)}, u32[]{:S(2)}) copy-start(bf16[128,2048]{1,0:T(8,128)(2,1)} %param.16) | copy-start | bytes 1572868
  128.7 18.2 %copy-start.42 = (f32[128,128]{0,1:T(8,128)S(1)}, f32[128,128]{0,1:T(8,128)}, u32[]{:S(2)}) copy-start(f32[128,128]{0,1:T(8,128)} %copy.213) | copy-start | bytes 196612
  128.7 18.2 %copy-start.58 = (f32[8]{0:T(128)S(1)}, f32[8]{0:T(128)}, u32[]{:S(2)}) copy-start(f32[8]{0:T(128)} %iota_convert_fusion) | copy-start | bytes 100
  128.7 18.3 %copy-start.39 = (bf16[128,128]{1,0:T(8,128)(2,1)S(1)}, bf16[128,128]{1,0:T(8,128)(2,1)}, u32[]{:S(2)}) copy-start(bf16[128,128]{1,0:T(8,128)(2,1)} %convert_element_type.156) | copy-start | bytes 98308
  128.7 18.5 %copy-start.44 = (f32[2048]{0:T(1024)S(1)}, f32[2048]{0:T(1024)}, u32[]{:S(2)}) copy-start(f32[2048]{0:T(1024)} %param.26) | copy-start | bytes 24580
  146.9 5.8 copy-start.59
  152.7 61.1 %all-to-all-start.1 = ((bf16[128,8,2048]{2,1,0:T(8,128)(2,1)}), bf16[128,8,2048]{2,1,0:T(8,128)(2,1)}, u32[]{:S(2)}, u32[]{:S(2)}) async-start(bf16[128,8,2048]{2,1,0:T(8,128)(2,1)} %convert_bitcast_fusion.1), calls=%async_computation.1 | async-start | bytes 8388608 | tf_op jit(solution)/shard_map/all_to_all | solution.py:599
  213.8 63.1 %all-to-all-start = ((bf16[128,8,2176]{2,1,0:T(8,128)(2,1)}), bf16[128,8,2176]{2,1,0:T(8,128)(2,1)}, u32[]{:S(2)}, u32[]{:S(2)}) async-start(bf16[128,8,2176]{2,1,0:T(8,128)(2,1)} %fusion.1), calls=%async_computation | async-start | bytes 8912896 | tf_op jit(solution)/shard_map/all_to_all | solution.py:560
  280.3 6.3 copy-start.16
  280.3 6.3 copy-start.28
  286.6 4.0 copy-start.70
  290.7 10.1 %copy-start.66 = (bf16[1,768,2048]{2,1,0:T(8,128)(2,1)S(1)}, bf16[1,768,2048]{2,1,0:T(8,128)(2,1)}, u32[]{:S(2)}) copy-start(bf16[1,768,2048]{2,1,0:T(8,128)(2,1)} %param.30) | copy-start | bytes 9437188
  305.8 60.1 %all-to-all-start.2 = ((bf16[128,8,2048]{2,1,0:T(8,128)(2,1)}), bf16[128,8,2048]{2,1,0:T(8,128)(2,1)}, u32[]{:S(2)}, u32[]{:S(2)}) async-start(bf16[128,8,2048]{2,1,0:T(8,128)(2,1)} %convert_bitcast_fusion), calls=%async_computation.2 | async-start | bytes 8388608 | tf_op jit(solution)/shard_map/all_to_all | solution.py:637
  316.0 5.0 copy-start.67
  316.0 5.0 copy-start.72
  321.0 3.8 copy-start.32
  321.0 3.8 copy-start.33
  327.3 44.9 %copy-start.46 = (f32[2,256,8]{1,2,0:T(8,128)S(1)}, f32[2,256,8]{1,2,0:T(8,128)}, u32[]{:S(2)}) copy-start(f32[2,256,8]{1,2,0:T(8,128)} %get-tuple-element.74) | copy-start | bytes 49156
  327.3 45.8 %copy-start.15 = (bf16[128,2048]{1,0:T(8,128)(2,1)S(1)}, bf16[128,2048]{1,0:T(8,128)(2,1)}, u32[]{:S(2)}) copy-start(bf16[128,2048]{1,0:T(8,128)(2,1)} %copy-done.14) | copy-start | bytes 1572868
  327.3 45.8 %copy-start.17 = (bf16[2048,128]{1,0:T(8,128)(2,1)S(1)}, bf16[2048,128]{1,0:T(8,128)(2,1)}, u32[]{:S(2)}) copy-start(bf16[2048,128]{1,0:T(8,128)(2,1)} %param.27) | copy-start | bytes 1572868
  327.3 46.7 %copy-start.60 = (f32[128]{0:T(128)S(1)}, f32[128]{0:T(128)}, u32[]{:S(2)}) copy-start(f32[128]{0:T(128)} %param.24) | copy-start | bytes 1540
  365.8 65.8 %all-to-all-start.3 = ((bf16[128,8,2304]{2,1,0:T(8,128)(2,1)}), bf16[128,8,2304]{2,1,0:T(8,128)(2,1)}, u32[]{:S(2)}, u32[]{:S(2)}) async-start(bf16[128,8,2304]{2,1,0:T(8,128)(2,1)} %maximum_bitcast_fusion), calls=%async_computation.3 | async-start | bytes 9437184 | tf_op jit(solution)/shard_map/all_to_all | solution.py:633
  373.4 10.1 %copy-start.52 = (f32[128]{0:T(128)}, f32[128]{0:T(128)S(1)}, u32[]{:S(2)}) copy-start(f32[128]{0:T(128)S(1)} %get-tuple-element.93) | copy-start | bytes 1540
  374.6 8.9 %copy-start.69 = (bf16[1024,768]{0,1:T(8,128)(2,1)S(1)}, bf16[1024,768]{0,1:T(8,128)(2,1)}, u32[]{:S(2)}) copy-start(bf16[1024,768]{0,1:T(8,128)(2,1)} %get-tuple-element.44) | copy-start | bytes 4718596
  383.5 8.6 %copy-start.73 = (bf16[1024,768]{0,1:T(8,128)(2,1)S(1)}, bf16[1024,768]{0,1:T(8,128)(2,1)}, u32[]{:S(2)}) copy-start(bf16[1024,768]{0,1:T(8,128)(2,1)} %get-tuple-element.48) | copy-start | bytes 4718596
  392.1 8.6 %copy-start.7 = (f32[128,2048]{1,0:T(8,128)S(1)}, f32[128,2048]{1,0:T(8,128)}, u32[]{:S(2)}) copy-start(f32[128,2048]{1,0:T(8,128)} %get-tuple-element.43) | copy-start | bytes 3145732
  438.0 3.7 copy-start.26
  439.6 4.2 copy-start.40
  461.9 5.6 copy-start.19
  462.0 5.6 copy-start.43
  462.0 5.6 copy-start.50
  476.2 3.5 copy-start.63
  479.7 9.4 %copy-start.12 = (f32[512,1280]{1,0:T(8,128)S(1)}, f32[512,1280]{1,0:T(8,128)}, u32[]{:S(2)}) copy-start(f32[512,1280]{1,0:T(8,128)} %copy-done.11) | copy-start | bytes 7864324
  479.7 9.4 %copy-start.55 = (f32[128]{0:T(128)S(1)}, f32[128]{0:T(128)}, u32[]{:S(2)}) copy-start(f32[128]{0:T(128)} %param.25) | copy-start | bytes 1540
  480.9 10.1 %copy-start.30 = (f32[2,256,8]{2,1,0:T(8,128)S(1)}, f32[2,256,8]{2,1,0:T(8,128)}, u32[]{:S(2)}) copy-start(f32[2,256,8]{2,1,0:T(8,128)} %copy.260) | copy-start | bytes 49156
  480.9 27.5 %all-to-all-start.5 = ((f32[128,16,128]{2,1,0:T(8,128)}), f32[128,16,128]{2,1,0:T(8,128)}, u32[]{:S(2)}, u32[]{:S(2)}) async-start(f32[128,16,128]{2,1,0:T(8,128)} %bitcast.298), calls=%async_computation.5 | async-start | bytes 2097152 | tf_op jit(solution)/shard_map/all_to_all | solution.py:689
  492.6 3.2 copy-start.53
  492.6 3.5 copy-start.20
  492.6 3.5 copy-start.35
  492.6 3.5 copy-start.51
  496.9 17.5 %copy-start.29 = (bf16[512,1024]{1,0:T(8,128)(2,1)S(1)}, bf16[512,1024]{1,0:T(8,128)(2,1)}, u32[]{:S(2)}) copy-start(bf16[512,1024]{1,0:T(8,128)(2,1)} %get-tuple-element.47) | copy-start | bytes 3145732
  510.8 34.8 %all-to-all-start.6 = ((f32[128,16,128]{2,1,0:T(8,128)}), f32[128,16,128]{2,1,0:T(8,128)S(1)}, u32[]{:S(2)}, u32[]{:S(2)}) async-start(f32[128,16,128]{2,1,0:T(8,128)} %broadcast_in_dim.155), calls=%async_computation.6 | async-start | bytes 2097152 | tf_op jit(solution)/shard_map/all_to_all | solution.py:691
  520.0 20.5 %copy-start.9 = (bf16[128,2048]{1,0:T(8,128)(2,1)S(1)}, bf16[128,2048]{1,0:T(8,128)(2,1)}, u32[]{:S(2)}) copy-start(bf16[128,2048]{1,0:T(8,128)(2,1)} %param.16) | copy-start | bytes 1572868
  520.0 20.5 %copy-start.45 = (f32[2048]{0:T(1024)S(1)}, f32[2048]{0:T(1024)}, u32[]{:S(2)}) copy-start(f32[2048]{0:T(1024)} %param.19) | copy-start | bytes 24580
  520.0 20.5 %copy-start.57 = (f32[128]{0:T(128)S(1)}, f32[128]{0:T(128)}, u32[]{:S(2)}) copy-start(f32[128]{0:T(128)} %copy-done.56) | copy-start | bytes 1540
  520.1 20.7 %copy-start.47 = (f32[2048]{0:T(1024)S(1)}, f32[2048]{0:T(1024)}, u32[]{:S(2)}) copy-start(f32[2048]{0:T(1024)} %get-tuple-element.28) | copy-start | bytes 24580
  520.1 20.7 %copy-start.68 = (bf16[2,2,128,2048]{3,2,1,0:T(8,128)(2,1)S(1)}, bf16[2,2,128,2048]{3,2,1,0:T(8,128)(2,1)}, u32[]{:S(2)}) copy-start(bf16[2,2,128,2048]{3,2,1,0:T(8,128)(2,1)} %get-tuple-element.20) | copy-start | bytes 6291460
  548.2 9.7 %copy-start.27 = (bf16[2,2,128,2048]{3,2,1,0:T(8,128)(2,1)S(1)}, bf16[2,2,128,2048]{3,2,1,0:T(8,128)(2,1)}, u32[]{:S(2)}) copy-start(bf16[2,2,128,2048]{3,2,1,0:T(8,128)(2,1)} %share_rows_3.1) | copy-start | bytes 6291460
  548.2 13.5 %slice-start = ((s8[5242880]{0:T(1024)(128)(4,1)}), s8[1048576]{0:T(1024)(128)(4,1)S(1)}, s32[]{:S(2)}) async-start(s8[5242880]{0:T(1024)(128)(4,1)} %bitcast.284), calls=%async_computation.7 | async-start | bytes 2097152
  548.2 114.1 %all-to-all-start.4 = ((f32[128,34,128]{2,1,0:T(8,128)}), f32[128,34,128]{2,1,0:T(8,128)}, u32[]{:S(2)}, u32[]{:S(2)}) async-start(f32[128,34,128]{2,1,0:T(8,128)} %broadcast_in_dim.154), calls=%async_computation.4 | async-start | bytes 5242880 | tf_op jit(solution)/shard_map/all_to_all | solution.py:685
  557.9 3.8 slice-start.1
  561.7 99.1 %copy-start.18 = (f32[128,2048]{1,0:T(8,128)S(1)}, f32[128,2048]{1,0:T(8,128)}, u32[]{:S(2)}) copy-start(f32[128,2048]{1,0:T(8,128)} %get-tuple-element.37) | copy-start | bytes 3145732
  561.8 99.1 %copy-start.65 = (f32[128]{0:T(128)S(1)}, f32[128]{0:T(128)}, u32[]{:S(2)}) copy-start(f32[128]{0:T(128)} %get-tuple-element.83) | copy-start | bytes 1540
  658.1 2.8 copy-start.3
  660.9 6.8 %copy-start.1 = (bf16[1,2048,768]{2,1,0:T(8,128)(2,1)S(1)}, bf16[1,2048,768]{2,1,0:T(8,128)(2,1)}, u32[]{:S(2)}) copy-start(bf16[1,2048,768]{2,1,0:T(8,128)(2,1)} %param.28) | copy-start | bytes 9437188
  (19 other events, 29.5 us)

commit v3 on v2

--- a/solution.py
+++ b/solution.py
@@ -1,3 +1,4 @@
+import functools
 import math
 
 import jax
@@ -65,7 +66,7 @@
     half = head_size // 2
     frequency = jnp.exp(-jnp.log(ROPE_BASE) * jnp.arange(half, dtype=F32) * 2.0 / head_size)
     angles = position.astype(F32)[:, None] * frequency[None, :]
-    return jnp.cos(angles)[:, None, :], jnp.sin(angles)[:, None, :]
+    return jnp.cos(angles), jnp.sin(angles)
 
 
 MESH = pl.DeviceIdType.MESH
@@ -73,6 +74,10 @@
 VMEM = pl.BlockSpec(memory_space=pltpu.VMEM)
 NX, NYH, NZ, NC = 4, 2, 4, 2
 RING = 4
+
+
+def cost(microseconds):
+    return pl.CostEstimate(flops=0, transcendentals=0, bytes_accessed=int(microseconds * 3.6e6))
 
 
 class Place:
@@ -236,6 +241,7 @@
     wa, wb, toks, docs = pl.pallas_call(
         gather_kernel,
         name="gather_weights",
+        cost_estimate=cost(60),
         out_shape=(
             jax.ShapeDtypeStruct((*lead, width_a), BF16),
             jax.ShapeDtypeStruct((*lead, width_b), BF16),
@@ -285,6 +291,7 @@
     toks = pl.pallas_call(
         share_kernel,
         name=f"share_rows_{ident}",
+        cost_estimate=cost(13),
         out_shape=jax.ShapeDtypeStruct((NC, 2, *tokens.shape), tokens.dtype),
         in_specs=[ANY],
         out_specs=ANY,
@@ -329,6 +336,7 @@
     return pl.pallas_call(
         reduce_kernel,
         name=f"reduce_rows_{ident}",
+        cost_estimate=cost(15),
         out_shape=jax.ShapeDtypeStruct((rows, width), F32),
         in_specs=[ANY],
         out_specs=VMEM,
@@ -490,6 +498,7 @@
     return pl.pallas_call(
         scatter_kernel,
         name="scatter_weights",
+        cost_estimate=cost(80),
         out_shape=tuple(jax.ShapeDtypeStruct((NC, rows, w), F32) for w in widths),
         in_specs=[ANY, ANY],
         out_specs=(VMEM, VMEM),
@@ -510,6 +519,149 @@
             collective_id=5, has_side_effects=True, vmem_limit_bytes=40 << 20
         ),
     )(grad_a.reshape(*lead, widths[0]), grad_b.reshape(*lead, widths[1]))
+
+
+def unit_rows(values):
+    return lax.rsqrt(jnp.mean(values * values, axis=-1, keepdims=True) + EPSILON)
+
+
+def turn(values, cosine, signed):
+    return values * cosine + pltpu.roll(values, values.shape[-1] // 2, 1) * signed
+
+
+def attend_kernel(scale, raw, bias, cosine, signed, qgain, kgain, query, kv, weights, mixed):
+    heads = query.shape[1] // cosine.shape[1]
+    hd = cosine.shape[1]
+    cos, sig = cosine[...], signed[...]
+    key_raw = raw[:, heads * hd : (heads + 1) * hd]
+    key = turn(key_raw * unit_rows(key_raw) * kgain[...], cos, sig).astype(BF16)
+    value = raw[:, (heads + 1) * hd :].astype(BF16)
+    kv[:, :hd] = key
+    kv[:, hd:] = value
+    for h in range(heads):
+        at = slice(h * hd, (h + 1) * hd)
+        head = raw[:, at]
+        rows = turn(head * unit_rows(head) * qgain[...], cos, sig).astype(BF16)
+        query[:, at] = rows
+        scores = dot_nt(rows, key) * scale + bias[0]
+        peak = jnp.max(scores, axis=-1, keepdims=True)
+        weight = jnp.exp(scores - peak)
+        weight = weight * (1.0 / jnp.sum(weight, axis=-1, keepdims=True))
+        weights[0, h] = weight
+        mixed[:, at] = dot_nn(weight.astype(BF16), value).astype(BF16)
+
+
+def attend(raw, bias, cosine, signed, query_gain, key_gain, scale):
+    groups, tokens = bias.shape[0], bias.shape[1]
+    hd = cosine.shape[1]
+    heads = raw.shape[1] // hd - 2
+    rows = groups * tokens
+
+    def block(cols):
+        return pl.BlockSpec((tokens, cols), lambda g: (g, 0))
+
+    gain = pl.BlockSpec((1, hd), lambda g: (0, 0))
+    square = pl.BlockSpec((1, tokens, tokens), lambda g: (g, 0, 0))
+    return pl.pallas_call(
+        functools.partial(attend_kernel, scale),
+        name="attend",
+        cost_estimate=cost(8),
+        grid=(groups,),
+        out_shape=(
+            jax.ShapeDtypeStruct((rows, heads * hd), BF16),
+            jax.ShapeDtypeStruct((rows, 2 * hd), BF16),
+            jax.ShapeDtypeStruct((groups, heads, tokens, tokens), F32),
+            jax.ShapeDtypeStruct((rows, heads * hd), BF16),
+        ),
+        in_specs=[block((heads + 2) * hd), square, block(hd), block(hd), gain, gain],
+        out_specs=(
+            block(heads * hd),
+            block(2 * hd),
+            pl.BlockSpec((1, heads, tokens, tokens), lambda g: (g, 0, 0, 0)),
+            block(heads * hd),
+        ),
+        compiler_params=pltpu.CompilerParams(vmem_limit_bytes=40 << 20),
+    )(raw, bias, cosine, signed, query_gain.reshape(1, hd), key_gain.reshape(1, hd))
+
+
+def norm_back(values, gain, upstream):
+    r = unit_rows(values)
+    scaled = upstream * gain
+    inner = jnp.mean(scaled * values, axis=-1, keepdims=True)
+    grad = r * scaled - values * (r * r * r * inner)
+    return grad, jnp.sum(upstream * values * r, axis=0, keepdims=True)
+
+
+def attend_back_kernel(
+    scale, raw, cosine, signed, qgain, kgain, query, kv, weights, grad_mixed, grad_raw, grad_gains
+):
+    hd = cosine.shape[1]
+    heads = query.shape[1] // hd
+    cos, sig = cosine[...], -signed[...]
+    key, value = kv[:, :hd], kv[:, hd:]
+    grad_key = jnp.zeros(key.shape, F32)
+    grad_value = jnp.zeros(key.shape, F32)
+    query_gains = jnp.zeros((1, hd), F32)
+    for h in range(heads):
+        at = slice(h * hd, (h + 1) * hd)
+        weight = weights[0, h]
+        grad_head = grad_mixed[:, at]
+        grad_value += dot_tn(weight.astype(BF16), grad_head)
+        grad_soft = dot_nt(grad_head, value)
+        delta = jnp.sum(weight * grad_soft, axis=-1, keepdims=True)
+        grad_scores = (weight * (grad_soft - delta)).astype(BF16)
+        grad_key += dot_tn(grad_scores, query[:, at])
+        turned = turn(dot_nn(grad_scores, key) * scale, cos, sig)
+        grad, gains = norm_back(raw[:, at], qgain[...], turned)
+        grad_raw[:, at] = grad.astype(BF16)
+        query_gains += gains
+    at = slice(heads * hd, (heads + 1) * hd)
+    grad, key_gains = norm_back(raw[:, at], kgain[...], turn(grad_key * scale, cos, sig))
+    grad_raw[:, at] = grad.astype(BF16)
+    grad_raw[:, (heads + 1) * hd :] = grad_value.astype(BF16)
+    gains = jnp.concatenate([query_gains, key_gains], axis=0)
+
+    @pl.when(pl.program_id(0) == 0)
+    def _():
+        grad_gains[...] = gains
+
+    @pl.when(pl.program_id(0) > 0)
+    def _():
+        grad_gains[...] += gains
+
+
+def attend_back(raw, cosine, signed, query_gain, key_gain, query, kv, weights, grad_mixed, scale):
+    groups, heads, tokens, _ = weights.shape
+    hd = cosine.shape[1]
+    rows = groups * tokens
+
+    def block(cols):
+        return pl.BlockSpec((tokens, cols), lambda g: (g, 0))
+
+    gain = pl.BlockSpec((1, hd), lambda g: (0, 0))
+    return pl.pallas_call(
+        functools.partial(attend_back_kernel, scale),
+        name="attend_back",
+        cost_estimate=cost(14),
+        grid=(groups,),
+        out_shape=(
+            jax.ShapeDtypeStruct((rows, (heads + 2) * hd), BF16),
+            jax.ShapeDtypeStruct((2, hd), F32),
+        ),
+        in_specs=[
+            block((heads + 2) * hd),
+            block(hd),
+            block(hd),
+            gain,
+            gain,
+            block(heads * hd),
+            block(2 * hd),
+            pl.BlockSpec((1, heads, tokens, tokens), lambda g: (g, 0, 0, 0)),
+            block(heads * hd),
+        ],
+        out_specs=(block((heads + 2) * hd), pl.BlockSpec((2, hd), lambda g: (0, 0))),
+        compiler_params=pltpu.CompilerParams(vmem_limit_bytes=40 << 20),
+    )(raw, cosine, signed, query_gain.reshape(1, hd), key_gain.reshape(1, hd), query, kv, weights, grad_mixed)
 
 
 def on_device(
@@ -556,11 +708,6 @@
         place[:, None, :] == lax.broadcasted_iota(jnp.int32, (1, cap, 1), 1).astype(F32)
     ).astype(BF16).reshape(slots, tok)
 
-    cot_out = dot_nn(spread, jnp.concatenate([cotangent, chosen.astype(BF16)], axis=1)).astype(BF16)
-    cot_in = lax.all_to_all(
-        cot_out.reshape(experts, cap, width + experts), both, split_axis=0, concat_axis=0, tiled=True
-    ).reshape(slots, width + experts)
-
     hidden = hidden_in.astype(F32)
     normed_local = rms_scale(hidden, attn_gain).astype(BF16)
 
@@ -575,26 +722,25 @@
         jnp.broadcast_to(doc_ids, (8, tokens)).astype(F32),
     )
 
+    spread_late, docs = lax.optimization_barrier((spread, docs))
+    cot_out = dot_nn(spread_late, jnp.concatenate([cotangent, chosen.astype(BF16)], axis=1)).astype(BF16)
+    cot_in = lax.all_to_all(
+        cot_out.reshape(experts, cap, width + experts), both, split_axis=0, concat_axis=0, tiled=True
+    ).reshape(slots, width + experts)
+
     position, allowed = jax.vmap(layout)(docs[:, 0])
-    cosine, sine = jax.vmap(lambda p: rotary(p, hd))(position)
+    cosine, sine = rotary(position.reshape(-1), hd)
+    cosine = jnp.concatenate([cosine, cosine], axis=1)
+    signed = jnp.concatenate([-sine, sine], axis=1)
+    bias = jnp.where(allowed, 0.0, MASKED).astype(F32)
     raw = dot_nn(normed, in_weights)
     heads = group * hd
-    query_raw = raw[:, :heads].reshape(NC, tokens, group, hd)
-    key_raw = raw[:, heads : heads + hd].reshape(NC, tokens, 1, hd)
-    values = raw[:, heads + hd :].astype(BF16).reshape(NC, tokens, hd)
-    query = rotate(rms_scale(query_raw, query_gain), cosine, sine).astype(BF16)
-    key = rotate(rms_scale(key_raw, key_gain), cosine, sine).astype(BF16)[:, :, 0]
-    scores = jnp.einsum("bqgd,btd->bgqt", query, key, preferred_element_type=F32) * scale
-    scores = jnp.where(allowed[:, None], scores, MASKED)
-    weight = jnp.exp(scores - jnp.max(scores, axis=-1, keepdims=True))
-    attention = weight / jnp.sum(weight, axis=-1, keepdims=True)
-    attention_low = attention.astype(BF16)
-    mixed = jnp.einsum("bgqt,btd->bqgd", attention_low, values, preferred_element_type=F32)
-    mixed = mixed.astype(BF16).reshape(NC * tokens, heads)
+    query, kv, attention, mixed = attend(raw, bias, cosine, signed, query_gain, key_gain, scale)
     attn_out = reduce(dot_nt(mixed, out_weights).astype(BF16), 2)
 
     residual = hidden + attn_out
     moe_input = rms_scale(residual, moe_gain).astype(BF16)
+    moe_input, cot_in = lax.optimization_barrier((moe_input, cot_in))
     sent = dot_nn(spread, moe_input).astype(BF16)
     rows = lax.all_to_all(
         sent.reshape(experts, cap, width), both, split_axis=0, concat_axis=0, tiled=True
@@ -634,12 +780,12 @@
         home_out.reshape(experts, cap, width + 2 * experts), both, split_axis=0, concat_axis=0, tiled=True
     ).reshape(slots, width + 2 * experts)
     expert_out = dot_nn(inner_low, down_mat).astype(BF16)
-    returned = lax.all_to_all(
-        expert_out.reshape(experts, cap, width), both, split_axis=0, concat_axis=0, tiled=True
-    ).reshape(slots, width)
     down_grad = dot_tn(inner_low, cot_rows)
     gate_grad = dot_tn(rows, grad_gate)
     up_grad = dot_tn(rows, grad_up)
+    home, down_grad, gate_grad, up_grad = lax.optimization_barrier(
+        (home, down_grad, gate_grad, up_grad)
+    )
 
     upstream = cotangent.astype(F32)
     summed = dot_tn(spread, home)
@@ -652,26 +798,16 @@
     moegain_part = jnp.sum(moegain_rows, axis=0)
     grad_residual = upstream + grad_norm
     grad_attn = share(grad_residual.astype(BF16), 3)
-    layer_out = (residual + dot_tn(spread, returned)).astype(BF16)
-
-    grad_mixed = dot_nn(grad_attn, out_weights).astype(BF16).reshape(NC, tokens, group, hd)
-    grad_values = jnp.einsum("bgqt,bqgd->btd", attention_low, grad_mixed, preferred_element_type=F32)
-    grad_soft = jnp.einsum("bqgd,btd->bgqt", grad_mixed, values, preferred_element_type=F32)
-    row_delta = jnp.sum(attention * grad_soft, axis=-1, keepdims=True)
-    grad_scores = (attention * (grad_soft - row_delta)).astype(BF16)
-    grad_query = jnp.einsum("bgqt,btd->bqgd", grad_scores, key, preferred_element_type=F32) * scale
-    grad_key = jnp.einsum("bgqt,bqgd->btd", grad_scores, query, preferred_element_type=F32) * scale
-    grad_query_raw, qgain_rows = rms_back(query_raw, query_gain, rotate(grad_query, cosine, -sine))
-    grad_key_raw, kgain_rows = rms_back(
-        key_raw, key_gain, rotate(grad_key[:, :, None], cosine, -sine)
-    )
-    grad_raw = jnp.concatenate(
-        [
-            grad_query_raw.astype(BF16).reshape(NC * tokens, heads),
-            grad_key_raw.astype(BF16).reshape(NC * tokens, hd),
-            grad_values.astype(BF16).reshape(NC * tokens, hd),
-        ],
-        axis=1,
+    pieces = router_part.reshape(experts, width // experts, experts)
+    piece = jnp.sum(lax.all_to_all(pieces, both, 0, 0, tiled=True), axis=0)
+    expert_out, grad_attn, piece = lax.optimization_barrier((expert_out, grad_attn, piece))
+    returned = lax.all_to_all(
+        expert_out.reshape(experts, cap, width), both, split_axis=0, concat_axis=0, tiled=True
+    ).reshape(slots, width)
+
+    grad_mixed = dot_nn(grad_attn, out_weights).astype(BF16)
+    grad_raw, head_gains = attend_back(
+        raw, cosine, signed, query_gain, key_gain, query, kv, attention, grad_mixed, scale
     )
     grad_normed = reduce(dot_nt(grad_raw, in_weights).astype(BF16), 4)
     in_grad, out_grad = scatter(
@@ -680,27 +816,15 @@
     grad_hidden, attngain_rows = rms_back(hidden, attn_gain, grad_normed)
     input_grad = grad_residual + grad_hidden
 
-    def all_sum(flat):
-        copies = jnp.broadcast_to(flat[None], (experts, *flat.shape))
-        return jnp.sum(lax.all_to_all(copies, both, 0, 0, tiled=True), axis=0)
-
-    def all_sum_long(rows):
-        pieces = rows.reshape(experts, rows.shape[0] // experts, rows.shape[1])
-        piece = jnp.sum(lax.all_to_all(pieces, both, 0, 0, tiled=True), axis=0)
-        copies = jnp.broadcast_to(piece[None], pieces.shape)
-        return lax.all_to_all(copies, both, 0, 0, tiled=True).reshape(rows.shape)
-
-    router_grad = all_sum_long(router_part)
-    gains = all_sum(
-        jnp.concatenate(
-            [
-                jnp.sum(attngain_rows, axis=0),
-                moegain_part,
-                jnp.sum(qgain_rows, axis=(0, 1, 2)),
-                jnp.sum(kgain_rows, axis=(0, 1, 2)),
-            ]
-        ).reshape(-1, hd)
-    ).reshape(-1)
+    gains = jnp.concatenate([jnp.sum(attngain_rows, axis=0), moegain_part, head_gains.reshape(-1)])
+    term = jnp.concatenate([piece, gains.reshape(-1, experts)], axis=0)
+    term, returned = lax.optimization_barrier((term, returned))
+    layer_out = (residual + dot_tn(spread, returned)).astype(BF16)
+    terms = lax.all_to_all(
+        jnp.broadcast_to(term[None], (experts, *term.shape)), both, 0, 0, tiled=True
+    )
+    router_grad = terms[:, : piece.shape[0]].reshape(width, experts)
+    gains = jnp.sum(terms[:, piece.shape[0] :], axis=0).reshape(-1)
     attngain_grad = gains[:width]
     moegain_grad = gains[width : 2 * width]
     qgain_grad = gains[2 * width : 2 * width + hd]

time: 680 us -> 586 us (0.86); the launches traced: 668 us -> 581 us
  waiting for transfers between devices: 176 us -> 66.4 us
  Pallas kernels: 226 us -> 298 us
  other arithmetic: 45.6 us -> 21.8 us
  local copies, waits for them, and re-layouts: 44.6 us -> 25 us
  matrix products: 129 us -> 115 us
  starting transfers between devices: 45.3 us -> 53.1 us
    pallas_call x5 -> x7, Pallas kernels: 226 us -> 298 us  [the longest x1 105 us: scatter(): pl.pallas_call(scatter_kernel, name='scatter_weights', cost_estimate=cost...]
    all_to_all x1, waiting for transfers between devices: 49 us -> 0.01 us  [on_device(): lax.all_to_all(cot_out.reshape(experts, cap, width + experts), both, spli...]
    all_to_all x1, waiting for transfers between devices: 38.5 us -> 0.01 us  [on_device(): lax.all_to_all(expert_out.reshape(experts, cap, width), both, split_axis=...]
    unnamed x162 -> x83, local copies, waits for them, and re-layouts: 18.5 us -> 3.97 us
    all_to_all x3 -> x2, waiting for transfers between devices: 11.5 us -> 0.01 us  [the longest x1 0.01 us: on_device(): piece = jnp.sum(lax.all_to_all(pieces, both, 0, 0, tiled=True), axis=0)]
    all_to_all x1, waiting for transfers between devices: 49.8 us -> 39.3 us  [on_device(): lax.all_to_all(sent.reshape(experts, cap, width), both, split_axis=0, con...]
    dot_general x5 -> x0, matrix products: 7.39 us -> none  [the longest x1 3.78 us: on_device(): jnp.einsum('bgqt,btd->bqgd', attention_low, values, preferred_element_typ...]
    all_to_all x3 -> x2, starting transfers between devices: 21.5 us -> 18.4 us  [the longest x1 11.2 us: on_device(): lax.all_to_all(jnp.broadcast_to(term[None], (experts, *term.shape)), both...]
  transfers between devices with their start and end apart: 7 -> 6, of which waited for: 5 -> 2; matrix products, arithmetic and copies ran while one was open for 13% -> 15% of each run, Pallas kernels for 17% -> 38%
where the time goes in v3:
time: 586 us; the launch traced here: 581 us
  Pallas kernels  298 us (51%)
  matrix products  115 us (20%)
  waiting for transfers between devices  66.4 us (11%)
  starting transfers between devices  53.1 us (9%)
  local copies, waits for them, and re-layouts  25 us (4%)
  other arithmetic  21.8 us (4%)
    pallas_call x1, Pallas kernels, scatter(): pl.pallas_call(scatter_kernel, name='scatter_weights', cost_estimate=cost...  105 us
    pallas_call x2, Pallas kernels, reduce(): pl.pallas_call(reduce_kernel, name=f'reduce_rows_{ident}', cost_estimate=...  80.8 us
    pallas_call x1, Pallas kernels, gather(): pl.pallas_call(gather_kernel, name='gather_weights', cost_estimate=cost(6...  75.2 us
    dot_general x10, matrix products, dot_nn(): lax.dot_general(a, b, (((1,), (0,)), ((), ())), preferred_element_type=F32)  47.7 us
    dot_general x8, matrix products, dot_tn(): lax.dot_general(a, b, (((0,), (0,)), ((), ())), preferred_element_type=F32)  40.7 us
    all_to_all x1, waiting for transfers between devices, on_device(): lax.all_to_all(sent.reshape(experts, cap, width), both, split_axis=0, con...  39.3 us
    all_to_all x1, waiting for transfers between devices, on_device(): lax.all_to_all(home_out.reshape(experts, cap, width + 2 * experts), both,...  27.1 us
    dot_general x6, matrix products, dot_nt(): lax.dot_general(a, b, (((1,), (1,)), ((), ())), preferred_element_type=F32)  26.6 us
  transfers between devices with their start and end apart: 6, of which 2 were waited for; matrix products, arithmetic and copies ran while one was open for 15% of the time, Pallas kernels for 38%

profile of v3, /device:TPU:1, one launch (start us, length us, event | category | flops | bytes accessed | tf_op | source)
XLA Modules:
  0.0 581.4 jit_solution(15860635952534552358)
XLA Ops:
  0.7 0.9 copy.52
  2.0 1.6 copy.73
  3.5 1.6 copy.72
  5.1 1.2 fusion.27
  6.3 0.7 convert_element_type.121
  7.1 0.7 copy_bitcast_fusion.1
  7.9 2.0 fusion.29.tok
  10.3 1.6 maximum_bitcast_fusion.2.sa
  12.5 75.2 %gather_weights.1 = (bf16[4,2,4,2,32,1280]{5,4,3,2,1,0:T(8,128)(2,1)}, bf16[4,2,4,2,32,1024]{5,4,3,2,1,0:T(8,128)(2,1)}, bf16[2,2,128,2048]{3,2,1,0:T(8,128)(2,1)}, f32[2,8,256]{2,1,0:T(8,128)}) custom-call(bf16[2,32,1280]{2,1,0:T(8,128)(2,1)} %maximum_bitcast_fusion.2.sa, bf16[2,32,1024]{2,1,0:T(8,128)(2,1)} %bitcast.172, bf16[128,2048]{1,0:T(8,128)(2,1)} %fusion.29.tok, ...), custom_call_target="tpu_custom_call" | custom-call | bytes 216000000 | tf_op jit(solution)/shard_map/gather_weights/pallas_call | solution.py:241
  87.7 4.4 fusion
  92.2 7.6 %all-to-all-start = ((bf16[128,8,2176]{2,1,0:T(8,128)(2,1)}), bf16[128,8,2176]{2,1,0:T(8,128)(2,1)}, u32[]{:S(2)}, u32[]{:S(2)}) async-start(bf16[128,8,2176]{2,1,0:T(8,128)(2,1)} %fusion), calls=%async_computation | async-start | bytes 8912896 | tf_op jit(solution)/shard_map/all_to_all | solution.py:727
  99.8 0.7 slice.81
  100.9 1.0 fusion.49
  102.4 6.1 %fusion.57.raw = f32[512,1280]{1,0:T(8,128)S(1)} fusion(bf16[512,2048]{1,0:T(8,128)(2,1)} %bitcast.184, bf16[2048,1280]{1,0:T(8,128)(2,1)} %bitcast.180), kind=kOutput, calls=%fused_computation.145 | convolution fusion | flops 2684354560 | bytes 9961472 | tf_op jit(solution)/shard_map/dot_general | solution.py:28
  108.6 8.1 %attend.1 = (bf16[512,1024]{1,0:T(8,128)(2,1)S(1)}, bf16[512,256]{1,0:T(8,128)(2,1)S(1)}, f32[2,8,256,256]{3,2,1,0:T(8,128)S(1)}, bf16[512,1024]{1,0:T(8,128)(2,1)S(1)}) custom-call(f32[512,1280]{1,0:T(8,128)S(1)} %fusion.57.raw, f32[2,256,256]{2,1,0:T(8,128)S(1)} %fusion.41.bias, f32[512,128]{1,0:T(8,128)S(1)} %pad_maximum_fusion.cosine, ...), custom_call_target="tpu_custom_call" | custom-call | bytes 28800000 | tf_op jit(solution)/shard_map/attend/pallas_call | solution.py:565
  116.7 1.0 copy-done.8
  117.7 0.7 copy-done.10
  118.4 2.4 convolution_convert_fusion.4
  120.8 40.3 %reduce_rows_2.1 = f32[128,2048]{1,0:T(8,128)S(1)} custom-call(bf16[2,2,128,2048]{3,2,1,0:T(8,128)(2,1)S(1)} %bitcast.161), custom_call_target="tpu_custom_call" | custom-call | bytes 54000000 | tf_op jit(solution)/shard_map/reduce_rows_2/pallas_call | solution.py:336
  161.4 1.0 copy-done.16
  162.3 1.0 multiply_convert_fusion.3
  163.3 4.4 convert_bitcast_fusion
  167.6 11.6 %all-to-all-start.1 = ((bf16[128,8,2048]{2,1,0:T(8,128)(2,1)}), bf16[128,8,2048]{2,1,0:T(8,128)(2,1)}, u32[]{:S(2)}, u32[]{:S(2)}) async-start(bf16[128,8,2048]{2,1,0:T(8,128)(2,1)} %convert_bitcast_fusion), calls=%async_computation.1 | async-start | bytes 8388608 | tf_op jit(solution)/shard_map/all_to_all | solution.py:745
  179.3 6.5 %copy.54 = bf16[1024,2176]{0,1:T(8,128)(2,1)} copy(bf16[1024,2176]{1,0:T(8,128)(2,1)} %bitcast.13) | data formatting | bytes 8912896 | tf_op jit(solution)/shard_map/optimization_barrier | solution.py:743
  185.7 8.3 %fusion.13 = f32[1024,768]{0,1:T(8,128)} fusion(bf16[1024,2176]{1,0:T(8,128)(2,1)} %bitcast.13, bf16[1,768,2048]{2,1,0:T(8,128)(2,1)} %param.30), kind=kOutput, calls=%fused_computation.20 | convolution fusion | flops 3221225472 | bytes 10485760 | tf_op jit(solution)/shard_map/dot_general | solution.py:20
  194.0 39.3 %all-to-all-done.1 = bf16[128,8,2048]{2,1,0:T(8,128)(2,1)} async-done(((bf16[128,8,2048]{2,1,0:T(8,128)(2,1)}), bf16[128,8,2048]{2,1,0:T(8,128)(2,1)}, u32[]{:S(2)}, u32[]{:S(2)}) %all-to-all-start.1) | async-done | bytes 4194336 | tf_op jit(solution)/shard_map/all_to_all | solution.py:745
  233.3 4.0 fusion.55
  237.5 5.5 fusion.5
  243.0 9.4 %multiply_convert_fusion.1 = (bf16[1024,768]{0,1:T(8,128)(2,1)}, f32[1024]{0:T(1024)S(1)}, bf16[1024,768]{0,1:T(8,128)(2,1)}, bf16[1024,768]{0,1:T(8,128)(2,1)}) fusion(f32[1024,768]{0,1:T(8,128)S(1)} %fusion.5, f32[1024,768]{0,1:T(8,128)S(1)} %copy-done.35, f32[1024]{0:T(1024)S(1)} %div.59, bf16[1,2048,768]{2,1,0:T(8,128)(2,1)S(1)} %copy-done, ...), kind=kOutput, calls=%fused_computation.31 | convolution fusion | flops 3236166656 | bytes 18358272 | tf_op jit(solution)/shard_map/dot_general | solution.py:28
  252.4 0.9 broadcast_select_fusion.1
  253.3 1.8 copy.56
  255.1 1.8 copy.55
  256.9 5.0 fusion.19
  262.0 3.7 add_convert_fusion
  265.8 2.5 maximum_bitcast_fusion
  268.2 5.6 all-to-all-start.2
  274.3 8.0 %convolution_convert_fusion.3 = bf16[1024,2048]{1,0:T(8,128)(2,1)} fusion(bf16[1024,768]{0,1:T(8,128)(2,1)} %get-tuple-element.81, bf16[1,768,2048]{2,1,0:T(8,128)(2,1)} %param.30), kind=kOutput, calls=%fused_computation.17 | convolution fusion | flops 3223322624 | bytes 8912896 | tf_op jit(solution)/shard_map/dot_general | solution.py:28
  282.3 7.7 %fusion.11 = f32[768,2048]{1,0:T(8,128)} fusion(bf16[1024,768]{0,1:T(8,128)(2,1)S(1)} %copy-done.36, bf16[1024,2176]{1,0:T(8,128)(2,1)} %bitcast.13), kind=kOutput, calls=%fused_computation.18 | convolution fusion | flops 3221225472 | bytes 12058624 | tf_op jit(solution)/shard_map/dot_general | solution.py:24
  290.1 8.6 %fusion.3 = f32[2048,768]{1,0:T(8,128)} fusion(bf16[1024,768]{0,1:T(8,128)(2,1)S(1)} %copy-done.34, bf16[128,8,2048]{2,1,0:T(8,128)(2,1)} %all-to-all-done.1), kind=kOutput, calls=%fused_computation.7 | convolution fusion | flops 3221225472 | bytes 12058624 | tf_op jit(solution)/shard_map/dot_general | solution.py:24
  298.7 8.5 %fusion.1 = f32[2048,768]{1,0:T(8,128)} fusion(bf16[1024,768]{0,1:T(8,128)(2,1)S(1)} %copy-done.38, bf16[128,8,2048]{2,1,0:T(8,128)(2,1)} %all-to-all-done.1), kind=kOutput, calls=%fused_computation.5 | convolution fusion | flops 3221225472 | bytes 12058624 | tf_op jit(solution)/shard_map/dot_general | solution.py:24
  307.1 27.1 %all-to-all-done.2 = bf16[128,8,2304]{2,1,0:T(8,128)(2,1)} async-done(((bf16[128,8,2304]{2,1,0:T(8,128)(2,1)}), bf16[128,8,2304]{2,1,0:T(8,128)(2,1)}, u32[]{:S(2)}, u32[]{:S(2)}) %all-to-all-start.2) | async-done | bytes 4718624 | tf_op jit(solution)/shard_map/all_to_all | solution.py:779
  334.2 3.3 fusion.39
  337.8 1.3 fusion.58
  339.2 7.2 %all-to-all-start.3 = ((f32[128,16,128]{2,1,0:T(8,128)}), f32[128,16,128]{2,1,0:T(8,128)}, u32[]{:S(2)}, u32[]{:S(2)}) async-start(f32[128,16,128]{2,1,0:T(8,128)} %bitcast.168), calls=%async_computation.3 | async-start | bytes 2097152 | tf_op jit(solution)/shard_map/all_to_all | solution.py:802
  346.3 1.6 multiply_reduce_fusion.1
  347.9 1.5 fusion.53
  349.5 22.9 %share_rows_3.1 = bf16[2,2,128,2048]{3,2,1,0:T(8,128)(2,1)} custom-call(bf16[128,2048]{1,0:T(8,128)(2,1)} %get-tuple-element.70.tok), custom_call_target="tpu_custom_call" | custom-call | bytes 46800000 | tf_op jit(solution)/shard_map/share_rows_3/pallas_call | solution.py:291
  372.4 1.4 reduce_sum.153
  373.7 9.9 %all-to-all-start.4 = ((bf16[128,8,2048]{2,1,0:T(8,128)(2,1)}), bf16[128,8,2048]{2,1,0:T(8,128)(2,1)}, u32[]{:S(2)}, u32[]{:S(2)}) async-start(bf16[128,8,2048]{2,1,0:T(8,128)(2,1)} %bitcast.167), calls=%async_computation.4 | async-start | bytes 8388608 | tf_op jit(solution)/shard_map/all_to_all | solution.py:804
  383.7 5.3 convolution_convert_fusion.6.grad_mixed
  389.0 6.6 %attend_back.1 = (bf16[512,1280]{1,0:T(8,128)(2,1)S(1)}, f32[2,128]{1,0:T(2,128)S(1)}) custom-call(f32[512,1280]{1,0:T(8,128)S(1)} %copy-done.3, f32[512,128]{1,0:T(8,128)S(1)} %copy-done.7, f32[512,128]{1,0:T(8,128)S(1)} %pad_maximum_fusion.1.signed, f32[1,128]{1,0:T(1,128)S(1)} %bitcast.163, f32[1,128]{1,0:T(1,128)S(1)} %bitcast.165, ...), custom_call_target="tpu_custom_call" | custom-call | bytes 50400000 | tf_op jit(solution)/shard_map/attend_back/pallas_call | solution.py:642
  395.7 5.6 convolution_convert_fusion.5
  401.3 40.5 %reduce_rows_4.1 = f32[128,2048]{1,0:T(8,128)S(1)} custom-call(bf16[2,2,128,2048]{3,2,1,0:T(8,128)(2,1)S(1)} %bitcast.160), custom_call_target="tpu_custom_call" | custom-call | bytes 54000000 | tf_op jit(solution)/shard_map/reduce_rows_4/pallas_call | solution.py:336
  442.2 2.1 broadcast_in_dim.122
  444.4 11.2 %all-to-all-start.5 = ((f32[128,50,128]{2,1,0:T(8,128)}), f32[128,50,128]{2,1,0:T(8,128)}, u32[]{:S(2)}, u32[]{:S(2)}) async-start(f32[128,50,128]{2,1,0:T(8,128)} %broadcast_in_dim.122), calls=%async_computation.5 | async-start | bytes 7340032 | tf_op jit(solution)/shard_map/all_to_all | solution.py:823
  455.6 4.1 convolution_convert_fusion.2
  459.7 3.2 convolution_convert_fusion
  463.0 104.6 %scatter_weights.1 = (f32[2,32,1280]{2,1,0:T(8,128)S(1)}, f32[2,32,1024]{2,1,0:T(8,128)S(1)}) custom-call(bf16[4,2,4,2,32,1280]{5,4,3,2,1,0:T(8,128)(2,1)S(1)} %bitcast.158, bf16[4,2,4,2,32,1024]{5,4,3,2,1,0:T(8,128)(2,1)S(1)} %bitcast.159), custom_call_target="tpu_custom_call" | custom-call | bytes 288000000 | tf_op jit(solution)/shard_map/scatter_weights/pallas_call | solution.py:498
  568.9 0.7 pad_maximum_fusion.2
  569.6 0.7 maximum_bitcast_fusion.1
  570.4 1.4 fusion.34
  571.8 4.0 fusion.23
  575.8 2.0 slice_reduce_fusion
  578.9 2.3 slice.114
  (124 shorter events, 6.2 us)
Async XLA Ops:
  0.6 242.4 %copy-start = (bf16[1,2048,768]{2,1,0:T(8,128)(2,1)S(1)}, bf16[1,2048,768]{2,1,0:T(8,128)(2,1)}, u32[]{:S(2)}) copy-start(bf16[1,2048,768]{2,1,0:T(8,128)(2,1)} %param.28) | copy-start | bytes 9437188
  92.2 71.1 %all-to-all-start = ((bf16[128,8,2176]{2,1,0:T(8,128)(2,1)}), bf16[128,8,2176]{2,1,0:T(8,128)(2,1)}, u32[]{:S(2)}, u32[]{:S(2)}) async-start(bf16[128,8,2176]{2,1,0:T(8,128)(2,1)} %fusion), calls=%async_computation | async-start | bytes 8912896 | tf_op jit(solution)/shard_map/all_to_all | solution.py:727
  102.0 6.5 %copy-start.6 = (f32[512,128]{1,0:T(8,128)}, f32[512,128]{1,0:T(8,128)S(1)}, u32[]{:S(2)}) copy-start(f32[512,128]{1,0:T(8,128)S(1)} %pad_maximum_fusion.cosine) | copy-start | bytes 786436
  102.4 6.2 %copy-start.12 = (f32[128]{0:T(128)S(1)}, f32[128]{0:T(128)}, u32[]{:S(2)}) copy-start(f32[128]{0:T(128)} %param.24) | copy-start | bytes 1540
  102.4 6.2 %copy-start.13 = (f32[128]{0:T(128)S(1)}, f32[128]{0:T(128)}, u32[]{:S(2)}) copy-start(f32[128]{0:T(128)} %param.25) | copy-start | bytes 1540
  102.4 16.0 %copy-start.30 = (bf16[4,2,4,2,32,1024]{5,4,3,2,1,0:T(8,128)(2,1)S(1)}, bf16[4,2,4,2,32,1024]{5,4,3,2,1,0:T(8,128)(2,1)}, u32[]{:S(2)}) copy-start(bf16[4,2,4,2,32,1024]{5,4,3,2,1,0:T(8,128)(2,1)} %get-tuple-element.44) | copy-start | bytes 12582916
  108.5 12.2 %copy-start.2 = (f32[512,1280]{1,0:T(8,128)}, f32[512,1280]{1,0:T(8,128)S(1)}, u32[]{:S(2)}) copy-start(f32[512,1280]{1,0:T(8,128)S(1)} %fusion.57.raw) | copy-start | bytes 7864324
  116.7 1.0 copy-start.8
  117.7 0.7 copy-start.10
  118.4 2.4 copy-start.4
  118.4 2.4 copy-start.14
  120.8 40.3 %copy-start.19 = (bf16[128,2048]{1,0:T(8,128)(2,1)S(1)}, bf16[128,2048]{1,0:T(8,128)(2,1)}, u32[]{:S(2)}) copy-start(bf16[128,2048]{1,0:T(8,128)(2,1)} %param.16) | copy-start | bytes 1572868
  120.8 41.5 %copy-start.28 = (f32[2048]{0:T(1024)S(1)}, f32[2048]{0:T(1024)}, u32[]{:S(2)}) copy-start(f32[2048]{0:T(1024)} %param.26) | copy-start | bytes 24580
  161.4 1.0 copy-start.16
  167.6 65.6 %all-to-all-start.1 = ((bf16[128,8,2048]{2,1,0:T(8,128)(2,1)}), bf16[128,8,2048]{2,1,0:T(8,128)(2,1)}, u32[]{:S(2)}, u32[]{:S(2)}) async-start(bf16[128,8,2048]{2,1,0:T(8,128)(2,1)} %convert_bitcast_fusion), calls=%async_computation.1 | async-start | bytes 8388608 | tf_op jit(solution)/shard_map/all_to_all | solution.py:745
  233.3 4.2 copy-start.31
  237.5 5.5 copy-start.35
  256.9 5.0 copy-start.32
  256.9 5.0 copy-start.37
  262.0 3.8 copy-start.26
  262.0 3.8 copy-start.27
  268.2 5.7 copy-start.22
  268.2 5.7 copy-start.23
  268.2 66.0 %all-to-all-start.2 = ((bf16[128,8,2304]{2,1,0:T(8,128)(2,1)}), bf16[128,8,2304]{2,1,0:T(8,128)(2,1)}, u32[]{:S(2)}, u32[]{:S(2)}) async-start(bf16[128,8,2304]{2,1,0:T(8,128)(2,1)} %maximum_bitcast_fusion), calls=%async_computation.2 | async-start | bytes 9437184 | tf_op jit(solution)/shard_map/all_to_all | solution.py:779
  274.3 8.0 %copy-start.36 = (bf16[1024,768]{0,1:T(8,128)(2,1)S(1)}, bf16[1024,768]{0,1:T(8,128)(2,1)}, u32[]{:S(2)}) copy-start(bf16[1024,768]{0,1:T(8,128)(2,1)} %get-tuple-element.81) | copy-start | bytes 4718596
  282.3 7.7 %copy-start.34 = (bf16[1024,768]{0,1:T(8,128)(2,1)S(1)}, bf16[1024,768]{0,1:T(8,128)(2,1)}, u32[]{:S(2)}) copy-start(bf16[1024,768]{0,1:T(8,128)(2,1)} %get-tuple-element.78) | copy-start | bytes 4718596
  290.1 8.6 %copy-start.38 = (bf16[1024,768]{0,1:T(8,128)(2,1)S(1)}, bf16[1024,768]{0,1:T(8,128)(2,1)}, u32[]{:S(2)}) copy-start(bf16[1024,768]{0,1:T(8,128)(2,1)} %get-tuple-element.80) | copy-start | bytes 4718596
  337.5 8.8 %copy-start.17 = (f32[128,2048]{1,0:T(8,128)S(1)}, f32[128,2048]{1,0:T(8,128)}, u32[]{:S(2)}) copy-start(f32[128,2048]{1,0:T(8,128)} %copy-done.16) | copy-start | bytes 3145732
  339.2 8.8 %copy-start.25 = (bf16[128,2048]{1,0:T(8,128)(2,1)S(1)}, bf16[128,2048]{1,0:T(8,128)(2,1)}, u32[]{:S(2)}) copy-start(bf16[128,2048]{1,0:T(8,128)(2,1)} %param.31) | copy-start | bytes 1572868
  339.2 33.2 %all-to-all-start.3 = ((f32[128,16,128]{2,1,0:T(8,128)}), f32[128,16,128]{2,1,0:T(8,128)}, u32[]{:S(2)}, u32[]{:S(2)}) async-start(f32[128,16,128]{2,1,0:T(8,128)} %bitcast.168), calls=%async_computation.3 | async-start | bytes 2097152 | tf_op jit(solution)/shard_map/all_to_all | solution.py:802
  373.7 68.5 %all-to-all-start.4 = ((bf16[128,8,2048]{2,1,0:T(8,128)(2,1)}), bf16[128,8,2048]{2,1,0:T(8,128)(2,1)}, u32[]{:S(2)}, u32[]{:S(2)}) async-start(bf16[128,8,2048]{2,1,0:T(8,128)(2,1)} %bitcast.167), calls=%async_computation.4 | async-start | bytes 8388608 | tf_op jit(solution)/shard_map/all_to_all | solution.py:804
  383.6 5.4 copy-start.3
  383.6 5.4 copy-start.5
  383.6 5.4 copy-start.7
  383.7 5.4 copy-start.9
  383.7 5.4 copy-start.11
  401.3 40.6 %copy-start.20 = (bf16[128,2048]{1,0:T(8,128)(2,1)S(1)}, bf16[128,2048]{1,0:T(8,128)(2,1)}, u32[]{:S(2)}) copy-start(bf16[128,2048]{1,0:T(8,128)(2,1)} %param.16) | copy-start | bytes 1572868
  401.3 40.6 %copy-start.29 = (f32[2048]{0:T(1024)S(1)}, f32[2048]{0:T(1024)}, u32[]{:S(2)}) copy-start(f32[2048]{0:T(1024)} %param.19) | copy-start | bytes 24580
  444.4 11.2 %copy-start.15 = (bf16[512,1024]{1,0:T(8,128)(2,1)S(1)}, bf16[512,1024]{1,0:T(8,128)(2,1)}, u32[]{:S(2)}) copy-start(bf16[512,1024]{1,0:T(8,128)(2,1)} %copy-done.14) | copy-start | bytes 3145732
  444.4 131.4 %all-to-all-start.5 = ((f32[128,50,128]{2,1,0:T(8,128)}), f32[128,50,128]{2,1,0:T(8,128)}, u32[]{:S(2)}, u32[]{:S(2)}) async-start(f32[128,50,128]{2,1,0:T(8,128)} %broadcast_in_dim.122), calls=%async_computation.5 | async-start | bytes 7340032 | tf_op jit(solution)/shard_map/all_to_all | solution.py:823
  455.6 4.1 copy-start.33
  462.9 107.4 %copy-start.21 = (bf16[128,2048]{1,0:T(8,128)(2,1)S(1)}, bf16[128,2048]{1,0:T(8,128)(2,1)}, u32[]{:S(2)}) copy-start(bf16[128,2048]{1,0:T(8,128)(2,1)} %param.16) | copy-start | bytes 1572868
  463.0 107.4 %copy-start.24 = (f32[128,2048]{1,0:T(8,128)S(1)}, f32[128,2048]{1,0:T(8,128)}, u32[]{:S(2)}) copy-start(f32[128,2048]{1,0:T(8,128)} %get-tuple-element.71) | copy-start | bytes 3145732
  567.6 4.2 copy-start.18
  571.8 9.4 %copy-start.1 = (bf16[1,2048,768]{2,1,0:T(8,128)(2,1)S(1)}, bf16[1,2048,768]{2,1,0:T(8,128)(2,1)}, u32[]{:S(2)}) copy-start(bf16[1,2048,768]{2,1,0:T(8,128)(2,1)} %param.28) | copy-start | bytes 9437188

commit v4 on v3

--- a/solution.py
+++ b/solution.py
@@ -145,7 +145,7 @@
             copy.wait_send()
 
 
-def gather_kernel(sa, sb, tok, doc, wa, wb, toks, docs, send, recv, local):
+def gather_kernel(q, k, v, o, tok, doc, wa, wb, toks, docs, send, recv, local):
     me = Place()
     x, yh, z, c, t = me.x, me.yh, me.z, me.c, me.t
     sibling = me.device(c=1 - c)
@@ -156,17 +156,23 @@
     greet([sibling, pair, partner, *ring_x, *ring_z])
     go = Copies(send, recv, local)
 
-    shards = ((sa, wa), (sb, wb))
-    cores = [go.put(s.at[1 - c], w.at[x, yh, z, c], sibling) for s, w in shards]
-    kept = [go.keep(s.at[c], w.at[x, yh, z, c]) for s, w in shards]
-    to_partner = go.put(tok, toks.at[c, t], partner)
-    rest = [go.keep(tok, toks.at[c, t]), go.keep(doc, docs.at[c])]
-    tail = [go.put(tok, toks.at[c, t], sibling), go.put(doc, docs.at[c], sibling)]
+    shards, start = [], 0
+    for ref, w in ((q, wa), (k, wa), (v, wa), (o, wb)):
+        cols = ref.shape[1] // NC
+        to = w.at[x, yh, z, c, :, pl.ds(0 if w is wb else start, cols)]
+        shards.append((ref, cols, to))
+        start += cols
+
+    def part(ref, cols, core):
+        return ref.at[:, pl.ds(pl.multiple_of(core * cols, cols), cols)]
+
+    cores = [go.put(part(ref, cols, 1 - c), to, sibling) for ref, cols, to in shards]
+    kept = [go.keep(part(ref, cols, c), to) for ref, cols, to in shards]
     for copy in kept:
         copy.wait()
     for copy in cores:
         copy.wait_recv()
-    pairs = [go.put(w.at[x, yh, z], w.at[x, yh, z], pair) for _, w in shards]
+    pairs = [go.put(w.at[x, yh, z], w.at[x, yh, z], pair) for w in (wa, wb)]
 
     ways = (
         (wa, x, z, ring_x, ring_z, lambda w, i, j, y: w.at[i, y, j], lambda w, j, y: w.at[:, y, j]),
@@ -212,17 +218,20 @@
         return out
 
     near = first(yh)
+    to_partner = go.put(tok, toks.at[c, t], partner)
+    rest = [go.keep(tok, toks.at[c, t]), go.keep(doc, docs.at[c])]
+    tail = [go.put(tok, toks.at[c, t], sibling), go.put(doc, docs.at[c], sibling)]
     near = second(yh, near)
+    near = third(yh, near)
     for copy in pairs:
         copy.wait_recv()
     far = first(1 - yh)
-    near = third(yh, near)
     far = second(1 - yh, far)
+    far = third(1 - yh, far)
+    near = fourth(yh, near)
     to_partner.wait_recv()
     other = toks.at[c, 1 - t]
     tail.append(go.put(other, other, sibling))
-    far = third(1 - yh, far)
-    near = fourth(yh, near)
     far = fourth(1 - yh, far)
     for up, down in near + far:
         up.wait_recv()
@@ -234,9 +243,10 @@
     go.finish()
 
 
-def gather(shard_a, shard_b, tokens, docs):
-    width_a, width_b = shard_a.shape[-1], shard_b.shape[-1]
-    rows = shard_a.shape[1]
+def gather(query, key, value, out, tokens, docs):
+    rows = query.shape[0]
+    width_a = (query.shape[1] + key.shape[1] + value.shape[1]) // NC
+    width_b = out.shape[1] // NC
     lead = (NX, NYH, NZ, NC, rows)
     wa, wb, toks, docs = pl.pallas_call(
         gather_kernel,
@@ -248,15 +258,15 @@
             jax.ShapeDtypeStruct((NC, 2, *tokens.shape), BF16),
             jax.ShapeDtypeStruct((NC, *docs.shape), docs.dtype),
         ),
-        in_specs=[ANY] * 4,
+        in_specs=[ANY] * 6,
         out_specs=(ANY,) * 4,
         scratch_shapes=[
-            pltpu.SemaphoreType.DMA((40,)),
-            pltpu.SemaphoreType.DMA((40,)),
-            pltpu.SemaphoreType.DMA((4,)),
+            pltpu.SemaphoreType.DMA((42,)),
+            pltpu.SemaphoreType.DMA((42,)),
+            pltpu.SemaphoreType.DMA((6,)),
         ],
         compiler_params=pltpu.CompilerParams(collective_id=1, has_side_effects=True),
-    )(shard_a, shard_b, tokens, docs)
+    )(query, key, value, out, tokens, docs)
     depth = NX * NYH * NZ * NC * rows
     return (
         wa.reshape(depth, width_a),
@@ -356,169 +366,240 @@
 
 
 def scatter_kernel(
-    ga, gb, oa, ob, ka, kb, ra, rb, qa, qb, sa, sb, ya, yb, ma, mb, ta, tb, ca, cb, send, recv, local
+    ga, gb, gains, piece, oq, ok, ov, oo, og, op, ka, kb, ra, rb, qa, qb, sa, sb, ya, yb, ma, mb, ta, tb, ca, cb,
+    ring_gains, sum_gains, pair_gains, send, recv, local
 ):
     me = Place()
     x, yh, z, c = me.x, me.yh, me.z, me.c
     sibling = me.device(c=1 - c)
     pair = me.device(yh=1 - yh)
+    partner = me.device(t=1 - me.t)
     ring_x = (me.device(x=after(x)), me.device(x=before(x)))
     ring_z = (me.device(z=after(z)), me.device(z=before(z)))
-    greet([sibling, pair, *ring_x, *ring_z])
+    round_x = (*ring_x, me.device(x=across(x)))
+    round_z = (*ring_z, me.device(z=across(z)))
+    greet([sibling, pair, partner, *round_x, *round_z])
     go = Copies(send, recv, local)
-
-    def slab_a(i, r):
-        return ga.at[i, :, :, r]
-
-    def slab_b(i, r):
-        return gb.at[:, :, i, r]
-
-    ways = ((slab_a, x, ring_x, ka, ra), (slab_b, z, ring_z, kb, rb))
-    cross, straight, kept = [], [], []
-    for slab, i, ring, k, r in ways:
-        cross.append((go.put(slab(across(i), 0), r.at[0], ring[0]), go.put(slab(across(i), 1), r.at[1], ring[1])))
-    for slab, i, ring, k, r in ways:
-        kept.append(
-            [
-                go.keep(slab(after(i), 0), k.at[0]),
-                go.keep(slab(before(i), 1), k.at[1]),
-                go.keep(slab(i, 0), k.at[2]),
-                go.keep(slab(i, 1), k.at[3]),
-            ]
-        )
-        straight.append((go.put(slab(after(i), 1), r.at[2], ring[0]), go.put(slab(before(i), 0), r.at[3], ring[1])))
-    summed = []
-    for (slab, i, ring, k, r), copies, own in zip(ways, cross, kept):
-        both = []
-        for side in range(2):
-            own[side].wait()
-            copies[side].wait_recv()
-
-            def add(n, _, k=k, r=r, side=side):
-                at = (side, n // k.shape[2], lax.rem(n, k.shape[2]))
-                k[at] = (k[at].astype(F32) + r[at].astype(F32)).astype(BF16)
+    chunks = (1 - yh, yh)
+
+    def around(n, term, own, peers):
+        ring_gains[n, own] = term
+        return [go.put(ring_gains.at[n, own], ring_gains.at[n, own], peer) for peer in peers]
+
+    def ring_sum(n, copies):
+        for copy in copies:
+            copy.wait_recv()
+        return (ring_gains[n, 0] + ring_gains[n, 1]) + (ring_gains[n, 2] + ring_gains[n, 3])
+
+    def swap(n, term, peer):
+        sum_gains[n] = term
+        return go.put(sum_gains.at[n], pair_gains.at[n], peer)
+
+    def swapped(n, copy):
+        copy.wait_recv()
+        return sum_gains[n] + pair_gains[n]
+
+
+    ways = (
+        (lambda i, y, h: ga.at[i, y, :, h], x, z, ring_x, ring_z, ka, ra, qa, sa),
+        (lambda i, y, h: gb.at[:, y, i, h], z, x, ring_z, ring_x, kb, rb, qb, sb),
+    )
+
+    def cross(n):
+        out = []
+        for slab, i, j, one, two, k, r, q, s in ways:
+            far = across(i)
+            out.append(
+                [go.put(slab(far, chunks[n], h), r.at[n, h], one[h]) for h in range(2)]
+            )
+        return out
+
+    def straight(n):
+        out = []
+        for slab, i, j, one, two, k, r, q, s in ways:
+            near = (after(i), before(i))
+            out.append(
+                [go.put(slab(near[h], chunks[n], 1 - h), r.at[n, 2 + h], one[h]) for h in range(2)]
+            )
+        return out
+
+    def hold(n):
+        out = []
+        for slab, i, j, one, two, k, r, q, s in ways:
+            parts = ((after(i), 0), (before(i), 1), (i, 0), (i, 1))
+            out.append(
+                [go.keep(slab(p, chunks[n], h), k.at[n, m]) for m, (p, h) in enumerate(parts)]
+            )
+        return out
+
+    def add(n, crossed, held):
+        out = []
+        for (slab, i, j, one, two, k, r, q, s), copies, own in zip(ways, crossed, held):
+            both = []
+            for h in range(2):
+                own[h].wait()
+                copies[h].wait_recv()
+
+                def step(m, _, k=k, r=r, h=h):
+                    k[n, h, m] = (k[n, h, m].astype(F32) + r[n, h, m].astype(F32)).astype(BF16)
+                    return 0
+
+                lax.fori_loop(0, k.shape[2], step, 0)
+                both.append(go.put(k.at[n, h], r.at[n, 4 + h], one[h]))
+            out.append(both)
+        return out
+
+    def close(n, straights, summed, held):
+        out = []
+        for (slab, i, j, one, two, k, r, q, s), a, b, own in zip(ways, straights, summed, held):
+            for h in range(2):
+                own[2 + h].wait()
+                a[h].wait_recv()
+                b[h].wait_recv()
+
+            def step(m, _, k=k, r=r):
+                for h in range(2):
+                    k[n, 2 + h, m] = (
+                        k[n, 2 + h, m].astype(F32)
+                        + r[n, 4 + h, m].astype(F32)
+                        + r[n, 3 - h, m].astype(F32)
+                    ).astype(BF16)
                 return 0
 
-            lax.fori_loop(0, k.shape[1] * k.shape[2], add, 0)
-            both.append(go.put(k.at[side], r.at[4 + side], ring[side]))
-        summed.append(both)
-    for (slab, i, ring, k, r), one, two, own in zip(ways, straight, summed, kept):
-        own[2].wait()
-        own[3].wait()
-        one[0].wait_recv()
-        one[1].wait_recv()
-        two[0].wait_recv()
-        two[1].wait_recv()
-
-        def close(n, _, k=k, r=r):
-            at = (n // k.shape[2], lax.rem(n, k.shape[2]))
-            for own, summed_side, straight_side in ((2, 4, 3), (3, 5, 2)):
-                k[(own, *at)] = (
-                    k[(own, *at)].astype(F32)
-                    + r[(summed_side, *at)].astype(F32)
-                    + r[(straight_side, *at)].astype(F32)
-                ).astype(BF16)
-            return 0
-
-        lax.fori_loop(0, k.shape[1] * k.shape[2], close, 0)
-
-    def part_a(r, j, y):
-        return ka.at[r, y, j]
-
-    def part_b(r, j, y):
-        return kb.at[r, j, y]
-
-    ways = ((part_a, z, ring_z, qa, sa), (part_b, x, ring_x, qb, sb))
-    cross, straight, summed = [], [], []
-    for part, j, ring, q, s in ways:
-        cross.append(
-            [
-                [go.put(part(2 + side, across(j), y), q.at[side, y], ring[side]) for y in range(NYH)]
-                for side in range(2)
-            ]
-        )
-    for part, j, ring, q, s in ways:
-        straight.append(
-            [
-                [go.put(part(3 - side, (after, before)[side](j), y), q.at[2 + side, y], ring[side]) for y in range(NYH)]
-                for side in range(2)
-            ]
-        )
-    for (part, j, ring, q, s), copies in zip(ways, cross):
-        both = []
-        for side in range(2):
-            sent = []
-            for y in range(NYH):
-                copies[side][y].wait_recv()
-                mine = part(2 + side, (after, before)[side](j), y)
-                s[side, y] = (mine[...].astype(F32) + q[side, y].astype(F32)).astype(BF16)
-                sent.append(go.put(s.at[side, y], q.at[4 + side, y], ring[side]))
-            both.append(sent)
-        summed.append(both)
-    for (part, j, ring, q, s), one, two in zip(ways, straight, summed):
-        for copies in (*one, *two):
-            for copy in copies:
-                copy.wait_recv()
-
-    def total(part, j, q, side, y):
-        return part(2 + side, j, y)[...].astype(F32) + q[4 + side, y].astype(F32) + q[3 - side, y].astype(F32)
-
-    ways = ((part_a, z, qa, ya, ma, ta, ca, oa), (part_b, x, qb, yb, mb, tb, cb, ob))
-    crossed = []
-    for part, j, q, yy, m, tt, cc, o in ways:
-        for side in range(2):
-            yy[side] = total(part, j, q, side, 1 - yh).astype(BF16)
-        crossed.append(go.put(yy, m, pair))
+            lax.fori_loop(0, k.shape[2], step, 0)
+            near = (after(j), before(j))
+            over = [go.put(k.at[n, 2 + h, across(j)], q.at[n, h], two[h]) for h in range(2)]
+            direct = [go.put(k.at[n, 3 - h, near[h]], q.at[n, 2 + h], two[h]) for h in range(2)]
+            out.append((over, direct))
+        return out
+
+    def add_second(n, closed):
+        out = []
+        for (slab, i, j, one, two, k, r, q, s), (over, direct) in zip(ways, closed):
+            near = (after(j), before(j))
+            both = []
+            for h in range(2):
+                over[h].wait_recv()
+                s[n, h] = (k[n, 2 + h, near[h]].astype(F32) + q[n, h].astype(F32)).astype(BF16)
+                both.append(go.put(s.at[n, h], q.at[n, 4 + h], two[h]))
+            out.append(both + direct)
+        return out
+
+    def total(n, added, w):
+        slab, i, j, one, two, k, r, q, s = ways[w]
+        for copy in added[w]:
+            copy.wait_recv()
+        return [
+            k[n, 2 + h, j].astype(F32) + q[n, 4 + h].astype(F32) + q[n, 3 - h].astype(F32)
+            for h in range(2)
+        ]
+
+    t = me.t
+
+    def spread(ref, peers):
+        return [go.put(ref, ref, peer) for peer in peers]
+
+    def arrived(copies):
+        for copy in copies:
+            copy.wait_recv()
+
+    terms = around(0, gains[...], x, round_x)
+    mine = op.at[x, yh, z, c, t]
+    held_piece = go.keep(piece, mine)
+    pieces = [go.put(piece, mine, sibling)]
+    cross_0, straight_0 = cross(0), straight(0)
+    held_0, held_1 = hold(0), hold(1)
+    terms = around(1, ring_sum(0, terms), z, round_z)
+    arrived(pieces)
+    held_piece.wait()
+    pieces = spread(op.at[x, yh, z, :, t], [partner])
+    cross_1 = cross(1)
+    sums_0 = add(0, cross_0, held_0)
+    straight_1 = straight(1)
+    arrived(pieces)
+    pieces = spread(op.at[x, yh, z], [pair])
+    sums_1 = add(1, cross_1, held_1)
+    arrived(pieces)
+    pieces = spread(op.at[x, :, z], round_x)
+    terms = swap(0, ring_sum(1, terms), pair)
+    closed_0 = close(0, straight_0, sums_0, held_0)
+    terms = swap(1, swapped(0, terms), partner)
+    arrived(pieces)
+    pieces = spread(op.at[:, :, z], round_z)
+    added_0 = add_second(0, closed_0)
+    ends = ((ya, ma, ta, ca), (yb, mb, tb, cb))
+    pairs = []
+    for w, (yy, m, tt, cc) in enumerate(ends):
+        for h, part in enumerate(total(0, added_0, w)):
+            yy[h] = part.astype(BF16)
+        pairs.append(go.put(yy, m, pair))
+    terms = swap(2, swapped(1, terms), sibling)
+    closed_1 = close(1, straight_1, sums_1, held_1)
+    added_1 = add_second(1, closed_1)
     last = []
-    for (part, j, q, yy, m, tt, cc, o), copy in zip(ways, crossed):
-        for side in range(2):
-            tt[side] = total(part, j, q, side, yh)
+    for w, (yy, m, tt, cc) in enumerate(ends):
+        parts = total(1, added_1, w)
+        pairs[w].wait_recv()
+        for h, part in enumerate(parts):
+            tt[h] = part + m[h].astype(F32)
+        last.append(go.put(tt.at[1 - c], cc, sibling))
+    og[...] = swapped(2, terms)
+    arrived(pieces)
+
+    def write(core, a, b):
+        start = 0
+        for out, held in ((oq, a), (ok, a), (ov, a), (oo, b)):
+            cols = out.shape[1] // NC
+            at = 0 if held is b else start
+            out[:, pl.ds(pl.multiple_of(core * cols, cols), cols)] = held[:, at : at + cols]
+            start += cols
+
+    write(c, ta[c], tb[c])
+    for copy in last:
         copy.wait_recv()
-        tt[...] += m[...].astype(F32)
-        last.append(go.put(tt.at[1 - c], cc, sibling))
-        o[c] = tt[c]
-    for (part, j, q, yy, m, tt, cc, o), copy in zip(ways, last):
-        copy.wait_recv()
-        o[1 - c] = cc[...]
+    write(1 - c, ca[...], cb[...])
     go.finish()
 
 
-def scatter(grad_a, grad_b):
+def scatter(grad_a, grad_b, gains, piece, columns):
     rows = grad_a.shape[0] // (NX * NYH * NZ * NC)
     lead = (NX, NYH, NZ, NC, rows)
     widths = (grad_a.shape[1], grad_b.shape[1])
 
     def each(shape, dtype):
         return [pltpu.VMEM((*shape, rows, w), dtype) for w in widths]
-
-    def held(count):
-        dims = ((NYH, NZ), (NX, NYH))
-        return [pltpu.VMEM((count, *d, rows, w), BF16) for d, w in zip(dims, widths)]
 
     return pl.pallas_call(
         scatter_kernel,
         name="scatter_weights",
         cost_estimate=cost(80),
-        out_shape=tuple(jax.ShapeDtypeStruct((NC, rows, w), F32) for w in widths),
-        in_specs=[ANY, ANY],
-        out_specs=(VMEM, VMEM),
+        out_shape=(
+            *(jax.ShapeDtypeStruct((rows, w), F32) for w in columns),
+            jax.ShapeDtypeStruct(gains.shape, F32),
+            jax.ShapeDtypeStruct((NX, NYH, NZ, NC, 2, *piece.shape), piece.dtype),
+        ),
+        in_specs=[ANY, ANY, VMEM, ANY],
+        out_specs=(*(VMEM,) * 5, ANY),
         scratch_shapes=[
-            *held(4),
-            *held(6),
-            *each((6, NYH), BF16),
-            *each((2, NYH), BF16),
+            *each((2, 4, RING), BF16),
+            *each((2, 6, RING), BF16),
+            *each((2, 6), BF16),
+            *each((2, 2), BF16),
             *each((2,), BF16),
             *each((2,), BF16),
             *each((2,), F32),
             *each((), F32),
-            pltpu.SemaphoreType.DMA((40,)),
-            pltpu.SemaphoreType.DMA((40,)),
-            pltpu.SemaphoreType.DMA((8,)),
+            pltpu.VMEM((2, RING, *gains.shape), F32),
+            pltpu.VMEM((3, *gains.shape), F32),
+            pltpu.VMEM((3, *gains.shape), F32),
+            pltpu.SemaphoreType.DMA((70,)),
+            pltpu.SemaphoreType.DMA((70,)),
+            pltpu.SemaphoreType.DMA((17,)),
         ],
         compiler_params=pltpu.CompilerParams(
             collective_id=5, has_side_effects=True, vmem_limit_bytes=40 << 20
         ),
-    )(grad_a.reshape(*lead, widths[0]), grad_b.reshape(*lead, widths[1]))
+    )(grad_a.reshape(*lead, widths[0]), grad_b.reshape(*lead, widths[1]), gains, piece)
 
 
 def unit_rows(values):
@@ -711,13 +792,11 @@
     hidden = hidden_in.astype(F32)
     normed_local = rms_scale(hidden, attn_gain).astype(BF16)
 
-    def core_parts(shards):
-        split = [s.reshape(s.shape[0], NC, s.shape[1] // NC) for s in shards]
-        return jnp.concatenate(split, axis=2).transpose(1, 0, 2)
-
     in_weights, out_weights, normed, docs = gather(
-        core_parts([query_weight, key_weight, value_weight]),
-        core_parts([output_weight.T]),
+        query_weight,
+        key_weight,
+        value_weight,
+        output_weight.T,
         normed_local,
         jnp.broadcast_to(doc_ids, (8, tokens)).astype(F32),
     )
@@ -798,8 +877,8 @@
     moegain_part = jnp.sum(moegain_rows, axis=0)
     grad_residual = upstream + grad_norm
     grad_attn = share(grad_residual.astype(BF16), 3)
-    pieces = router_part.reshape(experts, width // experts, experts)
-    piece = jnp.sum(lax.all_to_all(pieces, both, 0, 0, tiled=True), axis=0)
+    pieces = router_part.astype(BF16).reshape(experts, width // experts, experts)
+    piece = jnp.sum(lax.all_to_all(pieces, both, 0, 0, tiled=True).astype(F32), axis=0)
     expert_out, grad_attn, piece = lax.optimization_barrier((expert_out, grad_attn, piece))
     returned = lax.all_to_all(
         expert_out.reshape(experts, cap, width), both, split_axis=0, concat_axis=0, tiled=True
@@ -810,41 +889,33 @@
         raw, cosine, signed, query_gain, key_gain, query, kv, attention, grad_mixed, scale
     )
     grad_normed = reduce(dot_nt(grad_raw, in_weights).astype(BF16), 4)
-    in_grad, out_grad = scatter(
-        dot_tn(normed, grad_raw).astype(BF16), dot_tn(grad_attn, mixed).astype(BF16)
-    )
     grad_hidden, attngain_rows = rms_back(hidden, attn_gain, grad_normed)
     input_grad = grad_residual + grad_hidden
 
-    gains = jnp.concatenate([jnp.sum(attngain_rows, axis=0), moegain_part, head_gains.reshape(-1)])
-    term = jnp.concatenate([piece, gains.reshape(-1, experts)], axis=0)
-    term, returned = lax.optimization_barrier((term, returned))
+    gains = jnp.concatenate([jnp.sum(attngain_rows, axis=0), moegain_part]).reshape(-1, hd)
+    gains = jnp.concatenate([gains, head_gains, jnp.zeros((6, hd), F32)], axis=0)
+
     layer_out = (residual + dot_tn(spread, returned)).astype(BF16)
-    terms = lax.all_to_all(
-        jnp.broadcast_to(term[None], (experts, *term.shape)), both, 0, 0, tiled=True
-    )
-    router_grad = terms[:, : piece.shape[0]].reshape(width, experts)
-    gains = jnp.sum(terms[:, piece.shape[0] :], axis=0).reshape(-1)
-    attngain_grad = gains[:width]
-    moegain_grad = gains[width : 2 * width]
-    qgain_grad = gains[2 * width : 2 * width + hd]
-    kgain_grad = gains[2 * width + hd :]
-
-    def join(parts):
-        return jnp.concatenate([parts[i] for i in range(NC)], axis=1)
-
+    query_grad, key_grad, value_grad, out_grad, gains, router_grad = scatter(
+        dot_tn(normed, grad_raw).astype(BF16),
+        dot_tn(grad_attn, mixed).astype(BF16),
+        gains,
+        piece.astype(BF16),
+        (nq * hd, nkv * hd, nkv * hd, nq * hd),
+    )
+    at = width // hd
     return (
         layer_out,
         input_grad,
-        attngain_grad,
-        join(in_grad[:, :, :heads]),
-        join(in_grad[:, :, heads : heads + hd]),
-        join(in_grad[:, :, heads + hd :]),
-        join(out_grad).T,
-        qgain_grad,
-        kgain_grad,
-        moegain_grad,
-        router_grad,
+        gains[:at].reshape(-1),
+        query_grad,
+        key_grad,
+        value_grad,
+        out_grad.T,
+        gains[2 * at],
+        gains[2 * at + 1],
+        gains[at : 2 * at].reshape(-1),
+        router_grad.reshape(width, experts).astype(F32),
         gate_grad[None],
         up_grad[None],
         down_grad[None],

time: 586 us -> 525 us (0.90)
  Pallas kernels: 298 us -> 259 us
  starting transfers between devices: 53.1 us -> 43.7 us
  local copies, waits for them, and re-layouts: 25 us -> 18.9 us
    pallas_call x1, Pallas kernels: 105 us -> 74.7 us  [scatter(): pl.pallas_call(scatter_kernel, name='scatter_weights', cost_estimate=cost...]
    all_to_all x2 -> x1, starting transfers between devices: 18.4 us -> 6.71 us  [on_device(): lax.all_to_all(pieces, both, 0, 0, tiled=True).astype(F32)]
  transfers between devices with their start and end apart: 6 -> 5, of which waited for: 2 -> 2; matrix products, arithmetic and copies ran while one was open for 15% -> 16% of each run, Pallas kernels for 38% -> 36%
where the time goes in v4:
time: 525 us; the launch traced here: 521 us
  Pallas kernels  259 us (49%)
  matrix products  114 us (22%)
  waiting for transfers between devices  66.3 us (13%)
  starting transfers between devices  43.7 us (8%)
  local copies, waits for them, and re-layouts  18.9 us (4%)
  other arithmetic  17.4 us (3%)
    pallas_call x2, Pallas kernels, reduce(): pl.pallas_call(reduce_kernel, name=f'reduce_rows_{ident}', cost_estimate=...  80.8 us
    pallas_call x1, Pallas kernels, scatter(): pl.pallas_call(scatter_kernel, name='scatter_weights', cost_estimate=cost...  74.7 us
    pallas_call x1, Pallas kernels, gather(): pl.pallas_call(gather_kernel, name='gather_weights', cost_estimate=cost(6...  69.5 us
    dot_general x10, matrix products, dot_nn(): lax.dot_general(a, b, (((1,), (0,)), ((), ())), preferred_element_type=F32)  47.7 us
    all_to_all x1, waiting for transfers between devices, on_device(): lax.all_to_all(sent.reshape(experts, cap, width), both, split_axis=0, con...  39.3 us
    dot_general x8, matrix products, dot_tn(): lax.dot_general(a, b, (((0,), (0,)), ((), ())), preferred_element_type=F32)  39 us
    dot_general x6, matrix products, dot_nt(): lax.dot_general(a, b, (((1,), (1,)), ((), ())), preferred_element_type=F32)  27.5 us
    all_to_all x1, waiting for transfers between devices, on_device(): lax.all_to_all(home_out.reshape(experts, cap, width + 2 * experts), both,...  27 us
  transfers between devices with their start and end apart: 5, of which 2 were waited for; matrix products, arithmetic and copies ran while one was open for 16% of the time, Pallas kernels for 36%

profile of v4, /device:TPU:1, one launch (start us, length us, event | category | flops | bytes accessed | tf_op | source)
XLA Modules:
  0.0 520.9 jit_solution(6154374127271235664)
XLA Ops:
  0.7 0.9 copy.55
  2.0 1.2 fusion.28
  3.2 0.7 convert_element_type.138
  4.0 2.0 fusion.30.tok
  6.4 0.6 broadcast_in_dim.107.doc
  7.0 69.5 %gather_weights.1 = (bf16[4,2,4,2,32,1280]{5,4,3,2,1,0:T(8,128)(2,1)}, bf16[4,2,4,2,32,1024]{5,4,3,2,1,0:T(8,128)(2,1)}, bf16[2,2,128,2048]{3,2,1,0:T(8,128)(2,1)}, f32[2,8,256]{2,1,0:T(8,128)}) custom-call(bf16[32,2048]{1,0:T(8,128)(2,1)} %q.1, bf16[32,256]{1,0:T(8,128)(2,1)} %k.1, bf16[32,256]{1,0:T(8,128)(2,1)} %v.1, bf16[32,2048]{1,0:T(8,128)(2,1)} %bitcast.135, ...), custom_call_target="tpu_custom_call" | custom-call | bytes 216000000 | tf_op jit(solution)/shard_map/gather_weights/pallas_call | solution.py:251
  76.5 4.5 fusion
  81.0 9.7 %all-to-all-start = ((bf16[128,8,2176]{2,1,0:T(8,128)(2,1)}), bf16[128,8,2176]{2,1,0:T(8,128)(2,1)}, u32[]{:S(2)}, u32[]{:S(2)}) async-start(bf16[128,8,2176]{2,1,0:T(8,128)(2,1)} %fusion), calls=%async_computation | async-start | bytes 8912896 | tf_op jit(solution)/shard_map/all_to_all | solution.py:806
  90.7 0.7 slice.30
  91.7 1.0 fusion.51
  93.2 6.1 %fusion.59.raw = f32[512,1280]{1,0:T(8,128)S(1)} fusion(bf16[512,2048]{1,0:T(8,128)(2,1)} %bitcast.146, bf16[2048,1280]{1,0:T(8,128)(2,1)} %bitcast.142), kind=kOutput, calls=%fused_computation.131 | convolution fusion | flops 2684354560 | bytes 9961472 | tf_op jit(solution)/shard_map/dot_general | solution.py:28
  99.4 8.1 %attend.1 = (bf16[512,1024]{1,0:T(8,128)(2,1)S(1)}, bf16[512,256]{1,0:T(8,128)(2,1)S(1)}, f32[2,8,256,256]{3,2,1,0:T(8,128)S(1)}, bf16[512,1024]{1,0:T(8,128)(2,1)S(1)}) custom-call(f32[512,1280]{1,0:T(8,128)S(1)} %fusion.59.raw, f32[2,256,256]{2,1,0:T(8,128)S(1)} %fusion.42.bias, f32[512,128]{1,0:T(8,128)S(1)} %get-tuple-element.108.cosine, ...), custom_call_target="tpu_custom_call" | custom-call | bytes 28800000 | tf_op jit(solution)/shard_map/attend/pallas_call | solution.py:646
  107.5 1.0 copy-done.8
  108.5 0.7 copy-done.10
  109.1 2.4 convolution_convert_fusion.4
  111.6 40.4 %reduce_rows_2.1 = f32[128,2048]{1,0:T(8,128)S(1)} custom-call(bf16[2,2,128,2048]{3,2,1,0:T(8,128)(2,1)S(1)} %bitcast.126), custom_call_target="tpu_custom_call" | custom-call | bytes 54000000 | tf_op jit(solution)/shard_map/reduce_rows_2/pallas_call | solution.py:346
  152.2 0.6 multiply_multiply_fusion.1
  152.8 0.4 copy-done.18
  153.2 0.9 multiply_convert_fusion.3
  154.1 4.3 convert_bitcast_fusion
  158.5 11.6 %all-to-all-start.1 = ((bf16[128,8,2048]{2,1,0:T(8,128)(2,1)}), bf16[128,8,2048]{2,1,0:T(8,128)(2,1)}, u32[]{:S(2)}, u32[]{:S(2)}) async-start(bf16[128,8,2048]{2,1,0:T(8,128)(2,1)} %convert_bitcast_fusion), calls=%async_computation.1 | async-start | bytes 8388608 | tf_op jit(solution)/shard_map/all_to_all | solution.py:824
  170.1 6.5 %copy.57 = bf16[1024,2176]{0,1:T(8,128)(2,1)} copy(bf16[1024,2176]{1,0:T(8,128)(2,1)} %bitcast.11) | data formatting | bytes 8912896 | tf_op jit(solution)/shard_map/optimization_barrier | solution.py:822
  176.6 8.3 %fusion.13 = f32[1024,768]{0,1:T(8,128)} fusion(bf16[1024,2176]{1,0:T(8,128)(2,1)} %bitcast.11, bf16[1,768,2048]{2,1,0:T(8,128)(2,1)} %param.30), kind=kOutput, calls=%fused_computation.20 | convolution fusion | flops 3221225472 | bytes 10485760 | tf_op jit(solution)/shard_map/dot_general | solution.py:20
  184.9 39.3 %all-to-all-done.1 = bf16[128,8,2048]{2,1,0:T(8,128)(2,1)} async-done(((bf16[128,8,2048]{2,1,0:T(8,128)(2,1)}), bf16[128,8,2048]{2,1,0:T(8,128)(2,1)}, u32[]{:S(2)}, u32[]{:S(2)}) %all-to-all-start.1) | async-done | bytes 4194336 | tf_op jit(solution)/shard_map/all_to_all | solution.py:824
  224.1 4.0 fusion.57
  228.4 5.5 %fusion.5 = f32[1024,768]{0,1:T(8,128)S(1)} fusion(bf16[128,8,2048]{2,1,0:T(8,128)(2,1)} %all-to-all-done.1, bf16[1,2048,768]{2,1,0:T(8,128)(2,1)S(1)} %copy-done.32), kind=kOutput, calls=%fused_computation.9 | convolution fusion | flops 3221225472 | bytes 10485760 | tf_op jit(solution)/shard_map/dot_general | solution.py:28
  233.9 9.4 %multiply_convert_fusion.1 = (bf16[1024,768]{0,1:T(8,128)(2,1)}, f32[1024]{0:T(1024)S(1)}, bf16[1024,768]{0,1:T(8,128)(2,1)}, bf16[1024,768]{0,1:T(8,128)(2,1)}) fusion(f32[1024,768]{0,1:T(8,128)S(1)} %fusion.5, f32[1024,768]{0,1:T(8,128)S(1)} %copy-done.36, f32[1024]{0:T(1024)S(1)} %div.59, bf16[1,2048,768]{2,1,0:T(8,128)(2,1)S(1)} %copy-done, ...), kind=kOutput, calls=%fused_computation.31 | convolution fusion | flops 3236166656 | bytes 18358272 | tf_op jit(solution)/shard_map/dot_general | solution.py:28
  243.3 0.9 broadcast_select_fusion.1
  244.2 1.8 copy.59
  246.0 1.8 copy.58
  247.8 5.0 fusion.19
  252.9 3.7 add_convert_fusion
  256.6 2.5 maximum_bitcast_fusion
  259.1 5.6 %all-to-all-start.2 = ((bf16[128,8,2304]{2,1,0:T(8,128)(2,1)}), bf16[128,8,2304]{2,1,0:T(8,128)(2,1)}, u32[]{:S(2)}, u32[]{:S(2)}) async-start(bf16[128,8,2304]{2,1,0:T(8,128)(2,1)} %maximum_bitcast_fusion), calls=%async_computation.2 | async-start | bytes 9437184 | tf_op jit(solution)/shard_map/all_to_all | solution.py:858
  264.8 0.4 fusion.58
  265.2 8.0 %convolution_convert_fusion.3 = bf16[1024,2048]{1,0:T(8,128)(2,1)} fusion(bf16[1024,768]{0,1:T(8,128)(2,1)} %get-tuple-element.85, bf16[1,768,2048]{2,1,0:T(8,128)(2,1)} %param.30), kind=kOutput, calls=%fused_computation.17 | convolution fusion | flops 3223322624 | bytes 8912896 | tf_op jit(solution)/shard_map/dot_general | solution.py:28
  273.3 7.7 %fusion.11 = f32[768,2048]{1,0:T(8,128)} fusion(bf16[1024,768]{0,1:T(8,128)(2,1)S(1)} %copy-done.37, bf16[1024,2176]{1,0:T(8,128)(2,1)} %bitcast.11), kind=kOutput, calls=%fused_computation.18 | convolution fusion | flops 3221225472 | bytes 12058624 | tf_op jit(solution)/shard_map/dot_general | solution.py:24
  281.0 8.6 %fusion.3 = f32[2048,768]{1,0:T(8,128)} fusion(bf16[1024,768]{0,1:T(8,128)(2,1)S(1)} %copy-done.35, bf16[128,8,2048]{2,1,0:T(8,128)(2,1)} %all-to-all-done.1), kind=kOutput, calls=%fused_computation.7 | convolution fusion | flops 3221225472 | bytes 12058624 | tf_op jit(solution)/shard_map/dot_general | solution.py:24
  289.6 8.5 %fusion.1 = f32[2048,768]{1,0:T(8,128)} fusion(bf16[1024,768]{0,1:T(8,128)(2,1)S(1)} %copy-done.39, bf16[128,8,2048]{2,1,0:T(8,128)(2,1)} %all-to-all-done.1), kind=kOutput, calls=%fused_computation.5 | convolution fusion | flops 3221225472 | bytes 12058624 | tf_op jit(solution)/shard_map/dot_general | solution.py:24
  298.1 27.0 %all-to-all-done.2 = bf16[128,8,2304]{2,1,0:T(8,128)(2,1)} async-done(((bf16[128,8,2304]{2,1,0:T(8,128)(2,1)}), bf16[128,8,2304]{2,1,0:T(8,128)(2,1)}, u32[]{:S(2)}, u32[]{:S(2)}) %all-to-all-start.2) | async-done | bytes 4718624 | tf_op jit(solution)/shard_map/all_to_all | solution.py:858
  325.1 3.4 fusion.40
  328.8 2.5 multiply_reduce_fusion.1
  331.3 1.1 convolution_convert_fusion.6
  332.4 6.7 %all-to-all-start.3 = ((bf16[128,16,128]{2,1,0:T(8,128)(2,1)}), bf16[128,16,128]{2,1,0:T(8,128)(2,1)S(1)}, u32[]{:S(2)}, u32[]{:S(2)}) async-start(bf16[128,16,128]{2,1,0:T(8,128)(2,1)} %bitcast.20), calls=%async_computation.3 | async-start | bytes 1048576 | tf_op jit(solution)/shard_map/all_to_all | solution.py:881
  339.1 2.9 fusion.55
  342.0 18.8 %share_rows_3.1 = bf16[2,2,128,2048]{3,2,1,0:T(8,128)(2,1)} custom-call(bf16[128,2048]{1,0:T(8,128)(2,1)} %get-tuple-element.74.tok), custom_call_target="tpu_custom_call" | custom-call | bytes 46800000 | tf_op jit(solution)/shard_map/share_rows_3/pallas_call | solution.py:301
  361.0 10.1 %all-to-all-start.4 = ((bf16[128,8,2048]{2,1,0:T(8,128)(2,1)}), bf16[128,8,2048]{2,1,0:T(8,128)(2,1)}, u32[]{:S(2)}, u32[]{:S(2)}) async-start(bf16[128,8,2048]{2,1,0:T(8,128)(2,1)} %bitcast.132), calls=%async_computation.4 | async-start | bytes 8388608 | tf_op jit(solution)/shard_map/all_to_all | solution.py:883
  371.2 5.3 %convolution_convert_fusion.7.grad_mixed = bf16[512,1024]{1,0:T(8,128)(2,1)S(1)} fusion(bf16[512,2048]{1,0:T(8,128)(2,1)} %bitcast.133, bf16[2048,1024]{1,0:T(8,128)(2,1)} %bitcast.144), kind=kOutput, calls=%fused_computation.48 | convolution fusion | flops 2148007936 | bytes 7340032 | tf_op jit(solution)/shard_map/dot_general | solution.py:28
  376.6 6.7 %attend_back.1 = (bf16[512,1280]{1,0:T(8,128)(2,1)S(1)}, f32[2,128]{1,0:T(2,128)S(1)}) custom-call(f32[512,1280]{1,0:T(8,128)S(1)} %copy-done.3, f32[512,128]{1,0:T(8,128)S(1)} %get-tuple-element.108.cosine, f32[512,128]{1,0:T(8,128)S(1)} %copy-done.7, f32[1,128]{1,0:T(1,128)S(1)} %bitcast.129, f32[1,128]{1,0:T(1,128)S(1)} %bitcast.131, ...), custom_call_target="tpu_custom_call" | custom-call | bytes 50400000 | tf_op jit(solution)/shard_map/attend_back/pallas_call | solution.py:723
  383.3 5.6 %convolution_convert_fusion.5 = bf16[512,2048]{1,0:T(8,128)(2,1)S(1)} fusion(bf16[512,1280]{1,0:T(8,128)(2,1)S(1)} %get-tuple-element.56, bf16[2048,1280]{1,0:T(8,128)(2,1)} %bitcast.143), kind=kOutput, calls=%fused_computation.36 | convolution fusion | flops 2685403136 | bytes 8650752 | tf_op jit(solution)/shard_map/dot_general | solution.py:20
  388.9 40.4 %reduce_rows_4.1 = f32[128,2048]{1,0:T(8,128)S(1)} custom-call(bf16[2,2,128,2048]{3,2,1,0:T(8,128)(2,1)S(1)} %bitcast.125), custom_call_target="tpu_custom_call" | custom-call | bytes 54000000 | tf_op jit(solution)/shard_map/reduce_rows_4/pallas_call | solution.py:346
  429.4 0.3 fusion.36
  429.8 2.4 convolution_convert_fusion.2
  432.2 3.2 convolution_convert_fusion
  435.4 74.7 %scatter_weights.1 = (f32[32,2048]{1,0:T(8,128)S(1)}, f32[32,256]{1,0:T(8,128)S(1)}, f32[32,256]{1,0:T(8,128)S(1)}, f32[32,2048]{1,0:T(8,128)S(1)}, f32[40,128]{...) custom-call(bf16[4,2,4,2,32,1280]{5,4,3,2,1,0:T(8,128)(2,1)S(1)} %bitcast.123, ...), custom_call_target="tpu_custom_call" | custom-call | bytes 288000000 | tf_op jit(solution)/shard_map/scatter_weights/pallas_call | solution.py:572
  510.2 0.6 slice_bitcast_fusion.2
  510.7 0.6 slice_bitcast_fusion
  511.3 1.1 bitcast_convert_fusion
  512.4 1.4 fusion.33
  513.8 4.1 fusion.24
  518.0 0.7 copy.75
  518.7 0.6 copy.76
  519.3 0.6 copy.77
  519.9 0.7 copy.78
  (115 shorter events, 2.7 us)
Async XLA Ops:
  0.6 233.2 %copy-start = (bf16[1,2048,768]{2,1,0:T(8,128)(2,1)S(1)}, bf16[1,2048,768]{2,1,0:T(8,128)(2,1)}, u32[]{:S(2)}) copy-start(bf16[1,2048,768]{2,1,0:T(8,128)(2,1)} %param.28) | copy-start | bytes 9437188
  81.0 73.2 %all-to-all-start = ((bf16[128,8,2176]{2,1,0:T(8,128)(2,1)}), bf16[128,8,2176]{2,1,0:T(8,128)(2,1)}, u32[]{:S(2)}, u32[]{:S(2)}) async-start(bf16[128,8,2176]{2,1,0:T(8,128)(2,1)} %fusion), calls=%async_computation | async-start | bytes 8912896 | tf_op jit(solution)/shard_map/all_to_all | solution.py:806
  92.9 6.4 %copy-start.6 = (f32[512,128]{1,0:T(8,128)}, f32[512,128]{1,0:T(8,128)S(1)}, u32[]{:S(2)}) copy-start(f32[512,128]{1,0:T(8,128)S(1)} %get-tuple-element.109.signed) | copy-start | bytes 786436
  93.1 6.2 %copy-start.14 = (f32[128]{0:T(128)S(1)}, f32[128]{0:T(128)}, u32[]{:S(2)}) copy-start(f32[128]{0:T(128)} %param.24) | copy-start | bytes 1540
  93.2 6.2 %copy-start.15 = (f32[128]{0:T(128)S(1)}, f32[128]{0:T(128)}, u32[]{:S(2)}) copy-start(f32[128]{0:T(128)} %param.25) | copy-start | bytes 1540
  93.2 16.0 %copy-start.31 = (bf16[4,2,4,2,32,1024]{5,4,3,2,1,0:T(8,128)(2,1)S(1)}, bf16[4,2,4,2,32,1024]{5,4,3,2,1,0:T(8,128)(2,1)}, u32[]{:S(2)}) copy-start(bf16[4,2,4,2,32,1024]{5,4,3,2,1,0:T(8,128)(2,1)} %get-tuple-element.46) | copy-start | bytes 12582916
  99.3 12.2 %copy-start.2 = (f32[512,1280]{1,0:T(8,128)}, f32[512,1280]{1,0:T(8,128)S(1)}, u32[]{:S(2)}) copy-start(f32[512,1280]{1,0:T(8,128)S(1)} %fusion.59.raw) | copy-start | bytes 7864324
  107.5 1.0 copy-start.8
  108.5 0.7 copy-start.10
  109.1 2.4 copy-start.4
  109.1 2.4 copy-start.16
  111.6 40.4 %copy-start.20 = (bf16[128,2048]{1,0:T(8,128)(2,1)S(1)}, bf16[128,2048]{1,0:T(8,128)(2,1)}, u32[]{:S(2)}) copy-start(bf16[128,2048]{1,0:T(8,128)(2,1)} %param.16) | copy-start | bytes 1572868
  111.6 41.6 %copy-start.28 = (f32[2048]{0:T(1024)S(1)}, f32[2048]{0:T(1024)}, u32[]{:S(2)}) copy-start(f32[2048]{0:T(1024)} %param.26) | copy-start | bytes 24580
  152.2 1.0 copy-start.18
  158.5 65.7 %all-to-all-start.1 = ((bf16[128,8,2048]{2,1,0:T(8,128)(2,1)}), bf16[128,8,2048]{2,1,0:T(8,128)(2,1)}, u32[]{:S(2)}, u32[]{:S(2)}) async-start(bf16[128,8,2048]{2,1,0:T(8,128)(2,1)} %convert_bitcast_fusion), calls=%async_computation.1 | async-start | bytes 8388608 | tf_op jit(solution)/shard_map/all_to_all | solution.py:824
  224.1 4.2 copy-start.32
  228.4 5.5 %copy-start.36 = (f32[1024,768]{0,1:T(8,128)S(1)}, f32[1024,768]{0,1:T(8,128)}, u32[]{:S(2)}) copy-start(f32[1024,768]{0,1:T(8,128)} %fusion.13) | copy-start | bytes 9437188
  247.8 5.0 copy-start.33
  247.8 5.0 copy-start.38
  252.8 3.8 copy-start.26
  252.8 3.8 copy-start.27
  259.1 5.7 %copy-start.22 = (bf16[128,2048]{1,0:T(8,128)(2,1)S(1)}, bf16[128,2048]{1,0:T(8,128)(2,1)}, u32[]{:S(2)}) copy-start(bf16[128,2048]{1,0:T(8,128)(2,1)} %multiply_convert_fusion.3) | copy-start | bytes 1572868
  259.1 5.7 %copy-start.23 = (bf16[2048,128]{1,0:T(8,128)(2,1)S(1)}, bf16[2048,128]{1,0:T(8,128)(2,1)}, u32[]{:S(2)}) copy-start(bf16[2048,128]{1,0:T(8,128)(2,1)} %param.27) | copy-start | bytes 1572868
  259.1 66.0 %all-to-all-start.2 = ((bf16[128,8,2304]{2,1,0:T(8,128)(2,1)}), bf16[128,8,2304]{2,1,0:T(8,128)(2,1)}, u32[]{:S(2)}, u32[]{:S(2)}) async-start(bf16[128,8,2304]{2,1,0:T(8,128)(2,1)} %maximum_bitcast_fusion), calls=%async_computation.2 | async-start | bytes 9437184 | tf_op jit(solution)/shard_map/all_to_all | solution.py:858
  265.2 8.1 %copy-start.37 = (bf16[1024,768]{0,1:T(8,128)(2,1)S(1)}, bf16[1024,768]{0,1:T(8,128)(2,1)}, u32[]{:S(2)}) copy-start(bf16[1024,768]{0,1:T(8,128)(2,1)} %get-tuple-element.85) | copy-start | bytes 4718596
  273.3 7.7 %copy-start.35 = (bf16[1024,768]{0,1:T(8,128)(2,1)S(1)}, bf16[1024,768]{0,1:T(8,128)(2,1)}, u32[]{:S(2)}) copy-start(bf16[1024,768]{0,1:T(8,128)(2,1)} %get-tuple-element.82) | copy-start | bytes 4718596
  281.0 8.6 %copy-start.39 = (bf16[1024,768]{0,1:T(8,128)(2,1)S(1)}, bf16[1024,768]{0,1:T(8,128)(2,1)}, u32[]{:S(2)}) copy-start(bf16[1024,768]{0,1:T(8,128)(2,1)} %get-tuple-element.84) | copy-start | bytes 4718596
  325.1 3.7 copy-start.19
  328.7 10.4 %copy-start.30 = (f32[128]{0:T(128)S(1)}, f32[128]{0:T(128)}, u32[]{:S(2)}) copy-start(f32[128]{0:T(128)} %get-tuple-element.99) | copy-start | bytes 1540
  332.4 28.4 %all-to-all-start.3 = ((bf16[128,16,128]{2,1,0:T(8,128)(2,1)}), bf16[128,16,128]{2,1,0:T(8,128)(2,1)S(1)}, u32[]{:S(2)}, u32[]{:S(2)}) async-start(bf16[128,16,128]{2,1,0:T(8,128)(2,1)} %bitcast.20), calls=%async_computation.3 | async-start | bytes 1048576 | tf_op jit(solution)/shard_map/all_to_all | solution.py:881
  361.0 152.8 %all-to-all-start.4 = ((bf16[128,8,2048]{2,1,0:T(8,128)(2,1)}), bf16[128,8,2048]{2,1,0:T(8,128)(2,1)}, u32[]{:S(2)}, u32[]{:S(2)}) async-start(bf16[128,8,2048]{2,1,0:T(8,128)(2,1)} %bitcast.132), calls=%async_computation.4 | async-start | bytes 8388608 | tf_op jit(solution)/shard_map/all_to_all | solution.py:883
  371.1 5.4 %copy-start.3 = (f32[512,1280]{1,0:T(8,128)S(1)}, f32[512,1280]{1,0:T(8,128)}, u32[]{:S(2)}) copy-start(f32[512,1280]{1,0:T(8,128)} %copy-done.2) | copy-start | bytes 7864324
  371.2 5.4 %copy-start.5 = (f32[2,8,256,256]{3,2,1,0:T(8,128)S(1)}, f32[2,8,256,256]{3,2,1,0:T(8,128)}, u32[]{:S(2)}) copy-start(f32[2,8,256,256]{3,2,1,0:T(8,128)} %copy-done.4) | copy-start | bytes 12582916
  371.2 5.4 %copy-start.7 = (f32[512,128]{1,0:T(8,128)S(1)}, f32[512,128]{1,0:T(8,128)}, u32[]{:S(2)}) copy-start(f32[512,128]{1,0:T(8,128)} %copy-done.6) | copy-start | bytes 786436
  371.2 5.4 %copy-start.9 = (bf16[512,1024]{1,0:T(8,128)(2,1)S(1)}, bf16[512,1024]{1,0:T(8,128)(2,1)}, u32[]{:S(2)}) copy-start(bf16[512,1024]{1,0:T(8,128)(2,1)} %copy-done.8) | copy-start | bytes 3145732
  371.2 5.4 %copy-start.11 = (bf16[512,256]{1,0:T(8,128)(2,1)S(1)}, bf16[512,256]{1,0:T(8,128)(2,1)}, u32[]{:S(2)}) copy-start(bf16[512,256]{1,0:T(8,128)(2,1)} %copy-done.10) | copy-start | bytes 786436
  383.3 46.1 %copy-start.29 = (f32[2048]{0:T(1024)S(1)}, f32[2048]{0:T(1024)}, u32[]{:S(2)}) copy-start(f32[2048]{0:T(1024)} %param.19) | copy-start | bytes 24580
  388.9 40.5 %copy-start.21 = (bf16[128,2048]{1,0:T(8,128)(2,1)S(1)}, bf16[128,2048]{1,0:T(8,128)(2,1)}, u32[]{:S(2)}) copy-start(bf16[128,2048]{1,0:T(8,128)(2,1)} %param.16) | copy-start | bytes 1572868
  388.9 40.9 %copy-start.17 = (bf16[512,1024]{1,0:T(8,128)(2,1)S(1)}, bf16[512,1024]{1,0:T(8,128)(2,1)}, u32[]{:S(2)}) copy-start(bf16[512,1024]{1,0:T(8,128)(2,1)} %copy-done.16) | copy-start | bytes 3145732
  388.9 40.8 %copy-start.25 = (bf16[2,2,128,2048]{3,2,1,0:T(8,128)(2,1)S(1)}, bf16[2,2,128,2048]{3,2,1,0:T(8,128)(2,1)}, u32[]{:S(2)}) copy-start(bf16[2,2,128,2048]{3,2,1,0:T(8,128)(2,1)} %share_rows_3.1) | copy-start | bytes 6291460
  429.8 2.4 copy-start.34
  435.4 77.0 %copy-start.24 = (f32[128,2048]{1,0:T(8,128)S(1)}, f32[128,2048]{1,0:T(8,128)}, u32[]{:S(2)}) copy-start(f32[128,2048]{1,0:T(8,128)} %get-tuple-element.75) | copy-start | bytes 3145732
  510.1 2.3 copy-start.12
  512.4 8.2 %copy-start.1 = (bf16[1,2048,768]{2,1,0:T(8,128)(2,1)S(1)}, bf16[1,2048,768]{2,1,0:T(8,128)(2,1)}, u32[]{:S(2)}) copy-start(bf16[1,2048,768]{2,1,0:T(8,128)(2,1)} %param.28) | copy-start | bytes 9437188
  513.8 4.2 copy-start.13

commit v5 on v4

--- a/solution.py
+++ b/solution.py
@@ -88,11 +88,15 @@
         self.z = lax.rem(dp // NC, NZ)
         self.yh = lax.rem(dp // (NC * NZ), NYH)
         self.x = dp // (NC * NZ * NYH)
+        self.y = self.yh * 2 + self.t
 
     def device(self, x=None, yh=None, z=None, c=None, t=None):
         pick = lambda given, own: own if given is None else given
         x, yh, z, c = pick(x, self.x), pick(yh, self.yh), pick(z, self.z), pick(c, self.c)
         return (((x * NYH + yh) * NZ + z) * NC + c, pick(t, self.t))
+
+    def at_y(self, y):
+        return self.device(yh=y // 2, t=lax.rem(y, 2))
 
 
 def after(i):
@@ -147,97 +151,85 @@
 
 def gather_kernel(q, k, v, o, tok, doc, wa, wb, toks, docs, send, recv, local):
     me = Place()
-    x, yh, z, c, t = me.x, me.yh, me.z, me.c, me.t
+    x, yh, z, c, p = me.x, me.yh, me.z, me.c, me.y
     sibling = me.device(c=1 - c)
     pair = me.device(yh=1 - yh)
-    partner = me.device(t=1 - t)
     ring_x = (me.device(x=after(x)), me.device(x=before(x)))
     ring_z = (me.device(z=after(z)), me.device(z=before(z)))
-    greet([sibling, pair, partner, *ring_x, *ring_z])
+    ring_y = (me.at_y(after(p)), me.at_y(before(p)))
+    greet([sibling, pair, *ring_x, *ring_z, *ring_y])
     go = Copies(send, recv, local)
 
     shards, start = [], 0
     for ref, w in ((q, wa), (k, wa), (v, wa), (o, wb)):
-        cols = ref.shape[1] // NC
+        cols = ref.shape[1] // NYH
         to = w.at[x, yh, z, c, :, pl.ds(0 if w is wb else start, cols)]
         shards.append((ref, cols, to))
         start += cols
 
-    def part(ref, cols, core):
-        return ref.at[:, pl.ds(pl.multiple_of(core * cols, cols), cols)]
-
-    cores = [go.put(part(ref, cols, 1 - c), to, sibling) for ref, cols, to in shards]
-    kept = [go.keep(part(ref, cols, c), to) for ref, cols, to in shards]
+    def part(ref, cols, head):
+        return ref.at[:, pl.ds(pl.multiple_of(head * cols, cols), cols)]
+
+    pairs = [go.put(part(ref, cols, 1 - yh), to, pair) for ref, cols, to in shards]
+    kept = [go.keep(part(ref, cols, yh), to) for ref, cols, to in shards]
     for copy in kept:
         copy.wait()
-    for copy in cores:
-        copy.wait_recv()
-    pairs = [go.put(w.at[x, yh, z], w.at[x, yh, z], pair) for w in (wa, wb)]
-
-    ways = (
-        (wa, x, z, ring_x, ring_z, lambda w, i, j, y: w.at[i, y, j], lambda w, j, y: w.at[:, y, j]),
-        (wb, z, x, ring_z, ring_x, lambda w, i, j, y: w.at[j, y, i], lambda w, j, y: w.at[j, y]),
-    )
-
-    def first(y):
-        out = []
-        for w, i, j, one, two, unit, slab in ways:
-            own = unit(w, i, j, y)
-            out.append((go.put(own, own, one[0]), go.put(own, own, one[1])))
-        return out
-
-    def second(y, firsts):
-        out = []
-        for (w, i, j, one, two, unit, slab), (up, down) in zip(ways, firsts):
-            up.wait_recv()
-            low = unit(w, before(i), j, y).at[0]
-            a = go.put(low, low, one[0])
-            down.wait_recv()
-            high = unit(w, after(i), j, y).at[1]
-            out.append((a, go.put(high, high, one[1])))
-        return out
-
-    def third(y, seconds):
-        out = []
-        for (w, i, j, one, two, unit, slab), (up, down) in zip(ways, seconds):
-            up.wait_recv()
-            down.wait_recv()
-            own = slab(w, j, y)
-            out.append((go.put(own, own, two[0]), go.put(own, own, two[1])))
-        return out
-
-    def fourth(y, thirds):
-        out = []
-        for (w, i, j, one, two, unit, slab), (up, down) in zip(ways, thirds):
-            up.wait_recv()
-            low = slab(w, before(j), y).at[:, 0]
-            a = go.put(low, low, two[0])
-            down.wait_recv()
-            high = slab(w, after(j), y).at[:, 1]
-            out.append((a, go.put(high, high, two[1])))
-        return out
-
-    near = first(yh)
-    to_partner = go.put(tok, toks.at[c, t], partner)
-    rest = [go.keep(tok, toks.at[c, t]), go.keep(doc, docs.at[c])]
-    tail = [go.put(tok, toks.at[c, t], sibling), go.put(doc, docs.at[c], sibling)]
-    near = second(yh, near)
-    near = third(yh, near)
     for copy in pairs:
         copy.wait_recv()
-    far = first(1 - yh)
-    far = second(1 - yh, far)
-    far = third(1 - yh, far)
-    near = fourth(yh, near)
-    to_partner.wait_recv()
-    other = toks.at[c, 1 - t]
-    tail.append(go.put(other, other, sibling))
-    far = fourth(1 - yh, far)
-    for up, down in near + far:
-        up.wait_recv()
-        down.wait_recv()
-    for copy in tail:
-        copy.wait_recv()
+
+    ways = (
+        (x, z, ring_x, ring_z, lambda i, j: wa.at[i, :, j, c], lambda j: wa.at[:, :, j, c]),
+        (z, x, ring_z, ring_x, lambda i, j: wb.at[j, :, i, c], lambda j: wb.at[j, :, :, c]),
+    )
+
+    def both(ref, peers):
+        return [go.put(ref, ref, peer) for peer in peers]
+
+    def relay(low, high, copies, peers):
+        copies[0].wait_recv()
+        up = go.put(low.at[0], low.at[0], peers[0])
+        copies[1].wait_recv()
+        return [up, go.put(high.at[1], high.at[1], peers[1])]
+
+    def arrived(copies):
+        for copy in copies:
+            copy.wait_recv()
+
+    near = [both(unit(i, j), one) for i, j, one, two, unit, slab in ways]
+    own = [both(unit(i, j), two) for i, j, one, two, unit, slab in ways]
+    rows = [go.put(tok, toks.at[p], peer) for peer in ring_y]
+    rest = [go.keep(tok, toks.at[p]), go.keep(doc, docs.at[yh])]
+    tail = [go.put(doc, docs.at[yh], pair)]
+    far = [
+        relay(unit(before(i), j), unit(after(i), j), copies, one)
+        for (i, j, one, two, unit, slab), copies in zip(ways, near)
+    ]
+    low = [both(unit(before(i), j), two) for i, j, one, two, unit, slab in ways]
+    high = [both(unit(after(i), j), two) for i, j, one, two, unit, slab in ways]
+    last = []
+    for (i, j, one, two, unit, slab), copies in zip(ways, far):
+        arrived(copies)
+        last.append(both(unit(across(i), j), two))
+        tail.append(go.put(slab(j), slab(j), sibling))
+    half = tok.shape[0] // 2
+    rows[0].wait_recv()
+    piece = toks.at[before(p), pl.ds(0, half)]
+    tail.append(go.put(piece, piece, ring_y[0]))
+    rows[1].wait_recv()
+    piece = toks.at[after(p), pl.ds(half, half)]
+    tail.append(go.put(piece, piece, ring_y[1]))
+    ends = [[], []]
+    for place, copies in ((lambda i: i, own), (before, low), (after, high), (across, last)):
+        for n, (i, j, one, two, unit, slab) in enumerate(ways):
+            u = place(i)
+            ends[n] += relay(unit(u, before(j)), unit(u, after(j)), copies[n], two)
+    for i, j, one, two, unit, slab in ways:
+        tail.append(go.put(slab(before(j)), slab(before(j)), sibling))
+        tail.append(go.put(slab(after(j)), slab(after(j)), sibling))
+    for (i, j, one, two, unit, slab), copies in zip(ways, ends):
+        arrived(copies)
+        tail.append(go.put(slab(across(j)), slab(across(j)), sibling))
+    arrived(tail)
     for copy in rest:
         copy.wait()
     go.finish()
@@ -245,8 +237,8 @@
 
 def gather(query, key, value, out, tokens, docs):
     rows = query.shape[0]
-    width_a = (query.shape[1] + key.shape[1] + value.shape[1]) // NC
-    width_b = out.shape[1] // NC
+    width_a = (query.shape[1] + key.shape[1] + value.shape[1]) // NYH
+    width_b = out.shape[1] // NYH
     lead = (NX, NYH, NZ, NC, rows)
     wa, wb, toks, docs = pl.pallas_call(
         gather_kernel,
@@ -255,14 +247,14 @@
         out_shape=(
             jax.ShapeDtypeStruct((*lead, width_a), BF16),
             jax.ShapeDtypeStruct((*lead, width_b), BF16),
-            jax.ShapeDtypeStruct((NC, 2, *tokens.shape), BF16),
-            jax.ShapeDtypeStruct((NC, *docs.shape), docs.dtype),
+            jax.ShapeDtypeStruct((RING, *tokens.shape), BF16),
+            jax.ShapeDtypeStruct((NYH, *docs.shape), docs.dtype),
         ),
         in_specs=[ANY] * 6,
         out_specs=(ANY,) * 4,
         scratch_shapes=[
-            pltpu.SemaphoreType.DMA((42,)),
-            pltpu.SemaphoreType.DMA((42,)),
+            pltpu.SemaphoreType.DMA((57,)),
+            pltpu.SemaphoreType.DMA((57,)),
             pltpu.SemaphoreType.DMA((6,)),
         ],
         compiler_params=pltpu.CompilerParams(collective_id=1, has_side_effects=True),
@@ -271,27 +263,26 @@
     return (
         wa.reshape(depth, width_a),
         wb.reshape(depth, width_b),
-        toks.reshape(NC * 2 * tokens.shape[0], tokens.shape[1]),
+        toks.reshape(RING * tokens.shape[0], tokens.shape[1]),
         docs,
     )
 
 
 def share_kernel(tok, toks, send, recv, local):
     me = Place()
-    c, t = me.c, me.t
-    sibling, partner = me.device(c=1 - c), me.device(t=1 - t)
-    greet([sibling, partner])
+    p = me.y
+    ring = (me.at_y(after(p)), me.at_y(before(p)))
+    greet(ring)
     go = Copies(send, recv, local)
     half = tok.shape[0] // 2
-    parts = [pl.ds(i * half, half) for i in range(2)]
-    over = [go.put(tok.at[p], toks.at[c, t, p], partner) for p in parts]
-    near = [go.put(tok, toks.at[c, t], sibling)]
-    kept = go.keep(tok, toks.at[c, t])
-    for copy, p in zip(over, parts):
-        copy.wait_recv()
-        other = toks.at[c, 1 - t, p]
-        near.append(go.put(other, other, sibling))
-    for copy in near:
+    direct = [go.put(tok, toks.at[p], peer) for peer in ring]
+    kept = go.keep(tok, toks.at[p])
+    relays = []
+    for h, owner in enumerate((before(p), after(p))):
+        direct[h].wait_recv()
+        piece = toks.at[owner, pl.ds(h * half, half)]
+        relays.append(go.put(piece, piece, ring[h]))
+    for copy in relays:
         copy.wait_recv()
     kept.wait()
     go.finish()
@@ -302,47 +293,52 @@
         share_kernel,
         name=f"share_rows_{ident}",
         cost_estimate=cost(13),
-        out_shape=jax.ShapeDtypeStruct((NC, 2, *tokens.shape), tokens.dtype),
+        out_shape=jax.ShapeDtypeStruct((RING, *tokens.shape), tokens.dtype),
         in_specs=[ANY],
         out_specs=ANY,
         scratch_shapes=[
-            pltpu.SemaphoreType.DMA((5,)),
-            pltpu.SemaphoreType.DMA((5,)),
+            pltpu.SemaphoreType.DMA((4,)),
+            pltpu.SemaphoreType.DMA((4,)),
             pltpu.SemaphoreType.DMA((1,)),
         ],
         compiler_params=pltpu.CompilerParams(collective_id=ident, has_side_effects=True),
     )(tokens)
-    return toks.reshape(NC * 2 * tokens.shape[0], tokens.shape[1])
-
-
-def reduce_kernel(part, out, near, own, sums, far, send, recv, local):
+    return toks.reshape(RING * tokens.shape[0], tokens.shape[1])
+
+
+def reduce_kernel(part, out, held, own, got, send, recv, local):
     me = Place()
-    c, t = me.c, me.t
-    sibling, partner = me.device(c=1 - c), me.device(t=1 - t)
-    greet([sibling, partner])
+    p = me.y
+    ring = (me.at_y(after(p)), me.at_y(before(p)))
+    greet(ring)
     go = Copies(send, recv, local)
     half = out.shape[0] // 2
-    parts = [pl.ds(i * half, half) for i in range(2)]
-    away = [go.put(part.at[1 - c, 1 - t, p], near.at[0, p], sibling) for p in parts]
-    home = go.put(part.at[1 - c, t], near.at[1], sibling)
-    kept = [go.keep(part.at[c, 1 - t], own.at[0]), go.keep(part.at[c, t], own.at[1])]
-    kept[0].wait()
-    over = []
-    for copy, p in zip(away, parts):
+    halves = [pl.ds(h * half, half) for h in range(2)]
+    near = (after(p), before(p))
+    cross = [go.put(part.at[across(p), halves[h]], got.at[h], ring[h]) for h in range(2)]
+    kept = [go.keep(part.at[near[h], halves[h]], held.at[h]) for h in range(2)]
+    straight = [go.put(part.at[near[h], halves[1 - h]], got.at[2 + h], ring[h]) for h in range(2)]
+    mine = go.keep(part.at[p], own)
+    sums = []
+    for h in range(2):
+        kept[h].wait()
+        cross[h].wait_recv()
+        held[h] = (held[h].astype(F32) + got[h].astype(F32)).astype(BF16)
+        sums.append(go.put(held.at[h], got.at[4 + h], ring[h]))
+    mine.wait()
+    for copy in straight:
         copy.wait_recv()
-        sums[p] = (own[0, p].astype(F32) + near[0, p].astype(F32)).astype(BF16)
-        over.append(go.put(sums.at[p], far.at[p], partner))
-    kept[1].wait()
-    home.wait_recv()
-    out[...] = own[1].astype(F32) + near[1].astype(F32)
-    for copy, p in zip(over, parts):
-        copy.wait_recv()
-        out[p] += far[p].astype(F32)
+    for h in range(2):
+        sums[h].wait_recv()
+        out[halves[h]] = (
+            own[halves[h]].astype(F32) + got[4 + h].astype(F32) + got[3 - h].astype(F32)
+        )
     go.finish()
 
 
 def reduce(part, ident):
-    rows, width = part.shape[0] // (NC * 2), part.shape[1]
+    rows, width = part.shape[0] // RING, part.shape[1]
+    half = rows // 2
     return pl.pallas_call(
         reduce_kernel,
         name=f"reduce_rows_{ident}",
@@ -351,36 +347,34 @@
         in_specs=[ANY],
         out_specs=VMEM,
         scratch_shapes=[
-            pltpu.VMEM((2, rows, width), BF16),
-            pltpu.VMEM((2, rows, width), BF16),
+            pltpu.VMEM((2, half, width), BF16),
             pltpu.VMEM((rows, width), BF16),
-            pltpu.VMEM((rows, width), BF16),
-            pltpu.SemaphoreType.DMA((5,)),
-            pltpu.SemaphoreType.DMA((5,)),
-            pltpu.SemaphoreType.DMA((2,)),
+            pltpu.VMEM((6, half, width), BF16),
+            pltpu.SemaphoreType.DMA((6,)),
+            pltpu.SemaphoreType.DMA((6,)),
+            pltpu.SemaphoreType.DMA((3,)),
         ],
         compiler_params=pltpu.CompilerParams(
             collective_id=ident, has_side_effects=True, vmem_limit_bytes=24 << 20
         ),
-    )(part.reshape(NC, 2, rows, width))
+    )(part.reshape(RING, rows, width))
 
 
 def scatter_kernel(
-    ga, gb, gains, piece, oq, ok, ov, oo, og, op, ka, kb, ra, rb, qa, qb, sa, sb, ya, yb, ma, mb, ta, tb, ca, cb,
+    ga, gb, gains, piece, oq, ok, ov, oo, og, op, ka, kb, da, db, ra, rb, qa, qb, sa, sb, ta, tb, ua, ub, ma, mb,
     ring_gains, sum_gains, pair_gains, send, recv, local
 ):
     me = Place()
-    x, yh, z, c = me.x, me.yh, me.z, me.c
+    x, yh, z, c, t = me.x, me.yh, me.z, me.c, me.t
     sibling = me.device(c=1 - c)
     pair = me.device(yh=1 - yh)
-    partner = me.device(t=1 - me.t)
+    partner = me.device(t=1 - t)
     ring_x = (me.device(x=after(x)), me.device(x=before(x)))
     ring_z = (me.device(z=after(z)), me.device(z=before(z)))
     round_x = (*ring_x, me.device(x=across(x)))
     round_z = (*ring_z, me.device(z=across(z)))
     greet([sibling, pair, partner, *round_x, *round_z])
     go = Copies(send, recv, local)
-    chunks = (1 - yh, yh)
 
     def around(n, term, own, peers):
         ring_gains[n, own] = term
@@ -401,100 +395,10 @@
 
 
     ways = (
-        (lambda i, y, h: ga.at[i, y, :, h], x, z, ring_x, ring_z, ka, ra, qa, sa),
-        (lambda i, y, h: gb.at[:, y, i, h], z, x, ring_z, ring_x, kb, rb, qb, sb),
-    )
-
-    def cross(n):
-        out = []
-        for slab, i, j, one, two, k, r, q, s in ways:
-            far = across(i)
-            out.append(
-                [go.put(slab(far, chunks[n], h), r.at[n, h], one[h]) for h in range(2)]
-            )
-        return out
-
-    def straight(n):
-        out = []
-        for slab, i, j, one, two, k, r, q, s in ways:
-            near = (after(i), before(i))
-            out.append(
-                [go.put(slab(near[h], chunks[n], 1 - h), r.at[n, 2 + h], one[h]) for h in range(2)]
-            )
-        return out
-
-    def hold(n):
-        out = []
-        for slab, i, j, one, two, k, r, q, s in ways:
-            parts = ((after(i), 0), (before(i), 1), (i, 0), (i, 1))
-            out.append(
-                [go.keep(slab(p, chunks[n], h), k.at[n, m]) for m, (p, h) in enumerate(parts)]
-            )
-        return out
-
-    def add(n, crossed, held):
-        out = []
-        for (slab, i, j, one, two, k, r, q, s), copies, own in zip(ways, crossed, held):
-            both = []
-            for h in range(2):
-                own[h].wait()
-                copies[h].wait_recv()
-
-                def step(m, _, k=k, r=r, h=h):
-                    k[n, h, m] = (k[n, h, m].astype(F32) + r[n, h, m].astype(F32)).astype(BF16)
-                    return 0
-
-                lax.fori_loop(0, k.shape[2], step, 0)
-                both.append(go.put(k.at[n, h], r.at[n, 4 + h], one[h]))
-            out.append(both)
-        return out
-
-    def close(n, straights, summed, held):
-        out = []
-        for (slab, i, j, one, two, k, r, q, s), a, b, own in zip(ways, straights, summed, held):
-            for h in range(2):
-                own[2 + h].wait()
-                a[h].wait_recv()
-                b[h].wait_recv()
-
-            def step(m, _, k=k, r=r):
-                for h in range(2):
-                    k[n, 2 + h, m] = (
-                        k[n, 2 + h, m].astype(F32)
-                        + r[n, 4 + h, m].astype(F32)
-                        + r[n, 3 - h, m].astype(F32)
-                    ).astype(BF16)
-                return 0
-
-            lax.fori_loop(0, k.shape[2], step, 0)
-            near = (after(j), before(j))
-            over = [go.put(k.at[n, 2 + h, across(j)], q.at[n, h], two[h]) for h in range(2)]
-            direct = [go.put(k.at[n, 3 - h, near[h]], q.at[n, 2 + h], two[h]) for h in range(2)]
-            out.append((over, direct))
-        return out
-
-    def add_second(n, closed):
-        out = []
-        for (slab, i, j, one, two, k, r, q, s), (over, direct) in zip(ways, closed):
-            near = (after(j), before(j))
-            both = []
-            for h in range(2):
-                over[h].wait_recv()
-                s[n, h] = (k[n, 2 + h, near[h]].astype(F32) + q[n, h].astype(F32)).astype(BF16)
-                both.append(go.put(s.at[n, h], q.at[n, 4 + h], two[h]))
-            out.append(both + direct)
-        return out
-
-    def total(n, added, w):
-        slab, i, j, one, two, k, r, q, s = ways[w]
-        for copy in added[w]:
-            copy.wait_recv()
-        return [
-            k[n, 2 + h, j].astype(F32) + q[n, 4 + h].astype(F32) + q[n, 3 - h].astype(F32)
-            for h in range(2)
-        ]
-
-    t = me.t
+        (lambda i, h, n: ga.at[i, h, :, n], x, z, ring_x, ring_z, ka, da, ra, qa, sa, ta),
+        (lambda i, h, n: gb.at[:, h, i, n], z, x, ring_z, ring_x, kb, db, rb, qb, sb, tb),
+    )
+    places = (across, after, before, lambda i: i)
 
     def spread(ref, peers):
         return [go.put(ref, ref, peer) for peer in peers]
@@ -502,62 +406,110 @@
     def arrived(copies):
         for copy in copies:
             copy.wait_recv()
+
+    given, held = [[], []], [[], []]
+    for n, place in enumerate(places):
+        for w, (slab, i, j, one, two, k, d, r, q, s, u) in enumerate(ways):
+            given[w].append([go.put(slab(place(i), h, 1 - c), d.at[n, h], sibling) for h in range(2)])
+            held[w].append([go.keep(slab(place(i), h, c), k.at[n, h]) for h in range(2)])
+
+    def ready(w, n, h):
+        given[w][n][h].wait_recv()
+        held[w][n][h].wait()
+
+    def total(w, n, h, extra):
+        slab, i, j, one, two, k, d, r, q, s, u = ways[w]
+
+        def step(m, _):
+            value = k[n, h, m].astype(F32) + d[n, h, m].astype(F32)
+            for e in extra:
+                value += r[e, m].astype(F32)
+            k[n, h, m] = value.astype(BF16)
+            return 0
+
+        lax.fori_loop(0, k.shape[2], step, 0)
 
     terms = around(0, gains[...], x, round_x)
     mine = op.at[x, yh, z, c, t]
     held_piece = go.keep(piece, mine)
     pieces = [go.put(piece, mine, sibling)]
-    cross_0, straight_0 = cross(0), straight(0)
-    held_0, held_1 = hold(0), hold(1)
+    cross, straight, sums = [[], []], [[], []], [[], []]
+    for w, (slab, i, j, one, two, k, d, r, q, s, u) in enumerate(ways):
+        for h in range(2):
+            ready(w, 0, h)
+            total(w, 0, h, ())
+            cross[w].append(go.put(k.at[0, h], r.at[h], one[h]))
+    for w, (slab, i, j, one, two, k, d, r, q, s, u) in enumerate(ways):
+        for h in range(2):
+            ready(w, 1 + h, 1 - h)
+            total(w, 1 + h, 1 - h, ())
+            straight[w].append(go.put(k.at[1 + h, 1 - h], r.at[2 + h], one[h]))
     terms = around(1, ring_sum(0, terms), z, round_z)
     arrived(pieces)
     held_piece.wait()
     pieces = spread(op.at[x, yh, z, :, t], [partner])
-    cross_1 = cross(1)
-    sums_0 = add(0, cross_0, held_0)
-    straight_1 = straight(1)
+    for w, (slab, i, j, one, two, k, d, r, q, s, u) in enumerate(ways):
+        for h in range(2):
+            ready(w, 1 + h, h)
+            cross[w][h].wait_recv()
+            total(w, 1 + h, h, (h,))
+            sums[w].append(go.put(k.at[1 + h, h], r.at[4 + h], one[h]))
     arrived(pieces)
     pieces = spread(op.at[x, yh, z], [pair])
-    sums_1 = add(1, cross_1, held_1)
+    terms = swap(0, ring_sum(1, terms), pair)
+    for w in range(2):
+        for h in range(2):
+            ready(w, 3, h)
+            straight[w][1 - h].wait_recv()
+            total(w, 3, h, (3 - h,))
     arrived(pieces)
     pieces = spread(op.at[x, :, z], round_x)
-    terms = swap(0, ring_sum(1, terms), pair)
-    closed_0 = close(0, straight_0, sums_0, held_0)
     terms = swap(1, swapped(0, terms), partner)
+    over, direct, final = [[], []], [[], []], [[], []]
+    for w, (slab, i, j, one, two, k, d, r, q, s, u) in enumerate(ways):
+        near = (after(j), before(j))
+        for h in range(2):
+            sums[w][h].wait_recv()
+
+            def step(m, _, k=k, r=r, h=h):
+                k[3, h, m] = (k[3, h, m].astype(F32) + r[4 + h, m].astype(F32)).astype(BF16)
+                return 0
+
+            lax.fori_loop(0, k.shape[2], step, 0)
+            over[w].append(go.put(k.at[3, h, across(j)], q.at[h], two[h]))
+        for h in range(2):
+            direct[w].append(go.put(k.at[3, 1 - h, near[h]], q.at[2 + h], two[h]))
     arrived(pieces)
     pieces = spread(op.at[:, :, z], round_z)
-    added_0 = add_second(0, closed_0)
-    ends = ((ya, ma, ta, ca), (yb, mb, tb, cb))
-    pairs = []
-    for w, (yy, m, tt, cc) in enumerate(ends):
-        for h, part in enumerate(total(0, added_0, w)):
-            yy[h] = part.astype(BF16)
-        pairs.append(go.put(yy, m, pair))
     terms = swap(2, swapped(1, terms), sibling)
-    closed_1 = close(1, straight_1, sums_1, held_1)
-    added_1 = add_second(1, closed_1)
+    for w, (slab, i, j, one, two, k, d, r, q, s, u) in enumerate(ways):
+        near = (after(j), before(j))
+        for h in range(2):
+            over[w][h].wait_recv()
+            s[h] = (k[3, h, near[h]].astype(F32) + q[h].astype(F32)).astype(BF16)
+            final[w].append(go.put(s.at[h], q.at[4 + h], two[h]))
     last = []
-    for w, (yy, m, tt, cc) in enumerate(ends):
-        parts = total(1, added_1, w)
-        pairs[w].wait_recv()
-        for h, part in enumerate(parts):
-            tt[h] = part + m[h].astype(F32)
-        last.append(go.put(tt.at[1 - c], cc, sibling))
+    for w, ((slab, i, j, one, two, k, d, r, q, s, u), v, m) in enumerate(zip(ways, (ua, ub), (ma, mb))):
+        arrived(direct[w])
+        arrived(final[w])
+        for h in range(2):
+            u[h] = k[3, h, j].astype(F32) + q[4 + h].astype(F32) + q[3 - h].astype(F32)
+        v[...] = u[1 - yh].astype(BF16)
+        last.append(go.put(v, m, pair))
     og[...] = swapped(2, terms)
+
+    def write(head, a, b):
+        start = 0
+        for out, block in ((oq, a), (ok, a), (ov, a), (oo, b)):
+            cols = out.shape[1] // NYH
+            at = 0 if block is b else start
+            out[:, pl.ds(pl.multiple_of(head * cols, cols), cols)] = block[:, at : at + cols]
+            start += cols
+
+    write(yh, ta[yh], tb[yh])
+    arrived(last)
+    write(1 - yh, ma[...].astype(F32), mb[...].astype(F32))
     arrived(pieces)
-
-    def write(core, a, b):
-        start = 0
-        for out, held in ((oq, a), (ok, a), (ov, a), (oo, b)):
-            cols = out.shape[1] // NC
-            at = 0 if held is b else start
-            out[:, pl.ds(pl.multiple_of(core * cols, cols), cols)] = held[:, at : at + cols]
-            start += cols
-
-    write(c, ta[c], tb[c])
-    for copy in last:
-        copy.wait_recv()
-    write(1 - c, ca[...], cb[...])
     go.finish()
 
 
@@ -581,19 +533,19 @@
         in_specs=[ANY, ANY, VMEM, ANY],
         out_specs=(*(VMEM,) * 5, ANY),
         scratch_shapes=[
-            *each((2, 4, RING), BF16),
-            *each((2, 6, RING), BF16),
-            *each((2, 6), BF16),
-            *each((2, 2), BF16),
-            *each((2,), BF16),
+            *each((4, 2, RING), BF16),
+            *each((4, 2, RING), BF16),
+            *each((6, RING), BF16),
+            *each((6,), BF16),
             *each((2,), BF16),
             *each((2,), F32),
-            *each((), F32),
+            *each((), BF16),
+            *each((), BF16),
             pltpu.VMEM((2, RING, *gains.shape), F32),
             pltpu.VMEM((3, *gains.shape), F32),
             pltpu.VMEM((3, *gains.shape), F32),
-            pltpu.SemaphoreType.DMA((70,)),
-            pltpu.SemaphoreType.DMA((70,)),
+            pltpu.SemaphoreType.DMA((60,)),
+            pltpu.SemaphoreType.DMA((60,)),
             pltpu.SemaphoreType.DMA((17,)),
         ],
         compiler_params=pltpu.CompilerParams(

time: 525 us -> 490 us (0.933)
  Pallas kernels: 259 us -> 228 us
    pallas_call x1, Pallas kernels: 74.7 us -> 49.2 us  [scatter(): pl.pallas_call(scatter_kernel, name='scatter_weights', cost_estimate=cost...]
    pallas_call x1, Pallas kernels: 69.5 us -> 44.6 us  [gather(): pl.pallas_call(gather_kernel, name='gather_weights', cost_estimate=cost(6...]
    pallas_call x2, Pallas kernels: 80.8 us -> 93.7 us  [reduce(): pl.pallas_call(reduce_kernel, name=f'reduce_rows_{ident}', cost_estimate=...]
    pallas_call x1, Pallas kernels: 18.8 us -> 25.6 us  [share(): pl.pallas_call(share_kernel, name=f'share_rows_{ident}', cost_estimate=co...]
  transfers between devices with their start and end apart: 5 -> 5, of which waited for: 2 -> 2; matrix products, arithmetic and copies ran while one was open for 16% -> 17% of each run, Pallas kernels for 36% -> 38%
where the time goes in v5:
time: 490 us; the launch traced here: 485 us
  Pallas kernels  228 us (47%)
  matrix products  114 us (23%)
  waiting for transfers between devices  66.3 us (14%)
  starting transfers between devices  39.1 us (8%)
  local copies, waits for them, and re-layouts  18.9 us (4%)
  other arithmetic  17.4 us (4%)
    pallas_call x2, Pallas kernels, reduce(): pl.pallas_call(reduce_kernel, name=f'reduce_rows_{ident}', cost_estimate=...  93.7 us
    pallas_call x1, Pallas kernels, scatter(): pl.pallas_call(scatter_kernel, name='scatter_weights', cost_estimate=cost...  49.2 us
    dot_general x10, matrix products, dot_nn(): lax.dot_general(a, b, (((1,), (0,)), ((), ())), preferred_element_type=F32)  47.7 us
    pallas_call x1, Pallas kernels, gather(): pl.pallas_call(gather_kernel, name='gather_weights', cost_estimate=cost(6...  44.6 us
    all_to_all x1, waiting for transfers between devices, on_device(): lax.all_to_all(sent.reshape(experts, cap, width), both, split_axis=0, con...  39.3 us
    dot_general x8, matrix products, dot_tn(): lax.dot_general(a, b, (((0,), (0,)), ((), ())), preferred_element_type=F32)  39 us
    dot_general x6, matrix products, dot_nt(): lax.dot_general(a, b, (((1,), (1,)), ((), ())), preferred_element_type=F32)  27.5 us
    all_to_all x1, waiting for transfers between devices, on_device(): lax.all_to_all(home_out.reshape(experts, cap, width + 2 * experts), both,...  27 us
  transfers between devices with their start and end apart: 5, of which 2 were waited for; matrix products, arithmetic and copies ran while one was open for 17% of the time, Pallas kernels for 38%

profile of v5, /device:TPU:1, one launch (start us, length us, event | category | flops | bytes accessed | tf_op | source)
XLA Modules:
  0.0 485.5 jit_solution(17720770559265701765)
XLA Ops:
  0.7 0.9 copy.55
  2.0 1.2 fusion.28
  3.2 0.7 convert_element_type.138
  4.0 2.0 fusion.30.tok
  6.4 0.6 broadcast_in_dim.107.doc
  7.0 44.6 %gather_weights.1 = (bf16[4,2,4,2,32,1280]{5,4,3,2,1,0:T(8,128)(2,1)}, bf16[4,2,4,2,32,1024]{5,4,3,2,1,0:T(8,128)(2,1)}, bf16[4,128,2048]{2,1,0:T(8,128)(2,1)}, f32[2,8,256]{2,1,0:T(8,128)}) custom-call(bf16[32,2048]{1,0:T(8,128)(2,1)} %q.1, bf16[32,256]{1,0:T(8,128)(2,1)} %k.1, bf16[32,256]{1,0:T(8,128)(2,1)} %v.1, bf16[32,2048]{1,0:T(8,128)(2,1)} %bitcast.135, ...), custom_call_target="tpu_custom_call" | custom-call | bytes 216000000 | tf_op jit(solution)/shard_map/gather_weights/pallas_call | solution.py:243
  51.7 4.5 fusion
  56.1 6.4 %all-to-all-start = ((bf16[128,8,2176]{2,1,0:T(8,128)(2,1)}), bf16[128,8,2176]{2,1,0:T(8,128)(2,1)}, u32[]{:S(2)}, u32[]{:S(2)}) async-start(bf16[128,8,2176]{2,1,0:T(8,128)(2,1)} %fusion), calls=%async_computation | async-start | bytes 8912896 | tf_op jit(solution)/shard_map/all_to_all | solution.py:758
  62.5 0.7 slice.30
  63.6 1.0 fusion.51
  65.1 6.1 %fusion.59.raw = f32[512,1280]{1,0:T(8,128)S(1)} fusion(bf16[512,2048]{1,0:T(8,128)(2,1)} %bitcast.146, bf16[2048,1280]{1,0:T(8,128)(2,1)} %bitcast.142), kind=kOutput, calls=%fused_computation.131 | convolution fusion | flops 2684354560 | bytes 9961472 | tf_op jit(solution)/shard_map/dot_general | solution.py:28
  71.3 8.1 %attend.1 = (bf16[512,1024]{1,0:T(8,128)(2,1)S(1)}, bf16[512,256]{1,0:T(8,128)(2,1)S(1)}, f32[2,8,256,256]{3,2,1,0:T(8,128)S(1)}, bf16[512,1024]{1,0:T(8,128)(2,1)S(1)}) custom-call(f32[512,1280]{1,0:T(8,128)S(1)} %fusion.59.raw, f32[2,256,256]{2,1,0:T(8,128)S(1)} %fusion.42.bias, f32[512,128]{1,0:T(8,128)S(1)} %get-tuple-element.108.cosine, ...), custom_call_target="tpu_custom_call" | custom-call | bytes 28800000 | tf_op jit(solution)/shard_map/attend/pallas_call | solution.py:598
  79.4 1.0 copy-done.8
  80.4 0.7 copy-done.10
  81.0 2.4 convolution_convert_fusion.4
  83.5 46.7 %reduce_rows_2.1 = f32[128,2048]{1,0:T(8,128)S(1)} custom-call(bf16[4,128,2048]{2,1,0:T(8,128)(2,1)S(1)} %bitcast.126), custom_call_target="tpu_custom_call" | custom-call | bytes 54000000 | tf_op jit(solution)/shard_map/reduce_rows_2/pallas_call | solution.py:342
  130.4 0.6 multiply_multiply_fusion.1
  131.0 0.4 copy-done.18
  131.4 0.9 multiply_convert_fusion.3
  132.3 4.4 convert_bitcast_fusion
  136.7 10.9 %all-to-all-start.1 = ((bf16[128,8,2048]{2,1,0:T(8,128)(2,1)}), bf16[128,8,2048]{2,1,0:T(8,128)(2,1)}, u32[]{:S(2)}, u32[]{:S(2)}) async-start(bf16[128,8,2048]{2,1,0:T(8,128)(2,1)} %convert_bitcast_fusion), calls=%async_computation.1 | async-start | bytes 8388608 | tf_op jit(solution)/shard_map/all_to_all | solution.py:776
  147.6 6.5 %copy.57 = bf16[1024,2176]{0,1:T(8,128)(2,1)} copy(bf16[1024,2176]{1,0:T(8,128)(2,1)} %bitcast.11) | data formatting | bytes 8912896 | tf_op jit(solution)/shard_map/optimization_barrier | solution.py:774
  154.1 8.3 %fusion.13 = f32[1024,768]{0,1:T(8,128)} fusion(bf16[1024,2176]{1,0:T(8,128)(2,1)} %bitcast.11, bf16[1,768,2048]{2,1,0:T(8,128)(2,1)} %param.30), kind=kOutput, calls=%fused_computation.20 | convolution fusion | flops 3221225472 | bytes 10485760 | tf_op jit(solution)/shard_map/dot_general | solution.py:20
  162.4 39.3 %all-to-all-done.1 = bf16[128,8,2048]{2,1,0:T(8,128)(2,1)} async-done(((bf16[128,8,2048]{2,1,0:T(8,128)(2,1)}), bf16[128,8,2048]{2,1,0:T(8,128)(2,1)}, u32[]{:S(2)}, u32[]{:S(2)}) %all-to-all-start.1) | async-done | bytes 4194336 | tf_op jit(solution)/shard_map/all_to_all | solution.py:776
  201.7 4.0 fusion.57
  205.9 5.5 %fusion.5 = f32[1024,768]{0,1:T(8,128)S(1)} fusion(bf16[128,8,2048]{2,1,0:T(8,128)(2,1)} %all-to-all-done.1, bf16[1,2048,768]{2,1,0:T(8,128)(2,1)S(1)} %copy-done.32), kind=kOutput, calls=%fused_computation.9 | convolution fusion | flops 3221225472 | bytes 10485760 | tf_op jit(solution)/shard_map/dot_general | solution.py:28
  211.4 9.4 %multiply_convert_fusion.1 = (bf16[1024,768]{0,1:T(8,128)(2,1)}, f32[1024]{0:T(1024)S(1)}, bf16[1024,768]{0,1:T(8,128)(2,1)}, bf16[1024,768]{0,1:T(8,128)(2,1)}) fusion(f32[1024,768]{0,1:T(8,128)S(1)} %fusion.5, f32[1024,768]{0,1:T(8,128)S(1)} %copy-done.36, f32[1024]{0:T(1024)S(1)} %div.59, bf16[1,2048,768]{2,1,0:T(8,128)(2,1)S(1)} %copy-done, ...), kind=kOutput, calls=%fused_computation.31 | convolution fusion | flops 3236166656 | bytes 18358272 | tf_op jit(solution)/shard_map/dot_general | solution.py:28
  220.8 0.9 broadcast_select_fusion.1
  221.7 1.8 copy.59
  223.5 1.8 copy.58
  225.3 5.0 %fusion.19 = f32[1024,2048]{1,0:T(8,128)S(1)} fusion(bf16[1024,768]{0,1:T(8,128)(2,1)} %get-tuple-element.82, bf16[1,2048,768]{2,1,0:T(8,128)(2,1)S(1)} %copy-done), kind=kOutput, calls=%fused_computation.26 | convolution fusion | flops 3221225472 | bytes 13107200 | tf_op jit(solution)/shard_map/dot_general | solution.py:20
  230.4 3.7 add_convert_fusion
  234.1 2.5 maximum_bitcast_fusion
  236.6 5.6 %all-to-all-start.2 = ((bf16[128,8,2304]{2,1,0:T(8,128)(2,1)}), bf16[128,8,2304]{2,1,0:T(8,128)(2,1)}, u32[]{:S(2)}, u32[]{:S(2)}) async-start(bf16[128,8,2304]{2,1,0:T(8,128)(2,1)} %maximum_bitcast_fusion), calls=%async_computation.2 | async-start | bytes 9437184 | tf_op jit(solution)/shard_map/all_to_all | solution.py:810
  242.3 0.4 fusion.58
  242.8 8.0 %convolution_convert_fusion.3 = bf16[1024,2048]{1,0:T(8,128)(2,1)} fusion(bf16[1024,768]{0,1:T(8,128)(2,1)} %get-tuple-element.85, bf16[1,768,2048]{2,1,0:T(8,128)(2,1)} %param.30), kind=kOutput, calls=%fused_computation.17 | convolution fusion | flops 3223322624 | bytes 8912896 | tf_op jit(solution)/shard_map/dot_general | solution.py:28
  250.8 7.7 %fusion.11 = f32[768,2048]{1,0:T(8,128)} fusion(bf16[1024,768]{0,1:T(8,128)(2,1)S(1)} %copy-done.37, bf16[1024,2176]{1,0:T(8,128)(2,1)} %bitcast.11), kind=kOutput, calls=%fused_computation.18 | convolution fusion | flops 3221225472 | bytes 12058624 | tf_op jit(solution)/shard_map/dot_general | solution.py:24
  258.5 8.6 %fusion.3 = f32[2048,768]{1,0:T(8,128)} fusion(bf16[1024,768]{0,1:T(8,128)(2,1)S(1)} %copy-done.35, bf16[128,8,2048]{2,1,0:T(8,128)(2,1)} %all-to-all-done.1), kind=kOutput, calls=%fused_computation.7 | convolution fusion | flops 3221225472 | bytes 12058624 | tf_op jit(solution)/shard_map/dot_general | solution.py:24
  267.1 8.5 %fusion.1 = f32[2048,768]{1,0:T(8,128)} fusion(bf16[1024,768]{0,1:T(8,128)(2,1)S(1)} %copy-done.39, bf16[128,8,2048]{2,1,0:T(8,128)(2,1)} %all-to-all-done.1), kind=kOutput, calls=%fused_computation.5 | convolution fusion | flops 3221225472 | bytes 12058624 | tf_op jit(solution)/shard_map/dot_general | solution.py:24
  275.6 27.0 %all-to-all-done.2 = bf16[128,8,2304]{2,1,0:T(8,128)(2,1)} async-done(((bf16[128,8,2304]{2,1,0:T(8,128)(2,1)}), bf16[128,8,2304]{2,1,0:T(8,128)(2,1)}, u32[]{:S(2)}, u32[]{:S(2)}) %all-to-all-start.2) | async-done | bytes 4718624 | tf_op jit(solution)/shard_map/all_to_all | solution.py:810
  302.6 3.4 fusion.40
  306.3 2.5 multiply_reduce_fusion.1
  308.8 1.1 convolution_convert_fusion.6
  309.9 6.7 %all-to-all-start.3 = ((bf16[128,16,128]{2,1,0:T(8,128)(2,1)}), bf16[128,16,128]{2,1,0:T(8,128)(2,1)S(1)}, u32[]{:S(2)}, u32[]{:S(2)}) async-start(bf16[128,16,128]{2,1,0:T(8,128)(2,1)} %bitcast.20), calls=%async_computation.3 | async-start | bytes 1048576 | tf_op jit(solution)/shard_map/all_to_all | solution.py:833
  316.6 2.9 fusion.55
  319.5 25.6 %share_rows_3.1 = bf16[4,128,2048]{2,1,0:T(8,128)(2,1)} custom-call(bf16[128,2048]{1,0:T(8,128)(2,1)} %get-tuple-element.74.tok), custom_call_target="tpu_custom_call" | custom-call | bytes 46800000 | tf_op jit(solution)/shard_map/share_rows_3/pallas_call | solution.py:292
  345.3 9.4 %all-to-all-start.4 = ((bf16[128,8,2048]{2,1,0:T(8,128)(2,1)}), bf16[128,8,2048]{2,1,0:T(8,128)(2,1)}, u32[]{:S(2)}, u32[]{:S(2)}) async-start(bf16[128,8,2048]{2,1,0:T(8,128)(2,1)} %bitcast.132), calls=%async_computation.4 | async-start | bytes 8388608 | tf_op jit(solution)/shard_map/all_to_all | solution.py:835
  354.7 5.3 %convolution_convert_fusion.7.grad_mixed = bf16[512,1024]{1,0:T(8,128)(2,1)S(1)} fusion(bf16[512,2048]{1,0:T(8,128)(2,1)} %bitcast.133, bf16[2048,1024]{1,0:T(8,128)(2,1)} %bitcast.144), kind=kOutput, calls=%fused_computation.48 | convolution fusion | flops 2148007936 | bytes 7340032 | tf_op jit(solution)/shard_map/dot_general | solution.py:28
  360.1 6.7 %attend_back.1 = (bf16[512,1280]{1,0:T(8,128)(2,1)S(1)}, f32[2,128]{1,0:T(2,128)S(1)}) custom-call(f32[512,1280]{1,0:T(8,128)S(1)} %copy-done.3, f32[512,128]{1,0:T(8,128)S(1)} %get-tuple-element.108.cosine, f32[512,128]{1,0:T(8,128)S(1)} %copy-done.7, f32[1,128]{1,0:T(1,128)S(1)} %bitcast.129, f32[1,128]{1,0:T(1,128)S(1)} %bitcast.131, ...), custom_call_target="tpu_custom_call" | custom-call | bytes 50400000 | tf_op jit(solution)/shard_map/attend_back/pallas_call | solution.py:675
  366.8 5.6 %convolution_convert_fusion.5 = bf16[512,2048]{1,0:T(8,128)(2,1)S(1)} fusion(bf16[512,1280]{1,0:T(8,128)(2,1)S(1)} %get-tuple-element.56, bf16[2048,1280]{1,0:T(8,128)(2,1)} %bitcast.143), kind=kOutput, calls=%fused_computation.36 | convolution fusion | flops 2685403136 | bytes 8650752 | tf_op jit(solution)/shard_map/dot_general | solution.py:20
  372.5 47.0 %reduce_rows_4.1 = f32[128,2048]{1,0:T(8,128)S(1)} custom-call(bf16[4,128,2048]{2,1,0:T(8,128)(2,1)S(1)} %bitcast.125), custom_call_target="tpu_custom_call" | custom-call | bytes 54000000 | tf_op jit(solution)/shard_map/reduce_rows_4/pallas_call | solution.py:342
  419.5 0.3 fusion.36
  419.9 2.4 convolution_convert_fusion.2
  422.3 3.2 convolution_convert_fusion
  425.5 49.2 %scatter_weights.1 = (f32[32,2048]{1,0:T(8,128)S(1)}, f32[32,256]{1,0:T(8,128)S(1)}, f32[32,256]{1,0:T(8,128)S(1)}, f32[32,2048]{1,0:T(8,128)S(1)}, f32[40,128]{...) custom-call(bf16[4,2,4,2,32,1280]{5,4,3,2,1,0:T(8,128)(2,1)S(1)} %bitcast.123, ...), custom_call_target="tpu_custom_call" | custom-call | bytes 288000000 | tf_op jit(solution)/shard_map/scatter_weights/pallas_call | solution.py:524
  474.8 0.6 slice_bitcast_fusion.2
  475.3 0.6 slice_bitcast_fusion
  476.0 1.1 bitcast_convert_fusion
  477.0 1.4 fusion.33
  478.5 4.1 fusion.24
  482.6 0.7 copy.75
  483.3 0.6 copy.76
  483.9 0.6 copy.77
  484.5 0.7 copy.78
  (115 shorter events, 2.7 us)
Async XLA Ops:
  0.6 210.7 %copy-start = (bf16[1,2048,768]{2,1,0:T(8,128)(2,1)S(1)}, bf16[1,2048,768]{2,1,0:T(8,128)(2,1)}, u32[]{:S(2)}) copy-start(bf16[1,2048,768]{2,1,0:T(8,128)(2,1)} %param.28) | copy-start | bytes 9437188
  56.1 76.2 %all-to-all-start = ((bf16[128,8,2176]{2,1,0:T(8,128)(2,1)}), bf16[128,8,2176]{2,1,0:T(8,128)(2,1)}, u32[]{:S(2)}, u32[]{:S(2)}) async-start(bf16[128,8,2176]{2,1,0:T(8,128)(2,1)} %fusion), calls=%async_computation | async-start | bytes 8912896 | tf_op jit(solution)/shard_map/all_to_all | solution.py:758
  64.8 6.4 %copy-start.6 = (f32[512,128]{1,0:T(8,128)}, f32[512,128]{1,0:T(8,128)S(1)}, u32[]{:S(2)}) copy-start(f32[512,128]{1,0:T(8,128)S(1)} %get-tuple-element.109.signed) | copy-start | bytes 786436
  65.0 6.2 %copy-start.14 = (f32[128]{0:T(128)S(1)}, f32[128]{0:T(128)}, u32[]{:S(2)}) copy-start(f32[128]{0:T(128)} %param.24) | copy-start | bytes 1540
  65.1 6.2 %copy-start.15 = (f32[128]{0:T(128)S(1)}, f32[128]{0:T(128)}, u32[]{:S(2)}) copy-start(f32[128]{0:T(128)} %param.25) | copy-start | bytes 1540
  65.1 16.0 %copy-start.31 = (bf16[4,2,4,2,32,1024]{5,4,3,2,1,0:T(8,128)(2,1)S(1)}, bf16[4,2,4,2,32,1024]{5,4,3,2,1,0:T(8,128)(2,1)}, u32[]{:S(2)}) copy-start(bf16[4,2,4,2,32,1024]{5,4,3,2,1,0:T(8,128)(2,1)} %get-tuple-element.46) | copy-start | bytes 12582916
  71.2 12.2 %copy-start.2 = (f32[512,1280]{1,0:T(8,128)}, f32[512,1280]{1,0:T(8,128)S(1)}, u32[]{:S(2)}) copy-start(f32[512,1280]{1,0:T(8,128)S(1)} %fusion.59.raw) | copy-start | bytes 7864324
  79.4 1.0 copy-start.8
  80.3 0.7 copy-start.10
  81.0 2.4 copy-start.4
  81.0 2.4 copy-start.16
  83.4 46.7 %copy-start.20 = (bf16[128,2048]{1,0:T(8,128)(2,1)S(1)}, bf16[128,2048]{1,0:T(8,128)(2,1)}, u32[]{:S(2)}) copy-start(bf16[128,2048]{1,0:T(8,128)(2,1)} %param.16) | copy-start | bytes 1572868
  83.5 47.9 %copy-start.28 = (f32[2048]{0:T(1024)S(1)}, f32[2048]{0:T(1024)}, u32[]{:S(2)}) copy-start(f32[2048]{0:T(1024)} %param.26) | copy-start | bytes 24580
  130.4 1.0 copy-start.18
  136.7 65.0 %all-to-all-start.1 = ((bf16[128,8,2048]{2,1,0:T(8,128)(2,1)}), bf16[128,8,2048]{2,1,0:T(8,128)(2,1)}, u32[]{:S(2)}, u32[]{:S(2)}) async-start(bf16[128,8,2048]{2,1,0:T(8,128)(2,1)} %convert_bitcast_fusion), calls=%async_computation.1 | async-start | bytes 8388608 | tf_op jit(solution)/shard_map/all_to_all | solution.py:776
  201.7 4.2 copy-start.32
  205.9 5.5 %copy-start.36 = (f32[1024,768]{0,1:T(8,128)S(1)}, f32[1024,768]{0,1:T(8,128)}, u32[]{:S(2)}) copy-start(f32[1024,768]{0,1:T(8,128)} %fusion.13) | copy-start | bytes 9437188
  225.3 5.0 %copy-start.33 = (bf16[1,2048,768]{2,1,0:T(8,128)(2,1)S(1)}, bf16[1,2048,768]{2,1,0:T(8,128)(2,1)}, u32[]{:S(2)}) copy-start(bf16[1,2048,768]{2,1,0:T(8,128)(2,1)} %param.29) | copy-start | bytes 9437188
  225.3 5.0 %copy-start.38 = (bf16[1024,768]{0,1:T(8,128)(2,1)S(1)}, bf16[1024,768]{0,1:T(8,128)(2,1)}, u32[]{:S(2)}) copy-start(bf16[1024,768]{0,1:T(8,128)(2,1)} %get-tuple-element.84) | copy-start | bytes 4718596
  230.3 3.8 copy-start.26
  230.4 3.8 copy-start.27
  236.6 5.7 %copy-start.22 = (bf16[128,2048]{1,0:T(8,128)(2,1)S(1)}, bf16[128,2048]{1,0:T(8,128)(2,1)}, u32[]{:S(2)}) copy-start(bf16[128,2048]{1,0:T(8,128)(2,1)} %multiply_convert_fusion.3) | copy-start | bytes 1572868
  236.6 5.7 %copy-start.23 = (bf16[2048,128]{1,0:T(8,128)(2,1)S(1)}, bf16[2048,128]{1,0:T(8,128)(2,1)}, u32[]{:S(2)}) copy-start(bf16[2048,128]{1,0:T(8,128)(2,1)} %param.27) | copy-start | bytes 1572868
  236.6 66.0 %all-to-all-start.2 = ((bf16[128,8,2304]{2,1,0:T(8,128)(2,1)}), bf16[128,8,2304]{2,1,0:T(8,128)(2,1)}, u32[]{:S(2)}, u32[]{:S(2)}) async-start(bf16[128,8,2304]{2,1,0:T(8,128)(2,1)} %maximum_bitcast_fusion), calls=%async_computation.2 | async-start | bytes 9437184 | tf_op jit(solution)/shard_map/all_to_all | solution.py:810
  242.7 8.1 %copy-start.37 = (bf16[1024,768]{0,1:T(8,128)(2,1)S(1)}, bf16[1024,768]{0,1:T(8,128)(2,1)}, u32[]{:S(2)}) copy-start(bf16[1024,768]{0,1:T(8,128)(2,1)} %get-tuple-element.85) | copy-start | bytes 4718596
  250.8 7.7 %copy-start.35 = (bf16[1024,768]{0,1:T(8,128)(2,1)S(1)}, bf16[1024,768]{0,1:T(8,128)(2,1)}, u32[]{:S(2)}) copy-start(bf16[1024,768]{0,1:T(8,128)(2,1)} %get-tuple-element.82) | copy-start | bytes 4718596
  258.5 8.6 %copy-start.39 = (bf16[1024,768]{0,1:T(8,128)(2,1)S(1)}, bf16[1024,768]{0,1:T(8,128)(2,1)}, u32[]{:S(2)}) copy-start(bf16[1024,768]{0,1:T(8,128)(2,1)} %get-tuple-element.84) | copy-start | bytes 4718596
  302.6 3.7 copy-start.19
  306.2 10.4 %copy-start.30 = (f32[128]{0:T(128)S(1)}, f32[128]{0:T(128)}, u32[]{:S(2)}) copy-start(f32[128]{0:T(128)} %get-tuple-element.99) | copy-start | bytes 1540
  309.9 35.2 %all-to-all-start.3 = ((bf16[128,16,128]{2,1,0:T(8,128)(2,1)}), bf16[128,16,128]{2,1,0:T(8,128)(2,1)S(1)}, u32[]{:S(2)}, u32[]{:S(2)}) async-start(bf16[128,16,128]{2,1,0:T(8,128)(2,1)} %bitcast.20), calls=%async_computation.3 | async-start | bytes 1048576 | tf_op jit(solution)/shard_map/all_to_all | solution.py:833
  345.3 133.2 %all-to-all-start.4 = ((bf16[128,8,2048]{2,1,0:T(8,128)(2,1)}), bf16[128,8,2048]{2,1,0:T(8,128)(2,1)}, u32[]{:S(2)}, u32[]{:S(2)}) async-start(bf16[128,8,2048]{2,1,0:T(8,128)(2,1)} %bitcast.132), calls=%async_computation.4 | async-start | bytes 8388608 | tf_op jit(solution)/shard_map/all_to_all | solution.py:835
  354.7 5.4 %copy-start.3 = (f32[512,1280]{1,0:T(8,128)S(1)}, f32[512,1280]{1,0:T(8,128)}, u32[]{:S(2)}) copy-start(f32[512,1280]{1,0:T(8,128)} %copy-done.2) | copy-start | bytes 7864324
  354.7 5.4 %copy-start.5 = (f32[2,8,256,256]{3,2,1,0:T(8,128)S(1)}, f32[2,8,256,256]{3,2,1,0:T(8,128)}, u32[]{:S(2)}) copy-start(f32[2,8,256,256]{3,2,1,0:T(8,128)} %copy-done.4) | copy-start | bytes 12582916
  354.7 5.4 %copy-start.7 = (f32[512,128]{1,0:T(8,128)S(1)}, f32[512,128]{1,0:T(8,128)}, u32[]{:S(2)}) copy-start(f32[512,128]{1,0:T(8,128)} %copy-done.6) | copy-start | bytes 786436
  354.7 5.4 %copy-start.9 = (bf16[512,1024]{1,0:T(8,128)(2,1)S(1)}, bf16[512,1024]{1,0:T(8,128)(2,1)}, u32[]{:S(2)}) copy-start(bf16[512,1024]{1,0:T(8,128)(2,1)} %copy-done.8) | copy-start | bytes 3145732
  354.7 5.4 %copy-start.11 = (bf16[512,256]{1,0:T(8,128)(2,1)S(1)}, bf16[512,256]{1,0:T(8,128)(2,1)}, u32[]{:S(2)}) copy-start(bf16[512,256]{1,0:T(8,128)(2,1)} %copy-done.10) | copy-start | bytes 786436
  366.8 52.7 %copy-start.29 = (f32[2048]{0:T(1024)S(1)}, f32[2048]{0:T(1024)}, u32[]{:S(2)}) copy-start(f32[2048]{0:T(1024)} %param.19) | copy-start | bytes 24580
  372.5 47.1 %copy-start.21 = (bf16[128,2048]{1,0:T(8,128)(2,1)S(1)}, bf16[128,2048]{1,0:T(8,128)(2,1)}, u32[]{:S(2)}) copy-start(bf16[128,2048]{1,0:T(8,128)(2,1)} %param.16) | copy-start | bytes 1572868
  372.5 47.4 %copy-start.17 = (bf16[512,1024]{1,0:T(8,128)(2,1)S(1)}, bf16[512,1024]{1,0:T(8,128)(2,1)}, u32[]{:S(2)}) copy-start(bf16[512,1024]{1,0:T(8,128)(2,1)} %copy-done.16) | copy-start | bytes 3145732
  372.5 47.4 %copy-start.25 = (bf16[4,128,2048]{2,1,0:T(8,128)(2,1)S(1)}, bf16[4,128,2048]{2,1,0:T(8,128)(2,1)}, u32[]{:S(2)}) copy-start(bf16[4,128,2048]{2,1,0:T(8,128)(2,1)} %share_rows_3.1) | copy-start | bytes 6291460
  419.9 2.4 copy-start.34
  425.5 51.5 %copy-start.24 = (f32[128,2048]{1,0:T(8,128)S(1)}, f32[128,2048]{1,0:T(8,128)}, u32[]{:S(2)}) copy-start(f32[128,2048]{1,0:T(8,128)} %get-tuple-element.75) | copy-start | bytes 3145732
  474.8 2.3 copy-start.12
  477.0 8.2 %copy-start.1 = (bf16[1,2048,768]{2,1,0:T(8,128)(2,1)S(1)}, bf16[1,2048,768]{2,1,0:T(8,128)(2,1)}, u32[]{:S(2)}) copy-start(bf16[1,2048,768]{2,1,0:T(8,128)(2,1)} %param.28) | copy-start | bytes 9437188
  478.5 4.2 copy-start.13

commit v6 on v5

--- a/solution.py
+++ b/solution.py
@@ -697,6 +697,188 @@
     )(raw, cosine, signed, query_gain.reshape(1, hd), key_gain.reshape(1, hd), query, kv, weights, grad_mixed)
 
 
+DIMS = (NX, NYH, NZ, NC, 2)
+CHUNKS = (256, 256, 256, 256, 256, 256, 256, 128, 128)
+TURNS = ("xzy", "zyx", "yxz")
+
+
+class Route:
+    def __init__(self, me, go):
+        x, yh, z, c, t = me.x, me.yh, me.z, me.c, me.t
+        steps = (1, 3, 2)
+        turn = lambda i, d: lax.rem(i + d, RING)
+        self.go = go
+        self.own = {"x": (x, c), "z": (z,), "y": (yh, t)}
+        self.peers = {
+            "x": [((x, 1 - c), me.device(c=1 - c))]
+            + [
+                ((turn(x, d), e), me.device(x=turn(x, d), c=e))
+                for d in steps
+                for e in (c, 1 - c)
+            ],
+            "z": [((turn(z, d),), me.device(z=turn(z, d))) for d in steps],
+            "y": [
+                ((turn(me.y, d) // 2, lax.rem(turn(me.y, d), 2)), me.at_y(turn(me.y, d)))
+                for d in steps
+            ],
+        }
+
+    def everyone(self):
+        return [peer for axis in "xzy" for _, peer in self.peers[axis]]
+
+    @staticmethod
+    def view(ref, axis, at):
+        if axis == "x":
+            return ref.at[at[0], :, :, at[1]]
+        if axis == "z":
+            return ref.at[:, :, at[0]]
+        return ref.at[:, at[0], :, :, at[1]]
+
+    def send(self, axis, src, dst):
+        own = self.own[axis]
+        kept = self.go.keep(self.view(src, axis, own), self.view(dst, axis, own))
+        copies = [
+            self.go.put(self.view(src, axis, at), self.view(dst, axis, own), peer)
+            for at, peer in self.peers[axis]
+        ]
+        return kept, copies
+
+    @staticmethod
+    def wait(sent):
+        kept, copies = sent
+        for copy in copies:
+            copy.wait_recv()
+        kept.wait()
+
+
+def columns(ref, start, size):
+    return ref.at[:, :, :, :, :, :, pl.ds(start, size)]
+
+
+ORDER = ((0, 0), (1, 0), (0, 1), (2, 0), (1, 1), (0, 2), (2, 1), (1, 2), (2, 2))
+
+
+def enter_kernel(
+    sent, told, gate, up, down, router, rows, gate_pre, up_pre, logits, inner_up,
+    *rest,
+):
+    chunks = len(CHUNKS)
+    mids = rest[: 2 * chunks]
+    held = rest[2 * chunks : 3 * chunks]
+    told_v, gate_v, up_v, down_v, router_v, send, recv, local, loads = rest[3 * chunks :]
+    me = Place()
+    go = Copies(send, recv, local)
+    route = Route(me, go)
+    pulls = [
+        pltpu.make_async_copy(a, b, loads.at[n])
+        for n, (a, b) in enumerate(
+            ((told, told_v), (down, down_v), (gate, gate_v), (up, up_v), (router, router_v))
+        )
+    ]
+    for pull in pulls:
+        pull.start()
+    greet(route.everyone())
+    starts = [sum(CHUNKS[:n]) for n in range(chunks)]
+    sent_on = [None] * chunks
+    width = sent.shape[-1]
+    total = told_v.shape[0]
+    block = 256
+
+    def cotangent_block(n):
+        at = pl.ds(n * block, block)
+        inner_up[at] = dot_nt(told_v[at, :width], down_v[...])
+
+    def multiply(n, first):
+        cols = pl.ds(starts[n], CHUNKS[n])
+        flat = held[n].reshape(total, CHUNKS[n])
+
+        def step(m, _):
+            at = pl.ds(pl.multiple_of(m * block, block), block)
+            part = flat[at]
+            for out, weight in ((gate_pre, gate_v), (up_pre, up_v), (logits, router_v)):
+                term = dot_nn(part, weight[cols])
+                out[at] = term if first else out[at] + term
+            return 0
+
+        lax.fori_loop(0, total // block, step, 0)
+
+    outs = []
+    pending = list(range(total // block))
+    done = False
+    first = True
+    for triple, crossing in ORDER:
+        for n in range(3 * triple, 3 * triple + 3):
+            axis = TURNS[n % 3][crossing]
+            src = columns(sent, starts[n], CHUNKS[n]) if crossing == 0 else mids[2 * n + crossing - 1]
+            dst = held[n] if crossing == 2 else mids[2 * n + crossing]
+            if crossing > 0:
+                route.wait(sent_on[n])
+            sent_on[n] = route.send(axis, src, dst)
+        if (triple, crossing) == (1, 0):
+            for pull in pulls[:2]:
+                pull.wait()
+        if pending and (triple, crossing) not in ((0, 0),):
+            cotangent_block(pending.pop(0))
+        if (triple, crossing) == (2, 1):
+            while pending:
+                cotangent_block(pending.pop(0))
+            for pull in pulls[2:]:
+                pull.wait()
+        if (triple, crossing) in ((1, 2), (2, 2)):
+            ready = triple - 1
+            for n in range(3 * ready, 3 * ready + 3):
+                route.wait(sent_on[n])
+                outs.append(go.keep(held[n], columns(rows, starts[n], CHUNKS[n])))
+                multiply(n, first)
+                first = False
+    for n in range(chunks - 3, chunks):
+        route.wait(sent_on[n])
+        outs.append(go.keep(held[n], columns(rows, starts[n], CHUNKS[n])))
+        multiply(n, first)
+    for out in outs:
+        out.wait()
+    go.finish()
+
+
+def enter(sent, told, gate, up, down, router):
+    slots, width = sent.shape
+    hidden, experts = gate.shape[1], router.shape[1]
+    cap = slots // math.prod(DIMS)
+    lead = (*DIMS, cap)
+    chunks = len(CHUNKS)
+    rows, gate_pre, up_pre, logits, inner_up = pl.pallas_call(
+        enter_kernel,
+        name="enter_experts",
+        cost_estimate=cost(60),
+        out_shape=(
+            jax.ShapeDtypeStruct((*lead, width), BF16),
+            jax.ShapeDtypeStruct((slots, hidden), F32),
+            jax.ShapeDtypeStruct((slots, hidden), F32),
+            jax.ShapeDtypeStruct((slots, experts), F32),
+            jax.ShapeDtypeStruct((slots, hidden), F32),
+        ),
+        in_specs=[ANY] * 6,
+        out_specs=(ANY, VMEM, VMEM, VMEM, VMEM),
+        scratch_shapes=[
+            *(pltpu.VMEM((*lead, w), BF16) for w in CHUNKS for _ in range(2)),
+            *(pltpu.VMEM((*lead, w), BF16) for w in CHUNKS),
+            pltpu.VMEM(told.shape, BF16),
+            pltpu.VMEM(gate.shape, BF16),
+            pltpu.VMEM(up.shape, BF16),
+            pltpu.VMEM(down.shape, BF16),
+            pltpu.VMEM(router.shape, BF16),
+            pltpu.SemaphoreType.DMA((13 * chunks,)),
+            pltpu.SemaphoreType.DMA((13 * chunks,)),
+            pltpu.SemaphoreType.DMA((4 * chunks,)),
+            pltpu.SemaphoreType.DMA((5,)),
+        ],
+        compiler_params=pltpu.CompilerParams(
+            collective_id=6, has_side_effects=True, vmem_limit_bytes=58 << 20
+        ),
+    )(sent.reshape(*lead, width), told, gate, up, down, router)
+    return rows.reshape(slots, width), gate_pre, up_pre, logits, inner_up
+
+
 def on_device(
     hidden_in,
     doc_ids,
@@ -773,25 +955,22 @@
     moe_input = rms_scale(residual, moe_gain).astype(BF16)
     moe_input, cot_in = lax.optimization_barrier((moe_input, cot_in))
     sent = dot_nn(spread, moe_input).astype(BF16)
-    rows = lax.all_to_all(
-        sent.reshape(experts, cap, width), both, split_axis=0, concat_axis=0, tiled=True
-    ).reshape(slots, width)
+    gate_mat, up_mat, down_mat = gate_weight[0], up_weight[0], down_weight[0]
+    rows, gate_pre, up_pre, row_logits, inner_up = enter(
+        sent, cot_in, gate_mat, up_mat, down_mat, router_weight
+    )
     logits = dot_nn(moe_input, router_weight)
     masked = jnp.where(chosen > 0, logits, MASKED)
     probs = jnp.exp(masked - jnp.max(masked, axis=-1, keepdims=True))
     probs = probs / jnp.sum(probs, axis=-1, keepdims=True)
 
-    gate_mat, up_mat, down_mat = gate_weight[0], up_weight[0], down_weight[0]
     cot_rows = cot_in[:, :width]
-    inner_up = dot_nt(cot_rows, down_mat)
-    row_logits = jnp.where(cot_in[:, width:] > 0, dot_nn(rows, router_weight), MASKED)
+    row_logits = jnp.where(cot_in[:, width:] > 0, row_logits, MASKED)
     row_probs = jnp.exp(row_logits - jnp.max(row_logits, axis=-1, keepdims=True))
     mine = lax.broadcasted_iota(jnp.int32, (1, experts), 1) == me
     prob = jnp.sum(jnp.where(mine, row_probs, 0.0), axis=-1, keepdims=True) / jnp.sum(
         row_probs, axis=-1, keepdims=True
     )
-    gate_pre = dot_nn(rows, gate_mat)
-    up_pre = dot_nn(rows, up_mat)
     sigmoid = jax.nn.sigmoid(gate_pre)
     silu = gate_pre * sigmoid
     inner = silu * up_pre

time: 490 us -> 486 us (level)
  Pallas kernels: 228 us -> 295 us
  waiting for transfers between devices: 66.3 us -> 30.9 us
  matrix products: 114 us -> 79.6 us
  other arithmetic: 17.4 us -> 31 us
  starting transfers between devices: 39.1 us -> 29.5 us
  local copies, waits for them, and re-layouts: 18.9 us -> 13.5 us
    pallas_call x0 -> x1, Pallas kernels: none -> 66.4 us  [enter(): pl.pallas_call(enter_kernel, name='enter_experts', cost_estimate=cost(60)...]
    all_to_all x1 -> x0, waiting for transfers between devices: 39.3 us -> none  [on_device(): lax.all_to_all(sent.reshape(experts, cap, width), both, split_axis=0, con...]
    dot_general x10 -> x7, matrix products: 47.7 us -> 28.9 us  [dot_nn(): lax.dot_general(a, b, (((1,), (0,)), ((), ())), preferred_element_type=F32)]
    all_to_all x1 -> x0, starting transfers between devices: 10.9 us -> none  [on_device(): lax.all_to_all(sent.reshape(experts, cap, width), both, split_axis=0, con...]
    dot_general x6 -> x5, matrix products: 27.5 us -> 18.4 us  [dot_nt(): lax.dot_general(a, b, (((1,), (1,)), ((), ())), preferred_element_type=F32)]
    dot_general x8, matrix products: 39 us -> 32.3 us  [dot_tn(): lax.dot_general(a, b, (((0,), (0,)), ((), ())), preferred_element_type=F32)]
    optimization_barrier x1 -> x0, local copies, waits for them, and re-layouts: 6.49 us -> none  [on_device(): moe_input, cot_in = lax.optimization_barrier((moe_input, cot_in))]
    convert_element_type x0 -> x1, other arithmetic: none -> 6.05 us  [on_device(): (grad_inner * up_pre * sigmoid * (1.0 + gate_pre * (1.0 - sigmoid))).asty...]
  transfers between devices with their start and end apart: 5 -> 4, of which waited for: 2 -> 1; matrix products, arithmetic and copies ran while one was open for 17% -> 14% of each run, Pallas kernels for 38% -> 38%
where the time goes in v6:
time: 486 us; the launch traced here: 481 us
  Pallas kernels  295 us (61%)
  matrix products  79.6 us (16%)
  other arithmetic  31 us (6%)
  waiting for transfers between devices  30.9 us (6%)
  starting transfers between devices  29.5 us (6%)
  local copies, waits for them, and re-layouts  13.5 us (3%)
    pallas_call x2, Pallas kernels, reduce(): pl.pallas_call(reduce_kernel, name=f'reduce_rows_{ident}', cost_estimate=...  95.1 us
    pallas_call x1, Pallas kernels, enter(): pl.pallas_call(enter_kernel, name='enter_experts', cost_estimate=cost(60)...  66.4 us
    pallas_call x1, Pallas kernels, scatter(): pl.pallas_call(scatter_kernel, name='scatter_weights', cost_estimate=cost...  49.3 us
    pallas_call x1, Pallas kernels, gather(): pl.pallas_call(gather_kernel, name='gather_weights', cost_estimate=cost(6...  44.6 us
    dot_general x8, matrix products, dot_tn(): lax.dot_general(a, b, (((0,), (0,)), ((), ())), preferred_element_type=F32)  32.3 us
    all_to_all x1, waiting for transfers between devices, on_device(): lax.all_to_all(home_out.reshape(experts, cap, width + 2 * experts), both,...  30.9 us
    dot_general x7, matrix products, dot_nn(): lax.dot_general(a, b, (((1,), (0,)), ((), ())), preferred_element_type=F32)  28.9 us
    pallas_call x1, Pallas kernels, share(): pl.pallas_call(share_kernel, name=f'share_rows_{ident}', cost_estimate=co...  24.5 us
  transfers between devices with their start and end apart: 4, of which 1 were waited for; matrix products, arithmetic and copies ran while one was open for 14% of the time, Pallas kernels for 38%

profile of v6, /device:TPU:1, one launch (start us, length us, event | category | flops | bytes accessed | tf_op | source)
XLA Modules:
  0.0 481.0 jit_solution(13238624806737146162)
XLA Ops:
  0.7 0.8 copy.46
  1.9 1.2 fusion.6
  3.6 0.7 convert_element_type.138
  4.4 2.0 fusion.8.tok
  6.9 0.6 broadcast_in_dim.107.doc
  7.5 44.6 %gather_weights.1 = (bf16[4,2,4,2,32,1280]{5,4,3,2,1,0:T(8,128)(2,1)}, bf16[4,2,4,2,32,1024]{5,4,3,2,1,0:T(8,128)(2,1)}, bf16[4,128,2048]{2,1,0:T(8,128)(2,1)}, f32[2,8,256]{2,1,0:T(8,128)}) custom-call(bf16[32,2048]{1,0:T(8,128)(2,1)} %q.1, bf16[32,256]{1,0:T(8,128)(2,1)} %k.1, bf16[32,256]{1,0:T(8,128)(2,1)} %v.1, bf16[32,2048]{1,0:T(8,128)(2,1)} %bitcast.117, ...), custom_call_target="tpu_custom_call" | custom-call | bytes 216000000 | tf_op jit(solution)/shard_map/gather_weights/pallas_call | solution.py:243
  52.1 3.4 fusion
  55.5 6.4 %all-to-all-start = ((bf16[128,8,2176]{2,1,0:T(8,128)(2,1)}), bf16[128,8,2176]{2,1,0:T(8,128)(2,1)}, u32[]{:S(2)}, u32[]{:S(2)}) async-start(bf16[128,8,2176]{2,1,0:T(8,128)(2,1)} %fusion), calls=%async_computation | async-start | bytes 8912896 | tf_op jit(solution)/shard_map/all_to_all | solution.py:940
  62.0 0.7 slice.30
  63.0 1.0 fusion.29
  64.5 6.1 %fusion.41.raw = f32[512,1280]{1,0:T(8,128)S(1)} fusion(bf16[512,2048]{1,0:T(8,128)(2,1)} %bitcast.130, bf16[2048,1280]{1,0:T(8,128)(2,1)} %bitcast.124), kind=kOutput, calls=%fused_computation.116 | convolution fusion | flops 2684354560 | bytes 9961472 | tf_op jit(solution)/shard_map/dot_general | solution.py:28
  70.7 8.1 %attend.1 = (bf16[512,1024]{1,0:T(8,128)(2,1)S(1)}, bf16[512,256]{1,0:T(8,128)(2,1)S(1)}, f32[2,8,256,256]{3,2,1,0:T(8,128)S(1)}, bf16[512,1024]{1,0:T(8,128)(2,1)S(1)}) custom-call(f32[512,1280]{1,0:T(8,128)S(1)} %fusion.41.raw, f32[2,256,256]{2,1,0:T(8,128)S(1)} %fusion.20.bias, f32[512,128]{1,0:T(8,128)S(1)} %get-tuple-element.116.cosine, ...), custom_call_target="tpu_custom_call" | custom-call | bytes 28800000 | tf_op jit(solution)/shard_map/attend/pallas_call | solution.py:598
  78.8 2.4 convolution_convert_fusion.5
  81.4 48.2 %reduce_rows_2.1 = f32[128,2048]{1,0:T(8,128)S(1)} custom-call(bf16[4,128,2048]{2,1,0:T(8,128)(2,1)S(1)} %bitcast.102), custom_call_target="tpu_custom_call" | custom-call | bytes 54000000 | tf_op jit(solution)/shard_map/reduce_rows_2/pallas_call | solution.py:342
  129.6 1.0 copy-done.2
  130.6 1.6 multiply_reduce_fusion.3
  132.1 0.6 multiply_multiply_fusion.1
  133.2 1.0 multiply_convert_fusion.3
  134.2 4.4 convolution_convert_fusion.4
  138.5 66.4 %enter_experts.1 = (bf16[4,2,4,2,2,8,2048]{6,5,4,3,2,1,0:T(8,128)(2,1)}, f32[1024,768]{1,0:T(8,128)}, f32[1024,768]{1,0:T(8,128)}, f32[1024,128]{1,0:T(8,128)}, f32[1024,768]{1,0:T(8,128)}) custom-call(bf16[4,2,4,2,2,8,2048]{6,5,4,3,2,1,0:T(8,128)(2,1)} %bitcast.108, bf16[1024,2176]{1,0:T(8,128)(2,1)} %bitcast.11.told, bf16[2048,768]{1,0:T(8,128)(2,1)} %bitcast.111, ...), custom_call_target="tpu_custom_call" | custom-call | bytes 216000000 | tf_op jit(solution)/shard_map/enter_experts/pallas_call | solution.py:849
  204.9 1.3 fusion.30
  206.3 1.6 fusion.22
  207.9 6.1 %multiply_convert_fusion.1 = (bf16[1024,768]{1,0:T(8,128)(2,1)S(1)}, f32[1024]{0:T(1024)S(1)}, bf16[1024,768]{1,0:T(8,128)(2,1)S(1)}, bf16[1024,768]{1,0:T(8,128)(2,1)}) fusion(f32[1024,768]{1,0:T(8,128)} %get-tuple-element.56, f32[1024,768]{1,0:T(8,128)} %get-tuple-element.57, f32[1024,768]{1,0:T(8,128)} %get-tuple-element.58, f32[1024]{0:T(1024)S(1)} %div.59), kind=kLoop, calls=%fused_computation.12 | loop fusion | flops 14941184 | bytes 14163968 | tf_op jit(solution)/shard_map/convert_element_type | solution.py:980
  214.0 3.4 fusion.36
  217.8 3.8 add_convert_fusion
  221.6 2.5 maximum_bitcast_fusion
  224.1 6.2 %all-to-all-start.1 = ((bf16[128,8,2304]{2,1,0:T(8,128)(2,1)}), bf16[128,8,2304]{2,1,0:T(8,128)(2,1)}, u32[]{:S(2)}, u32[]{:S(2)}) async-start(bf16[128,8,2304]{2,1,0:T(8,128)(2,1)} %maximum_bitcast_fusion), calls=%async_computation.1 | async-start | bytes 9437184 | tf_op jit(solution)/shard_map/all_to_all | solution.py:989
  230.3 0.7 pad.3.clone
  230.9 1.6 fusion.40
  232.5 0.6 fusion.32
  233.1 8.0 %convolution_convert_fusion.3 = bf16[1024,2048]{1,0:T(8,128)(2,1)} fusion(bf16[1024,768]{1,0:T(8,128)(2,1)} %get-tuple-element.95, bf16[1,768,2048]{2,1,0:T(8,128)(2,1)} %param.30), kind=kOutput, calls=%fused_computation.8 | convolution fusion | flops 3223322624 | bytes 8912896 | tf_op jit(solution)/shard_map/dot_general | solution.py:28
  241.0 7.7 %fusion.1 = f32[768,2048]{1,0:T(8,128)} fusion(bf16[1024,768]{1,0:T(8,128)(2,1)S(1)} %copy-done.13, bf16[1024,2176]{1,0:T(8,128)(2,1)} %bitcast.11.told), kind=kOutput, calls=%fused_computation.5 | convolution fusion | flops 3221225472 | bytes 12058624 | tf_op jit(solution)/shard_map/dot_general | solution.py:24
  248.7 5.4 %fusion.42 = f32[2048,768]{1,0:T(8,128)} fusion(bf16[1024,2048]{1,0:T(8,128)(2,1)S(1)} %bitcast.128, bf16[1024,768]{1,0:T(8,128)(2,1)S(1)} %copy-done.23), kind=kOutput, calls=%fused_computation.117 | convolution fusion | flops 3221225472 | bytes 12058624 | tf_op jit(solution)/shard_map/dot_general | solution.py:24
  254.2 5.4 %fusion.43 = f32[2048,768]{1,0:T(8,128)} fusion(bf16[1024,2048]{1,0:T(8,128)(2,1)S(1)} %bitcast.129, bf16[1024,768]{1,0:T(8,128)(2,1)S(1)} %copy-done.21), kind=kOutput, calls=%fused_computation.118 | convolution fusion | flops 3221225472 | bytes 12058624 | tf_op jit(solution)/shard_map/dot_general | solution.py:24
  259.6 30.9 %all-to-all-done.1 = bf16[128,8,2304]{2,1,0:T(8,128)(2,1)} async-done(((bf16[128,8,2304]{2,1,0:T(8,128)(2,1)}), bf16[128,8,2304]{2,1,0:T(8,128)(2,1)}, u32[]{:S(2)}, u32[]{:S(2)}) %all-to-all-start.1) | async-done | bytes 4718624 | tf_op jit(solution)/shard_map/all_to_all | solution.py:989
  290.5 3.3 fusion.18
  293.8 1.0 copy-done.14
  294.8 0.7 fusion.39
  295.5 1.6 copy.51
  297.1 1.6 copy.52
  298.6 1.0 multiply_reduce_fusion.4
  299.6 0.7 multiply_convert_fusion.4
  300.3 3.2 multiply_reduce_fusion.1
  303.5 1.1 convolution_convert_fusion.7
  304.6 7.2 %all-to-all-start.2 = ((bf16[128,16,128]{2,1,0:T(8,128)(2,1)}), bf16[128,16,128]{2,1,0:T(8,128)(2,1)}, u32[]{:S(2)}, u32[]{:S(2)}) async-start(bf16[128,16,128]{2,1,0:T(8,128)(2,1)} %bitcast.116), calls=%async_computation.2 | async-start | bytes 1048576 | tf_op jit(solution)/shard_map/all_to_all | solution.py:1012
  311.8 3.2 fusion.38
  315.0 24.5 %share_rows_3.1 = bf16[4,128,2048]{2,1,0:T(8,128)(2,1)} custom-call(bf16[128,2048]{1,0:T(8,128)(2,1)} %get-tuple-element.84.tok), custom_call_target="tpu_custom_call" | custom-call | bytes 46800000 | tf_op jit(solution)/shard_map/share_rows_3/pallas_call | solution.py:292
  339.6 1.2 convert_reduce_fusion.piece
  340.7 9.8 %all-to-all-start.3 = ((bf16[128,8,2048]{2,1,0:T(8,128)(2,1)}), bf16[128,8,2048]{2,1,0:T(8,128)(2,1)}, u32[]{:S(2)}, u32[]{:S(2)}) async-start(bf16[128,8,2048]{2,1,0:T(8,128)(2,1)} %bitcast.110), calls=%async_computation.3 | async-start | bytes 8388608 | tf_op jit(solution)/shard_map/all_to_all | solution.py:1014
  350.5 5.3 %convolution_convert_fusion.8.grad_mixed = bf16[512,1024]{1,0:T(8,128)(2,1)S(1)} fusion(bf16[512,2048]{1,0:T(8,128)(2,1)} %bitcast.114, bf16[2048,1024]{1,0:T(8,128)(2,1)} %bitcast.126), kind=kOutput, calls=%fused_computation.29 | convolution fusion | flops 2148007936 | bytes 7340032 | tf_op jit(solution)/shard_map/dot_general | solution.py:28
  355.9 6.8 %attend_back.1 = (bf16[512,1280]{1,0:T(8,128)(2,1)S(1)}, f32[2,128]{1,0:T(2,128)S(1)}) custom-call(f32[512,1280]{1,0:T(8,128)S(1)} %fusion.41.raw, f32[512,128]{1,0:T(8,128)S(1)} %get-tuple-element.116.cosine, f32[512,128]{1,0:T(8,128)S(1)} %get-tuple-element.117.signed, f32[1,128]{1,0:T(1,128)S(1)} %bitcast.105, f32[1,128]{1,0:T(1,128)S(1)} %bitcast.107, ...), custom_call_target="tpu_custom_call" | custom-call | bytes 50400000 | tf_op jit(solution)/shard_map/attend_back/pallas_call | solution.py:675
  362.7 5.6 %convolution_convert_fusion.6 = bf16[512,2048]{1,0:T(8,128)(2,1)S(1)} fusion(bf16[512,1280]{1,0:T(8,128)(2,1)S(1)} %get-tuple-element.66, bf16[2048,1280]{1,0:T(8,128)(2,1)} %bitcast.125), kind=kOutput, calls=%fused_computation.17 | convolution fusion | flops 2685403136 | bytes 8650752 | tf_op jit(solution)/shard_map/dot_general | solution.py:20
  368.4 46.9 %reduce_rows_4.1 = f32[128,2048]{1,0:T(8,128)S(1)} custom-call(bf16[4,128,2048]{2,1,0:T(8,128)(2,1)S(1)} %bitcast.101), custom_call_target="tpu_custom_call" | custom-call | bytes 54000000 | tf_op jit(solution)/shard_map/reduce_rows_4/pallas_call | solution.py:342
  415.8 2.4 convolution_convert_fusion.2
  418.2 3.2 convolution_convert_fusion
  421.4 49.3 %scatter_weights.1 = (f32[32,2048]{1,0:T(8,128)S(1)}, f32[32,256]{1,0:T(8,128)S(1)}, f32[32,256]{1,0:T(8,128)S(1)}, f32[32,2048]{1,0:T(8,128)S(1)}, f32[40,128]{...) custom-call(bf16[4,2,4,2,32,1280]{5,4,3,2,1,0:T(8,128)(2,1)S(1)} %bitcast.99, ...), custom_call_target="tpu_custom_call" | custom-call | bytes 288000000 | tf_op jit(solution)/shard_map/scatter_weights/pallas_call | solution.py:524
  471.2 0.6 slice_bitcast_fusion
  471.8 1.1 bitcast_convert_fusion
  472.9 1.4 fusion.11
  474.3 3.8 fusion.5
  478.1 0.7 copy.63
  478.8 0.6 copy.64
  479.4 0.6 copy.65
  480.0 0.7 copy.66
  (105 shorter events, 4.2 us)
Async XLA Ops:
  0.6 51.5 %copy-start.19 = (bf16[128,2048]{1,0:T(8,128)(2,1)S(1)}, bf16[128,2048]{1,0:T(8,128)(2,1)}, u32[]{:S(2)}) copy-start(bf16[128,2048]{1,0:T(8,128)(2,1)} %param.31) | copy-start | bytes 1572868
  0.7 3.6 copy-start.31
  3.6 2.8 copy-start.27
  4.4 2.0 copy-start.24
  55.5 78.6 %all-to-all-start = ((bf16[128,8,2176]{2,1,0:T(8,128)(2,1)}), bf16[128,8,2176]{2,1,0:T(8,128)(2,1)}, u32[]{:S(2)}, u32[]{:S(2)}) async-start(bf16[128,8,2176]{2,1,0:T(8,128)(2,1)} %fusion), calls=%async_computation | async-start | bytes 8912896 | tf_op jit(solution)/shard_map/all_to_all | solution.py:940
  64.5 6.2 %copy-start.5 = (f32[128]{0:T(128)S(1)}, f32[128]{0:T(128)}, u32[]{:S(2)}) copy-start(f32[128]{0:T(128)} %param.24) | copy-start | bytes 1540
  64.5 6.2 %copy-start.6 = (f32[128]{0:T(128)S(1)}, f32[128]{0:T(128)}, u32[]{:S(2)}) copy-start(f32[128]{0:T(128)} %param.25) | copy-start | bytes 1540
  64.5 14.3 %copy-start.35 = (bf16[4,2,4,2,32,1024]{5,4,3,2,1,0:T(8,128)(2,1)S(1)}, bf16[4,2,4,2,32,1024]{5,4,3,2,1,0:T(8,128)(2,1)}, u32[]{:S(2)}) copy-start(bf16[4,2,4,2,32,1024]{5,4,3,2,1,0:T(8,128)(2,1)} %get-tuple-element.51) | copy-start | bytes 12582916
  78.8 2.4 copy-start
  78.8 2.4 copy-start.3
  78.8 2.6 copy-start.7
  81.4 51.8 %copy-start.25 = (f32[2048]{0:T(1024)S(1)}, f32[2048]{0:T(1024)}, u32[]{:S(2)}) copy-start(f32[2048]{0:T(1024)} %param.26) | copy-start | bytes 24580
  129.6 1.0 copy-start.2
  132.1 1.0 copy-start.9
  132.7 0.5 copy-start.29
  207.9 6.1 %copy-start.16 = (bf16[1,2048,768]{2,1,0:T(8,128)(2,1)S(1)}, bf16[1,2048,768]{2,1,0:T(8,128)(2,1)}, u32[]{:S(2)}) copy-start(bf16[1,2048,768]{2,1,0:T(8,128)(2,1)} %param.28) | copy-start | bytes 9437188
  214.0 3.5 copy-start.22
  214.0 3.8 copy-start.20
  214.0 3.8 copy-start.17
  224.1 66.4 %all-to-all-start.1 = ((bf16[128,8,2304]{2,1,0:T(8,128)(2,1)}), bf16[128,8,2304]{2,1,0:T(8,128)(2,1)}, u32[]{:S(2)}, u32[]{:S(2)}) async-start(bf16[128,8,2304]{2,1,0:T(8,128)(2,1)} %maximum_bitcast_fusion), calls=%async_computation.1 | async-start | bytes 9437184 | tf_op jit(solution)/shard_map/all_to_all | solution.py:989
  233.0 8.0 %copy-start.13 = (bf16[1024,768]{1,0:T(8,128)(2,1)S(1)}, bf16[1024,768]{1,0:T(8,128)(2,1)}, u32[]{:S(2)}) copy-start(bf16[1024,768]{1,0:T(8,128)(2,1)} %get-tuple-element.95) | copy-start | bytes 4718596
  241.0 7.7 %copy-start.23 = (bf16[1024,768]{1,0:T(8,128)(2,1)S(1)}, bf16[1024,768]{1,0:T(8,128)(2,1)}, u32[]{:S(2)}) copy-start(bf16[1024,768]{1,0:T(8,128)(2,1)} %copy-done.22) | copy-start | bytes 4718596
  241.0 7.7 %copy-start.36 = (bf16[4,2,4,2,2,8,2048]{6,5,4,3,2,1,0:T(8,128)(2,1)S(1)}, bf16[4,2,4,2,2,8,2048]{6,5,4,3,2,1,0:T(8,128)(2,1)}, u32[]{:S(2)}) copy-start(bf16[4,2,4,2,2,8,2048]{6,5,4,3,2,1,0:T(8,128)(2,1)} %get-tuple-element.59) | copy-start | bytes 12582916
  248.7 5.4 %copy-start.21 = (bf16[1024,768]{1,0:T(8,128)(2,1)S(1)}, bf16[1024,768]{1,0:T(8,128)(2,1)}, u32[]{:S(2)}) copy-start(bf16[1024,768]{1,0:T(8,128)(2,1)} %copy-done.20) | copy-start | bytes 4718596
  293.8 1.0 copy-start.14
  298.6 4.8 %copy-start.12 = (bf16[128,2048]{1,0:T(8,128)(2,1)S(1)}, bf16[128,2048]{1,0:T(8,128)(2,1)}, u32[]{:S(2)}) copy-start(bf16[128,2048]{1,0:T(8,128)(2,1)} %multiply_convert_fusion.3) | copy-start | bytes 1572868
  298.6 13.1 %copy-start.30 = (f32[128]{0:T(128)S(1)}, f32[128]{0:T(128)}, u32[]{:S(2)}) copy-start(f32[128]{0:T(128)} %copy-done.29) | copy-start | bytes 1540
  304.6 35.0 %all-to-all-start.2 = ((bf16[128,16,128]{2,1,0:T(8,128)(2,1)}), bf16[128,16,128]{2,1,0:T(8,128)(2,1)}, u32[]{:S(2)}, u32[]{:S(2)}) async-start(bf16[128,16,128]{2,1,0:T(8,128)(2,1)} %bitcast.116), calls=%async_computation.2 | async-start | bytes 1048576 | tf_op jit(solution)/shard_map/all_to_all | solution.py:1012
  340.7 133.5 %all-to-all-start.3 = ((bf16[128,8,2048]{2,1,0:T(8,128)(2,1)}), bf16[128,8,2048]{2,1,0:T(8,128)(2,1)}, u32[]{:S(2)}, u32[]{:S(2)}) async-start(bf16[128,8,2048]{2,1,0:T(8,128)(2,1)} %bitcast.110), calls=%async_computation.3 | async-start | bytes 8388608 | tf_op jit(solution)/shard_map/all_to_all | solution.py:1014
  350.5 5.3 %copy-start.1 = (f32[2,8,256,256]{3,2,1,0:T(8,128)S(1)}, f32[2,8,256,256]{3,2,1,0:T(8,128)}, u32[]{:S(2)}) copy-start(f32[2,8,256,256]{3,2,1,0:T(8,128)} %copy-done) | copy-start | bytes 12582916
  350.5 5.3 %copy-start.4 = (bf16[512,1024]{1,0:T(8,128)(2,1)S(1)}, bf16[512,1024]{1,0:T(8,128)(2,1)}, u32[]{:S(2)}) copy-start(bf16[512,1024]{1,0:T(8,128)(2,1)} %copy-done.3) | copy-start | bytes 3145732
  362.7 52.6 %copy-start.26 = (f32[2048]{0:T(1024)S(1)}, f32[2048]{0:T(1024)}, u32[]{:S(2)}) copy-start(f32[2048]{0:T(1024)} %param.19) | copy-start | bytes 24580
  362.7 52.6 %copy-start.28 = (f32[128]{0:T(128)S(1)}, f32[128]{0:T(128)}, u32[]{:S(2)}) copy-start(f32[128]{0:T(128)} %copy-done.27) | copy-start | bytes 1540
  368.4 47.0 %copy-start.11 = (bf16[128,2048]{1,0:T(8,128)(2,1)S(1)}, bf16[128,2048]{1,0:T(8,128)(2,1)}, u32[]{:S(2)}) copy-start(bf16[128,2048]{1,0:T(8,128)(2,1)} %param.16) | copy-start | bytes 1572868
  368.4 47.3 %copy-start.34 = (f32[40]{0:T(128)S(1)}, f32[40]{0:T(128)}, u32[]{:S(2)}) copy-start(f32[40]{0:T(128)} %pad.3.clone) | copy-start | bytes 484
  368.4 47.4 %copy-start.8 = (bf16[512,1024]{1,0:T(8,128)(2,1)S(1)}, bf16[512,1024]{1,0:T(8,128)(2,1)}, u32[]{:S(2)}) copy-start(bf16[512,1024]{1,0:T(8,128)(2,1)} %copy-done.7) | copy-start | bytes 3145732
  368.4 47.4 %copy-start.18 = (bf16[4,128,2048]{2,1,0:T(8,128)(2,1)S(1)}, bf16[4,128,2048]{2,1,0:T(8,128)(2,1)}, u32[]{:S(2)}) copy-start(bf16[4,128,2048]{2,1,0:T(8,128)(2,1)} %share_rows_3.1) | copy-start | bytes 6291460
  415.8 2.4 copy-start.37
  421.3 51.5 %copy-start.15 = (f32[128,2048]{1,0:T(8,128)S(1)}, f32[128,2048]{1,0:T(8,128)}, u32[]{:S(2)}) copy-start(f32[128,2048]{1,0:T(8,128)} %get-tuple-element.85) | copy-start | bytes 3145732
  421.3 51.5 %copy-start.33 = (f32[128]{0:T(128)S(1)}, f32[128]{0:T(128)}, u32[]{:S(2)}) copy-start(f32[128]{0:T(128)} %get-tuple-element.107) | copy-start | bytes 1540
  470.6 3.7 copy-start.10
  470.6 3.7 copy-start.32

commit v7 on v6

--- a/solution.py
+++ b/solution.py
@@ -94,6 +94,9 @@
         pick = lambda given, own: own if given is None else given
         x, yh, z, c = pick(x, self.x), pick(yh, self.yh), pick(z, self.z), pick(c, self.c)
         return (((x * NYH + yh) * NZ + z) * NC + c, pick(t, self.t))
+
+    def expert(self):
+        return ((((self.x * NYH + self.yh) * NZ + self.z) * NC) + self.c) * 2 + self.t
 
     def at_y(self, y):
         return self.device(yh=y // 2, t=lax.rem(y, 2))
@@ -699,6 +702,7 @@
 
 DIMS = (NX, NYH, NZ, NC, 2)
 CHUNKS = (256, 256, 256, 256, 256, 256, 256, 128, 128)
+BACK = (256,) * 9
 TURNS = ("xzy", "zyx", "yxz")
 
 
@@ -759,13 +763,14 @@
 
 
 def enter_kernel(
-    sent, told, gate, up, down, router, rows, gate_pre, up_pre, logits, inner_up,
-    *rest,
+    sent, told, gate, up, down, router, rows, inner_low, grad_gate, grad_up, extra, *rest
 ):
     chunks = len(CHUNKS)
     mids = rest[: 2 * chunks]
     held = rest[2 * chunks : 3 * chunks]
-    told_v, gate_v, up_v, down_v, router_v, send, recv, local, loads = rest[3 * chunks :]
+    (
+        told_v, gate_v, up_v, down_v, router_v, gate_pre, up_pre, logits, inner_up, send, recv, local, loads,
+    ) = rest[3 * chunks :]
     me = Place()
     go = Copies(send, recv, local)
     route = Route(me, go)
@@ -775,66 +780,85 @@
             ((told, told_v), (down, down_v), (gate, gate_v), (up, up_v), (router, router_v))
         )
     ]
-    for pull in pulls:
-        pull.start()
     greet(route.everyone())
     starts = [sum(CHUNKS[:n]) for n in range(chunks)]
     sent_on = [None] * chunks
+    outs = []
     width = sent.shape[-1]
     total = told_v.shape[0]
+    experts = router.shape[1]
+    index = me.expert()
     block = 256
 
-    def cotangent_block(n):
+    def cotangent(n):
         at = pl.ds(n * block, block)
         inner_up[at] = dot_nt(told_v[at, :width], down_v[...])
 
-    def multiply(n, first):
+    def multiply(n, close=False):
+        route.wait(sent_on[n])
+        outs.append(go.keep(held[n], columns(rows, starts[n], CHUNKS[n])))
         cols = pl.ds(starts[n], CHUNKS[n])
         flat = held[n].reshape(total, CHUNKS[n])
 
         def step(m, _):
             at = pl.ds(pl.multiple_of(m * block, block), block)
             part = flat[at]
+            terms = []
             for out, weight in ((gate_pre, gate_v), (up_pre, up_v), (logits, router_v)):
                 term = dot_nn(part, weight[cols])
-                out[at] = term if first else out[at] + term
+                if n > 0:
+                    term = out[at] + term
+                if not close:
+                    out[at] = term
+                terms.append(term)
+            if close:
+                finish(at, *terms)
             return 0
 
         lax.fori_loop(0, total // block, step, 0)
 
-    outs = []
-    pending = list(range(total // block))
-    done = False
-    first = True
+    def finish(at, before_gate, before_up, row_logits):
+        row_logits = jnp.where(told_v[at, width:] > 0, row_logits, MASKED)
+        powers = jnp.exp(row_logits - jnp.max(row_logits, axis=-1, keepdims=True))
+        lane = lax.broadcasted_iota(jnp.int32, (1, experts), 1) == index
+        prob = jnp.sum(jnp.where(lane, powers, 0.0), axis=-1, keepdims=True) / jnp.sum(
+            powers, axis=-1, keepdims=True
+        )
+        back = inner_up[at]
+        sigmoid = 1.0 / (1.0 + jnp.exp(-before_gate))
+        silu = before_gate * sigmoid
+        inner = silu * before_up
+        gate_up = jnp.sum(inner * back, axis=-1, keepdims=True)
+        inner_low[at] = (prob * inner).astype(BF16)
+        back = prob * back
+        grad_gate[at] = (back * before_up * sigmoid * (1.0 + before_gate * (1.0 - sigmoid))).astype(BF16)
+        grad_up[at] = (back * silu).astype(BF16)
+        high = gate_up.astype(BF16).astype(F32)
+        extra[at, :experts] = jnp.where(lane, high, 0.0).astype(BF16)
+        extra[at, experts:] = jnp.where(lane, gate_up - high, 0.0).astype(BF16)
+
+    blocks = list(range(total // block))
     for triple, crossing in ORDER:
         for n in range(3 * triple, 3 * triple + 3):
-            axis = TURNS[n % 3][crossing]
             src = columns(sent, starts[n], CHUNKS[n]) if crossing == 0 else mids[2 * n + crossing - 1]
             dst = held[n] if crossing == 2 else mids[2 * n + crossing]
             if crossing > 0:
                 route.wait(sent_on[n])
-            sent_on[n] = route.send(axis, src, dst)
+            sent_on[n] = route.send(TURNS[n % 3][crossing], src, dst)
+            if crossing == 2 and triple > 0:
+                multiply(n - 3)
+            elif blocks and triple + crossing > 1:
+                cotangent(blocks.pop(0))
         if (triple, crossing) == (1, 0):
+            for pull in pulls:
+                pull.start()
             for pull in pulls[:2]:
                 pull.wait()
-        if pending and (triple, crossing) not in ((0, 0),):
-            cotangent_block(pending.pop(0))
         if (triple, crossing) == (2, 1):
-            while pending:
-                cotangent_block(pending.pop(0))
             for pull in pulls[2:]:
                 pull.wait()
-        if (triple, crossing) in ((1, 2), (2, 2)):
-            ready = triple - 1
-            for n in range(3 * ready, 3 * ready + 3):
-                route.wait(sent_on[n])
-                outs.append(go.keep(held[n], columns(rows, starts[n], CHUNKS[n])))
-                multiply(n, first)
-                first = False
     for n in range(chunks - 3, chunks):
-        route.wait(sent_on[n])
-        outs.append(go.keep(held[n], columns(rows, starts[n], CHUNKS[n])))
-        multiply(n, first)
+        multiply(n, close=n == chunks - 1)
     for out in outs:
         out.wait()
     go.finish()
@@ -846,16 +870,17 @@
     cap = slots // math.prod(DIMS)
     lead = (*DIMS, cap)
     chunks = len(CHUNKS)
-    rows, gate_pre, up_pre, logits, inner_up = pl.pallas_call(
+    low = jax.ShapeDtypeStruct((slots, hidden), BF16)
+    rows, *rest = pl.pallas_call(
         enter_kernel,
         name="enter_experts",
         cost_estimate=cost(60),
         out_shape=(
             jax.ShapeDtypeStruct((*lead, width), BF16),
-            jax.ShapeDtypeStruct((slots, hidden), F32),
-            jax.ShapeDtypeStruct((slots, hidden), F32),
-            jax.ShapeDtypeStruct((slots, experts), F32),
-            jax.ShapeDtypeStruct((slots, hidden), F32),
+            low,
+            low,
+            low,
+            jax.ShapeDtypeStruct((slots, 2 * experts), BF16),
         ),
         in_specs=[ANY] * 6,
         out_specs=(ANY, VMEM, VMEM, VMEM, VMEM),
@@ -867,6 +892,10 @@
             pltpu.VMEM(up.shape, BF16),
             pltpu.VMEM(down.shape, BF16),
             pltpu.VMEM(router.shape, BF16),
+            pltpu.VMEM((slots, hidden), F32),
+            pltpu.VMEM((slots, hidden), F32),
+            pltpu.VMEM((slots, experts), F32),
+            pltpu.VMEM((slots, hidden), F32),
             pltpu.SemaphoreType.DMA((13 * chunks,)),
             pltpu.SemaphoreType.DMA((13 * chunks,)),
             pltpu.SemaphoreType.DMA((4 * chunks,)),
@@ -876,7 +905,141 @@
             collective_id=6, has_side_effects=True, vmem_limit_bytes=58 << 20
         ),
     )(sent.reshape(*lead, width), told, gate, up, down, router)
-    return rows.reshape(slots, width), gate_pre, up_pre, logits, inner_up
+    return rows.reshape(slots, width), *rest
+
+
+def leave_kernel(
+    grad_gate, grad_up, extra, inner_low, spread, gate, up, down, summed, expert_out, *rest
+):
+    chunks = len(BACK)
+    source = rest[: chunks - 1]
+    mids = rest[chunks - 1 : 3 * chunks - 1]
+    held = rest[3 * chunks - 1 : 4 * chunks - 1]
+    gate_g, up_g, inner_v, spread_v, gate_v, up_v, down_v, out_v, send, recv, local, loads, puts = rest[4 * chunks - 1 :]
+    me = Place()
+    go = Copies(send, recv, local)
+    route = Route(me, go)
+    starts = [sum(BACK[:n]) for n in range(chunks)]
+    total = gate_g.shape[0]
+    block = 256
+    pulls = {}
+    count = 0
+    for name, a, b in (("gg", grad_gate, gate_g), ("gu", grad_up, up_g)):
+        pulls[name] = pltpu.make_async_copy(a, b, loads.at[count])
+        count += 1
+    for n in range(chunks - 1):
+        cols = pl.ds(starts[n], BACK[n])
+        for name, a, b in ((("g", n), gate, gate_v), (("u", n), up, up_v)):
+            pulls[name] = pltpu.make_async_copy(a.at[cols], b.at[cols], loads.at[count])
+            count += 1
+    for name, a, b in (("inner", inner_low, inner_v), ("spread", spread, spread_v), ("down", down, down_v)):
+        pulls[name] = pltpu.make_async_copy(a, b, loads.at[count])
+        count += 1
+    late = ("inner", "spread", "down")
+    for name, pull in pulls.items():
+        if name not in late:
+            pull.start()
+    greet(route.everyone())
+    sent_on = [None] * chunks
+    pushes = []
+
+    def gradient(n):
+        cols = pl.ds(starts[n], BACK[n])
+        for name in (("g", n), ("u", n)):
+            pulls[name].wait()
+        flat = source[n].reshape(total, BACK[n])
+
+        def step(m, _):
+            at = pl.ds(pl.multiple_of(m * block, block), block)
+            flat[at] = (dot_nt(gate_g[at], gate_v[cols]) + dot_nt(up_g[at], up_v[cols])).astype(BF16)
+            return 0
+
+        lax.fori_loop(0, total // block, step, 0)
+
+    def result(m):
+        if m == 0:
+            pulls["inner"].wait()
+            pulls["down"].wait()
+        at = pl.ds(m * block, block)
+        out_v[at] = dot_nn(inner_v[at], down_v[...]).astype(BF16)
+        push = pltpu.make_async_copy(out_v.at[at], expert_out.at[at], puts.at[m])
+        push.start()
+        pushes.append(push)
+
+    def combine(n):
+        route.wait(sent_on[n])
+        summed[:, starts[n] : starts[n] + BACK[n]] = dot_tn(spread_v[...], held[n].reshape(total, BACK[n])[...])
+
+    results = list(range(total // block))
+    for triple, crossing in ORDER:
+        for n in range(3 * triple, 3 * triple + 3):
+            dst = held[n] if crossing == 2 else mids[2 * n + crossing]
+            if crossing > 0:
+                route.wait(sent_on[n])
+                src = mids[2 * n + crossing - 1]
+            elif n == chunks - 1:
+                src = extra
+            else:
+                if n == 0:
+                    pulls["gg"].wait()
+                    pulls["gu"].wait()
+                gradient(n)
+                src = source[n]
+            sent_on[n] = route.send(TURNS[n % 3][crossing], src, dst)
+            if crossing == 2 and triple > 0:
+                if n == 3:
+                    pulls["spread"].wait()
+                combine(n - 3)
+            elif results and triple + crossing > 1 and crossing > 0:
+                result(results.pop(0))
+        if (triple, crossing) == (1, 0):
+            for name in late:
+                pulls[name].start()
+    for n in range(chunks - 3, chunks):
+        combine(n)
+    for push in pushes:
+        push.wait()
+    go.finish()
+
+
+def leave(grad_gate, grad_up, extra, inner_low, spread, gate, up, down):
+    slots, hidden = grad_gate.shape
+    width, tok = gate.shape[0], spread.shape[1]
+    cap = slots // math.prod(DIMS)
+    lead = (*DIMS, cap)
+    chunks = len(BACK)
+    return pl.pallas_call(
+        leave_kernel,
+        name="leave_experts",
+        cost_estimate=cost(60),
+        out_shape=(
+            jax.ShapeDtypeStruct((tok, sum(BACK)), F32),
+            jax.ShapeDtypeStruct((slots, width), BF16),
+        ),
+        in_specs=[ANY] * 8,
+        out_specs=(VMEM, ANY),
+        scratch_shapes=[
+            *(pltpu.VMEM((*lead, w), BF16) for w in BACK[:-1]),
+            *(pltpu.VMEM((*lead, w), BF16) for w in BACK for _ in range(2)),
+            *(pltpu.VMEM((*lead, w), BF16) for w in BACK),
+            pltpu.VMEM(grad_gate.shape, BF16),
+            pltpu.VMEM(grad_up.shape, BF16),
+            pltpu.VMEM(inner_low.shape, BF16),
+            pltpu.VMEM(spread.shape, BF16),
+            pltpu.VMEM(gate.shape, BF16),
+            pltpu.VMEM(up.shape, BF16),
+            pltpu.VMEM(down.shape, BF16),
+            pltpu.VMEM((slots, width), BF16),
+            pltpu.SemaphoreType.DMA((13 * chunks,)),
+            pltpu.SemaphoreType.DMA((13 * chunks,)),
+            pltpu.SemaphoreType.DMA((3 * chunks,)),
+            pltpu.SemaphoreType.DMA((2 * chunks + 3,)),
+            pltpu.SemaphoreType.DMA((4,)),
+        ],
+        compiler_params=pltpu.CompilerParams(
+            collective_id=7, has_side_effects=True, vmem_limit_bytes=58 << 20
+        ),
+    )(grad_gate, grad_up, extra.reshape(*lead, extra.shape[1]), inner_low, spread, gate, up, down)
 
 
 def on_device(
@@ -909,7 +1072,6 @@
     slots = experts * cap
     scale = 1.0 / math.sqrt(hd)
     tokens = doc_ids.shape[1]
-    me = lax.axis_index(both)
 
     lane = lax.broadcasted_iota(jnp.int32, (1, 1, experts), 2)
     chosen = jnp.sum((expert_ids[:, :, None] == lane).astype(F32), axis=1)
@@ -956,49 +1118,18 @@
     moe_input, cot_in = lax.optimization_barrier((moe_input, cot_in))
     sent = dot_nn(spread, moe_input).astype(BF16)
     gate_mat, up_mat, down_mat = gate_weight[0], up_weight[0], down_weight[0]
-    rows, gate_pre, up_pre, row_logits, inner_up = enter(
+    rows, inner_low, grad_gate, grad_up, extra = enter(
         sent, cot_in, gate_mat, up_mat, down_mat, router_weight
+    )
+    summed, expert_out = leave(
+        grad_gate, grad_up, extra, inner_low, spread, gate_mat, up_mat, down_mat
     )
     logits = dot_nn(moe_input, router_weight)
     masked = jnp.where(chosen > 0, logits, MASKED)
     probs = jnp.exp(masked - jnp.max(masked, axis=-1, keepdims=True))
     probs = probs / jnp.sum(probs, axis=-1, keepdims=True)
 
-    cot_rows = cot_in[:, :width]
-    row_logits = jnp.where(cot_in[:, width:] > 0, row_logits, MASKED)
-    row_probs = jnp.exp(row_logits - jnp.max(row_logits, axis=-1, keepdims=True))
-    mine = lax.broadcasted_iota(jnp.int32, (1, experts), 1) == me
-    prob = jnp.sum(jnp.where(mine, row_probs, 0.0), axis=-1, keepdims=True) / jnp.sum(
-        row_probs, axis=-1, keepdims=True
-    )
-    sigmoid = jax.nn.sigmoid(gate_pre)
-    silu = gate_pre * sigmoid
-    inner = silu * up_pre
-    gate_up = jnp.sum(inner * inner_up, axis=-1, keepdims=True)
-    inner_low = (prob * inner).astype(BF16)
-    grad_inner = prob * inner_up
-    grad_gate = (grad_inner * up_pre * sigmoid * (1.0 + gate_pre * (1.0 - sigmoid))).astype(BF16)
-    grad_up = (grad_inner * silu).astype(BF16)
-    grad_rows = (dot_nt(grad_gate, gate_mat) + dot_nt(grad_up, up_mat)).astype(BF16)
-    gate_up_high = gate_up.astype(BF16)
-    gate_up_rest = (gate_up - gate_up_high.astype(F32)).astype(BF16)
-    none = jnp.zeros((), BF16)
-    home_out = jnp.concatenate(
-        [grad_rows, jnp.where(mine, gate_up_high, none), jnp.where(mine, gate_up_rest, none)], axis=1
-    )
-    home = lax.all_to_all(
-        home_out.reshape(experts, cap, width + 2 * experts), both, split_axis=0, concat_axis=0, tiled=True
-    ).reshape(slots, width + 2 * experts)
-    expert_out = dot_nn(inner_low, down_mat).astype(BF16)
-    down_grad = dot_tn(inner_low, cot_rows)
-    gate_grad = dot_tn(rows, grad_gate)
-    up_grad = dot_tn(rows, grad_up)
-    home, down_grad, gate_grad, up_grad = lax.optimization_barrier(
-        (home, down_grad, gate_grad, up_grad)
-    )
-
     upstream = cotangent.astype(F32)
-    summed = dot_tn(spread, home)
     gate_upstream = summed[:, width : width + experts] + summed[:, width + experts :]
     grad_chosen = probs * (gate_upstream - jnp.sum(probs * gate_upstream, axis=-1, keepdims=True))
     grad_logits = grad_chosen.astype(BF16)
@@ -1014,6 +1145,11 @@
     returned = lax.all_to_all(
         expert_out.reshape(experts, cap, width), both, split_axis=0, concat_axis=0, tiled=True
     ).reshape(slots, width)
+
+    cot_rows = cot_in[:, :width]
+    down_grad = dot_tn(inner_low, cot_rows)
+    gate_grad = dot_tn(rows, grad_gate)
+    up_grad = dot_tn(rows, grad_up)
 
     grad_mixed = dot_nn(grad_attn, out_weights).astype(BF16)
     grad_raw, head_gains = attend_back(

time: 486 us -> 488 us (level)
  Pallas kernels: 295 us -> 364 us
  waiting for transfers between devices: 30.9 us -> 0.01 us
  other arithmetic: 31 us -> 17 us
  matrix products: 79.6 us -> 70.5 us
  starting transfers between devices: 29.5 us -> 22.5 us
  local copies, waits for them, and re-layouts: 13.5 us -> 7.6 us
    pallas_call x0 -> x1, Pallas kernels: none -> 67.7 us  [leave(): pl.pallas_call(leave_kernel, name='leave_experts', cost_estimate=cost(60)...]
    all_to_all x1 -> x0, waiting for transfers between devices: 30.9 us -> none  [on_device(): lax.all_to_all(home_out.reshape(experts, cap, width + 2 * experts), both,...]
    dot_general x7 -> x6, matrix products: 28.9 us -> 20.8 us  [dot_nn(): lax.dot_general(a, b, (((1,), (0,)), ((), ())), preferred_element_type=F32)]
    dot_general x5 -> x3, matrix products: 18.4 us -> 10.8 us  [dot_nt(): lax.dot_general(a, b, (((1,), (1,)), ((), ())), preferred_element_type=F32)]
    convert_element_type x3 -> x0, other arithmetic: 6.73 us -> none  [the longest x1 6.05 us: on_device(): (grad_inner * up_pre * sigmoid * (1.0 + gate_pre * (1.0 - sigmoid))).asty...]
    dot_general x8 -> x7, matrix products: 32.3 us -> 38.9 us  [dot_tn(): lax.dot_general(a, b, (((0,), (0,)), ((), ())), preferred_element_type=F32)]
    all_to_all x1 -> x0, starting transfers between devices: 6.18 us -> none  [on_device(): lax.all_to_all(home_out.reshape(experts, cap, width + 2 * experts), both,...]
    unnamed x85 -> x82, local copies, waits for them, and re-layouts: 9.5 us -> 4.47 us
  transfers between devices with their start and end apart: 4 -> 3, of which waited for: 1 -> 0; matrix products, arithmetic and copies ran while one was open for 14% -> 11% of each run, Pallas kernels for 38% -> 38%
where the time goes in v7:
time: 488 us; the launch traced here: 483 us
  Pallas kernels  364 us (75%)
  matrix products  70.5 us (14%)
  starting transfers between devices  22.5 us (5%)
  other arithmetic  17 us (3%)
  local copies, waits for them, and re-layouts  7.6 us (2%)
    pallas_call x2, Pallas kernels, reduce(): pl.pallas_call(reduce_kernel, name=f'reduce_rows_{ident}', cost_estimate=...  95 us
    pallas_call x1, Pallas kernels, enter(): pl.pallas_call(enter_kernel, name='enter_experts', cost_estimate=cost(60)...  67.9 us
    pallas_call x1, Pallas kernels, leave(): pl.pallas_call(leave_kernel, name='leave_experts', cost_estimate=cost(60)...  67.7 us
    pallas_call x1, Pallas kernels, scatter(): pl.pallas_call(scatter_kernel, name='scatter_weights', cost_estimate=cost...  49.3 us
    pallas_call x1, Pallas kernels, gather(): pl.pallas_call(gather_kernel, name='gather_weights', cost_estimate=cost(6...  44.6 us
    dot_general x7, matrix products, dot_tn(): lax.dot_general(a, b, (((0,), (0,)), ((), ())), preferred_element_type=F32)  38.9 us
    pallas_call x1, Pallas kernels, share(): pl.pallas_call(share_kernel, name=f'share_rows_{ident}', cost_estimate=co...  24.6 us
    dot_general x6, matrix products, dot_nn(): lax.dot_general(a, b, (((1,), (0,)), ((), ())), preferred_element_type=F32)  20.8 us
  transfers between devices with their start and end apart: 3, of which 0 were waited for; matrix products, arithmetic and copies ran while one was open for 11% of the time, Pallas kernels for 38%

profile of v7, /device:TPU:1, one launch (start us, length us, event | category | flops | bytes accessed | tf_op | source)
XLA Modules:
  0.0 483.4 jit_solution(12521048220326144013)
XLA Ops:
  0.7 0.8 copy.45
  1.5 0.2 convert_reduce_fusion.1
  1.7 0.0 copy-start.20
  1.7 1.2 fusion.17
  3.0 0.5 multiply_multiply_fusion
  3.5 0.7 convert_element_type.96
  4.2 0.1 eq.59
  4.3 0.1 convolution_select_fusion.1
  4.4 0.1 copy.53
  4.5 0.2 fusion.29.spread
  4.8 2.1 fusion.19.tok
  6.9 0.6 broadcast_in_dim.33.doc
  7.5 44.6 %gather_weights.1 = (bf16[4,2,4,2,32,1280]{5,4,3,2,1,0:T(8,128)(2,1)}, bf16[4,2,4,2,32,1024]{5,4,3,2,1,0:T(8,128)(2,1)}, bf16[4,128,2048]{2,1,0:T(8,128)(2,1)}, f32[2,8,256]{2,1,0:T(8,128)}) custom-call(bf16[32,2048]{1,0:T(8,128)(2,1)} %q.1, bf16[32,256]{1,0:T(8,128)(2,1)} %k.1, bf16[32,256]{1,0:T(8,128)(2,1)} %v.1, bf16[32,2048]{1,0:T(8,128)(2,1)} %bitcast.107, ...), custom_call_target="tpu_custom_call" | custom-call | bytes 216000000 | tf_op jit(solution)/shard_map/gather_weights/pallas_call | solution.py:246
  52.1 4.4 fusion
  56.6 6.5 %all-to-all-start = ((bf16[128,8,2176]{2,1,0:T(8,128)(2,1)}), bf16[128,8,2176]{2,1,0:T(8,128)(2,1)}, u32[]{:S(2)}, u32[]{:S(2)}) async-start(bf16[128,8,2176]{2,1,0:T(8,128)(2,1)} %fusion), calls=%async_computation | async-start | bytes 8912896 | tf_op jit(solution)/shard_map/all_to_all | solution.py:1102
  63.1 0.7 slice.27
  63.8 0.3 select_reduce_fusion
  64.1 1.0 fusion.36
  65.1 0.2 pad_maximum_fusion
  65.3 0.2 fusion.30.bias
  65.6 6.1 %fusion.42.raw = f32[512,1280]{1,0:T(8,128)S(1)} fusion(bf16[512,2048]{1,0:T(8,128)(2,1)} %bitcast.120, bf16[2048,1280]{1,0:T(8,128)(2,1)} %bitcast.114), kind=kOutput, calls=%fused_computation.96 | convolution fusion | flops 2684354560 | bytes 9961472 | tf_op jit(solution)/shard_map/dot_general | solution.py:28
  71.7 8.1 %attend.1 = (bf16[512,1024]{1,0:T(8,128)(2,1)S(1)}, bf16[512,256]{1,0:T(8,128)(2,1)S(1)}, f32[2,8,256,256]{3,2,1,0:T(8,128)S(1)}, bf16[512,1024]{1,0:T(8,128)(2,1)S(1)}) custom-call(f32[512,1280]{1,0:T(8,128)S(1)} %fusion.42.raw, f32[2,256,256]{2,1,0:T(8,128)S(1)} %fusion.30.bias, f32[512,128]{1,0:T(8,128)S(1)} %get-tuple-element.98.cosine, ...), custom_call_target="tpu_custom_call" | custom-call | bytes 28800000 | tf_op jit(solution)/shard_map/attend/pallas_call | solution.py:601
  79.9 2.4 convolution_convert_fusion.4
  82.3 0.3 copy-done.6
  82.5 48.1 %reduce_rows_2.1 = f32[128,2048]{1,0:T(8,128)S(1)} custom-call(bf16[4,128,2048]{2,1,0:T(8,128)(2,1)S(1)} %bitcast.89), custom_call_target="tpu_custom_call" | custom-call | bytes 54000000 | tf_op jit(solution)/shard_map/reduce_rows_2/pallas_call | solution.py:345
  130.7 0.6 pad.3.clone
  131.3 0.2 multiply_reduce_fusion.2
  131.5 0.6 multiply_multiply_fusion.1
  132.1 0.5 copy-done.8
  132.6 1.0 multiply_convert_fusion
  133.6 4.5 convolution_convert_fusion.3
  138.0 0.4 fusion.41
  138.4 67.9 %enter_experts.1 = (bf16[4,2,4,2,2,8,2048]{6,5,4,3,2,1,0:T(8,128)(2,1)}, bf16[1024,768]{1,0:T(8,128)(2,1)}, bf16[1024,768]{1,0:T(8,128)(2,1)}, bf16[1024,768]{1,0:T(8,128)(2,1)}, bf16[1024,256]{1,0:T(8,128)(2,1)}) custom-call(bf16[4,2,4,2,2,8,2048]{6,5,4,3,2,1,0:T(8,128)(2,1)} %bitcast.95, bf16[1024,2176]{1,0:T(8,128)(2,1)} %bitcast.11.told, ...), custom_call_target="tpu_custom_call" | custom-call | bytes 216000000 | tf_op jit(solution)/shard_map/enter_experts/pallas_call | solution.py:874
  206.3 8.8 %fusion.5 = f32[1,768,2048]{2,1,0:T(8,128)} fusion(bf16[1024,768]{1,0:T(8,128)(2,1)} %get-tuple-element.56.inner_low, bf16[1024,2176]{1,0:T(8,128)(2,1)} %bitcast.11.told), kind=kOutput, calls=%fused_computation.7 | convolution fusion | flops 3221225472 | bytes 12058624 | tf_op jit(solution)/shard_map/dot_general | solution.py:24
  215.2 0.2 fusion.38
  215.4 67.7 %leave_experts.1 = (f32[128,2304]{1,0:T(8,128)}, bf16[1024,2048]{1,0:T(8,128)(2,1)}) custom-call(bf16[1024,768]{1,0:T(8,128)(2,1)} %get-tuple-element.53.grad_gate, bf16[1024,768]{1,0:T(8,128)(2,1)} %get-tuple-element.54.grad_up, bf16[4,2,4,2,2,8,256]{6,5,4,3,2,1,0:T(8,128)(2,1)} %bitcast.106, bf16[1024,768]{1,0:T(8,128)(2,1)} %get-tuple-element.56.inner_low, ...), custom_call_target="tpu_custom_call" | custom-call | bytes 216000000 | tf_op jit(solution)/shard_map/leave_experts/pallas_call | solution.py:1011
  283.1 1.1 multiply_reduce_fusion.3
  284.2 2.1 convolution_convert_fusion.6
  286.3 2.8 multiply_reduce_fusion
  289.1 6.3 %all-to-all-start.1 = ((bf16[128,16,128]{2,1,0:T(8,128)(2,1)}), bf16[128,16,128]{2,1,0:T(8,128)(2,1)}, u32[]{:S(2)}, u32[]{:S(2)}) async-start(bf16[128,16,128]{2,1,0:T(8,128)(2,1)} %bitcast.105), calls=%async_computation.1 | async-start | bytes 1048576 | tf_op jit(solution)/shard_map/all_to_all | solution.py:1143
  295.4 3.2 fusion.40
  298.6 24.6 %share_rows_3.1 = bf16[4,128,2048]{2,1,0:T(8,128)(2,1)} custom-call(bf16[128,2048]{1,0:T(8,128)(2,1)} %get-tuple-element.78.tok), custom_call_target="tpu_custom_call" | custom-call | bytes 46800000 | tf_op jit(solution)/shard_map/share_rows_3/pallas_call | solution.py:295
  323.2 9.0 %convolution_bitcast_fusion = f32[1,2048,768]{2,1,0:T(8,128)} fusion(bf16[1024,2048]{1,0:T(8,128)(2,1)} %bitcast.118, bf16[1024,768]{1,0:T(8,128)(2,1)} %get-tuple-element.54.grad_up), kind=kOutput, calls=%fused_computation.8 | convolution fusion | flops 3221225472 | bytes 12058624 | tf_op jit(solution)/shard_map/dot_general | solution.py:24
  332.2 5.5 %convolution_bitcast_fusion.1 = f32[1,2048,768]{2,1,0:T(8,128)} fusion(bf16[1024,2048]{1,0:T(8,128)(2,1)S(1)} %bitcast.119, bf16[1024,768]{1,0:T(8,128)(2,1)S(1)} %copy-done.19), kind=kOutput, calls=%fused_computation.9 | convolution fusion | flops 3221225472 | bytes 12058624 | tf_op jit(solution)/shard_map/dot_general | solution.py:24
  337.7 1.2 convert_reduce_fusion.piece
  338.9 9.7 %all-to-all-start.2 = ((bf16[128,8,2048]{2,1,0:T(8,128)(2,1)}), bf16[128,8,2048]{2,1,0:T(8,128)(2,1)}, u32[]{:S(2)}, u32[]{:S(2)}) async-start(bf16[128,8,2048]{2,1,0:T(8,128)(2,1)} %bitcast.102), calls=%async_computation.2 | async-start | bytes 8388608 | tf_op jit(solution)/shard_map/all_to_all | solution.py:1145
  348.7 5.3 %convolution_convert_fusion.7.grad_mixed = bf16[512,1024]{1,0:T(8,128)(2,1)S(1)} fusion(bf16[512,2048]{1,0:T(8,128)(2,1)} %bitcast.103, bf16[2048,1024]{1,0:T(8,128)(2,1)} %bitcast.116), kind=kOutput, calls=%fused_computation.25 | convolution fusion | flops 2148007936 | bytes 7340032 | tf_op jit(solution)/shard_map/dot_general | solution.py:28
  354.0 6.8 %attend_back.1 = (bf16[512,1280]{1,0:T(8,128)(2,1)S(1)}, f32[2,128]{1,0:T(2,128)S(1)}) custom-call(f32[512,1280]{1,0:T(8,128)S(1)} %fusion.42.raw, f32[512,128]{1,0:T(8,128)S(1)} %get-tuple-element.98.cosine, f32[512,128]{1,0:T(8,128)S(1)} %get-tuple-element.99.signed, f32[1,128]{1,0:T(1,128)S(1)} %bitcast.92, f32[1,128]{1,0:T(1,128)S(1)} %bitcast.94, ...), custom_call_target="tpu_custom_call" | custom-call | bytes 50400000 | tf_op jit(solution)/shard_map/attend_back/pallas_call | solution.py:678
  360.9 5.7 %convolution_convert_fusion.5 = bf16[512,2048]{1,0:T(8,128)(2,1)S(1)} fusion(bf16[512,1280]{1,0:T(8,128)(2,1)S(1)} %get-tuple-element.64, bf16[2048,1280]{1,0:T(8,128)(2,1)} %bitcast.115), kind=kOutput, calls=%fused_computation.13 | convolution fusion | flops 2685403136 | bytes 8650752 | tf_op jit(solution)/shard_map/dot_general | solution.py:20
  366.6 46.9 %reduce_rows_4.1 = f32[128,2048]{1,0:T(8,128)S(1)} custom-call(bf16[4,128,2048]{2,1,0:T(8,128)(2,1)S(1)} %bitcast.88), custom_call_target="tpu_custom_call" | custom-call | bytes 54000000 | tf_op jit(solution)/shard_map/reduce_rows_4/pallas_call | solution.py:345
  413.5 0.3 fusion.25
  413.8 0.1 maximum_maximum_fusion.gains
  413.9 2.4 convolution_convert_fusion.2
  416.3 3.2 convolution_convert_fusion
  419.5 49.3 %scatter_weights.1 = (f32[32,2048]{1,0:T(8,128)S(1)}, f32[32,256]{1,0:T(8,128)S(1)}, f32[32,256]{1,0:T(8,128)S(1)}, f32[32,2048]{1,0:T(8,128)S(1)}, f32[40,128]{...) custom-call(bf16[4,2,4,2,32,1280]{5,4,3,2,1,0:T(8,128)(2,1)S(1)} %bitcast.86, ...), custom_call_target="tpu_custom_call" | custom-call | bytes 288000000 | tf_op jit(solution)/shard_map/scatter_weights/pallas_call | solution.py:527
  468.8 0.5 slice_bitcast_fusion.2
  469.4 0.6 slice_bitcast_fusion
  470.0 1.1 bitcast_convert_fusion
  471.0 1.4 fusion.22
  472.5 7.8 %fusion.14 = bf16[128,2048]{1,0:T(8,128)(2,1)} fusion(f32[128,2048]{1,0:T(8,128)S(1)} %copy-done.10, bf16[128,8,2048]{2,1,0:T(8,128)(2,1)} %all-to-all-done.2, f32[128,128]{0,1:T(8,128)S(1)} %convolution_select_fusion.1, f32[8]{0:T(128)S(1)} %copy-done.30), kind=kOutput, calls=%fused_computation.17 | convolution fusion | flops 537526272 | bytes 5832736 | tf_op jit(solution)/shard_map/dot_general | solution.py:24
  480.3 0.7 copy.72
  481.0 0.6 copy.73
  481.6 0.6 copy.74
  482.3 0.7 copy.75
  (86 shorter events, 0.3 us)
Async XLA Ops:
  0.7 3.5 copy-start.29
  1.7 2.7 copy-start.20
  3.5 53.1 %copy-start.25 = (f32[128]{0:T(128)}, f32[128]{0:T(128)S(1)}, u32[]{:S(2)}) copy-start(f32[128]{0:T(128)S(1)} %get-tuple-element.92) | copy-start | bytes 1540
  4.3 52.3 %copy-start.24 = (f32[1024]{0:T(1024)}, f32[1024]{0:T(1024)S(1)}, u32[]{:S(2)}) copy-start(f32[1024]{0:T(1024)S(1)} %eq.59) | copy-start | bytes 12292
  4.7 51.8 %copy-start.17 = (bf16[1024,128]{1,0:T(8,128)(2,1)}, bf16[1024,128]{1,0:T(8,128)(2,1)S(1)}, u32[]{:S(2)}) copy-start(bf16[1024,128]{1,0:T(8,128)(2,1)S(1)} %fusion.29.spread) | copy-start | bytes 786436
  56.6 77.0 %all-to-all-start = ((bf16[128,8,2176]{2,1,0:T(8,128)(2,1)}), bf16[128,8,2176]{2,1,0:T(8,128)(2,1)}, u32[]{:S(2)}, u32[]{:S(2)}) async-start(bf16[128,8,2176]{2,1,0:T(8,128)(2,1)} %fusion), calls=%async_computation | async-start | bytes 8912896 | tf_op jit(solution)/shard_map/all_to_all | solution.py:1102
  65.6 6.2 %copy-start.4 = (f32[128]{0:T(128)S(1)}, f32[128]{0:T(128)}, u32[]{:S(2)}) copy-start(f32[128]{0:T(128)} %param.24) | copy-start | bytes 1540
  65.6 6.2 %copy-start.5 = (f32[128]{0:T(128)S(1)}, f32[128]{0:T(128)}, u32[]{:S(2)}) copy-start(f32[128]{0:T(128)} %param.25) | copy-start | bytes 1540
  65.6 14.3 %copy-start.34 = (bf16[4,2,4,2,32,1024]{5,4,3,2,1,0:T(8,128)(2,1)S(1)}, bf16[4,2,4,2,32,1024]{5,4,3,2,1,0:T(8,128)(2,1)}, u32[]{:S(2)}) copy-start(bf16[4,2,4,2,32,1024]{5,4,3,2,1,0:T(8,128)(2,1)} %get-tuple-element.49) | copy-start | bytes 12582916
  79.8 2.4 copy-start
  79.9 2.4 copy-start.2
  79.9 2.7 copy-start.6
  79.9 51.4 %copy-start.11 = (bf16[128,2048]{1,0:T(8,128)(2,1)S(1)}, bf16[128,2048]{1,0:T(8,128)(2,1)}, u32[]{:S(2)}) copy-start(bf16[128,2048]{1,0:T(8,128)(2,1)} %param.16) | copy-start | bytes 1572868
  82.5 50.1 %copy-start.22 = (f32[2048]{0:T(1024)S(1)}, f32[2048]{0:T(1024)}, u32[]{:S(2)}) copy-start(f32[2048]{0:T(1024)} %param.26) | copy-start | bytes 24580
  131.5 1.1 copy-start.8
  132.1 0.5 copy-start.27
  133.6 4.5 copy-start.13
  133.6 4.5 copy-start.14
  133.6 4.5 copy-start.21
  215.3 70.9 %copy-start.9 = (f32[128,2048]{1,0:T(8,128)S(1)}, f32[128,2048]{1,0:T(8,128)}, u32[]{:S(2)}) copy-start(f32[128,2048]{1,0:T(8,128)} %copy-done.8) | copy-start | bytes 3145732
  215.4 70.9 %copy-start.15 = (bf16[2048,128]{1,0:T(8,128)(2,1)S(1)}, bf16[2048,128]{1,0:T(8,128)(2,1)}, u32[]{:S(2)}) copy-start(bf16[2048,128]{1,0:T(8,128)(2,1)} %router.1) | copy-start | bytes 1572868
  215.4 70.9 %copy-start.28 = (f32[128]{0:T(128)S(1)}, f32[128]{0:T(128)}, u32[]{:S(2)}) copy-start(f32[128]{0:T(128)} %copy-done.27) | copy-start | bytes 1540
  283.1 12.3 %copy-start.33 = (f32[128]{0:T(128)S(1)}, f32[128]{0:T(128)}, u32[]{:S(2)}) copy-start(f32[128]{0:T(128)} %get-tuple-element.93) | copy-start | bytes 1540
  289.1 48.7 %all-to-all-start.1 = ((bf16[128,16,128]{2,1,0:T(8,128)(2,1)}), bf16[128,16,128]{2,1,0:T(8,128)(2,1)}, u32[]{:S(2)}, u32[]{:S(2)}) async-start(bf16[128,16,128]{2,1,0:T(8,128)(2,1)} %bitcast.105), calls=%async_computation.1 | async-start | bytes 1048576 | tf_op jit(solution)/shard_map/all_to_all | solution.py:1143
  323.2 9.1 %copy-start.19 = (bf16[1024,768]{1,0:T(8,128)(2,1)S(1)}, bf16[1024,768]{1,0:T(8,128)(2,1)}, u32[]{:S(2)}) copy-start(bf16[1024,768]{1,0:T(8,128)(2,1)} %get-tuple-element.53.grad_gate) | copy-start | bytes 4718596
  323.2 9.1 %copy-start.35 = (bf16[4,2,4,2,2,8,2048]{6,5,4,3,2,1,0:T(8,128)(2,1)S(1)}, bf16[4,2,4,2,2,8,2048]{6,5,4,3,2,1,0:T(8,128)(2,1)}, u32[]{:S(2)}) copy-start(bf16[4,2,4,2,2,8,2048]{6,5,4,3,2,1,0:T(8,128)(2,1)} %get-tuple-element.73) | copy-start | bytes 12582916
  338.9 133.6 %all-to-all-start.2 = ((bf16[128,8,2048]{2,1,0:T(8,128)(2,1)}), bf16[128,8,2048]{2,1,0:T(8,128)(2,1)}, u32[]{:S(2)}, u32[]{:S(2)}) async-start(bf16[128,8,2048]{2,1,0:T(8,128)(2,1)} %bitcast.102), calls=%async_computation.2 | async-start | bytes 8388608 | tf_op jit(solution)/shard_map/all_to_all | solution.py:1145
  348.7 5.3 %copy-start.1 = (f32[2,8,256,256]{3,2,1,0:T(8,128)S(1)}, f32[2,8,256,256]{3,2,1,0:T(8,128)}, u32[]{:S(2)}) copy-start(f32[2,8,256,256]{3,2,1,0:T(8,128)} %copy-done) | copy-start | bytes 12582916
  348.7 5.3 %copy-start.3 = (bf16[512,1024]{1,0:T(8,128)(2,1)S(1)}, bf16[512,1024]{1,0:T(8,128)(2,1)}, u32[]{:S(2)}) copy-start(bf16[512,1024]{1,0:T(8,128)(2,1)} %copy-done.2) | copy-start | bytes 3145732
  360.9 52.6 %copy-start.12 = (bf16[128,2048]{1,0:T(8,128)(2,1)S(1)}, bf16[128,2048]{1,0:T(8,128)(2,1)}, u32[]{:S(2)}) copy-start(bf16[128,2048]{1,0:T(8,128)(2,1)} %param.16) | copy-start | bytes 1572868
  360.9 52.6 %copy-start.23 = (f32[2048]{0:T(1024)S(1)}, f32[2048]{0:T(1024)}, u32[]{:S(2)}) copy-start(f32[2048]{0:T(1024)} %param.19) | copy-start | bytes 24580
  360.9 52.6 %copy-start.26 = (f32[128]{0:T(128)S(1)}, f32[128]{0:T(128)}, u32[]{:S(2)}) copy-start(f32[128]{0:T(128)} %copy-done.25) | copy-start | bytes 1540
  366.6 47.2 %copy-start.32 = (f32[40]{0:T(128)S(1)}, f32[40]{0:T(128)}, u32[]{:S(2)}) copy-start(f32[40]{0:T(128)} %pad.3.clone) | copy-start | bytes 484
  366.6 47.3 %copy-start.7 = (bf16[512,1024]{1,0:T(8,128)(2,1)S(1)}, bf16[512,1024]{1,0:T(8,128)(2,1)}, u32[]{:S(2)}) copy-start(bf16[512,1024]{1,0:T(8,128)(2,1)} %copy-done.6) | copy-start | bytes 3145732
  366.6 47.3 %copy-start.18 = (bf16[4,128,2048]{2,1,0:T(8,128)(2,1)S(1)}, bf16[4,128,2048]{2,1,0:T(8,128)(2,1)}, u32[]{:S(2)}) copy-start(bf16[4,128,2048]{2,1,0:T(8,128)(2,1)} %share_rows_3.1) | copy-start | bytes 6291460
  413.9 2.4 copy-start.36
  419.5 51.5 %copy-start.16 = (f32[128,2048]{1,0:T(8,128)S(1)}, f32[128,2048]{1,0:T(8,128)}, u32[]{:S(2)}) copy-start(f32[128,2048]{1,0:T(8,128)} %get-tuple-element.79) | copy-start | bytes 3145732
  419.5 51.5 %copy-start.31 = (f32[128]{0:T(128)S(1)}, f32[128]{0:T(128)}, u32[]{:S(2)}) copy-start(f32[128]{0:T(128)} %get-tuple-element.91) | copy-start | bytes 1540
  468.8 3.7 copy-start.10
  468.8 3.7 copy-start.30

commit v8 on v7

--- a/solution.py
+++ b/solution.py
@@ -271,42 +271,78 @@
     )
 
 
-def share_kernel(tok, toks, send, recv, local):
+def share_kernel(tok, part, toks, piece, got_x, sum_x, got_z, sum_z, got_y, send, recv, local):
     me = Place()
-    p = me.y
+    x, yh, z, c, p = me.x, me.yh, me.z, me.c, me.y
     ring = (me.at_y(after(p)), me.at_y(before(p)))
-    greet(ring)
     go = Copies(send, recv, local)
+    route = Route(me, go)
+    greet(route.everyone())
     half = tok.shape[0] // 2
     direct = [go.put(tok, toks.at[p], peer) for peer in ring]
     kept = go.keep(tok, toks.at[p])
+    own = go.keep(part.at[x, :, :, c], got_x.at[x * NC + c])
+    terms = [
+        go.put(part.at[at[0], :, :, at[1]], got_x.at[x * NC + c], peer)
+        for at, peer in route.peers["x"]
+    ]
+
+    def arrived(copies):
+        for copy in copies:
+            copy.wait_recv()
+
+    def added(got):
+        value = got[0].astype(F32)
+        for n in range(1, got.shape[0]):
+            value += got[n].astype(F32)
+        return value
+
+    own.wait()
+    arrived(terms)
+    sum_x[...] = added(got_x)
+    got_z[z] = sum_x[:, z]
+    terms = [go.put(sum_x.at[:, at[0]], got_z.at[z], peer) for at, peer in route.peers["z"]]
     relays = []
     for h, owner in enumerate((before(p), after(p))):
         direct[h].wait_recv()
-        piece = toks.at[owner, pl.ds(h * half, half)]
-        relays.append(go.put(piece, piece, ring[h]))
-    for copy in relays:
-        copy.wait_recv()
+        rows = toks.at[owner, pl.ds(h * half, half)]
+        relays.append(go.put(rows, rows, ring[h]))
+    arrived(terms)
+    sum_z[...] = added(got_z)
+    got_y[p] = sum_z[yh, me.t]
+    terms = [go.put(sum_z.at[at[0], at[1]], got_y.at[p], peer) for at, peer in route.peers["y"]]
+    arrived(terms)
+    piece[...] = added(got_y).astype(piece.dtype)
+    arrived(relays)
     kept.wait()
     go.finish()
 
 
-def share(tokens, ident):
-    toks = pl.pallas_call(
+def share(tokens, part, ident):
+    rows, lanes = part.shape[0] // math.prod(DIMS), part.shape[1]
+    toks, piece = pl.pallas_call(
         share_kernel,
         name=f"share_rows_{ident}",
-        cost_estimate=cost(13),
-        out_shape=jax.ShapeDtypeStruct((RING, *tokens.shape), tokens.dtype),
-        in_specs=[ANY],
-        out_specs=ANY,
+        cost_estimate=cost(20),
+        out_shape=(
+            jax.ShapeDtypeStruct((RING, *tokens.shape), tokens.dtype),
+            jax.ShapeDtypeStruct((rows, lanes), BF16),
+        ),
+        in_specs=[ANY, ANY],
+        out_specs=(ANY, VMEM),
         scratch_shapes=[
-            pltpu.SemaphoreType.DMA((4,)),
-            pltpu.SemaphoreType.DMA((4,)),
-            pltpu.SemaphoreType.DMA((1,)),
+            pltpu.VMEM((NX * NC, NYH, NZ, 2, rows, lanes), BF16),
+            pltpu.VMEM((NYH, NZ, 2, rows, lanes), F32),
+            pltpu.VMEM((NZ, NYH, 2, rows, lanes), F32),
+            pltpu.VMEM((NYH, 2, rows, lanes), F32),
+            pltpu.VMEM((RING, rows, lanes), F32),
+            pltpu.SemaphoreType.DMA((17,)),
+            pltpu.SemaphoreType.DMA((17,)),
+            pltpu.SemaphoreType.DMA((2,)),
         ],
         compiler_params=pltpu.CompilerParams(collective_id=ident, has_side_effects=True),
-    )(tokens)
-    return toks.reshape(RING * tokens.shape[0], tokens.shape[1])
+    )(tokens, part.reshape(*DIMS, rows, lanes))
+    return toks.reshape(RING * tokens.shape[0], tokens.shape[1]), piece
 
 
 def reduce_kernel(part, out, held, own, got, send, recv, local):
@@ -345,7 +381,7 @@
     return pl.pallas_call(
         reduce_kernel,
         name=f"reduce_rows_{ident}",
-        cost_estimate=cost(15),
+        cost_estimate=cost(1),
         out_shape=jax.ShapeDtypeStruct((rows, width), F32),
         in_specs=[ANY],
         out_specs=VMEM,
@@ -364,7 +400,7 @@
 
 
 def scatter_kernel(
-    ga, gb, gains, piece, oq, ok, ov, oo, og, op, ka, kb, da, db, ra, rb, qa, qb, sa, sb, ta, tb, ua, ub, ma, mb,
+    ga, gb, gains, piece, returned, slots, residual, oq, ok, ov, oo, og, op, layer, back_v, slots_v, ka, kb, da, db, ra, rb, qa, qb, sa, sb, ta, tb, ua, ub, ma, mb,
     ring_gains, sum_gains, pair_gains, send, recv, local
 ):
     me = Place()
@@ -436,6 +472,7 @@
     mine = op.at[x, yh, z, c, t]
     held_piece = go.keep(piece, mine)
     pieces = [go.put(piece, mine, sibling)]
+    pulls = [go.keep(returned, back_v), go.keep(slots, slots_v)]
     cross, straight, sums = [[], []], [[], []], [[], []]
     for w, (slab, i, j, one, two, k, d, r, q, s, u) in enumerate(ways):
         for h in range(2):
@@ -447,6 +484,11 @@
             ready(w, 1 + h, 1 - h)
             total(w, 1 + h, 1 - h, ())
             straight[w].append(go.put(k.at[1 + h, 1 - h], r.at[2 + h], one[h]))
+    for pull in pulls:
+        pull.wait()
+    for m in range(4):
+        cols = pl.ds(m * layer.shape[1] // 4, layer.shape[1] // 4)
+        layer[:, cols] = (residual[:, cols] + dot_tn(slots_v[...], back_v[:, cols])).astype(layer.dtype)
     terms = around(1, ring_sum(0, terms), z, round_z)
     arrived(pieces)
     held_piece.wait()
@@ -516,7 +558,7 @@
     go.finish()
 
 
-def scatter(grad_a, grad_b, gains, piece, columns):
+def scatter(grad_a, grad_b, gains, piece, returned, slots, residual, columns):
     rows = grad_a.shape[0] // (NX * NYH * NZ * NC)
     lead = (NX, NYH, NZ, NC, rows)
     widths = (grad_a.shape[1], grad_b.shape[1])
@@ -532,10 +574,13 @@
             *(jax.ShapeDtypeStruct((rows, w), F32) for w in columns),
             jax.ShapeDtypeStruct(gains.shape, F32),
             jax.ShapeDtypeStruct((NX, NYH, NZ, NC, 2, *piece.shape), piece.dtype),
+            jax.ShapeDtypeStruct(residual.shape, BF16),
         ),
-        in_specs=[ANY, ANY, VMEM, ANY],
-        out_specs=(*(VMEM,) * 5, ANY),
+        in_specs=[ANY, ANY, VMEM, ANY, ANY, ANY, VMEM],
+        out_specs=(*(VMEM,) * 5, ANY, VMEM),
         scratch_shapes=[
+            pltpu.VMEM(returned.shape, BF16),
+            pltpu.VMEM(slots.shape, BF16),
             *each((4, 2, RING), BF16),
             *each((4, 2, RING), BF16),
             *each((6, RING), BF16),
@@ -549,12 +594,12 @@
             pltpu.VMEM((3, *gains.shape), F32),
             pltpu.SemaphoreType.DMA((60,)),
             pltpu.SemaphoreType.DMA((60,)),
-            pltpu.SemaphoreType.DMA((17,)),
+            pltpu.SemaphoreType.DMA((19,)),
         ],
         compiler_params=pltpu.CompilerParams(
-            collective_id=5, has_side_effects=True, vmem_limit_bytes=40 << 20
+            collective_id=5, has_side_effects=True, vmem_limit_bytes=48 << 20
         ),
-    )(grad_a.reshape(*lead, widths[0]), grad_b.reshape(*lead, widths[1]), gains, piece)
+    )(grad_a.reshape(*lead, widths[0]), grad_b.reshape(*lead, widths[1]), gains, piece, returned, slots, residual)
 
 
 def unit_rows(values):
@@ -678,7 +723,7 @@
     return pl.pallas_call(
         functools.partial(attend_back_kernel, scale),
         name="attend_back",
-        cost_estimate=cost(14),
+        cost_estimate=cost(1),
         grid=(groups,),
         out_shape=(
             jax.ShapeDtypeStruct((rows, (heads + 2) * hd), BF16),
@@ -1138,36 +1183,41 @@
     grad_norm, moegain_rows = rms_back(residual, moe_gain, grad_moe_input)
     moegain_part = jnp.sum(moegain_rows, axis=0)
     grad_residual = upstream + grad_norm
-    grad_attn = share(grad_residual.astype(BF16), 3)
-    pieces = router_part.astype(BF16).reshape(experts, width // experts, experts)
-    piece = jnp.sum(lax.all_to_all(pieces, both, 0, 0, tiled=True).astype(F32), axis=0)
-    expert_out, grad_attn, piece = lax.optimization_barrier((expert_out, grad_attn, piece))
+    grad_attn, piece = share(grad_residual.astype(BF16), router_part.astype(BF16), 3)
+    expert_out, grad_attn = lax.optimization_barrier((expert_out, grad_attn))
     returned = lax.all_to_all(
         expert_out.reshape(experts, cap, width), both, split_axis=0, concat_axis=0, tiled=True
     ).reshape(slots, width)
 
-    cot_rows = cot_in[:, :width]
-    down_grad = dot_tn(inner_low, cot_rows)
-    gate_grad = dot_tn(rows, grad_gate)
-    up_grad = dot_tn(rows, grad_up)
-
     grad_mixed = dot_nn(grad_attn, out_weights).astype(BF16)
     grad_raw, head_gains = attend_back(
         raw, cosine, signed, query_gain, key_gain, query, kv, attention, grad_mixed, scale
     )
-    grad_normed = reduce(dot_nt(grad_raw, in_weights).astype(BF16), 4)
+    inner_low, rows, cot_in, grad_raw = lax.optimization_barrier(
+        (inner_low, rows, cot_in, grad_raw)
+    )
+    down_grad = dot_tn(inner_low, cot_in[:, :width])
+    gate_grad = dot_tn(rows, grad_gate)
+    up_grad = dot_tn(rows, grad_up)
+    normed_part, down_grad, gate_grad, up_grad = lax.optimization_barrier(
+        (dot_nt(grad_raw, in_weights).astype(BF16), down_grad, gate_grad, up_grad)
+    )
+    grad_normed = reduce(normed_part, 4)
+    grad_normed, returned = lax.optimization_barrier((grad_normed, returned))
     grad_hidden, attngain_rows = rms_back(hidden, attn_gain, grad_normed)
     input_grad = grad_residual + grad_hidden
 
     gains = jnp.concatenate([jnp.sum(attngain_rows, axis=0), moegain_part]).reshape(-1, hd)
     gains = jnp.concatenate([gains, head_gains, jnp.zeros((6, hd), F32)], axis=0)
 
-    layer_out = (residual + dot_tn(spread, returned)).astype(BF16)
-    query_grad, key_grad, value_grad, out_grad, gains, router_grad = scatter(
+    query_grad, key_grad, value_grad, out_grad, gains, router_grad, layer_out = scatter(
         dot_tn(normed, grad_raw).astype(BF16),
         dot_tn(grad_attn, mixed).astype(BF16),
         gains,
-        piece.astype(BF16),
+        piece,
+        returned,
+        spread,
+        residual,
         (nq * hd, nkv * hd, nkv * hd, nq * hd),
     )
     at = width // hd

time: 488 us -> 445 us (0.912)
  Pallas kernels: 364 us -> 345 us
  matrix products: 70.5 us -> 59.6 us
  starting transfers between devices: 22.5 us -> 15.1 us
    pallas_call x2, Pallas kernels: 95 us -> 78 us  [reduce(): pl.pallas_call(reduce_kernel, name=f'reduce_rows_{ident}', cost_estimate=...]
    dot_general x7 -> x6, matrix products: 38.9 us -> 29.8 us  [dot_tn(): lax.dot_general(a, b, (((0,), (0,)), ((), ())), preferred_element_type=F32)]
    all_to_all x1 -> x0, starting transfers between devices: 6.31 us -> none  [on_device(): lax.all_to_all(pieces, both, 0, 0, tiled=True).astype(F32)]
  transfers between devices with their start and end apart: 3 -> 2, of which waited for: 0 -> 0; matrix products, arithmetic and copies ran while one was open for 11% -> 12% of each run, Pallas kernels for 38% -> 21%
where the time goes in v8:
time: 445 us; the launch traced here: 441 us
  Pallas kernels  345 us (78%)
  matrix products  59.6 us (13%)
  starting transfers between devices  15.1 us (3%)
  other arithmetic  13.1 us (3%)
  local copies, waits for them, and re-layouts  7.12 us (2%)
    pallas_call x2, Pallas kernels, reduce(): pl.pallas_call(reduce_kernel, name=f'reduce_rows_{ident}', cost_estimate=...  78 us
    pallas_call x1, Pallas kernels, enter(): pl.pallas_call(enter_kernel, name='enter_experts', cost_estimate=cost(60)...  68 us
    pallas_call x1, Pallas kernels, leave(): pl.pallas_call(leave_kernel, name='leave_experts', cost_estimate=cost(60)...  67.5 us
    pallas_call x1, Pallas kernels, scatter(): pl.pallas_call(scatter_kernel, name='scatter_weights', cost_estimate=cost...  48.9 us
    pallas_call x1, Pallas kernels, gather(): pl.pallas_call(gather_kernel, name='gather_weights', cost_estimate=cost(6...  44.6 us
    dot_general x6, matrix products, dot_tn(): lax.dot_general(a, b, (((0,), (0,)), ((), ())), preferred_element_type=F32)  29.8 us
    pallas_call x1, Pallas kernels, share(): pl.pallas_call(share_kernel, name=f'share_rows_{ident}', cost_estimate=co...  22.8 us
    dot_general x6, matrix products, dot_nn(): lax.dot_general(a, b, (((1,), (0,)), ((), ())), preferred_element_type=F32)  19.8 us
  transfers between devices with their start and end apart: 2, of which 0 were waited for; matrix products, arithmetic and copies ran while one was open for 12% of the time, Pallas kernels for 21%

profile of v8, /device:TPU:1, one launch (start us, length us, event | category | flops | bytes accessed | tf_op | source)
XLA Modules:
  0.0 440.9 jit_solution(16367418683029227018)
XLA Ops:
  0.7 0.8 copy.38
  1.5 0.2 convert_reduce_fusion
  1.8 0.1 convolution_select_fusion.1
  1.9 0.1 copy.40
  2.0 0.1 eq.55
  2.1 1.2 fusion.3
  3.4 0.7 convert_element_type.85
  4.0 0.2 fusion.15.spread.slots
  4.3 2.1 fusion.5.tok
  6.4 0.6 broadcast_in_dim.33.doc
  7.0 44.6 %gather_weights.1 = (bf16[4,2,4,2,32,1280]{5,4,3,2,1,0:T(8,128)(2,1)}, bf16[4,2,4,2,32,1024]{5,4,3,2,1,0:T(8,128)(2,1)}, bf16[4,128,2048]{2,1,0:T(8,128)(2,1)}, f32[2,8,256]{2,1,0:T(8,128)}) custom-call(bf16[32,2048]{1,0:T(8,128)(2,1)} %q.1, bf16[32,256]{1,0:T(8,128)(2,1)} %k.1, bf16[32,256]{1,0:T(8,128)(2,1)} %v.1, bf16[32,2048]{1,0:T(8,128)(2,1)} %bitcast.98, ...), custom_call_target="tpu_custom_call" | custom-call | bytes 216000000 | tf_op jit(solution)/shard_map/gather_weights/pallas_call | solution.py:246
  51.6 3.4 fusion
  55.0 6.5 %all-to-all-start = ((bf16[128,8,2176]{2,1,0:T(8,128)(2,1)}), bf16[128,8,2176]{2,1,0:T(8,128)(2,1)}, u32[]{:S(2)}, u32[]{:S(2)}) async-start(bf16[128,8,2176]{2,1,0:T(8,128)(2,1)} %fusion), calls=%async_computation | async-start | bytes 8912896 | tf_op jit(solution)/shard_map/all_to_all | solution.py:1147
  61.6 0.7 slice.27
  62.4 0.3 select_reduce_fusion
  62.7 1.0 fusion.19
  63.7 0.2 pad_maximum_fusion
  63.9 0.2 fusion.16.bias
  64.1 0.0 copy-start.8
  64.1 6.1 %fusion.25.raw = f32[512,1280]{1,0:T(8,128)S(1)} fusion(bf16[512,2048]{1,0:T(8,128)(2,1)} %bitcast.111, bf16[2048,1280]{1,0:T(8,128)(2,1)} %bitcast.105), kind=kOutput, calls=%fused_computation.84 | convolution fusion | flops 2684354560 | bytes 9961472 | tf_op jit(solution)/shard_map/dot_general | solution.py:28
  70.3 8.1 %attend.1 = (bf16[512,1024]{1,0:T(8,128)(2,1)S(1)}, bf16[512,256]{1,0:T(8,128)(2,1)S(1)}, f32[2,8,256,256]{3,2,1,0:T(8,128)S(1)}, bf16[512,1024]{1,0:T(8,128)(2,1)S(1)}) custom-call(f32[512,1280]{1,0:T(8,128)S(1)} %fusion.25.raw, f32[2,256,256]{2,1,0:T(8,128)S(1)} %fusion.16.bias, f32[512,128]{1,0:T(8,128)S(1)} %get-tuple-element.122.cosine, ...), custom_call_target="tpu_custom_call" | custom-call | bytes 28800000 | tf_op jit(solution)/shard_map/attend/pallas_call | solution.py:646
  78.4 0.0 copy-start.4
  78.4 2.4 convolution_convert_fusion.4
  80.9 0.0 copy-start.21
  80.9 48.3 %reduce_rows_2.1 = f32[128,2048]{1,0:T(8,128)S(1)} custom-call(bf16[4,128,2048]{2,1,0:T(8,128)(2,1)S(1)} %bitcast.79), custom_call_target="tpu_custom_call" | custom-call | bytes 3600000 | tf_op jit(solution)/shard_map/reduce_rows_2/pallas_call | solution.py:381
  129.2 0.1 pad.3.clone
  129.3 0.2 multiply_reduce_fusion.2
  129.5 1.0 multiply_convert_fusion
  130.5 4.4 %convolution_convert_fusion.3 = bf16[1024,2048]{1,0:T(8,128)(2,1)} fusion(bf16[128,2048]{1,0:T(8,128)(2,1)} %multiply_convert_fusion, f32[1024]{0:T(1024)S(1)} %eq.55, f32[128,128]{1,0:T(8,128)S(1)} %copy.40), kind=kOutput, calls=%fused_computation.6 | convolution fusion | flops 539099136 | bytes 4788224 | tf_op jit(solution)/shard_map/dot_general | solution.py:28
  134.9 0.4 fusion.24
  135.3 0.2 fusion.21
  135.5 68.0 %enter_experts.1 = (bf16[4,2,4,2,2,8,2048]{6,5,4,3,2,1,0:T(8,128)(2,1)}, bf16[1024,768]{1,0:T(8,128)(2,1)}, bf16[1024,768]{1,0:T(8,128)(2,1)}, bf16[1024,768]{1,0:T(8,128)(2,1)}, bf16[1024,256]{1,0:T(8,128)(2,1)}) custom-call(bf16[4,2,4,2,2,8,2048]{6,5,4,3,2,1,0:T(8,128)(2,1)} %bitcast.85, bf16[1024,2176]{1,0:T(8,128)(2,1)} %bitcast.11.told, ...), custom_call_target="tpu_custom_call" | custom-call | bytes 216000000 | tf_op jit(solution)/shard_map/enter_experts/pallas_call | solution.py:919
  203.5 0.0 copy-start.15
  203.5 67.5 %leave_experts.1 = (f32[128,2304]{1,0:T(8,128)}, bf16[1024,2048]{1,0:T(8,128)(2,1)}) custom-call(bf16[1024,768]{1,0:T(8,128)(2,1)} %get-tuple-element.70.grad_gate, bf16[1024,768]{1,0:T(8,128)(2,1)} %get-tuple-element.71.grad_up, bf16[4,2,4,2,2,8,256]{6,5,4,3,2,1,0:T(8,128)(2,1)} %bitcast.97, bf16[1024,768]{1,0:T(8,128)(2,1)} %get-tuple-element.79.inner_low, ...), custom_call_target="tpu_custom_call" | custom-call | bytes 216000000 | tf_op jit(solution)/shard_map/leave_experts/pallas_call | solution.py:1056
  271.0 0.0 copy-start.18
  271.0 1.1 multiply_reduce_fusion.3
  272.1 2.1 convolution_convert_fusion.6
  274.2 1.9 multiply_reduce_fusion
  276.1 1.5 fusion.23
  277.6 22.8 %share_rows_3.1 = (bf16[4,128,2048]{2,1,0:T(8,128)(2,1)}, bf16[16,128]{1,0:T(8,128)(2,1)}) custom-call(bf16[128,2048]{1,0:T(8,128)(2,1)} %get-tuple-element.102.tok, bf16[4,2,4,2,2,16,128]{6,5,4,3,2,1,0:T(8,128)(2,1)} %bitcast.96), custom_call_target="tpu_custom_call" | custom-call | bytes 72000000 | tf_op jit(solution)/shard_map/share_rows_3/pallas_call | solution.py:323
  300.5 8.5 %all-to-all-start.1 = ((bf16[128,8,2048]{2,1,0:T(8,128)(2,1)}), bf16[128,8,2048]{2,1,0:T(8,128)(2,1)}, u32[]{:S(2)}, u32[]{:S(2)}) async-start(bf16[128,8,2048]{2,1,0:T(8,128)(2,1)} %bitcast.94), calls=%async_computation.1 | async-start | bytes 8388608 | tf_op jit(solution)/shard_map/all_to_all | solution.py:1188
  309.0 0.0 copy-start.1
  309.0 0.0 copy-start.5
  309.0 5.3 %convolution_convert_fusion.7.grad_mixed = bf16[512,1024]{1,0:T(8,128)(2,1)S(1)} fusion(bf16[512,2048]{1,0:T(8,128)(2,1)} %bitcast.113, bf16[2048,1024]{1,0:T(8,128)(2,1)} %bitcast.107), kind=kOutput, calls=%fused_computation.17 | convolution fusion | flops 2148007936 | bytes 7340032 | tf_op jit(solution)/shard_map/dot_general | solution.py:28
  314.3 6.7 %attend_back.1 = (bf16[512,1280]{1,0:T(8,128)(2,1)S(1)}, f32[2,128]{1,0:T(2,128)S(1)}) custom-call(f32[512,1280]{1,0:T(8,128)S(1)} %copy-done.1, f32[512,128]{1,0:T(8,128)S(1)} %get-tuple-element.122.cosine, f32[512,128]{1,0:T(8,128)S(1)} %get-tuple-element.123.signed, f32[1,128]{1,0:T(1,128)S(1)} %bitcast.82, f32[1,128]{1,0:T(1,128)S(1)} %bitcast.84, ...), custom_call_target="tpu_custom_call" | custom-call | bytes 3600000 | tf_op jit(solution)/shard_map/attend_back/pallas_call | solution.py:723
  321.1 5.8 %convolution_convert_fusion.5 = bf16[512,2048]{1,0:T(8,128)(2,1)S(1)} fusion(bf16[512,1280]{1,0:T(8,128)(2,1)S(1)} %get-tuple-element.78, bf16[2048,1280]{1,0:T(8,128)(2,1)} %bitcast.106), kind=kOutput, calls=%fused_computation.8 | convolution fusion | flops 2685403136 | bytes 8650752 | tf_op jit(solution)/shard_map/dot_general | solution.py:20
  326.9 5.5 %fusion.27 = f32[2048,768]{1,0:T(8,128)} fusion(bf16[1024,2048]{1,0:T(8,128)(2,1)S(1)} %bitcast.109, bf16[1024,768]{1,0:T(8,128)(2,1)S(1)} %copy-done.20), kind=kOutput, calls=%fused_computation.86 | convolution fusion | flops 3221225472 | bytes 12058624 | tf_op jit(solution)/shard_map/dot_general | solution.py:24
  332.4 5.5 %fusion.26 = f32[2048,768]{1,0:T(8,128)} fusion(bf16[1024,2048]{1,0:T(8,128)(2,1)S(1)} %bitcast.110, bf16[1024,768]{1,0:T(8,128)(2,1)S(1)} %copy-done.19), kind=kOutput, calls=%fused_computation.85 | convolution fusion | flops 3221225472 | bytes 12058624 | tf_op jit(solution)/shard_map/dot_general | solution.py:24
  337.9 7.5 %fusion.1 = f32[768,2048]{1,0:T(8,128)} fusion(bf16[1024,768]{1,0:T(8,128)(2,1)S(1)} %copy-done.13, bf16[1024,2176]{1,0:T(8,128)(2,1)} %bitcast.11.told), kind=kOutput, calls=%fused_computation.3 | convolution fusion | flops 3221225472 | bytes 12058624 | tf_op jit(solution)/shard_map/dot_general | solution.py:24
  345.5 29.6 %reduce_rows_4.1 = f32[128,2048]{1,0:T(8,128)S(1)} custom-call(bf16[4,128,2048]{2,1,0:T(8,128)(2,1)S(1)} %bitcast.78), custom_call_target="tpu_custom_call" | custom-call | bytes 3600000 | tf_op jit(solution)/shard_map/reduce_rows_4/pallas_call | solution.py:381
  375.1 4.4 convolution_convert_fusion.2
  379.6 4.7 %convolution_convert_fusion = bf16[2048,1280]{1,0:T(8,128)(2,1)} fusion(bf16[512,2048]{1,0:T(8,128)(2,1)S(1)} %bitcast.112, bf16[512,1280]{1,0:T(8,128)(2,1)S(1)} %get-tuple-element.78), kind=kOutput, calls=%fused_computation | convolution fusion | flops 2686976000 | bytes 8650752 | tf_op jit(solution)/shard_map/dot_general | solution.py:24
  384.3 0.3 fusion.11
  384.6 0.1 maximum_maximum_fusion.gains
  384.6 48.9 %scatter_weights.1 = (f32[32,2048]{1,0:T(8,128)S(1)}, f32[32,256]{1,0:T(8,128)S(1)}, f32[32,256]{1,0:T(8,128)S(1)}, f32[32,2048]{1,0:T(8,128)S(1)}, f32[40,128]{...) custom-call(bf16[4,2,4,2,32,1280]{5,4,3,2,1,0:T(8,128)(2,1)} %bitcast.93, ...), custom_call_target="tpu_custom_call" | custom-call | bytes 288000000 | tf_op jit(solution)/shard_map/scatter_weights/pallas_call | solution.py:569
  433.6 0.6 slice_bitcast_fusion
  434.2 0.5 slice_bitcast_fusion.2
  434.7 1.1 bitcast_convert_fusion
  435.8 1.4 fusion.10
  437.2 0.8 copy.56
  438.0 0.7 copy.57
  438.7 0.6 copy.58
  439.3 0.6 copy.59
  439.9 0.7 copy.60
  (63 shorter events, 0.2 us)
Async XLA Ops:
  0.6 51.0 %copy-start.17 = (bf16[128,2048]{1,0:T(8,128)(2,1)S(1)}, bf16[128,2048]{1,0:T(8,128)(2,1)}, u32[]{:S(2)}) copy-start(bf16[128,2048]{1,0:T(8,128)(2,1)} %param.31) | copy-start | bytes 1572868
  4.3 50.8 %copy-start.2 = (bf16[1024,128]{1,0:T(8,128)(2,1)}, bf16[1024,128]{1,0:T(8,128)(2,1)S(1)}, u32[]{:S(2)}) copy-start(bf16[1024,128]{1,0:T(8,128)(2,1)S(1)} %fusion.15.spread.slots) | copy-start | bytes 786436
  55.0 75.5 %all-to-all-start = ((bf16[128,8,2176]{2,1,0:T(8,128)(2,1)}), bf16[128,8,2176]{2,1,0:T(8,128)(2,1)}, u32[]{:S(2)}, u32[]{:S(2)}) async-start(bf16[128,8,2176]{2,1,0:T(8,128)(2,1)} %fusion), calls=%async_computation | async-start | bytes 8912896 | tf_op jit(solution)/shard_map/all_to_all | solution.py:1147
  64.1 6.2 %copy-start.7 = (f32[128]{0:T(128)S(1)}, f32[128]{0:T(128)}, u32[]{:S(2)}) copy-start(f32[128]{0:T(128)} %param.24) | copy-start | bytes 1540
  64.1 6.2 %copy-start.8 = (f32[128]{0:T(128)S(1)}, f32[128]{0:T(128)}, u32[]{:S(2)}) copy-start(f32[128]{0:T(128)} %param.25) | copy-start | bytes 1540
  64.1 14.3 %copy-start.23 = (bf16[4,2,4,2,32,1024]{5,4,3,2,1,0:T(8,128)(2,1)S(1)}, bf16[4,2,4,2,32,1024]{5,4,3,2,1,0:T(8,128)(2,1)}, u32[]{:S(2)}) copy-start(bf16[4,2,4,2,32,1024]{5,4,3,2,1,0:T(8,128)(2,1)} %get-tuple-element.61) | copy-start | bytes 12582916
  70.3 10.5 %copy-start = (f32[512,1280]{1,0:T(8,128)}, f32[512,1280]{1,0:T(8,128)S(1)}, u32[]{:S(2)}) copy-start(f32[512,1280]{1,0:T(8,128)S(1)} %fusion.25.raw) | copy-start | bytes 7864324
  78.4 2.4 copy-start.4
  78.4 2.4 copy-start.9
  80.8 48.5 %copy-start.11 = (bf16[128,2048]{1,0:T(8,128)(2,1)S(1)}, bf16[128,2048]{1,0:T(8,128)(2,1)}, u32[]{:S(2)}) copy-start(bf16[128,2048]{1,0:T(8,128)(2,1)} %param.16) | copy-start | bytes 1572868
  80.9 48.7 %copy-start.21 = (f32[2048]{0:T(1024)S(1)}, f32[2048]{0:T(1024)}, u32[]{:S(2)}) copy-start(f32[2048]{0:T(1024)} %param.26) | copy-start | bytes 24580
  130.5 4.4 %copy-start.12 = (bf16[128,2048]{1,0:T(8,128)(2,1)S(1)}, bf16[128,2048]{1,0:T(8,128)(2,1)}, u32[]{:S(2)}) copy-start(bf16[128,2048]{1,0:T(8,128)(2,1)} %multiply_convert_fusion) | copy-start | bytes 1572868
  130.5 4.4 %copy-start.14 = (bf16[2048,128]{1,0:T(8,128)(2,1)S(1)}, bf16[2048,128]{1,0:T(8,128)(2,1)}, u32[]{:S(2)}) copy-start(bf16[2048,128]{1,0:T(8,128)(2,1)} %router.1) | copy-start | bytes 1572868
  203.5 70.8 %copy-start.15 = (bf16[2048,128]{1,0:T(8,128)(2,1)S(1)}, bf16[2048,128]{1,0:T(8,128)(2,1)}, u32[]{:S(2)}) copy-start(bf16[2048,128]{1,0:T(8,128)(2,1)} %router.1) | copy-start | bytes 1572868
  271.0 5.1 %copy-start.18 = (bf16[128,2048]{1,0:T(8,128)(2,1)S(1)}, bf16[128,2048]{1,0:T(8,128)(2,1)}, u32[]{:S(2)}) copy-start(bf16[128,2048]{1,0:T(8,128)(2,1)} %param.31) | copy-start | bytes 1572868
  300.5 83.8 %all-to-all-start.1 = ((bf16[128,8,2048]{2,1,0:T(8,128)(2,1)}), bf16[128,8,2048]{2,1,0:T(8,128)(2,1)}, u32[]{:S(2)}, u32[]{:S(2)}) async-start(bf16[128,8,2048]{2,1,0:T(8,128)(2,1)} %bitcast.94), calls=%async_computation.1 | async-start | bytes 8388608 | tf_op jit(solution)/shard_map/all_to_all | solution.py:1188
  309.0 5.3 %copy-start.1 = (f32[512,1280]{1,0:T(8,128)S(1)}, f32[512,1280]{1,0:T(8,128)}, u32[]{:S(2)}) copy-start(f32[512,1280]{1,0:T(8,128)} %copy-done) | copy-start | bytes 7864324
  309.0 5.3 %copy-start.5 = (f32[2,8,256,256]{3,2,1,0:T(8,128)S(1)}, f32[2,8,256,256]{3,2,1,0:T(8,128)}, u32[]{:S(2)}) copy-start(f32[2,8,256,256]{3,2,1,0:T(8,128)} %copy-done.4) | copy-start | bytes 12582916
  321.0 5.8 %copy-start.20 = (bf16[1024,768]{1,0:T(8,128)(2,1)S(1)}, bf16[1024,768]{1,0:T(8,128)(2,1)}, u32[]{:S(2)}) copy-start(bf16[1024,768]{1,0:T(8,128)(2,1)} %get-tuple-element.71.grad_up) | copy-start | bytes 4718596
  321.0 5.8 %copy-start.24 = (bf16[4,2,4,2,2,8,2048]{6,5,4,3,2,1,0:T(8,128)(2,1)S(1)}, bf16[4,2,4,2,2,8,2048]{6,5,4,3,2,1,0:T(8,128)(2,1)}, u32[]{:S(2)}) copy-start(bf16[4,2,4,2,2,8,2048]{6,5,4,3,2,1,0:T(8,128)(2,1)} %get-tuple-element.66) | copy-start | bytes 12582916
  326.9 5.5 %copy-start.19 = (bf16[1024,768]{1,0:T(8,128)(2,1)S(1)}, bf16[1024,768]{1,0:T(8,128)(2,1)}, u32[]{:S(2)}) copy-start(bf16[1024,768]{1,0:T(8,128)(2,1)} %get-tuple-element.70.grad_gate) | copy-start | bytes 4718596
  332.4 5.5 %copy-start.13 = (bf16[1024,768]{1,0:T(8,128)(2,1)S(1)}, bf16[1024,768]{1,0:T(8,128)(2,1)}, u32[]{:S(2)}) copy-start(bf16[1024,768]{1,0:T(8,128)(2,1)} %get-tuple-element.79.inner_low) | copy-start | bytes 4718596
  345.5 29.6 %copy-start.10 = (bf16[512,1024]{1,0:T(8,128)(2,1)S(1)}, bf16[512,1024]{1,0:T(8,128)(2,1)}, u32[]{:S(2)}) copy-start(bf16[512,1024]{1,0:T(8,128)(2,1)} %copy-done.9) | copy-start | bytes 3145732
  345.5 29.7 %copy-start.26 = (bf16[4,128,2048]{2,1,0:T(8,128)(2,1)S(1)}, bf16[4,128,2048]{2,1,0:T(8,128)(2,1)}, u32[]{:S(2)}) copy-start(bf16[4,128,2048]{2,1,0:T(8,128)(2,1)} %get-tuple-element.75) | copy-start | bytes 6291460
  375.1 4.4 %copy-start.25 = (bf16[4,128,2048]{2,1,0:T(8,128)(2,1)S(1)}, bf16[4,128,2048]{2,1,0:T(8,128)(2,1)}, u32[]{:S(2)}) copy-start(bf16[4,128,2048]{2,1,0:T(8,128)(2,1)} %get-tuple-element.56) | copy-start | bytes 6291460
  379.5 4.7 %copy-start.22 = (f32[2048]{0:T(1024)S(1)}, f32[2048]{0:T(1024)}, u32[]{:S(2)}) copy-start(f32[2048]{0:T(1024)} %param.19) | copy-start | bytes 24580
  379.5 5.1 %copy-start.3 = (bf16[1024,128]{1,0:T(8,128)(2,1)S(1)}, bf16[1024,128]{1,0:T(8,128)(2,1)}, u32[]{:S(2)}) copy-start(bf16[1024,128]{1,0:T(8,128)(2,1)} %copy-done.2) | copy-start | bytes 786436
  379.5 5.1 %copy-start.6 = (bf16[16,128]{1,0:T(8,128)(2,1)S(1)}, bf16[16,128]{1,0:T(8,128)(2,1)}, u32[]{:S(2)}) copy-start(bf16[16,128]{1,0:T(8,128)(2,1)} %get-tuple-element.86.piece) | copy-start | bytes 12292
  384.6 51.1 %copy-start.16 = (f32[128,2048]{1,0:T(8,128)S(1)}, f32[128,2048]{1,0:T(8,128)}, u32[]{:S(2)}) copy-start(f32[128,2048]{1,0:T(8,128)} %get-tuple-element.103) | copy-start | bytes 3145732

commit v9 on v8

--- a/solution.py
+++ b/solution.py
@@ -126,6 +126,7 @@
         self.send, self.recv, self.local = send, recv, local
         self.n = self.m = 0
         self.sent = []
+        self.waited = set()
 
     def put(self, src, dst, peer):
         copy = pltpu.make_async_remote_copy(
@@ -147,9 +148,15 @@
         copy.start()
         return copy
 
+    def release(self, copies):
+        for copy in copies:
+            copy.wait_send()
+            self.waited.add(id(copy))
+
     def finish(self):
         for copy in self.sent:
-            copy.wait_send()
+            if id(copy) not in self.waited:
+                copy.wait_send()
 
 
 def gather_kernel(q, k, v, o, tok, doc, wa, wb, toks, docs, send, recv, local):
@@ -807,46 +814,84 @@
 ORDER = ((0, 0), (1, 0), (0, 1), (2, 0), (1, 1), (0, 2), (2, 1), (1, 2), (2, 2))
 
 
-def enter_kernel(
-    sent, told, gate, up, down, router, rows, inner_low, grad_gate, grad_up, extra, *rest
+def experts_kernel(
+    tokens, spread, told, gate, up, down, router, rows, inner_low, grad_gate, grad_up, summed, expert_out, *rest
 ):
     chunks = len(CHUNKS)
-    mids = rest[: 2 * chunks]
-    held = rest[2 * chunks : 3 * chunks]
-    (
-        told_v, gate_v, up_v, down_v, router_v, gate_pre, up_pre, logits, inner_up, send, recv, local, loads,
-    ) = rest[3 * chunks :]
+    taken = iter(rest)
+    take = lambda count: [next(taken) for _ in range(count)]
+    first = take(4)
+    mids_in, held_in = take(2 * chunks), take(chunks)
+    mids_out, held_out = take(2 * chunks), take(chunks)
+    last_source, extra = take(2)
+    first += [extra, last_source]
+    tokens_v, spread_v, asked_v, blocks_v, gate_v, up_v, down_v, router_v = take(8)
+    gate_pre, up_pre, logits, inner_up, inner_v, gate_g, up_g = take(7)
+    send, recv, local, back_send, back_recv, back_local, loads, told_sem, puts = take(9)
     me = Place()
-    go = Copies(send, recv, local)
-    route = Route(me, go)
-    pulls = [
-        pltpu.make_async_copy(a, b, loads.at[n])
+    go, back = Copies(send, recv, local), Copies(back_send, back_recv, back_local)
+    way_in, way_out = Route(me, go), Route(me, back)
+    width = tokens.shape[1]
+    slots, lanes = spread.shape[0], router.shape[1]
+    block = 256
+    index = me.expert()
+    starts = [sum(CHUNKS[:n]) for n in range(chunks)]
+    blocks = list(range(slots // block))
+
+    early = [pltpu.make_async_copy(a, b, loads.at[n]) for n, (a, b) in enumerate(((tokens, tokens_v), (spread, spread_v)))]
+    late = [
+        pltpu.make_async_copy(a, b, loads.at[2 + n])
         for n, (a, b) in enumerate(
-            ((told, told_v), (down, down_v), (gate, gate_v), (up, up_v), (router, router_v))
+            ((down, down_v), (gate, gate_v), (up, up_v), (router, router_v), (told.at[:, pl.ds(width, lanes)], asked_v))
         )
     ]
-    greet(route.everyone())
-    starts = [sum(CHUNKS[:n]) for n in range(chunks)]
-    sent_on = [None] * chunks
+    for pull in early:
+        pull.start()
+    greet(way_in.everyone())
+    for pull in early:
+        pull.wait()
+
+    def load(m):
+        at = pl.ds(m * block, block)
+        return pltpu.make_async_copy(told.at[at, pl.ds(0, width)], blocks_v.at[m % 2], told_sem.at[m % 2])
+
+    def each_block(step):
+        def run(m, _):
+            step(pl.ds(pl.multiple_of(m * block, block), block))
+            return 0
+
+        lax.fori_loop(0, slots // block, run, 0)
+
+    sent_on, started = [None] * chunks, [None] * chunks
     outs = []
-    width = sent.shape[-1]
-    total = told_v.shape[0]
-    experts = router.shape[1]
-    index = me.expert()
-    block = 256
-
-    def cotangent(n):
-        at = pl.ds(n * block, block)
-        inner_up[at] = dot_nt(told_v[at, :width], down_v[...])
+
+    def dispatch(n):
+        buffer = first[n % 6]
+        if n >= 6:
+            go.release(started[n - 6][1])
+        cols = pl.ds(starts[n], CHUNKS[n])
+        flat = buffer.reshape(slots, buffer.shape[-1])
+
+        def step(at):
+            flat[at, : CHUNKS[n]] = dot_nn(spread_v[at], tokens_v[:, cols]).astype(BF16)
+
+        each_block(step)
+        return columns(buffer, 0, CHUNKS[n])
+
+    def cotangent(m):
+        load(m).wait()
+        at = pl.ds(m * block, block)
+        inner_up[at] = dot_nt(blocks_v[m % 2], down_v[...])
+        if m + 2 < len(blocks):
+            load(m + 2).start()
 
     def multiply(n, close=False):
-        route.wait(sent_on[n])
-        outs.append(go.keep(held[n], columns(rows, starts[n], CHUNKS[n])))
+        way_in.wait(sent_on[n])
+        outs.append(go.keep(held_in[n], columns(rows, starts[n], CHUNKS[n])))
         cols = pl.ds(starts[n], CHUNKS[n])
-        flat = held[n].reshape(total, CHUNKS[n])
-
-        def step(m, _):
-            at = pl.ds(pl.multiple_of(m * block, block), block)
+        flat = held_in[n].reshape(slots, CHUNKS[n])
+
+        def step(at):
             part = flat[at]
             terms = []
             for out, weight in ((gate_pre, gate_v), (up_pre, up_v), (logits, router_v)):
@@ -858,233 +903,184 @@
                 terms.append(term)
             if close:
                 finish(at, *terms)
-            return 0
-
-        lax.fori_loop(0, total // block, step, 0)
+
+        each_block(step)
 
     def finish(at, before_gate, before_up, row_logits):
-        row_logits = jnp.where(told_v[at, width:] > 0, row_logits, MASKED)
+        row_logits = jnp.where(asked_v[at] > 0, row_logits, MASKED)
         powers = jnp.exp(row_logits - jnp.max(row_logits, axis=-1, keepdims=True))
-        lane = lax.broadcasted_iota(jnp.int32, (1, experts), 1) == index
+        lane = lax.broadcasted_iota(jnp.int32, (1, lanes), 1) == index
         prob = jnp.sum(jnp.where(lane, powers, 0.0), axis=-1, keepdims=True) / jnp.sum(
             powers, axis=-1, keepdims=True
         )
-        back = inner_up[at]
+        after_inner = inner_up[at]
         sigmoid = 1.0 / (1.0 + jnp.exp(-before_gate))
         silu = before_gate * sigmoid
         inner = silu * before_up
-        gate_up = jnp.sum(inner * back, axis=-1, keepdims=True)
-        inner_low[at] = (prob * inner).astype(BF16)
-        back = prob * back
-        grad_gate[at] = (back * before_up * sigmoid * (1.0 + before_gate * (1.0 - sigmoid))).astype(BF16)
-        grad_up[at] = (back * silu).astype(BF16)
+        gate_up = jnp.sum(inner * after_inner, axis=-1, keepdims=True)
+        inner_v[at] = (prob * inner).astype(BF16)
+        after_inner = prob * after_inner
+        gate_g[at] = (after_inner * before_up * sigmoid * (1.0 + before_gate * (1.0 - sigmoid))).astype(BF16)
+        up_g[at] = (after_inner * silu).astype(BF16)
         high = gate_up.astype(BF16).astype(F32)
-        extra[at, :experts] = jnp.where(lane, high, 0.0).astype(BF16)
-        extra[at, experts:] = jnp.where(lane, gate_up - high, 0.0).astype(BF16)
-
-    blocks = list(range(total // block))
+        flat = extra.reshape(slots, 2 * lanes)
+        flat[at, :lanes] = jnp.where(lane, high, 0.0).astype(BF16)
+        flat[at, lanes:] = jnp.where(lane, gate_up - high, 0.0).astype(BF16)
+
+    todo = list(blocks)
     for triple, crossing in ORDER:
         for n in range(3 * triple, 3 * triple + 3):
-            src = columns(sent, starts[n], CHUNKS[n]) if crossing == 0 else mids[2 * n + crossing - 1]
-            dst = held[n] if crossing == 2 else mids[2 * n + crossing]
-            if crossing > 0:
-                route.wait(sent_on[n])
-            sent_on[n] = route.send(TURNS[n % 3][crossing], src, dst)
+            if n >= 6 and crossing == 2:
+                go.release(started[n - 2][1] if n < 8 else [])
+            if crossing == 0:
+                src = dispatch(n)
+            else:
+                way_in.wait(sent_on[n])
+                src = mids_in[2 * n + crossing - 1]
+            dst = held_in[n] if crossing == 2 else mids_in[2 * n + crossing]
+            sent_on[n] = way_in.send(TURNS[n % 3][crossing], src, dst)
+            if crossing == 0:
+                started[n] = sent_on[n]
             if crossing == 2 and triple > 0:
                 multiply(n - 3)
-            elif blocks and triple + crossing > 1:
-                cotangent(blocks.pop(0))
+            elif todo and triple + crossing > 1 and crossing > 0:
+                cotangent(todo.pop(0))
         if (triple, crossing) == (1, 0):
-            for pull in pulls:
+            load(0).start()
+            load(1).start()
+            for pull in late:
                 pull.start()
-            for pull in pulls[:2]:
-                pull.wait()
+            late[0].wait()
         if (triple, crossing) == (2, 1):
-            for pull in pulls[2:]:
+            while todo:
+                cotangent(todo.pop(0))
+            for pull in late[1:]:
                 pull.wait()
     for n in range(chunks - 3, chunks):
         multiply(n, close=n == chunks - 1)
+    results = [
+        pltpu.make_async_copy(a, b, puts.at[n])
+        for n, (a, b) in enumerate(((inner_v, inner_low), (gate_g, grad_gate), (up_g, grad_up)))
+    ]
+    for result in results:
+        result.start()
     for out in outs:
         out.wait()
+
+    begins = [sum(BACK[:n]) for n in range(chunks)]
+    sources = [*held_in[: chunks - 2], last_source]
+    sent_back = [None] * chunks
+    pushes = [None] * len(blocks)
+
+    def gradient(n):
+        cols = pl.ds(begins[n], BACK[n])
+        flat = sources[n].reshape(slots, BACK[n])
+
+        def step(at):
+            flat[at] = (dot_nt(gate_g[at], gate_v[cols]) + dot_nt(up_g[at], up_v[cols])).astype(BF16)
+
+        each_block(step)
+
+    def outcome(m):
+        if m >= 2:
+            pushes[m - 2].wait()
+        at = pl.ds(m * block, block)
+        blocks_v[m % 2] = dot_nn(inner_v[at], down_v[...]).astype(BF16)
+        pushes[m] = pltpu.make_async_copy(blocks_v.at[m % 2], expert_out.at[at], puts.at[3 + m])
+        pushes[m].start()
+
+    def combine(n):
+        way_out.wait(sent_back[n])
+        summed[:, begins[n] : begins[n] + BACK[n]] = dot_tn(
+            spread_v[...], held_out[n].reshape(slots, BACK[n])[...]
+        )
+
+    todo = list(blocks)
+    for triple, crossing in ORDER:
+        for n in range(3 * triple, 3 * triple + 3):
+            dst = held_out[n] if crossing == 2 else mids_out[2 * n + crossing]
+            if crossing > 0:
+                way_out.wait(sent_back[n])
+                src = mids_out[2 * n + crossing - 1]
+            elif n == chunks - 1:
+                src = extra
+            else:
+                gradient(n)
+                src = sources[n]
+            sent_back[n] = way_out.send(TURNS[n % 3][crossing], src, dst)
+            if crossing == 2 and triple > 0:
+                combine(n - 3)
+            elif todo and triple + crossing > 1 and crossing > 0:
+                outcome(todo.pop(0))
+    for n in range(chunks - 3, chunks):
+        combine(n)
+    for copy in (*results, *pushes[-2:]):
+        copy.wait()
     go.finish()
-
-
-def enter(sent, told, gate, up, down, router):
-    slots, width = sent.shape
-    hidden, experts = gate.shape[1], router.shape[1]
-    cap = slots // math.prod(DIMS)
-    lead = (*DIMS, cap)
+    back.finish()
+
+
+def experts(tokens, spread, told, gate, up, down, router):
+    tok, width = tokens.shape
+    slots = spread.shape[0]
+    hidden, lanes = gate.shape[1], router.shape[1]
+    lead = (*DIMS, slots // math.prod(DIMS))
     chunks = len(CHUNKS)
     low = jax.ShapeDtypeStruct((slots, hidden), BF16)
-    rows, *rest = pl.pallas_call(
-        enter_kernel,
-        name="enter_experts",
-        cost_estimate=cost(60),
+
+    def held(widths):
+        return [pltpu.VMEM((*lead, w), BF16) for w in widths]
+
+    twice = lambda widths: [w for w in widths for _ in range(2)]
+    rows, *others = pl.pallas_call(
+        experts_kernel,
+        name="experts",
+        cost_estimate=cost(120),
         out_shape=(
             jax.ShapeDtypeStruct((*lead, width), BF16),
             low,
             low,
             low,
-            jax.ShapeDtypeStruct((slots, 2 * experts), BF16),
+            jax.ShapeDtypeStruct((tok, sum(BACK)), F32),
+            jax.ShapeDtypeStruct((slots, width), BF16),
         ),
-        in_specs=[ANY] * 6,
-        out_specs=(ANY, VMEM, VMEM, VMEM, VMEM),
+        in_specs=[ANY] * 7,
+        out_specs=(ANY, ANY, ANY, ANY, VMEM, ANY),
         scratch_shapes=[
-            *(pltpu.VMEM((*lead, w), BF16) for w in CHUNKS for _ in range(2)),
-            *(pltpu.VMEM((*lead, w), BF16) for w in CHUNKS),
-            pltpu.VMEM(told.shape, BF16),
+            *held(CHUNKS[:4]),
+            *held(twice(CHUNKS)),
+            *held(CHUNKS),
+            *held(twice(BACK)),
+            *held(BACK),
+            *held((BACK[-2], BACK[-1])),
+            pltpu.VMEM(tokens.shape, BF16),
+            pltpu.VMEM(spread.shape, BF16),
+            pltpu.VMEM((slots, lanes), BF16),
+            pltpu.VMEM((2, 256, width), BF16),
             pltpu.VMEM(gate.shape, BF16),
             pltpu.VMEM(up.shape, BF16),
             pltpu.VMEM(down.shape, BF16),
             pltpu.VMEM(router.shape, BF16),
             pltpu.VMEM((slots, hidden), F32),
             pltpu.VMEM((slots, hidden), F32),
-            pltpu.VMEM((slots, experts), F32),
+            pltpu.VMEM((slots, lanes), F32),
             pltpu.VMEM((slots, hidden), F32),
+            *(pltpu.VMEM((slots, hidden), BF16) for _ in range(3)),
             pltpu.SemaphoreType.DMA((13 * chunks,)),
             pltpu.SemaphoreType.DMA((13 * chunks,)),
             pltpu.SemaphoreType.DMA((4 * chunks,)),
-            pltpu.SemaphoreType.DMA((5,)),
-        ],
-        compiler_params=pltpu.CompilerParams(
-            collective_id=6, has_side_effects=True, vmem_limit_bytes=58 << 20
-        ),
-    )(sent.reshape(*lead, width), told, gate, up, down, router)
-    return rows.reshape(slots, width), *rest
-
-
-def leave_kernel(
-    grad_gate, grad_up, extra, inner_low, spread, gate, up, down, summed, expert_out, *rest
-):
-    chunks = len(BACK)
-    source = rest[: chunks - 1]
-    mids = rest[chunks - 1 : 3 * chunks - 1]
-    held = rest[3 * chunks - 1 : 4 * chunks - 1]
-    gate_g, up_g, inner_v, spread_v, gate_v, up_v, down_v, out_v, send, recv, local, loads, puts = rest[4 * chunks - 1 :]
-    me = Place()
-    go = Copies(send, recv, local)
-    route = Route(me, go)
-    starts = [sum(BACK[:n]) for n in range(chunks)]
-    total = gate_g.shape[0]
-    block = 256
-    pulls = {}
-    count = 0
-    for name, a, b in (("gg", grad_gate, gate_g), ("gu", grad_up, up_g)):
-        pulls[name] = pltpu.make_async_copy(a, b, loads.at[count])
-        count += 1
-    for n in range(chunks - 1):
-        cols = pl.ds(starts[n], BACK[n])
-        for name, a, b in ((("g", n), gate, gate_v), (("u", n), up, up_v)):
-            pulls[name] = pltpu.make_async_copy(a.at[cols], b.at[cols], loads.at[count])
-            count += 1
-    for name, a, b in (("inner", inner_low, inner_v), ("spread", spread, spread_v), ("down", down, down_v)):
-        pulls[name] = pltpu.make_async_copy(a, b, loads.at[count])
-        count += 1
-    late = ("inner", "spread", "down")
-    for name, pull in pulls.items():
-        if name not in late:
-            pull.start()
-    greet(route.everyone())
-    sent_on = [None] * chunks
-    pushes = []
-
-    def gradient(n):
-        cols = pl.ds(starts[n], BACK[n])
-        for name in (("g", n), ("u", n)):
-            pulls[name].wait()
-        flat = source[n].reshape(total, BACK[n])
-
-        def step(m, _):
-            at = pl.ds(pl.multiple_of(m * block, block), block)
-            flat[at] = (dot_nt(gate_g[at], gate_v[cols]) + dot_nt(up_g[at], up_v[cols])).astype(BF16)
-            return 0
-
-        lax.fori_loop(0, total // block, step, 0)
-
-    def result(m):
-        if m == 0:
-            pulls["inner"].wait()
-            pulls["down"].wait()
-        at = pl.ds(m * block, block)
-        out_v[at] = dot_nn(inner_v[at], down_v[...]).astype(BF16)
-        push = pltpu.make_async_copy(out_v.at[at], expert_out.at[at], puts.at[m])
-        push.start()
-        pushes.append(push)
-
-    def combine(n):
-        route.wait(sent_on[n])
-        summed[:, starts[n] : starts[n] + BACK[n]] = dot_tn(spread_v[...], held[n].reshape(total, BACK[n])[...])
-
-    results = list(range(total // block))
-    for triple, crossing in ORDER:
-        for n in range(3 * triple, 3 * triple + 3):
-            dst = held[n] if crossing == 2 else mids[2 * n + crossing]
-            if crossing > 0:
-                route.wait(sent_on[n])
-                src = mids[2 * n + crossing - 1]
-            elif n == chunks - 1:
-                src = extra
-            else:
-                if n == 0:
-                    pulls["gg"].wait()
-                    pulls["gu"].wait()
-                gradient(n)
-                src = source[n]
-            sent_on[n] = route.send(TURNS[n % 3][crossing], src, dst)
-            if crossing == 2 and triple > 0:
-                if n == 3:
-                    pulls["spread"].wait()
-                combine(n - 3)
-            elif results and triple + crossing > 1 and crossing > 0:
-                result(results.pop(0))
-        if (triple, crossing) == (1, 0):
-            for name in late:
-                pulls[name].start()
-    for n in range(chunks - 3, chunks):
-        combine(n)
-    for push in pushes:
-        push.wait()
-    go.finish()
-
-
-def leave(grad_gate, grad_up, extra, inner_low, spread, gate, up, down):
-    slots, hidden = grad_gate.shape
-    width, tok = gate.shape[0], spread.shape[1]
-    cap = slots // math.prod(DIMS)
-    lead = (*DIMS, cap)
-    chunks = len(BACK)
-    return pl.pallas_call(
-        leave_kernel,
-        name="leave_experts",
-        cost_estimate=cost(60),
-        out_shape=(
-            jax.ShapeDtypeStruct((tok, sum(BACK)), F32),
-            jax.ShapeDtypeStruct((slots, width), BF16),
-        ),
-        in_specs=[ANY] * 8,
-        out_specs=(VMEM, ANY),
-        scratch_shapes=[
-            *(pltpu.VMEM((*lead, w), BF16) for w in BACK[:-1]),
-            *(pltpu.VMEM((*lead, w), BF16) for w in BACK for _ in range(2)),
-            *(pltpu.VMEM((*lead, w), BF16) for w in BACK),
-            pltpu.VMEM(grad_gate.shape, BF16),
-            pltpu.VMEM(grad_up.shape, BF16),
-            pltpu.VMEM(inner_low.shape, BF16),
-            pltpu.VMEM(spread.shape, BF16),
-            pltpu.VMEM(gate.shape, BF16),
-            pltpu.VMEM(up.shape, BF16),
-            pltpu.VMEM(down.shape, BF16),
-            pltpu.VMEM((slots, width), BF16),
             pltpu.SemaphoreType.DMA((13 * chunks,)),
             pltpu.SemaphoreType.DMA((13 * chunks,)),
             pltpu.SemaphoreType.DMA((3 * chunks,)),
-            pltpu.SemaphoreType.DMA((2 * chunks + 3,)),
-            pltpu.SemaphoreType.DMA((4,)),
+            pltpu.SemaphoreType.DMA((7,)),
+            pltpu.SemaphoreType.DMA((2,)),
+            pltpu.SemaphoreType.DMA((7,)),
         ],
         compiler_params=pltpu.CompilerParams(
-            collective_id=7, has_side_effects=True, vmem_limit_bytes=58 << 20
+            collective_id=6, has_side_effects=True, vmem_limit_bytes=61 << 20
         ),
-    )(grad_gate, grad_up, extra.reshape(*lead, extra.shape[1]), inner_low, spread, gate, up, down)
+    )(tokens, spread, told, gate, up, down, router)
+    return rows.reshape(slots, width), *others
 
 
 def on_device(
@@ -1111,14 +1107,14 @@
     nkv = key_weight.shape[1] // hd
     nq = query_weight.shape[1] // hd
     group = nq // nkv
-    experts = router_weight.shape[1]
+    count = router_weight.shape[1]
     routes = expert_ids.shape[1]
-    cap = tok * routes // experts
-    slots = experts * cap
+    cap = tok * routes // count
+    slots = count * cap
     scale = 1.0 / math.sqrt(hd)
     tokens = doc_ids.shape[1]
 
-    lane = lax.broadcasted_iota(jnp.int32, (1, 1, experts), 2)
+    lane = lax.broadcasted_iota(jnp.int32, (1, 1, count), 2)
     chosen = jnp.sum((expert_ids[:, :, None] == lane).astype(F32), axis=1)
     below = (
         lax.broadcasted_iota(jnp.int32, (tok, tok), 1)
@@ -1145,8 +1141,8 @@
     spread_late, docs = lax.optimization_barrier((spread, docs))
     cot_out = dot_nn(spread_late, jnp.concatenate([cotangent, chosen.astype(BF16)], axis=1)).astype(BF16)
     cot_in = lax.all_to_all(
-        cot_out.reshape(experts, cap, width + experts), both, split_axis=0, concat_axis=0, tiled=True
-    ).reshape(slots, width + experts)
+        cot_out.reshape(count, cap, width + count), both, split_axis=0, concat_axis=0, tiled=True
+    ).reshape(slots, width + count)
 
     position, allowed = jax.vmap(layout)(docs[:, 0])
     cosine, sine = rotary(position.reshape(-1), hd)
@@ -1161,13 +1157,9 @@
     residual = hidden + attn_out
     moe_input = rms_scale(residual, moe_gain).astype(BF16)
     moe_input, cot_in = lax.optimization_barrier((moe_input, cot_in))
-    sent = dot_nn(spread, moe_input).astype(BF16)
     gate_mat, up_mat, down_mat = gate_weight[0], up_weight[0], down_weight[0]
-    rows, inner_low, grad_gate, grad_up, extra = enter(
-        sent, cot_in, gate_mat, up_mat, down_mat, router_weight
-    )
-    summed, expert_out = leave(
-        grad_gate, grad_up, extra, inner_low, spread, gate_mat, up_mat, down_mat
+    rows, inner_low, grad_gate, grad_up, summed, expert_out = experts(
+        moe_input, spread, cot_in, gate_mat, up_mat, down_mat, router_weight
     )
     logits = dot_nn(moe_input, router_weight)
     masked = jnp.where(chosen > 0, logits, MASKED)
@@ -1175,7 +1167,7 @@
     probs = probs / jnp.sum(probs, axis=-1, keepdims=True)
 
     upstream = cotangent.astype(F32)
-    gate_upstream = summed[:, width : width + experts] + summed[:, width + experts :]
+    gate_upstream = summed[:, width : width + count] + summed[:, width + count :]
     grad_chosen = probs * (gate_upstream - jnp.sum(probs * gate_upstream, axis=-1, keepdims=True))
     grad_logits = grad_chosen.astype(BF16)
     grad_moe_input = summed[:, :width] + dot_nt(grad_logits, router_weight)
@@ -1186,7 +1178,7 @@
     grad_attn, piece = share(grad_residual.astype(BF16), router_part.astype(BF16), 3)
     expert_out, grad_attn = lax.optimization_barrier((expert_out, grad_attn))
     returned = lax.all_to_all(
-        expert_out.reshape(experts, cap, width), both, split_axis=0, concat_axis=0, tiled=True
+        expert_out.reshape(count, cap, width), both, split_axis=0, concat_axis=0, tiled=True
     ).reshape(slots, width)
 
     grad_mixed = dot_nn(grad_attn, out_weights).astype(BF16)
@@ -1232,7 +1224,7 @@
         gains[2 * at],
         gains[2 * at + 1],
         gains[at : 2 * at].reshape(-1),
-        router_grad.reshape(width, experts).astype(F32),
+        router_grad.reshape(width, count).astype(F32),
         gate_grad[None],
         up_grad[None],
         down_grad[None],

time: 445 us -> 439 us (0.987)
    pallas_call x2 -> x1, Pallas kernels: 135 us -> 132 us  [experts(): pl.pallas_call(experts_kernel, name='experts', cost_estimate=cost(120), o...]
    dot_general x6 -> x5, matrix products: 19.8 us -> 16.5 us  [dot_nn(): lax.dot_general(a, b, (((1,), (0,)), ((), ())), preferred_element_type=F32)]
where the time goes in v9:
time: 439 us; the launch traced here: 435 us
  Pallas kernels  341 us (78%)
  matrix products  56.6 us (13%)
  starting transfers between devices  15.1 us (3%)
  other arithmetic  13 us (3%)
  local copies, waits for them, and re-layouts  7.17 us (2%)
    pallas_call x1, Pallas kernels, experts(): pl.pallas_call(experts_kernel, name='experts', cost_estimate=cost(120), o...  132 us
    pallas_call x2, Pallas kernels, reduce(): pl.pallas_call(reduce_kernel, name=f'reduce_rows_{ident}', cost_estimate=...  78 us
    pallas_call x1, Pallas kernels, scatter(): pl.pallas_call(scatter_kernel, name='scatter_weights', cost_estimate=cost...  48.9 us
    pallas_call x1, Pallas kernels, gather(): pl.pallas_call(gather_kernel, name='gather_weights', cost_estimate=cost(6...  44.6 us
    dot_general x6, matrix products, dot_tn(): lax.dot_general(a, b, (((0,), (0,)), ((), ())), preferred_element_type=F32)  29.9 us
    pallas_call x1, Pallas kernels, share(): pl.pallas_call(share_kernel, name=f'share_rows_{ident}', cost_estimate=co...  23.2 us
    dot_general x5, matrix products, dot_nn(): lax.dot_general(a, b, (((1,), (0,)), ((), ())), preferred_element_type=F32)  16.5 us
    dot_general x3, matrix products, dot_nt(): lax.dot_general(a, b, (((1,), (1,)), ((), ())), preferred_element_type=F32)  10.2 us
  transfers between devices with their start and end apart: 2, of which 0 were waited for; matrix products, arithmetic and copies ran while one was open for 12% of the time, Pallas kernels for 21%

profile of v9, /device:TPU:1, one launch (start us, length us, event | category | flops | bytes accessed | tf_op | source)
XLA Modules:
  0.0 434.8 jit_solution(2742994865573714847)
XLA Ops:
  0.6 0.0 copy-start.14
  0.7 0.8 copy.38
  1.5 0.2 convert_reduce_fusion
  1.8 1.2 fusion.3
  3.0 0.7 convert_element_type.82
  3.7 0.1 convolution_select_fusion.1
  3.8 0.1 copy.40
  4.0 0.1 eq.54
  4.0 2.0 fusion.5.tok
  6.1 0.2 fusion.15.spread.slots
  6.3 0.0 copy-start.2
  6.3 0.7 broadcast_in_dim.33.doc
  6.9 44.6 %gather_weights.1 = (bf16[4,2,4,2,32,1280]{5,4,3,2,1,0:T(8,128)(2,1)}, bf16[4,2,4,2,32,1024]{5,4,3,2,1,0:T(8,128)(2,1)}, bf16[4,128,2048]{2,1,0:T(8,128)(2,1)}, f32[2,8,256]{2,1,0:T(8,128)}) custom-call(bf16[32,2048]{1,0:T(8,128)(2,1)} %q.1, bf16[32,256]{1,0:T(8,128)(2,1)} %k.1, bf16[32,256]{1,0:T(8,128)(2,1)} %v.1, bf16[32,2048]{1,0:T(8,128)(2,1)} %bitcast.89, ...), custom_call_target="tpu_custom_call" | custom-call | bytes 216000000 | tf_op jit(solution)/shard_map/gather_weights/pallas_call | solution.py:253
  51.6 3.4 fusion
  55.0 6.5 %all-to-all-start = ((bf16[128,8,2176]{2,1,0:T(8,128)(2,1)}), bf16[128,8,2176]{2,1,0:T(8,128)(2,1)}, u32[]{:S(2)}, u32[]{:S(2)}) async-start(bf16[128,8,2176]{2,1,0:T(8,128)(2,1)} %fusion), calls=%async_computation | async-start | bytes 8912896 | tf_op jit(solution)/shard_map/all_to_all | solution.py:1143
  61.6 0.7 slice.27
  62.3 0.3 select_reduce_fusion
  62.6 1.0 fusion.17
  63.6 0.2 pad_maximum_fusion
  63.8 0.2 fusion.16.bias
  64.0 0.0 copy-start.7
  64.1 0.0 copy-start.8
  64.1 6.1 %fusion.23.raw = f32[512,1280]{1,0:T(8,128)S(1)} fusion(bf16[512,2048]{1,0:T(8,128)(2,1)} %bitcast.102, bf16[2048,1280]{1,0:T(8,128)(2,1)} %bitcast.96), kind=kOutput, calls=%fused_computation.81 | convolution fusion | flops 2684354560 | bytes 9961472 | tf_op jit(solution)/shard_map/dot_general | solution.py:28
  70.2 0.0 copy-start
  70.3 8.1 %attend.1 = (bf16[512,1024]{1,0:T(8,128)(2,1)S(1)}, bf16[512,256]{1,0:T(8,128)(2,1)S(1)}, f32[2,8,256,256]{3,2,1,0:T(8,128)S(1)}, bf16[512,1024]{1,0:T(8,128)(2,1)S(1)}) custom-call(f32[512,1280]{1,0:T(8,128)S(1)} %fusion.23.raw, f32[2,256,256]{2,1,0:T(8,128)S(1)} %fusion.16.bias, f32[512,128]{1,0:T(8,128)S(1)} %get-tuple-element.120.cosine, ...), custom_call_target="tpu_custom_call" | custom-call | bytes 28800000 | tf_op jit(solution)/shard_map/attend/pallas_call | solution.py:653
  78.4 0.0 copy-start.4
  78.4 0.0 copy-start.9
  78.4 2.4 convolution_convert_fusion.3
  80.8 0.0 copy-start.11
  80.8 48.4 %reduce_rows_2.1 = f32[128,2048]{1,0:T(8,128)S(1)} custom-call(bf16[4,128,2048]{2,1,0:T(8,128)(2,1)S(1)} %bitcast.75), custom_call_target="tpu_custom_call" | custom-call | bytes 3600000 | tf_op jit(solution)/shard_map/reduce_rows_2/pallas_call | solution.py:388
  129.2 0.1 pad.3.clone
  129.3 0.2 multiply_reduce_fusion.2
  129.5 1.0 multiply_convert_fusion.tokens
  130.5 1.6 fusion.22
  132.0 0.2 fusion.19
  132.2 131.8 %experts.1 = (bf16[4,2,4,2,2,8,2048]{6,5,4,3,2,1,0:T(8,128)(2,1)}, bf16[1024,768]{1,0:T(8,128)(2,1)}, bf16[1024,768]{1,0:T(8,128)(2,1)}, bf16[1024,768]{1,0:T(8,...) custom-call(bf16[128,2048]{1,0:T(8,128)(2,1)} %multiply_convert_fusion.tokens, bf16[1024,128]{1,0:T(8,128)(2,1)} %copy-done.2, ...), custom_call_target="tpu_custom_call" | custom-call | bytes 432000000 | tf_op jit(solution)/shard_map/experts/pallas_call | solution.py:1035
  264.1 1.1 multiply_reduce_fusion.3
  265.2 2.3 convolution_convert_fusion.5
  267.5 2.0 multiply_reduce_fusion
  269.5 1.5 fusion.21
  271.1 23.2 %share_rows_3.1 = (bf16[4,128,2048]{2,1,0:T(8,128)(2,1)}, bf16[16,128]{1,0:T(8,128)(2,1)}) custom-call(bf16[128,2048]{1,0:T(8,128)(2,1)} %get-tuple-element.100.tok, bf16[4,2,4,2,2,16,128]{6,5,4,3,2,1,0:T(8,128)(2,1)} %bitcast.88), custom_call_target="tpu_custom_call" | custom-call | bytes 72000000 | tf_op jit(solution)/shard_map/share_rows_3/pallas_call | solution.py:330
  294.3 8.6 %all-to-all-start.1 = ((bf16[128,8,2048]{2,1,0:T(8,128)(2,1)}), bf16[128,8,2048]{2,1,0:T(8,128)(2,1)}, u32[]{:S(2)}, u32[]{:S(2)}) async-start(bf16[128,8,2048]{2,1,0:T(8,128)(2,1)} %bitcast.83), calls=%async_computation.1 | async-start | bytes 8388608 | tf_op jit(solution)/shard_map/all_to_all | solution.py:1180
  302.9 0.0 copy-start.1
  303.0 5.3 %convolution_convert_fusion.6.grad_mixed = bf16[512,1024]{1,0:T(8,128)(2,1)S(1)} fusion(bf16[512,2048]{1,0:T(8,128)(2,1)} %bitcast.104, bf16[2048,1024]{1,0:T(8,128)(2,1)} %bitcast.98), kind=kOutput, calls=%fused_computation.16 | convolution fusion | flops 2148007936 | bytes 7340032 | tf_op jit(solution)/shard_map/dot_general | solution.py:28
  308.3 6.7 %attend_back.1 = (bf16[512,1280]{1,0:T(8,128)(2,1)S(1)}, f32[2,128]{1,0:T(2,128)S(1)}) custom-call(f32[512,1280]{1,0:T(8,128)S(1)} %copy-done.1, f32[512,128]{1,0:T(8,128)S(1)} %get-tuple-element.120.cosine, f32[512,128]{1,0:T(8,128)S(1)} %get-tuple-element.121.signed, f32[1,128]{1,0:T(1,128)S(1)} %bitcast.78, f32[1,128]{1,0:T(1,128)S(1)} %bitcast.80, ...), custom_call_target="tpu_custom_call" | custom-call | bytes 3600000 | tf_op jit(solution)/shard_map/attend_back/pallas_call | solution.py:730
  315.0 5.8 %convolution_convert_fusion.4 = bf16[512,2048]{1,0:T(8,128)(2,1)S(1)} fusion(bf16[512,1280]{1,0:T(8,128)(2,1)S(1)} %get-tuple-element.74, bf16[2048,1280]{1,0:T(8,128)(2,1)} %bitcast.97), kind=kOutput, calls=%fused_computation.7 | convolution fusion | flops 2685403136 | bytes 8650752 | tf_op jit(solution)/shard_map/dot_general | solution.py:20
  320.8 5.5 %fusion.25 = f32[2048,768]{1,0:T(8,128)} fusion(bf16[1024,2048]{1,0:T(8,128)(2,1)S(1)} %bitcast.100, bf16[1024,768]{1,0:T(8,128)(2,1)S(1)} %copy-done.24), kind=kOutput, calls=%fused_computation.83 | convolution fusion | flops 3221225472 | bytes 12058624 | tf_op jit(solution)/shard_map/dot_general | solution.py:24
  326.4 5.5 %fusion.24 = f32[2048,768]{1,0:T(8,128)} fusion(bf16[1024,2048]{1,0:T(8,128)(2,1)S(1)} %bitcast.101, bf16[1024,768]{1,0:T(8,128)(2,1)S(1)} %copy-done.23), kind=kOutput, calls=%fused_computation.82 | convolution fusion | flops 3221225472 | bytes 12058624 | tf_op jit(solution)/shard_map/dot_general | solution.py:24
  331.9 7.5 %fusion.1 = f32[768,2048]{1,0:T(8,128)} fusion(bf16[1024,768]{1,0:T(8,128)(2,1)S(1)} %copy-done.16, bf16[1024,2176]{1,0:T(8,128)(2,1)} %bitcast.11.told), kind=kOutput, calls=%fused_computation.3 | convolution fusion | flops 3221225472 | bytes 12058624 | tf_op jit(solution)/shard_map/dot_general | solution.py:24
  339.4 29.6 %reduce_rows_4.1 = f32[128,2048]{1,0:T(8,128)S(1)} custom-call(bf16[4,128,2048]{2,1,0:T(8,128)(2,1)S(1)} %bitcast.74), custom_call_target="tpu_custom_call" | custom-call | bytes 3600000 | tf_op jit(solution)/shard_map/reduce_rows_4/pallas_call | solution.py:388
  369.1 4.3 convolution_convert_fusion.2
  373.4 4.7 %convolution_convert_fusion = bf16[2048,1280]{1,0:T(8,128)(2,1)} fusion(bf16[512,2048]{1,0:T(8,128)(2,1)S(1)} %bitcast.103, bf16[512,1280]{1,0:T(8,128)(2,1)S(1)} %get-tuple-element.74), kind=kOutput, calls=%fused_computation | convolution fusion | flops 2686976000 | bytes 8650752 | tf_op jit(solution)/shard_map/dot_general | solution.py:24
  378.2 0.3 fusion.11
  378.5 0.1 maximum_maximum_fusion.gains
  378.6 48.9 %scatter_weights.1 = (f32[32,2048]{1,0:T(8,128)S(1)}, f32[32,256]{1,0:T(8,128)S(1)}, f32[32,256]{1,0:T(8,128)S(1)}, f32[32,2048]{1,0:T(8,128)S(1)}, f32[40,128]{...) custom-call(bf16[4,2,4,2,32,1280]{5,4,3,2,1,0:T(8,128)(2,1)} %bitcast.82, ...), custom_call_target="tpu_custom_call" | custom-call | bytes 288000000 | tf_op jit(solution)/shard_map/scatter_weights/pallas_call | solution.py:576
  427.5 0.6 slice_bitcast_fusion
  428.1 0.5 slice_bitcast_fusion.2
  428.6 1.1 bitcast_convert_fusion
  429.7 1.4 fusion.10
  431.1 0.8 copy.56
  431.9 0.7 copy.57
  432.6 0.6 copy.58
  433.2 0.6 copy.59
  433.8 0.7 copy.60
  (57 shorter events, 0.2 us)
Async XLA Ops:
  0.6 50.9 %copy-start.14 = (bf16[128,2048]{1,0:T(8,128)(2,1)S(1)}, bf16[128,2048]{1,0:T(8,128)(2,1)}, u32[]{:S(2)}) copy-start(bf16[128,2048]{1,0:T(8,128)(2,1)} %param.31) | copy-start | bytes 1572868
  6.3 48.7 %copy-start.2 = (bf16[1024,128]{1,0:T(8,128)(2,1)}, bf16[1024,128]{1,0:T(8,128)(2,1)S(1)}, u32[]{:S(2)}) copy-start(bf16[1024,128]{1,0:T(8,128)(2,1)S(1)} %fusion.15.spread.slots) | copy-start | bytes 786436
  55.0 75.5 %all-to-all-start = ((bf16[128,8,2176]{2,1,0:T(8,128)(2,1)}), bf16[128,8,2176]{2,1,0:T(8,128)(2,1)}, u32[]{:S(2)}, u32[]{:S(2)}) async-start(bf16[128,8,2176]{2,1,0:T(8,128)(2,1)} %fusion), calls=%async_computation | async-start | bytes 8912896 | tf_op jit(solution)/shard_map/all_to_all | solution.py:1143
  64.0 6.2 %copy-start.7 = (f32[128]{0:T(128)S(1)}, f32[128]{0:T(128)}, u32[]{:S(2)}) copy-start(f32[128]{0:T(128)} %param.24) | copy-start | bytes 1540
  64.1 6.2 %copy-start.8 = (f32[128]{0:T(128)S(1)}, f32[128]{0:T(128)}, u32[]{:S(2)}) copy-start(f32[128]{0:T(128)} %param.25) | copy-start | bytes 1540
  64.1 14.3 %copy-start.19 = (bf16[4,2,4,2,32,1024]{5,4,3,2,1,0:T(8,128)(2,1)S(1)}, bf16[4,2,4,2,32,1024]{5,4,3,2,1,0:T(8,128)(2,1)}, u32[]{:S(2)}) copy-start(bf16[4,2,4,2,32,1024]{5,4,3,2,1,0:T(8,128)(2,1)} %get-tuple-element.60) | copy-start | bytes 12582916
  70.2 10.5 %copy-start = (f32[512,1280]{1,0:T(8,128)}, f32[512,1280]{1,0:T(8,128)S(1)}, u32[]{:S(2)}) copy-start(f32[512,1280]{1,0:T(8,128)S(1)} %fusion.23.raw) | copy-start | bytes 7864324
  78.4 2.4 copy-start.4
  78.4 2.4 copy-start.9
  80.8 48.5 %copy-start.11 = (bf16[128,2048]{1,0:T(8,128)(2,1)S(1)}, bf16[128,2048]{1,0:T(8,128)(2,1)}, u32[]{:S(2)}) copy-start(bf16[128,2048]{1,0:T(8,128)(2,1)} %param.16) | copy-start | bytes 1572868
  80.8 48.7 %copy-start.17 = (f32[2048]{0:T(1024)S(1)}, f32[2048]{0:T(1024)}, u32[]{:S(2)}) copy-start(f32[2048]{0:T(1024)} %param.26) | copy-start | bytes 24580
  264.1 5.5 %copy-start.15 = (bf16[128,2048]{1,0:T(8,128)(2,1)S(1)}, bf16[128,2048]{1,0:T(8,128)(2,1)}, u32[]{:S(2)}) copy-start(bf16[128,2048]{1,0:T(8,128)(2,1)} %param.31) | copy-start | bytes 1572868
  294.3 83.8 %all-to-all-start.1 = ((bf16[128,8,2048]{2,1,0:T(8,128)(2,1)}), bf16[128,8,2048]{2,1,0:T(8,128)(2,1)}, u32[]{:S(2)}, u32[]{:S(2)}) async-start(bf16[128,8,2048]{2,1,0:T(8,128)(2,1)} %bitcast.83), calls=%async_computation.1 | async-start | bytes 8388608 | tf_op jit(solution)/shard_map/all_to_all | solution.py:1180
  302.9 5.3 %copy-start.1 = (f32[512,1280]{1,0:T(8,128)S(1)}, f32[512,1280]{1,0:T(8,128)}, u32[]{:S(2)}) copy-start(f32[512,1280]{1,0:T(8,128)} %copy-done) | copy-start | bytes 7864324
  302.9 5.3 %copy-start.5 = (f32[2,8,256,256]{3,2,1,0:T(8,128)S(1)}, f32[2,8,256,256]{3,2,1,0:T(8,128)}, u32[]{:S(2)}) copy-start(f32[2,8,256,256]{3,2,1,0:T(8,128)} %copy-done.4) | copy-start | bytes 12582916
  315.0 5.8 %copy-start.20 = (bf16[4,2,4,2,2,8,2048]{6,5,4,3,2,1,0:T(8,128)(2,1)S(1)}, bf16[4,2,4,2,2,8,2048]{6,5,4,3,2,1,0:T(8,128)(2,1)}, u32[]{:S(2)}) copy-start(bf16[4,2,4,2,2,8,2048]{6,5,4,3,2,1,0:T(8,128)(2,1)} %get-tuple-element.65) | copy-start | bytes 12582916
  315.0 5.8 %copy-start.24 = (bf16[1024,768]{1,0:T(8,128)(2,1)S(1)}, bf16[1024,768]{1,0:T(8,128)(2,1)}, u32[]{:S(2)}) copy-start(bf16[1024,768]{1,0:T(8,128)(2,1)} %get-tuple-element.79) | copy-start | bytes 4718596
  320.8 5.6 %copy-start.23 = (bf16[1024,768]{1,0:T(8,128)(2,1)S(1)}, bf16[1024,768]{1,0:T(8,128)(2,1)}, u32[]{:S(2)}) copy-start(bf16[1024,768]{1,0:T(8,128)(2,1)} %get-tuple-element.78) | copy-start | bytes 4718596
  326.4 5.5 %copy-start.16 = (bf16[1024,768]{1,0:T(8,128)(2,1)S(1)}, bf16[1024,768]{1,0:T(8,128)(2,1)}, u32[]{:S(2)}) copy-start(bf16[1024,768]{1,0:T(8,128)(2,1)} %get-tuple-element.75) | copy-start | bytes 4718596
  339.4 29.6 %copy-start.10 = (bf16[512,1024]{1,0:T(8,128)(2,1)S(1)}, bf16[512,1024]{1,0:T(8,128)(2,1)}, u32[]{:S(2)}) copy-start(bf16[512,1024]{1,0:T(8,128)(2,1)} %copy-done.9) | copy-start | bytes 3145732
  339.4 29.7 %copy-start.22 = (bf16[4,128,2048]{2,1,0:T(8,128)(2,1)S(1)}, bf16[4,128,2048]{2,1,0:T(8,128)(2,1)}, u32[]{:S(2)}) copy-start(bf16[4,128,2048]{2,1,0:T(8,128)(2,1)} %get-tuple-element.71) | copy-start | bytes 6291460
  369.1 4.3 copy-start.21
  373.4 4.8 %copy-start.12 = (bf16[128,2048]{1,0:T(8,128)(2,1)S(1)}, bf16[128,2048]{1,0:T(8,128)(2,1)}, u32[]{:S(2)}) copy-start(bf16[128,2048]{1,0:T(8,128)(2,1)} %param.16) | copy-start | bytes 1572868
  373.4 4.8 %copy-start.18 = (f32[2048]{0:T(1024)S(1)}, f32[2048]{0:T(1024)}, u32[]{:S(2)}) copy-start(f32[2048]{0:T(1024)} %param.19) | copy-start | bytes 24580
  373.4 5.1 %copy-start.3 = (bf16[1024,128]{1,0:T(8,128)(2,1)S(1)}, bf16[1024,128]{1,0:T(8,128)(2,1)}, u32[]{:S(2)}) copy-start(bf16[1024,128]{1,0:T(8,128)(2,1)} %copy-done.2) | copy-start | bytes 786436
  373.4 5.1 %copy-start.6 = (bf16[16,128]{1,0:T(8,128)(2,1)S(1)}, bf16[16,128]{1,0:T(8,128)(2,1)}, u32[]{:S(2)}) copy-start(bf16[16,128]{1,0:T(8,128)(2,1)} %get-tuple-element.84.piece) | copy-start | bytes 12292
  378.5 51.1 %copy-start.13 = (f32[128,2048]{1,0:T(8,128)S(1)}, f32[128,2048]{1,0:T(8,128)}, u32[]{:S(2)}) copy-start(f32[128,2048]{1,0:T(8,128)} %get-tuple-element.101) | copy-start | bytes 3145732

commit v10 on v9

--- a/solution.py
+++ b/solution.py
@@ -74,6 +74,7 @@
 VMEM = pl.BlockSpec(memory_space=pltpu.VMEM)
 NX, NYH, NZ, NC = 4, 2, 4, 2
 RING = 4
+EARLY = 256
 
 
 def cost(microseconds):
@@ -159,7 +160,11 @@
                 copy.wait_send()
 
 
-def gather_kernel(q, k, v, o, tok, doc, wa, wb, toks, docs, send, recv, local):
+def gather_kernel(
+    q, k, v, o, hidden, gain, doc, spread, cot, chosen, wa, wb, toks, docs, told, later, *rest
+):
+    sources, mids = rest[:3], rest[3:9]
+    tok, stage, send, recv, local = rest[9:]
     me = Place()
     x, yh, z, c, p = me.x, me.yh, me.z, me.c, me.y
     sibling = me.device(c=1 - c)
@@ -167,8 +172,43 @@
     ring_x = (me.device(x=after(x)), me.device(x=before(x)))
     ring_z = (me.device(z=after(z)), me.device(z=before(z)))
     ring_y = (me.at_y(after(p)), me.at_y(before(p)))
-    greet([sibling, pair, *ring_x, *ring_z, *ring_y])
     go = Copies(send, recv, local)
+    route = Route(me, go)
+    greet(route.everyone())
+    slots, block = spread.shape[0], 256
+
+    def dispatch(n):
+        cols = pl.ds(n * EARLY, EARLY)
+        flat = sources[n].reshape(slots, EARLY)
+
+        def step(m, _):
+            at = pl.ds(pl.multiple_of(m * block, block), block)
+            flat[at] = dot_nn(spread[at], cot[:, cols]).astype(BF16)
+            return 0
+
+        lax.fori_loop(0, slots // block, step, 0)
+        return sources[n]
+
+    pushes = [None] * (slots // block)
+
+    def layout_later(m):
+        if m >= 2:
+            pushes[m - 2].wait()
+        at = pl.ds(m * block, block)
+        cut = cot.shape[1] - 3 * EARLY
+        stage[m % 2, :, :cut] = dot_nn(spread[at], cot[:, 3 * EARLY :]).astype(BF16)
+        stage[m % 2, :, cut:] = dot_nn(spread[at], chosen[...]).astype(BF16)
+        pushes[m] = go.keep(stage.at[m % 2], later.at[at])
+
+    crossed = [None] * 3
+
+    def cross(step):
+        for n in range(3):
+            if step > 0:
+                route.wait(crossed[n])
+            src = dispatch(n) if step == 0 else mids[2 * n + step - 1]
+            dst = columns(told, n * EARLY, EARLY) if step == 2 else mids[2 * n + step]
+            crossed[n] = route.send(TURNS[n][step], src, dst)
 
     shards, start = [], 0
     for ref, w in ((q, wa), (k, wa), (v, wa), (o, wb)):
@@ -182,6 +222,8 @@
 
     pairs = [go.put(part(ref, cols, 1 - yh), to, pair) for ref, cols, to in shards]
     kept = [go.keep(part(ref, cols, yh), to) for ref, cols, to in shards]
+    rows = hidden[...].astype(F32)
+    tok[...] = (rows * unit_rows(rows) * gain[...]).astype(BF16)
     for copy in kept:
         copy.wait()
     for copy in pairs:
@@ -208,19 +250,23 @@
     near = [both(unit(i, j), one) for i, j, one, two, unit, slab in ways]
     own = [both(unit(i, j), two) for i, j, one, two, unit, slab in ways]
     rows = [go.put(tok, toks.at[p], peer) for peer in ring_y]
-    rest = [go.keep(tok, toks.at[p]), go.keep(doc, docs.at[yh])]
+    kept_rows = [go.keep(tok, toks.at[p]), go.keep(doc, docs.at[yh])]
     tail = [go.put(doc, docs.at[yh], pair)]
+    cross(0)
     far = [
         relay(unit(before(i), j), unit(after(i), j), copies, one)
         for (i, j, one, two, unit, slab), copies in zip(ways, near)
     ]
     low = [both(unit(before(i), j), two) for i, j, one, two, unit, slab in ways]
     high = [both(unit(after(i), j), two) for i, j, one, two, unit, slab in ways]
+    layout_later(0)
     last = []
     for (i, j, one, two, unit, slab), copies in zip(ways, far):
         arrived(copies)
         last.append(both(unit(across(i), j), two))
         tail.append(go.put(slab(j), slab(j), sibling))
+    cross(1)
+    layout_later(1)
     half = tok.shape[0] // 2
     rows[0].wait_recv()
     piece = toks.at[before(p), pl.ds(0, half)]
@@ -233,6 +279,10 @@
         for n, (i, j, one, two, unit, slab) in enumerate(ways):
             u = place(i)
             ends[n] += relay(unit(u, before(j)), unit(u, after(j)), copies[n], two)
+        if copies is high:
+            cross(2)
+            layout_later(2)
+            layout_later(3)
     for i, j, one, two, unit, slab in ways:
         tail.append(go.put(slab(before(j)), slab(before(j)), sibling))
         tail.append(go.put(slab(after(j)), slab(after(j)), sibling))
@@ -240,41 +290,55 @@
         arrived(copies)
         tail.append(go.put(slab(across(j)), slab(across(j)), sibling))
     arrived(tail)
-    for copy in rest:
+    for copy in (*kept_rows, *pushes[-2:]):
         copy.wait()
+    for sent in crossed:
+        route.wait(sent)
     go.finish()
 
 
-def gather(query, key, value, out, tokens, docs):
+def gather(query, key, value, out, hidden, gain, docs, spread, cot, chosen):
     rows = query.shape[0]
     width_a = (query.shape[1] + key.shape[1] + value.shape[1]) // NYH
     width_b = out.shape[1] // NYH
     lead = (NX, NYH, NZ, NC, rows)
-    wa, wb, toks, docs = pl.pallas_call(
+    slots, width = spread.shape[0], cot.shape[1]
+    blocks = (*DIMS, slots // math.prod(DIMS))
+    left = width - 3 * EARLY + chosen.shape[1]
+    wa, wb, toks, docs, told, later = pl.pallas_call(
         gather_kernel,
         name="gather_weights",
         cost_estimate=cost(60),
         out_shape=(
             jax.ShapeDtypeStruct((*lead, width_a), BF16),
             jax.ShapeDtypeStruct((*lead, width_b), BF16),
-            jax.ShapeDtypeStruct((RING, *tokens.shape), BF16),
+            jax.ShapeDtypeStruct((RING, *hidden.shape), BF16),
             jax.ShapeDtypeStruct((NYH, *docs.shape), docs.dtype),
+            jax.ShapeDtypeStruct((*blocks, 3 * EARLY), BF16),
+            jax.ShapeDtypeStruct((slots, left), BF16),
         ),
-        in_specs=[ANY] * 6,
-        out_specs=(ANY,) * 4,
+        in_specs=[*(ANY,) * 4, VMEM, VMEM, ANY, VMEM, VMEM, VMEM],
+        out_specs=(ANY,) * 6,
         scratch_shapes=[
-            pltpu.SemaphoreType.DMA((57,)),
-            pltpu.SemaphoreType.DMA((57,)),
-            pltpu.SemaphoreType.DMA((6,)),
+            *(pltpu.VMEM((*blocks, EARLY), BF16) for _ in range(9)),
+            pltpu.VMEM(hidden.shape, BF16),
+            pltpu.VMEM((2, 256, left), BF16),
+            pltpu.SemaphoreType.DMA((96,)),
+            pltpu.SemaphoreType.DMA((96,)),
+            pltpu.SemaphoreType.DMA((19,)),
         ],
-        compiler_params=pltpu.CompilerParams(collective_id=1, has_side_effects=True),
-    )(query, key, value, out, tokens, docs)
+        compiler_params=pltpu.CompilerParams(
+            collective_id=1, has_side_effects=True, vmem_limit_bytes=24 << 20
+        ),
+    )(query, key, value, out, hidden, gain.reshape(1, -1), docs, spread, cot, chosen)
     depth = NX * NYH * NZ * NC * rows
     return (
         wa.reshape(depth, width_a),
         wb.reshape(depth, width_b),
-        toks.reshape(RING * tokens.shape[0], tokens.shape[1]),
+        toks.reshape(RING * hidden.shape[0], hidden.shape[1]),
         docs,
+        told.reshape(slots, 3 * EARLY),
+        later,
     )
 
 
@@ -815,7 +879,7 @@
 
 
 def experts_kernel(
-    tokens, spread, told, gate, up, down, router, rows, inner_low, grad_gate, grad_up, summed, expert_out, *rest
+    tokens, spread, told, later, gate, up, down, router, rows, inner_low, grad_gate, grad_up, summed, expert_out, *rest
 ):
     chunks = len(CHUNKS)
     taken = iter(rest)
@@ -842,7 +906,7 @@
     late = [
         pltpu.make_async_copy(a, b, loads.at[2 + n])
         for n, (a, b) in enumerate(
-            ((down, down_v), (gate, gate_v), (up, up_v), (router, router_v), (told.at[:, pl.ds(width, lanes)], asked_v))
+            ((down, down_v), (gate, gate_v), (up, up_v), (router, router_v), (later.at[:, pl.ds(width - told.shape[1], lanes)], asked_v))
         )
     ]
     for pull in early:
@@ -852,8 +916,13 @@
         pull.wait()
 
     def load(m):
-        at = pl.ds(m * block, block)
-        return pltpu.make_async_copy(told.at[at, pl.ds(0, width)], blocks_v.at[m % 2], told_sem.at[m % 2])
+        at, cut = pl.ds(m * block, block), told.shape[1]
+        return [
+            pltpu.make_async_copy(told.at[at], blocks_v.at[m % 2, :, pl.ds(0, cut)], told_sem.at[0, m % 2]),
+            pltpu.make_async_copy(
+                later.at[at, pl.ds(0, width - cut)], blocks_v.at[m % 2, :, pl.ds(cut, width - cut)], told_sem.at[1, m % 2]
+            ),
+        ]
 
     def each_block(step):
         def run(m, _):
@@ -879,11 +948,13 @@
         return columns(buffer, 0, CHUNKS[n])
 
     def cotangent(m):
-        load(m).wait()
+        for pull in load(m):
+            pull.wait()
         at = pl.ds(m * block, block)
         inner_up[at] = dot_nt(blocks_v[m % 2], down_v[...])
         if m + 2 < len(blocks):
-            load(m + 2).start()
+            for pull in load(m + 2):
+                pull.start()
 
     def multiply(n, close=False):
         way_in.wait(sent_on[n])
@@ -946,9 +1017,7 @@
             elif todo and triple + crossing > 1 and crossing > 0:
                 cotangent(todo.pop(0))
         if (triple, crossing) == (1, 0):
-            load(0).start()
-            load(1).start()
-            for pull in late:
+            for pull in (*load(0), *load(1), *late):
                 pull.start()
             late[0].wait()
         if (triple, crossing) == (2, 1):
@@ -1020,7 +1089,7 @@
     back.finish()
 
 
-def experts(tokens, spread, told, gate, up, down, router):
+def experts(tokens, spread, told, later, gate, up, down, router):
     tok, width = tokens.shape
     slots = spread.shape[0]
     hidden, lanes = gate.shape[1], router.shape[1]
@@ -1044,7 +1113,7 @@
             jax.ShapeDtypeStruct((tok, sum(BACK)), F32),
             jax.ShapeDtypeStruct((slots, width), BF16),
         ),
-        in_specs=[ANY] * 7,
+        in_specs=[ANY] * 8,
         out_specs=(ANY, ANY, ANY, ANY, VMEM, ANY),
         scratch_shapes=[
             *held(CHUNKS[:4]),
@@ -1073,13 +1142,13 @@
             pltpu.SemaphoreType.DMA((13 * chunks,)),
             pltpu.SemaphoreType.DMA((3 * chunks,)),
             pltpu.SemaphoreType.DMA((7,)),
-            pltpu.SemaphoreType.DMA((2,)),
+            pltpu.SemaphoreType.DMA((2, 2)),
             pltpu.SemaphoreType.DMA((7,)),
         ],
         compiler_params=pltpu.CompilerParams(
             collective_id=6, has_side_effects=True, vmem_limit_bytes=61 << 20
         ),
-    )(tokens, spread, told, gate, up, down, router)
+    )(tokens, spread, told, later, gate, up, down, router)
     return rows.reshape(slots, width), *others
 
 
@@ -1127,22 +1196,22 @@
     ).astype(BF16).reshape(slots, tok)
 
     hidden = hidden_in.astype(F32)
-    normed_local = rms_scale(hidden, attn_gain).astype(BF16)
-
-    in_weights, out_weights, normed, docs = gather(
+
+    in_weights, out_weights, normed, docs, told, later = gather(
         query_weight,
         key_weight,
         value_weight,
         output_weight.T,
-        normed_local,
+        hidden_in,
+        attn_gain,
         jnp.broadcast_to(doc_ids, (8, tokens)).astype(F32),
+        spread,
+        cotangent,
+        chosen.astype(BF16),
     )
-
-    spread_late, docs = lax.optimization_barrier((spread, docs))
-    cot_out = dot_nn(spread_late, jnp.concatenate([cotangent, chosen.astype(BF16)], axis=1)).astype(BF16)
-    cot_in = lax.all_to_all(
-        cot_out.reshape(count, cap, width + count), both, split_axis=0, concat_axis=0, tiled=True
-    ).reshape(slots, width + count)
+    later = lax.all_to_all(
+        later.reshape(count, cap, later.shape[1]), both, split_axis=0, concat_axis=0, tiled=True
+    ).reshape(slots, later.shape[1])
 
     position, allowed = jax.vmap(layout)(docs[:, 0])
     cosine, sine = rotary(position.reshape(-1), hd)
@@ -1156,10 +1225,10 @@
 
     residual = hidden + attn_out
     moe_input = rms_scale(residual, moe_gain).astype(BF16)
-    moe_input, cot_in = lax.optimization_barrier((moe_input, cot_in))
+    moe_input, later = lax.optimization_barrier((moe_input, later))
     gate_mat, up_mat, down_mat = gate_weight[0], up_weight[0], down_weight[0]
     rows, inner_low, grad_gate, grad_up, summed, expert_out = experts(
-        moe_input, spread, cot_in, gate_mat, up_mat, down_mat, router_weight
+        moe_input, spread, told, later, gate_mat, up_mat, down_mat, router_weight
     )
     logits = dot_nn(moe_input, router_weight)
     masked = jnp.where(chosen > 0, logits, MASKED)
@@ -1185,10 +1254,11 @@
     grad_raw, head_gains = attend_back(
         raw, cosine, signed, query_gain, key_gain, query, kv, attention, grad_mixed, scale
     )
-    inner_low, rows, cot_in, grad_raw = lax.optimization_barrier(
-        (inner_low, rows, cot_in, grad_raw)
+    inner_low, rows, told, later, grad_raw = lax.optimization_barrier(
+        (inner_low, rows, told, later, grad_raw)
     )
-    down_grad = dot_tn(inner_low, cot_in[:, :width])
+    cot_rows = jnp.concatenate([told, later[:, : width - told.shape[1]]], axis=1)
+    down_grad = dot_tn(inner_low, cot_rows)
     gate_grad = dot_tn(rows, grad_gate)
     up_grad = dot_tn(rows, grad_up)
     normed_part, down_grad, gate_grad, up_grad = lax.optimization_barrier(

time: 439 us -> 441 us (level)
  local copies, waits for them, and re-layouts: 7.17 us -> 23.1 us
  matrix products: 56.6 us -> 46.4 us
    pallas_call x1, Pallas kernels: 44.6 us -> 62.9 us  [gather(): pl.pallas_call(gather_kernel, name='gather_weights', cost_estimate=cost(6...]
    unnamed x58 -> x102, local copies, waits for them, and re-layouts: 4.41 us -> 19.6 us
    pallas_call x2, Pallas kernels: 78 us -> 63.6 us  [reduce(): pl.pallas_call(reduce_kernel, name=f'reduce_rows_{ident}', cost_estimate=...]
    dot_general x5 -> x4, matrix products: 16.5 us -> 11.3 us  [dot_nn(): lax.dot_general(a, b, (((1,), (0,)), ((), ())), preferred_element_type=F32)]
  transfers between devices with their start and end apart: 2 -> 2, of which waited for: 0 -> 0; matrix products, arithmetic and copies ran while one was open for 12% -> 11% of each run, Pallas kernels for 21% -> 18%
where the time goes in v10:
time: 441 us; the launch traced here: 436 us
  Pallas kernels  343 us (78%)
  matrix products  46.4 us (11%)
  local copies, waits for them, and re-layouts  23.1 us (5%)
  starting transfers between devices  13 us (3%)
  other arithmetic  9 us (2%)
    pallas_call x1, Pallas kernels, experts(): pl.pallas_call(experts_kernel, name='experts', cost_estimate=cost(120), o...  129 us
    pallas_call x2, Pallas kernels, reduce(): pl.pallas_call(reduce_kernel, name=f'reduce_rows_{ident}', cost_estimate=...  63.6 us
    pallas_call x1, Pallas kernels, gather(): pl.pallas_call(gather_kernel, name='gather_weights', cost_estimate=cost(6...  62.9 us
    pallas_call x1, Pallas kernels, scatter(): pl.pallas_call(scatter_kernel, name='scatter_weights', cost_estimate=cost...  48.7 us
    dot_general x6, matrix products, dot_tn(): lax.dot_general(a, b, (((0,), (0,)), ((), ())), preferred_element_type=F32)  27.7 us
    pallas_call x1, Pallas kernels, share(): pl.pallas_call(share_kernel, name=f'share_rows_{ident}', cost_estimate=co...  23.5 us
    unnamed x102, local copies, waits for them, and re-layouts  19.6 us
    dot_general x4, matrix products, dot_nn(): lax.dot_general(a, b, (((1,), (0,)), ((), ())), preferred_element_type=F32)  11.3 us
  transfers between devices with their start and end apart: 2, of which 0 were waited for; matrix products, arithmetic and copies ran while one was open for 11% of the time, Pallas kernels for 18%

profile of v10, /device:TPU:1, one launch (start us, length us, event | category | flops | bytes accessed | tf_op | source)
XLA Modules:
  0.0 435.7 jit_solution(1615925845868483612)
XLA Ops:
  0.6 0.8 copy.38
  1.4 0.2 convert_reduce_fusion
  1.7 0.1 convolution_select_fusion.1
  1.8 0.1 copy.40
  2.0 0.1 eq.54
  2.1 0.7 convert_element_type.74
  2.7 0.2 fusion.11.spread.slots
  3.0 1.1 copy-done.2
  4.1 1.0 copy-done.10
  5.1 0.9 copy-done.18
  6.0 0.9 copy-done.19
  7.0 0.7 copy-done.20
  7.7 0.7 copy-done.22
  8.4 0.7 copy-done.23
  9.1 62.9 %gather_weights.1 = (bf16[4,2,4,2,32,1280]{5,4,3,2,1,0:T(8,128)(2,1)S(1)}, bf16[4,2,4,2,32,1024]{5,4,3,2,1,0:T(8,128)(2,1)S(1)}, bf16[4,128,2048]{2,1,0:T(8,128)...) custom-call(bf16[32,2048]{1,0:T(8,128)(2,1)S(1)} %copy-done.18, ...), custom_call_target="tpu_custom_call" | custom-call | bytes 216000000 | tf_op jit(solution)/shard_map/gather_weights/pallas_call | solution.py:308
  72.0 1.2 copy-done.12
  73.2 2.4 copy-done.27
  75.6 2.0 copy-done.28
  77.6 1.4 copy-done.30
  79.0 5.0 %all-to-all-start = ((bf16[128,8,1408]{2,1,0:T(8,128)(2,1)}), bf16[128,8,1408]{2,1,0:T(8,128)(2,1)}, u32[]{:S(2)}, u32[]{:S(2)}) async-start(bf16[128,8,1408]{2,1,0:T(8,128)(2,1)} %bitcast.11), calls=%async_computation | async-start | bytes 5767168 | tf_op jit(solution)/shard_map/all_to_all | solution.py:1212
  84.0 0.3 select_reduce_fusion
  84.3 1.0 fusion.13
  85.3 0.2 pad_maximum_fusion
  85.6 0.2 fusion.12.bias
  85.8 5.5 %fusion.19.raw = f32[512,1280]{1,0:T(8,128)S(1)} fusion(bf16[512,2048]{1,0:T(8,128)(2,1)S(1)} %bitcast.91, bf16[2048,1280]{1,0:T(8,128)(2,1)} %bitcast.85), kind=kOutput, calls=%fused_computation.75 | convolution fusion | flops 2684354560 | bytes 9961472 | tf_op jit(solution)/shard_map/dot_general | solution.py:28
  91.4 8.1 %attend.1 = (bf16[512,1024]{1,0:T(8,128)(2,1)S(1)}, bf16[512,256]{1,0:T(8,128)(2,1)S(1)}, f32[2,8,256,256]{3,2,1,0:T(8,128)S(1)}, bf16[512,1024]{1,0:T(8,128)(2,1)S(1)}) custom-call(f32[512,1280]{1,0:T(8,128)S(1)} %fusion.19.raw, f32[2,256,256]{2,1,0:T(8,128)S(1)} %fusion.12.bias, f32[512,128]{1,0:T(8,128)S(1)} %get-tuple-element.123.cosine, ...), custom_call_target="tpu_custom_call" | custom-call | bytes 28800000 | tf_op jit(solution)/shard_map/attend/pallas_call | solution.py:717
  99.5 1.0 copy-done.14
  100.5 0.7 copy-done.16
  101.2 2.4 convolution_convert_fusion.2
  103.6 31.2 %reduce_rows_2.1 = f32[128,2048]{1,0:T(8,128)S(1)} custom-call(bf16[4,128,2048]{2,1,0:T(8,128)(2,1)S(1)} %bitcast.75), custom_call_target="tpu_custom_call" | custom-call | bytes 3600000 | tf_op jit(solution)/shard_map/reduce_rows_2/pallas_call | solution.py:452
  135.0 0.3 multiply_reduce_fusion.2
  135.3 0.2 multiply_convert_fusion.tokens
  135.5 0.4 copy-done.36
  135.9 0.4 fusion.18
  136.3 0.2 fusion.15
  136.5 129.1 %experts.1 = (bf16[4,2,4,2,2,8,2048]{6,5,4,3,2,1,0:T(8,128)(2,1)}, bf16[1024,768]{1,0:T(8,128)(2,1)}, bf16[1024,768]{1,0:T(8,128)(2,1)}, bf16[1024,768]{1,0:T(8,...) custom-call(bf16[128,2048]{1,0:T(8,128)(2,1)} %copy-done.35, bf16[1024,128]{1,0:T(8,128)(2,1)} %copy-done.4, ...), custom_call_target="tpu_custom_call" | custom-call | bytes 432000000 | tf_op jit(solution)/shard_map/experts/pallas_call | solution.py:1104
  265.6 1.1 multiply_reduce_fusion.3
  266.7 2.3 convolution_convert_fusion.4
  269.0 1.9 multiply_reduce_fusion
  270.9 1.5 fusion.17
  272.4 23.5 %share_rows_3.1 = (bf16[4,128,2048]{2,1,0:T(8,128)(2,1)}, bf16[16,128]{1,0:T(8,128)(2,1)}) custom-call(bf16[128,2048]{1,0:T(8,128)(2,1)} %get-tuple-element.102.tok, bf16[4,2,4,2,2,16,128]{6,5,4,3,2,1,0:T(8,128)(2,1)} %bitcast.99), custom_call_target="tpu_custom_call" | custom-call | bytes 72000000 | tf_op jit(solution)/shard_map/share_rows_3/pallas_call | solution.py:394
  296.0 8.0 %all-to-all-start.1 = ((bf16[128,8,2048]{2,1,0:T(8,128)(2,1)}), bf16[128,8,2048]{2,1,0:T(8,128)(2,1)}, u32[]{:S(2)}, u32[]{:S(2)}) async-start(bf16[128,8,2048]{2,1,0:T(8,128)(2,1)} %bitcast.94), calls=%async_computation.1 | async-start | bytes 8388608 | tf_op jit(solution)/shard_map/all_to_all | solution.py:1249
  304.1 5.3 %convolution_convert_fusion.5.grad_mixed = bf16[512,1024]{1,0:T(8,128)(2,1)S(1)} fusion(bf16[512,2048]{1,0:T(8,128)(2,1)} %bitcast.108, bf16[2048,1024]{1,0:T(8,128)(2,1)} %bitcast.89), kind=kOutput, calls=%fused_computation.15 | convolution fusion | flops 2148007936 | bytes 7340032 | tf_op jit(solution)/shard_map/dot_general | solution.py:28
  309.4 6.6 %attend_back.1 = (bf16[512,1280]{1,0:T(8,128)(2,1)S(1)}, f32[2,128]{1,0:T(2,128)S(1)}) custom-call(f32[512,1280]{1,0:T(8,128)S(1)} %copy-done.1, f32[512,128]{1,0:T(8,128)S(1)} %get-tuple-element.123.cosine, f32[512,128]{1,0:T(8,128)S(1)} %copy-done.9, f32[1,128]{1,0:T(1,128)S(1)} %bitcast.82, f32[1,128]{1,0:T(1,128)S(1)} %bitcast.84, ...), custom_call_target="tpu_custom_call" | custom-call | bytes 3600000 | tf_op jit(solution)/shard_map/attend_back/pallas_call | solution.py:794
  316.0 2.1 slice.31
  318.1 0.1 copy-done.13
  318.2 5.4 %fusion = f32[768,2048]{1,0:T(8,128)} fusion(bf16[1024,768]{1,0:T(8,128)(2,1)S(1)} %copy-done.44, bf16[1024,1280]{1,0:T(8,128)(2,1)S(1)} %slice.31, bf16[1024,768]{1,0:T(8,128)(2,1)S(1)} %bitcast.77), kind=kOutput, calls=%fused_computation.1 | convolution fusion | flops 3229614080 | bytes 12058624 | tf_op jit(solution)/shard_map/dot_general | solution.py:24
  323.7 3.1 convolution_convert_fusion.3
  326.8 5.4 %fusion.21 = f32[2048,768]{1,0:T(8,128)} fusion(bf16[1024,2048]{1,0:T(8,128)(2,1)S(1)} %bitcast.106, bf16[1024,768]{1,0:T(8,128)(2,1)S(1)} %copy-done.43), kind=kOutput, calls=%fused_computation.77 | convolution fusion | flops 3221225472 | bytes 12058624 | tf_op jit(solution)/shard_map/dot_general | solution.py:24
  332.3 5.5 %fusion.20 = f32[2048,768]{1,0:T(8,128)} fusion(bf16[1024,2048]{1,0:T(8,128)(2,1)S(1)} %bitcast.107, bf16[1024,768]{1,0:T(8,128)(2,1)S(1)} %copy-done.42), kind=kOutput, calls=%fused_computation.76 | convolution fusion | flops 3221225472 | bytes 12058624 | tf_op jit(solution)/shard_map/dot_general | solution.py:24
  337.8 32.4 %reduce_rows_4.1 = f32[128,2048]{1,0:T(8,128)S(1)} custom-call(bf16[4,128,2048]{2,1,0:T(8,128)(2,1)S(1)} %bitcast.74), custom_call_target="tpu_custom_call" | custom-call | bytes 3600000 | tf_op jit(solution)/shard_map/reduce_rows_4/pallas_call | solution.py:452
  370.2 4.3 convolution_convert_fusion.1
  374.5 4.7 %convolution_convert_fusion = bf16[2048,1280]{1,0:T(8,128)(2,1)} fusion(bf16[512,2048]{1,0:T(8,128)(2,1)S(1)} %bitcast.92, bf16[512,1280]{1,0:T(8,128)(2,1)S(1)} %get-tuple-element.75), kind=kOutput, calls=%fused_computation | convolution fusion | flops 2686976000 | bytes 8650752 | tf_op jit(solution)/shard_map/dot_general | solution.py:24
  379.3 0.3 fusion.10
  379.6 48.7 %scatter_weights.1 = (f32[32,2048]{1,0:T(8,128)S(1)}, f32[32,256]{1,0:T(8,128)S(1)}, f32[32,256]{1,0:T(8,128)S(1)}, f32[32,2048]{1,0:T(8,128)S(1)}, f32[40,128]{...) custom-call(bf16[4,2,4,2,32,1280]{5,4,3,2,1,0:T(8,128)(2,1)} %bitcast.93, ...), custom_call_target="tpu_custom_call" | custom-call | bytes 288000000 | tf_op jit(solution)/shard_map/scatter_weights/pallas_call | solution.py:640
  428.4 0.6 slice_bitcast_fusion
  429.0 0.5 slice_bitcast_fusion.2
  429.5 1.1 bitcast_convert_fusion
  430.6 1.4 fusion.9
  432.0 0.8 copy.56
  432.8 0.7 copy.57
  433.5 0.6 copy.58
  434.1 0.6 copy.59
  434.7 0.7 copy.60
  (100 shorter events, 0.5 us)
Async XLA Ops:
  2.9 76.0 %copy-start.4 = (bf16[1024,128]{1,0:T(8,128)(2,1)}, bf16[1024,128]{1,0:T(8,128)(2,1)S(1)}, u32[]{:S(2)}) copy-start(bf16[1024,128]{1,0:T(8,128)(2,1)S(1)} %fusion.11.spread.slots) | copy-start | bytes 786436
  3.0 1.1 copy-start.2
  4.1 1.0 copy-start.10
  5.1 0.9 copy-start.18
  6.0 0.9 copy-start.19
  7.0 0.7 copy-start.20
  7.6 0.7 copy-start.22
  8.4 0.7 copy-start.23
  72.0 1.2 copy-start.12
  73.2 2.4 copy-start.27
  75.6 2.0 copy-start.28
  77.6 1.4 copy-start.30
  79.0 56.5 %all-to-all-start = ((bf16[128,8,1408]{2,1,0:T(8,128)(2,1)}), bf16[128,8,1408]{2,1,0:T(8,128)(2,1)}, u32[]{:S(2)}, u32[]{:S(2)}) async-start(bf16[128,8,1408]{2,1,0:T(8,128)(2,1)} %bitcast.11), calls=%async_computation | async-start | bytes 5767168 | tf_op jit(solution)/shard_map/all_to_all | solution.py:1212
  84.0 1.8 copy-start.31
  85.5 5.8 %copy-start.8 = (f32[512,128]{1,0:T(8,128)}, f32[512,128]{1,0:T(8,128)S(1)}, u32[]{:S(2)}) copy-start(f32[512,128]{1,0:T(8,128)S(1)} %get-tuple-element.124.signed) | copy-start | bytes 786436
  85.8 5.6 %copy-start.25 = (f32[128]{0:T(128)S(1)}, f32[128]{0:T(128)}, u32[]{:S(2)}) copy-start(f32[128]{0:T(128)} %param.24) | copy-start | bytes 1540
  85.8 5.6 %copy-start.26 = (f32[128]{0:T(128)S(1)}, f32[128]{0:T(128)}, u32[]{:S(2)}) copy-start(f32[128]{0:T(128)} %param.25) | copy-start | bytes 1540
  85.8 15.4 %copy-start.29 = (bf16[4,2,4,2,32,1024]{5,4,3,2,1,0:T(8,128)(2,1)S(1)}, bf16[4,2,4,2,32,1024]{5,4,3,2,1,0:T(8,128)(2,1)}, u32[]{:S(2)}) copy-start(bf16[4,2,4,2,32,1024]{5,4,3,2,1,0:T(8,128)(2,1)} %copy-done.28) | copy-start | bytes 12582916
  91.3 12.2 %copy-start = (f32[512,1280]{1,0:T(8,128)}, f32[512,1280]{1,0:T(8,128)S(1)}, u32[]{:S(2)}) copy-start(f32[512,1280]{1,0:T(8,128)S(1)} %fusion.19.raw) | copy-start | bytes 7864324
  99.5 1.0 copy-start.14
  100.5 0.7 copy-start.16
  101.2 2.4 copy-start.6
  101.2 2.4 copy-start.33
  103.6 31.4 %copy-start.3 = (bf16[128,2048]{1,0:T(8,128)(2,1)S(1)}, bf16[128,2048]{1,0:T(8,128)(2,1)}, u32[]{:S(2)}) copy-start(bf16[128,2048]{1,0:T(8,128)(2,1)} %hidden.1) | copy-start | bytes 1572868
  103.6 31.7 %copy-start.39 = (f32[2048]{0:T(1024)S(1)}, f32[2048]{0:T(1024)}, u32[]{:S(2)}) copy-start(f32[2048]{0:T(1024)} %param.26) | copy-start | bytes 24580
  134.9 1.0 copy-start.36
  135.4 1.0 copy-start.35
  136.5 132.6 %copy-start.37 = (bf16[2048,128]{1,0:T(8,128)(2,1)S(1)}, bf16[2048,128]{1,0:T(8,128)(2,1)}, u32[]{:S(2)}) copy-start(bf16[2048,128]{1,0:T(8,128)(2,1)} %router.1) | copy-start | bytes 1572868
  265.6 5.3 %copy-start.11 = (bf16[128,2048]{1,0:T(8,128)(2,1)S(1)}, bf16[128,2048]{1,0:T(8,128)(2,1)}, u32[]{:S(2)}) copy-start(bf16[128,2048]{1,0:T(8,128)(2,1)} %cot.1) | copy-start | bytes 1572868
  296.0 83.3 %all-to-all-start.1 = ((bf16[128,8,2048]{2,1,0:T(8,128)(2,1)}), bf16[128,8,2048]{2,1,0:T(8,128)(2,1)}, u32[]{:S(2)}, u32[]{:S(2)}) async-start(bf16[128,8,2048]{2,1,0:T(8,128)(2,1)} %bitcast.94), calls=%async_computation.1 | async-start | bytes 8388608 | tf_op jit(solution)/shard_map/all_to_all | solution.py:1249
  304.0 5.4 %copy-start.1 = (f32[512,1280]{1,0:T(8,128)S(1)}, f32[512,1280]{1,0:T(8,128)}, u32[]{:S(2)}) copy-start(f32[512,1280]{1,0:T(8,128)} %copy-done) | copy-start | bytes 7864324
  304.0 5.4 %copy-start.7 = (f32[2,8,256,256]{3,2,1,0:T(8,128)S(1)}, f32[2,8,256,256]{3,2,1,0:T(8,128)}, u32[]{:S(2)}) copy-start(f32[2,8,256,256]{3,2,1,0:T(8,128)} %copy-done.6) | copy-start | bytes 12582916
  304.0 5.4 %copy-start.9 = (f32[512,128]{1,0:T(8,128)S(1)}, f32[512,128]{1,0:T(8,128)}, u32[]{:S(2)}) copy-start(f32[512,128]{1,0:T(8,128)} %copy-done.8) | copy-start | bytes 786436
  304.0 5.4 %copy-start.15 = (bf16[512,1024]{1,0:T(8,128)(2,1)S(1)}, bf16[512,1024]{1,0:T(8,128)(2,1)}, u32[]{:S(2)}) copy-start(bf16[512,1024]{1,0:T(8,128)(2,1)} %copy-done.14) | copy-start | bytes 3145732
  304.0 5.4 %copy-start.17 = (bf16[512,256]{1,0:T(8,128)(2,1)S(1)}, bf16[512,256]{1,0:T(8,128)(2,1)}, u32[]{:S(2)}) copy-start(bf16[512,256]{1,0:T(8,128)(2,1)} %copy-done.16) | copy-start | bytes 786436
  309.4 8.7 %copy-start.44 = (bf16[1024,768]{1,0:T(8,128)(2,1)S(1)}, bf16[1024,768]{1,0:T(8,128)(2,1)}, u32[]{:S(2)}) copy-start(bf16[1024,768]{1,0:T(8,128)(2,1)} %get-tuple-element.76) | copy-start | bytes 4718596
  316.0 2.2 copy-start.13
  316.0 7.6 %slice-start = ((s8[5242880]{0:T(1024)(128)(4,1)}), s8[4194304]{0:T(1024)(128)(4,1)S(1)}, s32[]{:S(2)}) async-start(s8[5242880]{0:T(1024)(128)(4,1)} %bitcast.86), calls=%async_computation.2 | async-start | bytes 8388608
  318.2 5.5 %slice-start.1 = ((s8[5242880]{0:T(1024)(128)(4,1)}), s8[1048576]{0:T(1024)(128)(4,1)S(1)}, s32[]{:S(2)}) async-start(s8[5242880]{0:T(1024)(128)(4,1)} %bitcast.86), calls=%async_computation.3 | async-start | bytes 2097152
  323.6 3.2 copy-start.40
  323.7 3.2 copy-start.43
  326.8 5.4 %copy-start.42 = (bf16[1024,768]{1,0:T(8,128)(2,1)S(1)}, bf16[1024,768]{1,0:T(8,128)(2,1)}, u32[]{:S(2)}) copy-start(bf16[1024,768]{1,0:T(8,128)(2,1)} %get-tuple-element.80) | copy-start | bytes 4718596
  337.8 32.4 %copy-start.34 = (bf16[512,1024]{1,0:T(8,128)(2,1)S(1)}, bf16[512,1024]{1,0:T(8,128)(2,1)}, u32[]{:S(2)}) copy-start(bf16[512,1024]{1,0:T(8,128)(2,1)} %copy-done.33) | copy-start | bytes 3145732
  337.8 32.4 %copy-start.41 = (bf16[4,128,2048]{2,1,0:T(8,128)(2,1)S(1)}, bf16[4,128,2048]{2,1,0:T(8,128)(2,1)}, u32[]{:S(2)}) copy-start(bf16[4,128,2048]{2,1,0:T(8,128)(2,1)} %get-tuple-element.72) | copy-start | bytes 6291460
  370.2 4.3 copy-start.32
  374.5 4.7 %copy-start.21 = (f32[2048]{0:T(1024)S(1)}, f32[2048]{0:T(1024)}, u32[]{:S(2)}) copy-start(f32[2048]{0:T(1024)} %param.19) | copy-start | bytes 24580
  374.5 5.1 %copy-start.5 = (bf16[1024,128]{1,0:T(8,128)(2,1)S(1)}, bf16[1024,128]{1,0:T(8,128)(2,1)}, u32[]{:S(2)}) copy-start(bf16[1024,128]{1,0:T(8,128)(2,1)} %copy-done.4) | copy-start | bytes 786436
  374.5 5.1 %copy-start.24 = (bf16[16,128]{1,0:T(8,128)(2,1)S(1)}, bf16[16,128]{1,0:T(8,128)(2,1)}, u32[]{:S(2)}) copy-start(bf16[16,128]{1,0:T(8,128)(2,1)} %get-tuple-element.86.piece) | copy-start | bytes 12292
  379.6 50.9 %copy-start.38 = (f32[128,2048]{1,0:T(8,128)S(1)}, f32[128,2048]{1,0:T(8,128)}, u32[]{:S(2)}) copy-start(f32[128,2048]{1,0:T(8,128)} %get-tuple-element.103) | copy-start | bytes 3145732

commit v11 on v10

--- a/solution.py
+++ b/solution.py
@@ -161,10 +161,10 @@
 
 
 def gather_kernel(
-    q, k, v, o, hidden, gain, doc, spread, cot, chosen, wa, wb, toks, docs, told, later, *rest
+    q, k, v, o, hidden_h, gain, doc, spread_h, cot_h, chosen_h, wa, wb, toks, docs, told, later, *rest
 ):
     sources, mids = rest[:3], rest[3:9]
-    tok, stage, send, recv, local = rest[9:]
+    hidden, spread, cot, chosen, tok, stage, send, recv, local = rest[9:]
     me = Place()
     x, yh, z, c, p = me.x, me.yh, me.z, me.c, me.y
     sibling = me.device(c=1 - c)
@@ -174,6 +174,7 @@
     ring_y = (me.at_y(after(p)), me.at_y(before(p)))
     go = Copies(send, recv, local)
     route = Route(me, go)
+    pulls = [go.keep(a, b) for a, b in ((hidden_h, hidden), (spread_h, spread), (cot_h, cot), (chosen_h, chosen))]
     greet(route.everyone())
     slots, block = spread.shape[0], 256
 
@@ -222,6 +223,8 @@
 
     pairs = [go.put(part(ref, cols, 1 - yh), to, pair) for ref, cols, to in shards]
     kept = [go.keep(part(ref, cols, yh), to) for ref, cols, to in shards]
+    for pull in pulls:
+        pull.wait()
     rows = hidden[...].astype(F32)
     tok[...] = (rows * unit_rows(rows) * gain[...]).astype(BF16)
     for copy in kept:
@@ -317,18 +320,18 @@
             jax.ShapeDtypeStruct((*blocks, 3 * EARLY), BF16),
             jax.ShapeDtypeStruct((slots, left), BF16),
         ),
-        in_specs=[*(ANY,) * 4, VMEM, VMEM, ANY, VMEM, VMEM, VMEM],
+        in_specs=[*(ANY,) * 5, VMEM, *(ANY,) * 4],
         out_specs=(ANY,) * 6,
         scratch_shapes=[
             *(pltpu.VMEM((*blocks, EARLY), BF16) for _ in range(9)),
-            pltpu.VMEM(hidden.shape, BF16),
+            *(pltpu.VMEM(a.shape, BF16) for a in (hidden, spread, cot, chosen, hidden)),
             pltpu.VMEM((2, 256, left), BF16),
             pltpu.SemaphoreType.DMA((96,)),
             pltpu.SemaphoreType.DMA((96,)),
-            pltpu.SemaphoreType.DMA((19,)),
+            pltpu.SemaphoreType.DMA((23,)),
         ],
         compiler_params=pltpu.CompilerParams(
-            collective_id=1, has_side_effects=True, vmem_limit_bytes=24 << 20
+            collective_id=1, has_side_effects=True, vmem_limit_bytes=60 << 20
         ),
     )(query, key, value, out, hidden, gain.reshape(1, -1), docs, spread, cot, chosen)
     depth = NX * NYH * NZ * NC * rows

time: 441 us -> 432 us (0.980)
  local copies, waits for them, and re-layouts: 23.1 us -> 9.37 us
    unnamed x102 -> x64, local copies, waits for them, and re-layouts: 19.6 us -> 4.46 us
  transfers between devices with their start and end apart: 2 -> 2, of which waited for: 0 -> 0; matrix products, arithmetic and copies ran while one was open for 11% -> 11% of each run, Pallas kernels for 18% -> 19%
where the time goes in v11:
time: 432 us; the launch traced here: 427 us
  Pallas kernels  345 us (80%)
  matrix products  47.7 us (11%)
  starting transfers between devices  13.1 us (3%)
  other arithmetic  10.5 us (2%)
  local copies, waits for them, and re-layouts  9.37 us (2%)
    pallas_call x1, Pallas kernels, experts(): pl.pallas_call(experts_kernel, name='experts', cost_estimate=cost(120), o...  129 us
    pallas_call x1, Pallas kernels, gather(): pl.pallas_call(gather_kernel, name='gather_weights', cost_estimate=cost(6...  64.7 us
    pallas_call x2, Pallas kernels, reduce(): pl.pallas_call(reduce_kernel, name=f'reduce_rows_{ident}', cost_estimate=...  64.3 us
    pallas_call x1, Pallas kernels, scatter(): pl.pallas_call(scatter_kernel, name='scatter_weights', cost_estimate=cost...  48.7 us
    dot_general x6, matrix products, dot_tn(): lax.dot_general(a, b, (((0,), (0,)), ((), ())), preferred_element_type=F32)  27.7 us
    pallas_call x1, Pallas kernels, share(): pl.pallas_call(share_kernel, name=f'share_rows_{ident}', cost_estimate=co...  23.5 us
    dot_general x4, matrix products, dot_nn(): lax.dot_general(a, b, (((1,), (0,)), ((), ())), preferred_element_type=F32)  12.5 us
  transfers between devices with their start and end apart: 2, of which 0 were waited for; matrix products, arithmetic and copies ran while one was open for 11% of the time, Pallas kernels for 19%

profile of v11, /device:TPU:1, one launch (start us, length us, event | category | flops | bytes accessed | tf_op | source)
XLA Modules:
  0.0 427.3 jit_solution(12496946896798729572)
XLA Ops:
  0.6 0.8 copy.38
  1.4 0.2 convert_reduce_fusion
  1.7 0.0 copy-start.15
  1.7 0.1 convolution_select_fusion.1
  1.9 0.1 copy.40
  2.0 0.1 eq.54
  2.1 0.7 convert_element_type.74
  2.7 0.9 fusion.11.spread_h.spread.slots
  3.7 0.6 broadcast_in_dim.33.doc
  4.3 64.7 %gather_weights.1 = (bf16[4,2,4,2,32,1280]{5,4,3,2,1,0:T(8,128)(2,1)}, bf16[4,2,4,2,32,1024]{5,4,3,2,1,0:T(8,128)(2,1)}, bf16[4,128,2048]{2,1,0:T(8,128)(2,1)}, ...) custom-call(bf16[32,2048]{1,0:T(8,128)(2,1)} %q.1, ...), custom_call_target="tpu_custom_call" | custom-call | bytes 216000000 | tf_op jit(solution)/shard_map/gather_weights/pallas_call | solution.py:311
  68.9 5.0 %all-to-all-start = ((bf16[128,8,1408]{2,1,0:T(8,128)(2,1)}), bf16[128,8,1408]{2,1,0:T(8,128)(2,1)}, u32[]{:S(2)}, u32[]{:S(2)}) async-start(bf16[128,8,1408]{2,1,0:T(8,128)(2,1)} %bitcast.87), calls=%async_computation | async-start | bytes 5767168 | tf_op jit(solution)/shard_map/all_to_all | solution.py:1215
  74.0 0.9 slice.27
  74.9 0.3 select_reduce_fusion
  75.2 1.0 fusion.13
  76.2 0.2 pad_maximum_fusion
  76.4 0.2 fusion.12.bias
  76.6 0.0 copy-start.6
  76.6 0.0 copy-start.7
  76.6 5.5 %fusion.19.raw = f32[512,1280]{1,0:T(8,128)S(1)} fusion(bf16[512,2048]{1,0:T(8,128)(2,1)S(1)} %bitcast.107, bf16[2048,1280]{1,0:T(8,128)(2,1)} %bitcast.99), kind=kOutput, calls=%fused_computation.75 | convolution fusion | flops 2684354560 | bytes 9961472 | tf_op jit(solution)/shard_map/dot_general | solution.py:28
  82.2 0.0 copy-start
  82.2 8.1 %attend.1 = (bf16[512,1024]{1,0:T(8,128)(2,1)S(1)}, bf16[512,256]{1,0:T(8,128)(2,1)S(1)}, f32[2,8,256,256]{3,2,1,0:T(8,128)S(1)}, bf16[512,1024]{1,0:T(8,128)(2,1)S(1)}) custom-call(f32[512,1280]{1,0:T(8,128)S(1)} %fusion.19.raw, f32[2,256,256]{2,1,0:T(8,128)S(1)} %fusion.12.bias, f32[512,128]{1,0:T(8,128)S(1)} %get-tuple-element.123.cosine, ...), custom_call_target="tpu_custom_call" | custom-call | bytes 28800000 | tf_op jit(solution)/shard_map/attend/pallas_call | solution.py:720
  90.3 0.0 copy-start.3
  90.3 0.0 copy-start.8
  90.3 2.4 convolution_convert_fusion.2
  92.7 0.0 copy-start.10
  92.7 0.0 copy-start.16
  92.8 31.9 %reduce_rows_2.1 = f32[128,2048]{1,0:T(8,128)S(1)} custom-call(bf16[4,128,2048]{2,1,0:T(8,128)(2,1)S(1)} %bitcast.75), custom_call_target="tpu_custom_call" | custom-call | bytes 3600000 | tf_op jit(solution)/shard_map/reduce_rows_2/pallas_call | solution.py:455
  124.7 0.1 pad.3.clone
  124.7 0.3 multiply_reduce_fusion.2
  125.1 1.0 multiply_convert_fusion.tokens
  126.0 1.6 fusion.18
  127.6 0.2 fusion.15
  127.8 129.2 %experts.1 = (bf16[4,2,4,2,2,8,2048]{6,5,4,3,2,1,0:T(8,128)(2,1)}, bf16[1024,768]{1,0:T(8,128)(2,1)}, bf16[1024,768]{1,0:T(8,128)(2,1)}, bf16[1024,768]{1,0:T(8,...) custom-call(bf16[128,2048]{1,0:T(8,128)(2,1)} %multiply_convert_fusion.tokens, ...), custom_call_target="tpu_custom_call" | custom-call | bytes 432000000 | tf_op jit(solution)/shard_map/experts/pallas_call | solution.py:1107
  257.0 0.0 copy-start.13
  257.0 1.1 multiply_reduce_fusion.3
  258.1 2.3 convolution_convert_fusion.4
  260.4 2.0 multiply_reduce_fusion
  262.5 1.5 fusion.17
  264.0 23.5 %share_rows_3.1 = (bf16[4,128,2048]{2,1,0:T(8,128)(2,1)}, bf16[16,128]{1,0:T(8,128)(2,1)}) custom-call(bf16[128,2048]{1,0:T(8,128)(2,1)} %get-tuple-element.102.tok, bf16[4,2,4,2,2,16,128]{6,5,4,3,2,1,0:T(8,128)(2,1)} %bitcast.88), custom_call_target="tpu_custom_call" | custom-call | bytes 72000000 | tf_op jit(solution)/shard_map/share_rows_3/pallas_call | solution.py:397
  287.5 8.1 %all-to-all-start.1 = ((bf16[128,8,2048]{2,1,0:T(8,128)(2,1)}), bf16[128,8,2048]{2,1,0:T(8,128)(2,1)}, u32[]{:S(2)}, u32[]{:S(2)}) async-start(bf16[128,8,2048]{2,1,0:T(8,128)(2,1)} %bitcast.82), calls=%async_computation.1 | async-start | bytes 8388608 | tf_op jit(solution)/shard_map/all_to_all | solution.py:1252
  295.6 0.0 copy-start.1
  295.6 5.3 %convolution_convert_fusion.5.grad_mixed = bf16[512,1024]{1,0:T(8,128)(2,1)S(1)} fusion(bf16[512,2048]{1,0:T(8,128)(2,1)} %bitcast.109, bf16[2048,1024]{1,0:T(8,128)(2,1)} %bitcast.103), kind=kOutput, calls=%fused_computation.15 | convolution fusion | flops 2148007936 | bytes 7340032 | tf_op jit(solution)/shard_map/dot_general | solution.py:28
  301.0 6.7 %attend_back.1 = (bf16[512,1280]{1,0:T(8,128)(2,1)S(1)}, f32[2,128]{1,0:T(2,128)S(1)}) custom-call(f32[512,1280]{1,0:T(8,128)S(1)} %copy-done.1, f32[512,128]{1,0:T(8,128)S(1)} %get-tuple-element.123.cosine, f32[512,128]{1,0:T(8,128)S(1)} %get-tuple-element.124.signed, f32[1,128]{1,0:T(1,128)S(1)} %bitcast.78, f32[1,128]{1,0:T(1,128)S(1)} %bitcast.80, ...), custom_call_target="tpu_custom_call" | custom-call | bytes 3600000 | tf_op jit(solution)/shard_map/attend_back/pallas_call | solution.py:797
  307.7 2.1 slice.31
  309.8 0.1 copy-done.14
  309.9 5.5 %fusion = f32[768,2048]{1,0:T(8,128)} fusion(bf16[1024,768]{1,0:T(8,128)(2,1)S(1)} %copy-done.25, bf16[1024,1280]{1,0:T(8,128)(2,1)S(1)} %slice.31, bf16[1024,768]{1,0:T(8,128)(2,1)S(1)} %bitcast.90), kind=kOutput, calls=%fused_computation.1 | convolution fusion | flops 3229614080 | bytes 12058624 | tf_op jit(solution)/shard_map/dot_general | solution.py:24
  315.3 3.1 convolution_convert_fusion.3
  318.5 5.4 %fusion.21 = f32[2048,768]{1,0:T(8,128)} fusion(bf16[1024,2048]{1,0:T(8,128)(2,1)S(1)} %bitcast.105, bf16[1024,768]{1,0:T(8,128)(2,1)S(1)} %copy-done.24), kind=kOutput, calls=%fused_computation.77 | convolution fusion | flops 3221225472 | bytes 12058624 | tf_op jit(solution)/shard_map/dot_general | solution.py:24
  323.9 5.4 %fusion.20 = f32[2048,768]{1,0:T(8,128)} fusion(bf16[1024,2048]{1,0:T(8,128)(2,1)S(1)} %bitcast.106, bf16[1024,768]{1,0:T(8,128)(2,1)S(1)} %copy-done.23), kind=kOutput, calls=%fused_computation.76 | convolution fusion | flops 3221225472 | bytes 12058624 | tf_op jit(solution)/shard_map/dot_general | solution.py:24
  329.4 32.4 %reduce_rows_4.1 = f32[128,2048]{1,0:T(8,128)S(1)} custom-call(bf16[4,128,2048]{2,1,0:T(8,128)(2,1)S(1)} %bitcast.74), custom_call_target="tpu_custom_call" | custom-call | bytes 3600000 | tf_op jit(solution)/shard_map/reduce_rows_4/pallas_call | solution.py:455
  361.8 4.4 %convolution_convert_fusion.1 = bf16[2048,1024]{1,0:T(8,128)(2,1)} fusion(bf16[512,2048]{1,0:T(8,128)(2,1)S(1)} %bitcast.110, bf16[512,1024]{1,0:T(8,128)(2,1)S(1)} %copy-done.9), kind=kOutput, calls=%fused_computation.5 | convolution fusion | flops 2149580800 | bytes 7340032 | tf_op jit(solution)/shard_map/dot_general | solution.py:24
  366.2 4.7 %convolution_convert_fusion = bf16[2048,1280]{1,0:T(8,128)(2,1)} fusion(bf16[512,2048]{1,0:T(8,128)(2,1)S(1)} %bitcast.108, bf16[512,1280]{1,0:T(8,128)(2,1)S(1)} %get-tuple-element.75), kind=kOutput, calls=%fused_computation | convolution fusion | flops 2686976000 | bytes 8650752 | tf_op jit(solution)/shard_map/dot_general | solution.py:24
  370.9 0.3 fusion.10
  371.2 0.1 maximum_maximum_fusion.gains
  371.3 48.7 %scatter_weights.1 = (f32[32,2048]{1,0:T(8,128)S(1)}, f32[32,256]{1,0:T(8,128)S(1)}, f32[32,256]{1,0:T(8,128)S(1)}, f32[32,2048]{1,0:T(8,128)S(1)}, f32[40,128]{...) custom-call(bf16[4,2,4,2,32,1280]{5,4,3,2,1,0:T(8,128)(2,1)} %bitcast.81, ...), custom_call_target="tpu_custom_call" | custom-call | bytes 288000000 | tf_op jit(solution)/shard_map/scatter_weights/pallas_call | solution.py:643
  420.0 0.6 slice_bitcast_fusion
  420.6 0.5 slice_bitcast_fusion.2
  421.1 1.1 bitcast_convert_fusion
  422.2 1.4 fusion.9
  423.6 0.8 copy.56
  424.4 0.7 copy.57
  425.1 0.6 copy.58
  425.7 0.6 copy.59
  426.4 0.7 copy.60
  (62 shorter events, 0.2 us)
Async XLA Ops:
  1.7 2.6 copy-start.15
  68.9 57.1 %all-to-all-start = ((bf16[128,8,1408]{2,1,0:T(8,128)(2,1)}), bf16[128,8,1408]{2,1,0:T(8,128)(2,1)}, u32[]{:S(2)}, u32[]{:S(2)}) async-start(bf16[128,8,1408]{2,1,0:T(8,128)(2,1)} %bitcast.87), calls=%async_computation | async-start | bytes 5767168 | tf_op jit(solution)/shard_map/all_to_all | solution.py:1215
  74.0 2.6 copy-start.20
  76.6 5.6 %copy-start.6 = (f32[128]{0:T(128)S(1)}, f32[128]{0:T(128)}, u32[]{:S(2)}) copy-start(f32[128]{0:T(128)} %param.24) | copy-start | bytes 1540
  76.6 5.6 %copy-start.7 = (f32[128]{0:T(128)S(1)}, f32[128]{0:T(128)}, u32[]{:S(2)}) copy-start(f32[128]{0:T(128)} %param.25) | copy-start | bytes 1540
  76.6 13.7 %copy-start.18 = (bf16[4,2,4,2,32,1024]{5,4,3,2,1,0:T(8,128)(2,1)S(1)}, bf16[4,2,4,2,32,1024]{5,4,3,2,1,0:T(8,128)(2,1)}, u32[]{:S(2)}) copy-start(bf16[4,2,4,2,32,1024]{5,4,3,2,1,0:T(8,128)(2,1)} %get-tuple-element.60) | copy-start | bytes 12582916
  82.2 10.5 %copy-start = (f32[512,1280]{1,0:T(8,128)}, f32[512,1280]{1,0:T(8,128)S(1)}, u32[]{:S(2)}) copy-start(f32[512,1280]{1,0:T(8,128)S(1)} %fusion.19.raw) | copy-start | bytes 7864324
  90.3 2.4 copy-start.3
  90.3 2.4 copy-start.8
  92.7 32.0 %copy-start.10 = (bf16[128,2048]{1,0:T(8,128)(2,1)S(1)}, bf16[128,2048]{1,0:T(8,128)(2,1)}, u32[]{:S(2)}) copy-start(bf16[128,2048]{1,0:T(8,128)(2,1)} %hidden_h.1) | copy-start | bytes 1572868
  92.7 32.3 %copy-start.16 = (f32[2048]{0:T(1024)S(1)}, f32[2048]{0:T(1024)}, u32[]{:S(2)}) copy-start(f32[2048]{0:T(1024)} %param.26) | copy-start | bytes 24580
  257.0 5.5 %copy-start.13 = (bf16[128,2048]{1,0:T(8,128)(2,1)S(1)}, bf16[128,2048]{1,0:T(8,128)(2,1)}, u32[]{:S(2)}) copy-start(bf16[128,2048]{1,0:T(8,128)(2,1)} %cot_h.1) | copy-start | bytes 1572868
  287.5 83.4 %all-to-all-start.1 = ((bf16[128,8,2048]{2,1,0:T(8,128)(2,1)}), bf16[128,8,2048]{2,1,0:T(8,128)(2,1)}, u32[]{:S(2)}, u32[]{:S(2)}) async-start(bf16[128,8,2048]{2,1,0:T(8,128)(2,1)} %bitcast.82), calls=%async_computation.1 | async-start | bytes 8388608 | tf_op jit(solution)/shard_map/all_to_all | solution.py:1252
  295.6 5.3 %copy-start.1 = (f32[512,1280]{1,0:T(8,128)S(1)}, f32[512,1280]{1,0:T(8,128)}, u32[]{:S(2)}) copy-start(f32[512,1280]{1,0:T(8,128)} %copy-done) | copy-start | bytes 7864324
  295.6 5.3 %copy-start.4 = (f32[2,8,256,256]{3,2,1,0:T(8,128)S(1)}, f32[2,8,256,256]{3,2,1,0:T(8,128)}, u32[]{:S(2)}) copy-start(f32[2,8,256,256]{3,2,1,0:T(8,128)} %copy-done.3) | copy-start | bytes 12582916
  300.9 8.8 %copy-start.25 = (bf16[1024,768]{1,0:T(8,128)(2,1)S(1)}, bf16[1024,768]{1,0:T(8,128)(2,1)}, u32[]{:S(2)}) copy-start(bf16[1024,768]{1,0:T(8,128)(2,1)} %get-tuple-element.76) | copy-start | bytes 4718596
  307.7 2.2 copy-start.14
  307.7 7.6 %slice-start = ((s8[5242880]{0:T(1024)(128)(4,1)}), s8[4194304]{0:T(1024)(128)(4,1)S(1)}, s32[]{:S(2)}) async-start(s8[5242880]{0:T(1024)(128)(4,1)} %bitcast.100), calls=%async_computation.2 | async-start | bytes 8388608
  309.9 5.5 %slice-start.1 = ((s8[5242880]{0:T(1024)(128)(4,1)}), s8[1048576]{0:T(1024)(128)(4,1)S(1)}, s32[]{:S(2)}) async-start(s8[5242880]{0:T(1024)(128)(4,1)} %bitcast.100), calls=%async_computation.3 | async-start | bytes 2097152
  315.3 3.2 copy-start.19
  315.3 3.2 copy-start.24
  318.5 5.4 %copy-start.23 = (bf16[1024,768]{1,0:T(8,128)(2,1)S(1)}, bf16[1024,768]{1,0:T(8,128)(2,1)}, u32[]{:S(2)}) copy-start(bf16[1024,768]{1,0:T(8,128)(2,1)} %get-tuple-element.80) | copy-start | bytes 4718596
  329.4 32.4 %copy-start.9 = (bf16[512,1024]{1,0:T(8,128)(2,1)S(1)}, bf16[512,1024]{1,0:T(8,128)(2,1)}, u32[]{:S(2)}) copy-start(bf16[512,1024]{1,0:T(8,128)(2,1)} %copy-done.8) | copy-start | bytes 3145732
  329.4 32.4 %copy-start.22 = (bf16[4,128,2048]{2,1,0:T(8,128)(2,1)S(1)}, bf16[4,128,2048]{2,1,0:T(8,128)(2,1)}, u32[]{:S(2)}) copy-start(bf16[4,128,2048]{2,1,0:T(8,128)(2,1)} %get-tuple-element.72) | copy-start | bytes 6291460
  361.8 4.4 %copy-start.21 = (bf16[4,128,2048]{2,1,0:T(8,128)(2,1)S(1)}, bf16[4,128,2048]{2,1,0:T(8,128)(2,1)}, u32[]{:S(2)}) copy-start(bf16[4,128,2048]{2,1,0:T(8,128)(2,1)} %get-tuple-element.56) | copy-start | bytes 6291460
  366.2 4.7 %copy-start.11 = (bf16[128,2048]{1,0:T(8,128)(2,1)S(1)}, bf16[128,2048]{1,0:T(8,128)(2,1)}, u32[]{:S(2)}) copy-start(bf16[128,2048]{1,0:T(8,128)(2,1)} %hidden_h.1) | copy-start | bytes 1572868
  366.2 4.7 %copy-start.17 = (f32[2048]{0:T(1024)S(1)}, f32[2048]{0:T(1024)}, u32[]{:S(2)}) copy-start(f32[2048]{0:T(1024)} %param.19) | copy-start | bytes 24580
  366.2 5.1 %copy-start.2 = (bf16[1024,128]{1,0:T(8,128)(2,1)S(1)}, bf16[1024,128]{1,0:T(8,128)(2,1)}, u32[]{:S(2)}) copy-start(bf16[1024,128]{1,0:T(8,128)(2,1)} %fusion.11.spread_h.spread.slots) | copy-start | bytes 786436
  366.2 5.1 %copy-start.5 = (bf16[16,128]{1,0:T(8,128)(2,1)S(1)}, bf16[16,128]{1,0:T(8,128)(2,1)}, u32[]{:S(2)}) copy-start(bf16[16,128]{1,0:T(8,128)(2,1)} %get-tuple-element.86.piece) | copy-start | bytes 12292
  371.3 50.9 %copy-start.12 = (f32[128,2048]{1,0:T(8,128)S(1)}, f32[128,2048]{1,0:T(8,128)}, u32[]{:S(2)}) copy-start(f32[128,2048]{1,0:T(8,128)} %get-tuple-element.103) | copy-start | bytes 3145732

commit v12 on v11

--- a/solution.py
+++ b/solution.py
@@ -262,14 +262,13 @@
     ]
     low = [both(unit(before(i), j), two) for i, j, one, two, unit, slab in ways]
     high = [both(unit(after(i), j), two) for i, j, one, two, unit, slab in ways]
-    layout_later(0)
     last = []
     for (i, j, one, two, unit, slab), copies in zip(ways, far):
         arrived(copies)
         last.append(both(unit(across(i), j), two))
         tail.append(go.put(slab(j), slab(j), sibling))
+    layout_later(0)
     cross(1)
-    layout_later(1)
     half = tok.shape[0] // 2
     rows[0].wait_recv()
     piece = toks.at[before(p), pl.ds(0, half)]
@@ -284,11 +283,11 @@
             ends[n] += relay(unit(u, before(j)), unit(u, after(j)), copies[n], two)
         if copies is high:
             cross(2)
-            layout_later(2)
-            layout_later(3)
     for i, j, one, two, unit, slab in ways:
         tail.append(go.put(slab(before(j)), slab(before(j)), sibling))
         tail.append(go.put(slab(after(j)), slab(after(j)), sibling))
+    for m in range(1, slots // block):
+        layout_later(m)
     for (i, j, one, two, unit, slab), copies in zip(ways, ends):
         arrived(copies)
         tail.append(go.put(slab(across(j)), slab(across(j)), sibling))
@@ -353,7 +352,9 @@
     route = Route(me, go)
     greet(route.everyone())
     half = tok.shape[0] // 2
-    direct = [go.put(tok, toks.at[p], peer) for peer in ring]
+    halves = [pl.ds(h * half, half) for h in range(2)]
+    direct = [go.put(tok.at[halves[h]], toks.at[p, halves[h]], ring[h]) for h in range(2)]
+    others = [go.put(tok.at[halves[1 - h]], toks.at[p, halves[1 - h]], ring[h]) for h in range(2)]
     kept = go.keep(tok, toks.at[p])
     own = go.keep(part.at[x, :, :, c], got_x.at[x * NC + c])
     terms = [
@@ -379,7 +380,7 @@
     relays = []
     for h, owner in enumerate((before(p), after(p))):
         direct[h].wait_recv()
-        rows = toks.at[owner, pl.ds(h * half, half)]
+        rows = toks.at[owner, halves[h]]
         relays.append(go.put(rows, rows, ring[h]))
     arrived(terms)
     sum_z[...] = added(got_z)
@@ -387,6 +388,7 @@
     terms = [go.put(sum_z.at[at[0], at[1]], got_y.at[p], peer) for at, peer in route.peers["y"]]
     arrived(terms)
     piece[...] = added(got_y).astype(piece.dtype)
+    arrived(others)
     arrived(relays)
     kept.wait()
     go.finish()
@@ -410,8 +412,8 @@
             pltpu.VMEM((NZ, NYH, 2, rows, lanes), F32),
             pltpu.VMEM((NYH, 2, rows, lanes), F32),
             pltpu.VMEM((RING, rows, lanes), F32),
-            pltpu.SemaphoreType.DMA((17,)),
-            pltpu.SemaphoreType.DMA((17,)),
+            pltpu.SemaphoreType.DMA((19,)),
+            pltpu.SemaphoreType.DMA((19,)),
             pltpu.SemaphoreType.DMA((2,)),
         ],
         compiler_params=pltpu.CompilerParams(collective_id=ident, has_side_effects=True),
@@ -1034,8 +1036,6 @@
         pltpu.make_async_copy(a, b, puts.at[n])
         for n, (a, b) in enumerate(((inner_v, inner_low), (gate_g, grad_gate), (up_g, grad_up)))
     ]
-    for result in results:
-        result.start()
     for out in outs:
         out.wait()
 
@@ -1084,6 +1084,9 @@
                 combine(n - 3)
             elif todo and triple + crossing > 1 and crossing > 0:
                 outcome(todo.pop(0))
+        if (triple, crossing) == (1, 0):
+            for result in results:
+                result.start()
     for n in range(chunks - 3, chunks):
         combine(n)
     for copy in (*results, *pushes[-2:]):

time: 432 us -> 430 us (level)
  no operation moved by 1% of the time
where the time goes in v12:
time: 430 us; the launch traced here: 425 us
  Pallas kernels  344 us (80%)
  matrix products  47.7 us (11%)
  starting transfers between devices  12.4 us (3%)
  other arithmetic  10.5 us (2%)
  local copies, waits for them, and re-layouts  9.37 us (2%)
    pallas_call x1, Pallas kernels, experts(): pl.pallas_call(experts_kernel, name='experts', cost_estimate=cost(120), o...  129 us
    pallas_call x1, Pallas kernels, gather(): pl.pallas_call(gather_kernel, name='gather_weights', cost_estimate=cost(6...  64.7 us
    pallas_call x2, Pallas kernels, reduce(): pl.pallas_call(reduce_kernel, name=f'reduce_rows_{ident}', cost_estimate=...  64.3 us
    pallas_call x1, Pallas kernels, scatter(): pl.pallas_call(scatter_kernel, name='scatter_weights', cost_estimate=cost...  48.7 us
    dot_general x6, matrix products, dot_tn(): lax.dot_general(a, b, (((0,), (0,)), ((), ())), preferred_element_type=F32)  27.7 us
    pallas_call x1, Pallas kernels, share(): pl.pallas_call(share_kernel, name=f'share_rows_{ident}', cost_estimate=co...  22 us
    dot_general x4, matrix products, dot_nn(): lax.dot_general(a, b, (((1,), (0,)), ((), ())), preferred_element_type=F32)  12.5 us
  transfers between devices with their start and end apart: 2, of which 0 were waited for; matrix products, arithmetic and copies ran while one was open for 11% of the time, Pallas kernels for 19%

profile of v12, /device:TPU:1, one launch (start us, length us, event | category | flops | bytes accessed | tf_op | source)
XLA Modules:
  0.0 425.1 jit_solution(13658922252227929485)
XLA Ops:
  0.6 0.8 copy.38
  1.4 0.2 convert_reduce_fusion
  1.7 0.0 copy-start.15
  1.7 0.1 convolution_select_fusion.1
  1.9 0.1 copy.40
  2.0 0.1 eq.54
  2.1 0.7 convert_element_type.74
  2.7 0.9 fusion.11.spread_h.spread.slots
  3.7 0.6 broadcast_in_dim.33.doc
  4.3 64.7 %gather_weights.1 = (bf16[4,2,4,2,32,1280]{5,4,3,2,1,0:T(8,128)(2,1)}, bf16[4,2,4,2,32,1024]{5,4,3,2,1,0:T(8,128)(2,1)}, bf16[4,128,2048]{2,1,0:T(8,128)(2,1)}, ...) custom-call(bf16[32,2048]{1,0:T(8,128)(2,1)} %q.1, ...), custom_call_target="tpu_custom_call" | custom-call | bytes 216000000 | tf_op jit(solution)/shard_map/gather_weights/pallas_call | solution.py:310
  68.9 5.0 %all-to-all-start = ((bf16[128,8,1408]{2,1,0:T(8,128)(2,1)}), bf16[128,8,1408]{2,1,0:T(8,128)(2,1)}, u32[]{:S(2)}, u32[]{:S(2)}) async-start(bf16[128,8,1408]{2,1,0:T(8,128)(2,1)} %bitcast.87), calls=%async_computation | async-start | bytes 5767168 | tf_op jit(solution)/shard_map/all_to_all | solution.py:1218
  74.0 0.9 slice.27
  74.9 0.3 select_reduce_fusion
  75.2 1.0 fusion.13
  76.2 0.2 pad_maximum_fusion
  76.4 0.2 fusion.12.bias
  76.6 0.0 copy-start.6
  76.6 0.0 copy-start.7
  76.6 5.5 %fusion.19.raw = f32[512,1280]{1,0:T(8,128)S(1)} fusion(bf16[512,2048]{1,0:T(8,128)(2,1)S(1)} %bitcast.107, bf16[2048,1280]{1,0:T(8,128)(2,1)} %bitcast.99), kind=kOutput, calls=%fused_computation.75 | convolution fusion | flops 2684354560 | bytes 9961472 | tf_op jit(solution)/shard_map/dot_general | solution.py:28
  82.2 0.0 copy-start
  82.2 8.1 %attend.1 = (bf16[512,1024]{1,0:T(8,128)(2,1)S(1)}, bf16[512,256]{1,0:T(8,128)(2,1)S(1)}, f32[2,8,256,256]{3,2,1,0:T(8,128)S(1)}, bf16[512,1024]{1,0:T(8,128)(2,1)S(1)}) custom-call(f32[512,1280]{1,0:T(8,128)S(1)} %fusion.19.raw, f32[2,256,256]{2,1,0:T(8,128)S(1)} %fusion.12.bias, f32[512,128]{1,0:T(8,128)S(1)} %get-tuple-element.123.cosine, ...), custom_call_target="tpu_custom_call" | custom-call | bytes 28800000 | tf_op jit(solution)/shard_map/attend/pallas_call | solution.py:722
  90.3 0.0 copy-start.3
  90.3 0.0 copy-start.8
  90.3 2.4 convolution_convert_fusion.2
  92.7 0.0 copy-start.10
  92.7 0.0 copy-start.16
  92.8 31.9 %reduce_rows_2.1 = f32[128,2048]{1,0:T(8,128)S(1)} custom-call(bf16[4,128,2048]{2,1,0:T(8,128)(2,1)S(1)} %bitcast.75), custom_call_target="tpu_custom_call" | custom-call | bytes 3600000 | tf_op jit(solution)/shard_map/reduce_rows_2/pallas_call | solution.py:457
  124.7 0.1 pad.3.clone
  124.7 0.3 multiply_reduce_fusion.2
  125.1 1.0 multiply_convert_fusion.tokens
  126.0 1.6 fusion.18
  127.6 0.2 fusion.15
  127.8 129.3 %experts.1 = (bf16[4,2,4,2,2,8,2048]{6,5,4,3,2,1,0:T(8,128)(2,1)}, bf16[1024,768]{1,0:T(8,128)(2,1)}, bf16[1024,768]{1,0:T(8,128)(2,1)}, bf16[1024,768]{1,0:T(8,...) custom-call(bf16[128,2048]{1,0:T(8,128)(2,1)} %multiply_convert_fusion.tokens, ...), custom_call_target="tpu_custom_call" | custom-call | bytes 432000000 | tf_op jit(solution)/shard_map/experts/pallas_call | solution.py:1110
  257.0 0.0 copy-start.13
  257.1 1.1 multiply_reduce_fusion.3
  258.2 2.3 convolution_convert_fusion.4
  260.5 2.0 multiply_reduce_fusion
  262.5 1.5 fusion.17
  264.1 22.0 %share_rows_3.1 = (bf16[4,128,2048]{2,1,0:T(8,128)(2,1)}, bf16[16,128]{1,0:T(8,128)(2,1)}) custom-call(bf16[128,2048]{1,0:T(8,128)(2,1)} %get-tuple-element.102.tok, bf16[4,2,4,2,2,16,128]{6,5,4,3,2,1,0:T(8,128)(2,1)} %bitcast.88), custom_call_target="tpu_custom_call" | custom-call | bytes 72000000 | tf_op jit(solution)/shard_map/share_rows_3/pallas_call | solution.py:399
  286.0 7.3 %all-to-all-start.1 = ((bf16[128,8,2048]{2,1,0:T(8,128)(2,1)}), bf16[128,8,2048]{2,1,0:T(8,128)(2,1)}, u32[]{:S(2)}, u32[]{:S(2)}) async-start(bf16[128,8,2048]{2,1,0:T(8,128)(2,1)} %bitcast.82), calls=%async_computation.1 | async-start | bytes 8388608 | tf_op jit(solution)/shard_map/all_to_all | solution.py:1255
  293.3 0.0 copy-start.1
  293.4 5.3 %convolution_convert_fusion.5.grad_mixed = bf16[512,1024]{1,0:T(8,128)(2,1)S(1)} fusion(bf16[512,2048]{1,0:T(8,128)(2,1)} %bitcast.109, bf16[2048,1024]{1,0:T(8,128)(2,1)} %bitcast.103), kind=kOutput, calls=%fused_computation.15 | convolution fusion | flops 2148007936 | bytes 7340032 | tf_op jit(solution)/shard_map/dot_general | solution.py:28
  298.7 6.7 %attend_back.1 = (bf16[512,1280]{1,0:T(8,128)(2,1)S(1)}, f32[2,128]{1,0:T(2,128)S(1)}) custom-call(f32[512,1280]{1,0:T(8,128)S(1)} %copy-done.1, f32[512,128]{1,0:T(8,128)S(1)} %get-tuple-element.123.cosine, f32[512,128]{1,0:T(8,128)S(1)} %get-tuple-element.124.signed, f32[1,128]{1,0:T(1,128)S(1)} %bitcast.78, f32[1,128]{1,0:T(1,128)S(1)} %bitcast.80, ...), custom_call_target="tpu_custom_call" | custom-call | bytes 3600000 | tf_op jit(solution)/shard_map/attend_back/pallas_call | solution.py:799
  305.4 2.1 slice.31
  307.5 0.1 copy-done.14
  307.6 5.5 %fusion = f32[768,2048]{1,0:T(8,128)} fusion(bf16[1024,768]{1,0:T(8,128)(2,1)S(1)} %copy-done.25, bf16[1024,1280]{1,0:T(8,128)(2,1)S(1)} %slice.31, bf16[1024,768]{1,0:T(8,128)(2,1)S(1)} %bitcast.90), kind=kOutput, calls=%fused_computation.1 | convolution fusion | flops 3229614080 | bytes 12058624 | tf_op jit(solution)/shard_map/dot_general | solution.py:24
  313.1 3.1 convolution_convert_fusion.3
  316.3 5.4 %fusion.21 = f32[2048,768]{1,0:T(8,128)} fusion(bf16[1024,2048]{1,0:T(8,128)(2,1)S(1)} %bitcast.105, bf16[1024,768]{1,0:T(8,128)(2,1)S(1)} %copy-done.24), kind=kOutput, calls=%fused_computation.77 | convolution fusion | flops 3221225472 | bytes 12058624 | tf_op jit(solution)/shard_map/dot_general | solution.py:24
  321.7 5.4 %fusion.20 = f32[2048,768]{1,0:T(8,128)} fusion(bf16[1024,2048]{1,0:T(8,128)(2,1)S(1)} %bitcast.106, bf16[1024,768]{1,0:T(8,128)(2,1)S(1)} %copy-done.23), kind=kOutput, calls=%fused_computation.76 | convolution fusion | flops 3221225472 | bytes 12058624 | tf_op jit(solution)/shard_map/dot_general | solution.py:24
  327.1 32.4 %reduce_rows_4.1 = f32[128,2048]{1,0:T(8,128)S(1)} custom-call(bf16[4,128,2048]{2,1,0:T(8,128)(2,1)S(1)} %bitcast.74), custom_call_target="tpu_custom_call" | custom-call | bytes 3600000 | tf_op jit(solution)/shard_map/reduce_rows_4/pallas_call | solution.py:457
  359.5 4.4 %convolution_convert_fusion.1 = bf16[2048,1024]{1,0:T(8,128)(2,1)} fusion(bf16[512,2048]{1,0:T(8,128)(2,1)S(1)} %bitcast.110, bf16[512,1024]{1,0:T(8,128)(2,1)S(1)} %copy-done.9), kind=kOutput, calls=%fused_computation.5 | convolution fusion | flops 2149580800 | bytes 7340032 | tf_op jit(solution)/shard_map/dot_general | solution.py:24
  363.9 4.7 %convolution_convert_fusion = bf16[2048,1280]{1,0:T(8,128)(2,1)} fusion(bf16[512,2048]{1,0:T(8,128)(2,1)S(1)} %bitcast.108, bf16[512,1280]{1,0:T(8,128)(2,1)S(1)} %get-tuple-element.75), kind=kOutput, calls=%fused_computation | convolution fusion | flops 2686976000 | bytes 8650752 | tf_op jit(solution)/shard_map/dot_general | solution.py:24
  368.7 0.3 fusion.10
  369.0 0.1 maximum_maximum_fusion.gains
  369.1 48.7 %scatter_weights.1 = (f32[32,2048]{1,0:T(8,128)S(1)}, f32[32,256]{1,0:T(8,128)S(1)}, f32[32,256]{1,0:T(8,128)S(1)}, f32[32,2048]{1,0:T(8,128)S(1)}, f32[40,128]{...) custom-call(bf16[4,2,4,2,32,1280]{5,4,3,2,1,0:T(8,128)(2,1)} %bitcast.81, ...), custom_call_target="tpu_custom_call" | custom-call | bytes 288000000 | tf_op jit(solution)/shard_map/scatter_weights/pallas_call | solution.py:645
  417.8 0.6 slice_bitcast_fusion
  418.4 0.5 slice_bitcast_fusion.2
  418.9 1.1 bitcast_convert_fusion
  420.0 1.4 fusion.9
  421.4 0.8 copy.56
  422.2 0.7 copy.57
  422.9 0.6 copy.58
  423.5 0.6 copy.59
  424.1 0.7 copy.60
  (62 shorter events, 0.2 us)
Async XLA Ops:
  1.7 2.6 copy-start.15
  68.9 57.1 %all-to-all-start = ((bf16[128,8,1408]{2,1,0:T(8,128)(2,1)}), bf16[128,8,1408]{2,1,0:T(8,128)(2,1)}, u32[]{:S(2)}, u32[]{:S(2)}) async-start(bf16[128,8,1408]{2,1,0:T(8,128)(2,1)} %bitcast.87), calls=%async_computation | async-start | bytes 5767168 | tf_op jit(solution)/shard_map/all_to_all | solution.py:1218
  74.0 2.6 copy-start.20
  76.6 5.6 %copy-start.6 = (f32[128]{0:T(128)S(1)}, f32[128]{0:T(128)}, u32[]{:S(2)}) copy-start(f32[128]{0:T(128)} %param.24) | copy-start | bytes 1540
  76.6 5.6 %copy-start.7 = (f32[128]{0:T(128)S(1)}, f32[128]{0:T(128)}, u32[]{:S(2)}) copy-start(f32[128]{0:T(128)} %param.25) | copy-start | bytes 1540
  76.6 13.7 %copy-start.18 = (bf16[4,2,4,2,32,1024]{5,4,3,2,1,0:T(8,128)(2,1)S(1)}, bf16[4,2,4,2,32,1024]{5,4,3,2,1,0:T(8,128)(2,1)}, u32[]{:S(2)}) copy-start(bf16[4,2,4,2,32,1024]{5,4,3,2,1,0:T(8,128)(2,1)} %get-tuple-element.60) | copy-start | bytes 12582916
  82.2 10.5 %copy-start = (f32[512,1280]{1,0:T(8,128)}, f32[512,1280]{1,0:T(8,128)S(1)}, u32[]{:S(2)}) copy-start(f32[512,1280]{1,0:T(8,128)S(1)} %fusion.19.raw) | copy-start | bytes 7864324
  90.3 2.4 copy-start.3
  90.3 2.4 copy-start.8
  92.7 32.0 %copy-start.10 = (bf16[128,2048]{1,0:T(8,128)(2,1)S(1)}, bf16[128,2048]{1,0:T(8,128)(2,1)}, u32[]{:S(2)}) copy-start(bf16[128,2048]{1,0:T(8,128)(2,1)} %hidden_h.1) | copy-start | bytes 1572868
  92.7 32.3 %copy-start.16 = (f32[2048]{0:T(1024)S(1)}, f32[2048]{0:T(1024)}, u32[]{:S(2)}) copy-start(f32[2048]{0:T(1024)} %param.26) | copy-start | bytes 24580
  257.0 5.5 %copy-start.13 = (bf16[128,2048]{1,0:T(8,128)(2,1)S(1)}, bf16[128,2048]{1,0:T(8,128)(2,1)}, u32[]{:S(2)}) copy-start(bf16[128,2048]{1,0:T(8,128)(2,1)} %cot_h.1) | copy-start | bytes 1572868
  286.0 82.7 %all-to-all-start.1 = ((bf16[128,8,2048]{2,1,0:T(8,128)(2,1)}), bf16[128,8,2048]{2,1,0:T(8,128)(2,1)}, u32[]{:S(2)}, u32[]{:S(2)}) async-start(bf16[128,8,2048]{2,1,0:T(8,128)(2,1)} %bitcast.82), calls=%async_computation.1 | async-start | bytes 8388608 | tf_op jit(solution)/shard_map/all_to_all | solution.py:1255
  293.3 5.3 %copy-start.1 = (f32[512,1280]{1,0:T(8,128)S(1)}, f32[512,1280]{1,0:T(8,128)}, u32[]{:S(2)}) copy-start(f32[512,1280]{1,0:T(8,128)} %copy-done) | copy-start | bytes 7864324
  293.4 5.3 %copy-start.4 = (f32[2,8,256,256]{3,2,1,0:T(8,128)S(1)}, f32[2,8,256,256]{3,2,1,0:T(8,128)}, u32[]{:S(2)}) copy-start(f32[2,8,256,256]{3,2,1,0:T(8,128)} %copy-done.3) | copy-start | bytes 12582916
  298.7 8.8 %copy-start.25 = (bf16[1024,768]{1,0:T(8,128)(2,1)S(1)}, bf16[1024,768]{1,0:T(8,128)(2,1)}, u32[]{:S(2)}) copy-start(bf16[1024,768]{1,0:T(8,128)(2,1)} %get-tuple-element.76) | copy-start | bytes 4718596
  305.4 2.2 copy-start.14
  305.4 7.6 %slice-start = ((s8[5242880]{0:T(1024)(128)(4,1)}), s8[4194304]{0:T(1024)(128)(4,1)S(1)}, s32[]{:S(2)}) async-start(s8[5242880]{0:T(1024)(128)(4,1)} %bitcast.100), calls=%async_computation.2 | async-start | bytes 8388608
  307.6 5.5 %slice-start.1 = ((s8[5242880]{0:T(1024)(128)(4,1)}), s8[1048576]{0:T(1024)(128)(4,1)S(1)}, s32[]{:S(2)}) async-start(s8[5242880]{0:T(1024)(128)(4,1)} %bitcast.100), calls=%async_computation.3 | async-start | bytes 2097152
  313.1 3.2 copy-start.19
  313.1 3.2 copy-start.24
  316.3 5.4 %copy-start.23 = (bf16[1024,768]{1,0:T(8,128)(2,1)S(1)}, bf16[1024,768]{1,0:T(8,128)(2,1)}, u32[]{:S(2)}) copy-start(bf16[1024,768]{1,0:T(8,128)(2,1)} %get-tuple-element.80) | copy-start | bytes 4718596
  327.1 32.4 %copy-start.9 = (bf16[512,1024]{1,0:T(8,128)(2,1)S(1)}, bf16[512,1024]{1,0:T(8,128)(2,1)}, u32[]{:S(2)}) copy-start(bf16[512,1024]{1,0:T(8,128)(2,1)} %copy-done.8) | copy-start | bytes 3145732
  327.1 32.4 %copy-start.22 = (bf16[4,128,2048]{2,1,0:T(8,128)(2,1)S(1)}, bf16[4,128,2048]{2,1,0:T(8,128)(2,1)}, u32[]{:S(2)}) copy-start(bf16[4,128,2048]{2,1,0:T(8,128)(2,1)} %get-tuple-element.72) | copy-start | bytes 6291460
  359.5 4.4 %copy-start.21 = (bf16[4,128,2048]{2,1,0:T(8,128)(2,1)S(1)}, bf16[4,128,2048]{2,1,0:T(8,128)(2,1)}, u32[]{:S(2)}) copy-start(bf16[4,128,2048]{2,1,0:T(8,128)(2,1)} %get-tuple-element.56) | copy-start | bytes 6291460
  363.9 4.7 %copy-start.11 = (bf16[128,2048]{1,0:T(8,128)(2,1)S(1)}, bf16[128,2048]{1,0:T(8,128)(2,1)}, u32[]{:S(2)}) copy-start(bf16[128,2048]{1,0:T(8,128)(2,1)} %hidden_h.1) | copy-start | bytes 1572868
  363.9 4.7 %copy-start.17 = (f32[2048]{0:T(1024)S(1)}, f32[2048]{0:T(1024)}, u32[]{:S(2)}) copy-start(f32[2048]{0:T(1024)} %param.19) | copy-start | bytes 24580
  363.9 5.1 %copy-start.2 = (bf16[1024,128]{1,0:T(8,128)(2,1)S(1)}, bf16[1024,128]{1,0:T(8,128)(2,1)}, u32[]{:S(2)}) copy-start(bf16[1024,128]{1,0:T(8,128)(2,1)} %fusion.11.spread_h.spread.slots) | copy-start | bytes 786436
  363.9 5.1 %copy-start.5 = (bf16[16,128]{1,0:T(8,128)(2,1)S(1)}, bf16[16,128]{1,0:T(8,128)(2,1)}, u32[]{:S(2)}) copy-start(bf16[16,128]{1,0:T(8,128)(2,1)} %get-tuple-element.86.piece) | copy-start | bytes 12292
  369.1 50.9 %copy-start.12 = (f32[128,2048]{1,0:T(8,128)S(1)}, f32[128,2048]{1,0:T(8,128)}, u32[]{:S(2)}) copy-start(f32[128,2048]{1,0:T(8,128)} %get-tuple-element.103) | copy-start | bytes 3145732
